TPU v7x, 256 devices: a whole 4x4x8 slice. The times are simulated.
256 devices in a mesh: chain: 4 (over z_lo, core), mesh: 16 (over z_hi, y), probe: 4 (over x).
Axes of the slice: x: 4, y: 4, z: 8 (z_hi: 4, z_lo: 2; z = z_hi * 2 + z_lo), core: 2. Of those that a mesh axis runs over, the one named last changes fastest.
Arguments:
- signs: int32 [256, 8, 4096], P('probe', 'chain', 'mesh'), may hold values from 0 to 1
- border_signs: int32 [256, 512], P('probe'), may hold values from 0 to 1
- inverse_factors: bfloat16 [8, 4096, 4096], P('chain', 'mesh'), may hold values from -2 to 2, as said below
- couplings: bfloat16 [8, 32, 4, 128, 128], P('chain', 'mesh'), may hold values from -0.15625 to 0.15625
- coupling_cols: int32 [8, 32, 4], P('chain', 'mesh'), may hold values from 0 to 31, all different within a row
- border_rows: bfloat16 [8, 512, 4096], P('chain', None, 'mesh'), may hold values from -0.046875 to 0.046875
- border_inverse: bfloat16 [512, 512], replicated, may hold values from -2 to 2, as said below
Outputs:
- solved: bfloat16 [256, 8, 4096], P('probe', 'chain', 'mesh')
- border_solved: float32 [256, 512], P('probe')
- node_var: float32 [8, 4096], P('chain', 'mesh')
- border_var: float32 [512], replicated
Inputs may be any that keep to these rules, and one draw needn't show every extreme that they name: `inverse_factors`: lower triangular; diagonal entries between 0.5 and 2. `border_inverse`: lower triangular; diagonal entries between 0.5 and 2. `coupling_cols`: the 4 block columns of one block row differ.
All inputs are finite; a program needn't handle non-finite values.
Results may differ from a plain program's by a relative error of at most 0.015.
Values may be sent and summed in bfloat16 or wider, within the bound.
No kernel may reach another device: no remote copies, remote signals or barrier semaphores. Data moves between devices by JAX's collectives and lax.ppermute only.
A program may use at most 64 MiB of HBM per device.

v0:
```python
import functools

import jax
import jax.numpy as jnp
from jax import lax
from jax.experimental import pallas as pl
from jax.experimental.pallas import tpu as pltpu
from jax.sharding import Mesh, PartitionSpec as P

AXES = ("zl", "core", "zh", "y", "x")
CHAIN, NODES = ("zl", "core"), ("zh", "y")
NT = (((1,), (1,)), ((), ()))


def start_one_of(use_first, first, second):
    @pl.when(use_first)
    def _():
        for copy in first:
            copy.start()

    @pl.when(jnp.logical_not(use_first))
    def _():
        for copy in second:
            copy.start()


def arrange_kernel(place, own_ref, other_ref, *refs, per_core):
    outs, sems = refs[:-1], refs[-1]

    def copies(source, step):
        return [pltpu.make_async_copy(source(step % per_core), outs[step], sems.at[step])]

    waits = []
    for step in range(len(outs)):
        own, other = copies(own_ref, step), copies(other_ref, step)
        start_one_of(place[0] == step // per_core, own, other)
        waits += own
    for copy in waits:
        copy.wait()


def factor_kernel(place, own_ref, other_ref, *refs, per_core):
    arrange_kernel(place, lambda i: own_ref.at[i], lambda i: other_ref.at[i], *refs, per_core=per_core)


def coupling_kernel(place, own_ref, other_ref, after, *refs, per_core):
    size = refs[0].shape[1]
    arrange_kernel(
        place,
        lambda i: own_ref.at[:, pl.ds(i * size, size)],
        lambda i: other_ref.at[:, pl.ds(i * size, size)],
        *refs,
        per_core=per_core,
    )


def couple_kernel(cols, x_ref, s_ref, c_ref, out_ref, *, step, slots):
    lines, tall, block = c_ref.shape
    rows = tall // (slots * block)
    per = x_ref.shape[2] // block
    probes = x_ref.shape[1]

    def body(k, carry):
        for row in range(rows):
            total = None
            for slot in range(0, slots, 2):
                left, right = [], []
                for pair in range(2):
                    col = cols[k, (step * rows + row) * slots + slot + pair]
                    lanes = pl.ds(pl.multiple_of((col % per) * block, block), block)
                    left.append(x_ref[col // per, :, lanes])
                    at = (row * slots + slot + pair) * block
                    right.append(c_ref[k, at : at + block, :])
                term = lax.dot_general(
                    jnp.concatenate(left, axis=1),
                    jnp.concatenate(right, axis=1),
                    NT,
                    preferred_element_type=jnp.float32,
                )
                total = term if total is None else total + term
            at = (row * s_ref.shape[1]) // rows + step * probes
            source = s_ref[k, at : at + probes, :].astype(jnp.float32)
            lanes = pl.ds(pl.multiple_of((k * rows + row) * block, block), block)
            out_ref[:, lanes] = (source - total).astype(jnp.bfloat16)
        return carry

    lax.fori_loop(0, lines, body, 0)


def finish(total, outs):
    result = total.astype(jnp.bfloat16)
    outs[0][...] = result
    if len(outs) > 1:
        for peer in range(outs[1].shape[0]):
            outs[1][peer] = result


def first_kernel(r_ref, l_ref, *outs):
    width = r_ref.shape[2]

    def body(i, total):
        for j in range(4):
            lanes = pl.ds(pl.multiple_of((i * 4 + j) * width, width), width)
            total = total + lax.dot_general(
                r_ref[i * 4 + j], l_ref[:, lanes], NT, preferred_element_type=jnp.float32
            )
        return total

    start = jnp.zeros((r_ref.shape[1], l_ref.shape[0]), jnp.float32)
    finish(lax.fori_loop(0, r_ref.shape[0] // 4, body, start), outs)


def apply_kernel(place, *refs, lines):
    pieces, l_ref, outs = refs[:lines], refs[lines], refs[lines + 1 :]
    width = l_ref.shape[0]

    def body(zh, total):
        for k in range(lines):
            y = lax.rem(place[2] + lines - k, lines)
            lanes = pl.ds(pl.multiple_of((zh * lines + y) * width, width), width)
            here = pl.ds(pl.multiple_of(zh * width, width), width)
            total = total + lax.dot_general(
                pieces[k][:, here], l_ref[:, lanes], NT, preferred_element_type=jnp.float32
            )
        return total

    start = jnp.zeros((pieces[0].shape[0], width), jnp.float32)
    finish(lax.fori_loop(0, pieces[0].shape[1] // width, body, start), outs)


VMEM = pl.BlockSpec(memory_space=pltpu.VMEM)
SMEM = pl.BlockSpec(memory_space=pltpu.SMEM)
HBM = pl.BlockSpec(memory_space=pltpu.HBM)
PARAMS = pltpu.CompilerParams(vmem_limit_bytes=16 << 20)


def arrange(kernel, place, own, other, steps, shape, name, *after):
    return pl.pallas_call(
        functools.partial(kernel, per_core=steps // 2),
        out_shape=tuple([jax.ShapeDtypeStruct(shape, jnp.bfloat16)] * steps),
        in_specs=[SMEM] + [HBM] * (2 + len(after)),
        out_specs=tuple([HBM] * steps),
        scratch_shapes=[pltpu.SemaphoreType.DMA((steps,))],
        compiler_params=PARAMS,
        cost_estimate=pl.CostEstimate(
            flops=0, transcendentals=0, bytes_accessed=4 * steps * shape[0] * shape[1]
        ),
        name=name,
    )(place, own, other, *after)


def couple(cols, pieces, source, c, step, slots):
    lines, tall, block = c.shape
    return pl.pallas_call(
        functools.partial(couple_kernel, step=step, slots=slots),
        out_shape=jax.ShapeDtypeStruct((pieces.shape[1], lines * tall // slots), jnp.bfloat16),
        in_specs=[SMEM, VMEM, VMEM, VMEM],
        out_specs=VMEM,
        compiler_params=PARAMS,
        name="couple",
    )(cols, pieces, source, c)


def apply_factor(place, pieces, factor, peers):
    first = not isinstance(pieces, list)
    probes = pieces.shape[1] if first else pieces[0].shape[0]
    rows = factor.shape[0]
    shapes = [jax.ShapeDtypeStruct((probes, rows), jnp.bfloat16)]
    if peers:
        shapes.append(jax.ShapeDtypeStruct((peers, probes, rows), jnp.bfloat16))
    kernel = first_kernel if first else functools.partial(apply_kernel, lines=len(pieces))
    operands = (pieces, factor) if first else (place, *pieces, factor)
    return pl.pallas_call(
        kernel,
        out_shape=tuple(shapes),
        in_specs=[VMEM, VMEM] if first else [SMEM] + [VMEM] * (len(pieces) + 1),
        out_specs=tuple([VMEM] * len(shapes)),
        compiler_params=PARAMS,
        name="apply",
    )(*operands)


def line(value, axis):
    size = lax.axis_size(axis)
    moved = {
        k: lax.ppermute(value, axis, [(i, (i + k) % size) for i in range(size)])
        for k in range(1, size)
    }
    return [value] + [moved[k] for k in range(1, size)]


def swap(value):
    return lax.ppermute(value, "core", [(0, 1), (1, 0)])


def shards(
    signs, border_signs, inverse_factors, couplings, coupling_cols, border_rows, border_inverse
):
    local_probes, own_steps, local = signs.shape
    cores, turns = lax.axis_size("core"), lax.axis_size("zl")
    peers = lax.axis_size("zh") * lax.axis_size("y")
    probes = local_probes // cores
    steps = own_steps * cores
    core = lax.axis_index("core")
    first = core == 0
    place = jnp.stack([core, lax.axis_index("zh"), lax.axis_index("y")]).astype(jnp.int32)

    def in_order(own, other):
        return jnp.concatenate([jnp.where(first, own, other), jnp.where(first, other, own)], axis=0)

    source = (2 * signs - 1).astype(jnp.bfloat16).reshape(cores, probes, own_steps, local)
    source = source.transpose(0, 2, 1, 3)
    other_half = swap(jnp.where(first, source[1], source[0]))
    source = in_order(jnp.where(first, source[0], source[1]), other_half)
    spread = jnp.broadcast_to(source[0][None], (peers, probes, local))
    begin = lax.all_to_all(spread, NODES, 0, 0)
    slots, block = couplings.shape[2:4]
    cols = in_order(coupling_cols, swap(coupling_cols)).reshape(1, -1).astype(jnp.bfloat16)
    width = cols.shape[1]
    cols = jnp.pad(cols, ((0, 15), (0, block - width)))
    flat = source.reshape(steps * probes, local)
    halves = [flat[:, i : i + block] for i in range(0, local, block)]
    bundle = jnp.concatenate([couplings.reshape(-1, block)] + halves + [cols], axis=0)
    shared = lax.all_gather(bundle, "zh", axis=0)
    at = couplings.size // block
    until = at + steps * probes * local // block
    tall = at // own_steps

    factors = arrange(
        factor_kernel, place, inverse_factors, swap(inverse_factors), steps, inverse_factors.shape[1:], "factors"
    )

    pieces = None
    for turn in range(turns):
        results = []
        for step in range(steps):
            if pieces is None:
                resid = begin
            else:
                resid = line(couple(cols, pieces, source, blocks[step], step, slots), "y")
            more = step + 1 < steps
            outs = apply_factor(place, resid, factors[step], peers if more else 0)
            results.append(outs[0])
            if turn + step == 0:
                shared, after = lax.optimization_barrier((shared, outs[0]))
                source = shared[:, at:until]
                cols = shared[:, until, :width].astype(jnp.int32)
                blocks = arrange(
                    coupling_kernel, place, shared, swap(shared), steps, (shared.shape[0], tall, block), "couplings", after
                )
            if more:
                pieces = lax.all_to_all(outs[1], NODES, 0, 0)
        if turn + 1 < turns:
            moved = lax.ppermute(outs[0], "zl", [(turn, turn + 1)])
            pieces = lax.all_to_all(jnp.broadcast_to(moved[None], (peers, probes, local)), NODES, 0, 0)

    rows4 = in_order(border_rows, swap(border_rows))
    partial = jnp.zeros((probes, border_rows.shape[1]), jnp.float32)
    for step in range(steps):
        partial = partial + lax.dot_general(results[step], rows4[step], NT, preferred_element_type=jnp.float32)
    for axis in ("y", "zh", "zl"):
        partial = functools.reduce(jnp.add, line(partial, axis))
    halves = border_signs.reshape(cores, probes, -1)
    border_source = (2 * jnp.where(first, halves[0], halves[1]) - 1).astype(jnp.float32)
    border_resid = (border_source - partial).astype(jnp.bfloat16)
    own_border = lax.dot_general(border_resid, border_inverse, NT, preferred_element_type=jnp.float32)
    border_solved = in_order(own_border, swap(own_border))

    solved4 = jnp.stack(results)
    mine = jnp.where(first, solved4[:own_steps], solved4[own_steps:])
    theirs = swap(jnp.where(first, solved4[own_steps:], solved4[:own_steps]))
    solved = jnp.concatenate([jnp.where(first, mine, theirs), jnp.where(first, theirs, mine)], axis=1)
    solved = solved.transpose(1, 0, 2)

    total_probes = local_probes * lax.axis_size("x")
    node_sums = jnp.sum(jnp.square(solved.astype(jnp.float32)), axis=0)
    border_sums = jnp.sum(jnp.square(border_solved), axis=0)
    node_sums, border_sums = lax.psum((node_sums, border_sums), "x")
    return solved, border_solved, node_sums / total_probes, border_sums / total_probes


def solution(mesh):
    sizes = mesh.shape
    devices = mesh.devices.reshape(2, sizes["chain"] // 2, 4, sizes["mesh"] // 4, sizes["probe"])
    return jax.shard_map(
        shards,
        mesh=Mesh(devices, AXES),
        in_specs=(
            P("x", CHAIN, NODES),
            P("x", None),
            P(CHAIN, NODES, None),
            P(CHAIN, NODES, None, None, None),
            P(CHAIN, NODES, None),
            P(CHAIN, None, NODES),
            P(),
        ),
        out_specs=(P("x", CHAIN, NODES), P("x", None), P(CHAIN, NODES), P()),
        check_vma=False,
    )
```

profile of v0, /device:TPU:1, one launch (start us, length us, event | category | flops | bytes accessed | tf_op | source)
XLA Modules:
  0.0 324.3 jit_solution(5067690691768473704)
XLA Ops:
  8.2 3.3 %collective-permute-start = (bf16[2,32,256]{2,1,0:T(8,128)(2,1)S(1)}, bf16[2,32,256]{2,1,0:T(8,128)(2,1)S(1)}, u32[]{:S(2)}, u32[]{:S(2)}) collective-permute-start(bf16[2,32,256]{2,1,0:T(8,128)(2,1)S(1)} %select_bitcast_fusion), channel_id=1, source_target_pairs={{0,64},{64,0},{1,65},{65,1},{2,66},{66,2},{3,67},{67,3},{4,68},{68... | collective-permute-start | bytes 98312 | tf_op jit(solution)/shard_map/ppermute | solution.py:193
  13.8 1.9 fusion.3
  16.4 9.2 %all-to-all-start = ((bf16[16,32,256]{2,1,0:T(8,128)(2,1)}), bf16[16,32,256]{2,1,0:T(8,128)(2,1)S(1)}, u32[]{:S(2)}, u32[]{:S(2)}) async-start(bf16[16,32,256]{2,1,0:T(8,128)(2,1)} %broadcast_in_dim.14), calls=%async_computation | async-start | bytes 524288 | tf_op jit(solution)/shard_map/all_to_all | solution.py:216
  25.7 2.2 copy-done.19
  27.9 3.1 factors.1
  36.4 1.6 copy-done.5
  38.0 1.8 apply.8
  39.8 33.4 %all-gather.3.cloned.1.call-done = bf16[9280,128]{1,0:T(8,128)(2,1)} async-done(((bf16[2320,128]{1,0:T(8,128)(2,1)}), bf16[9280,128]{1,0:T(8,128)(2,1)}) %all-gather.3.cloned.1.call-update) | async-done | bytes 2375696 | tf_op jit(solution)/shard_map/all_gather | solution.py:224
  73.6 9.0 %all-to-all-start.1 = ((bf16[16,32,256]{2,1,0:T(8,128)(2,1)}), bf16[16,32,256]{2,1,0:T(8,128)(2,1)S(1)}, u32[]{:S(2)}, u32[]{:S(2)}) async-start(bf16[16,32,256]{2,1,0:T(8,128)(2,1)} %get-tuple-element.27), calls=%async_computation.1 | async-start | bytes 524288 | tf_op jit(solution)/shard_map/all_to_all | solution.py:252
  84.3 1.7 copy-done.20
  86.0 2.1 couplings.1
  96.3 2.3 collective-permute-start.5
  101.7 1.6 copy-done.2
  103.3 2.2 apply.9
  105.5 18.9 %all_to_all.40.x_ref = bf16[16,32,256]{2,1,0:T(8,128)(2,1)S(1)} all-to-all(bf16[16,32,256]{2,1,0:T(8,128)(2,1)S(1)} %get-tuple-element.31), channel_id=1, replica_groups=mesh['zl'=2,'core'=2,'zh'=4,'y'=4,'x'=4] {'zh','y'}, dimensions={0} | all-to-all | bytes 524288 | tf_op jit(solution)/shard_map/all_to_all | solution.py:252
  125.8 2.6 collective-permute-start.8
  128.4 1.5 collective-permute-start.9
  131.5 2.2 apply.10
  133.8 15.2 %all_to_all.41.x_ref = bf16[16,32,256]{2,1,0:T(8,128)(2,1)S(1)} all-to-all(bf16[16,32,256]{2,1,0:T(8,128)(2,1)S(1)} %get-tuple-element.34), channel_id=1, replica_groups=mesh['zl'=2,'core'=2,'zh'=4,'y'=4,'x'=4] {'zh','y'}, dimensions={0} | all-to-all | bytes 524288 | tf_op jit(solution)/shard_map/all_to_all | solution.py:252
  150.4 2.2 collective-permute-start.11
  156.0 1.6 apply.11
  157.6 2.6 collective-permute-start.13
  161.1 15.6 %all_to_all.42.x_ref = bf16[16,32,256]{2,1,0:T(8,128)(2,1)S(1)} all-to-all(bf16[16,32,256]{2,1,0:T(8,128)(2,1)S(1)} %broadcast_in_dim.15), channel_id=1, replica_groups=mesh['zl'=2,'core'=2,'zh'=4,'y'=4,'x'=4] {'zh','y'}, dimensions={0} | all-to-all | bytes 524288 | tf_op jit(solution)/shard_map/all_to_all | solution.py:255
  178.3 1.9 collective-permute-start.15
  181.8 2.1 collective-permute-done.14.refs_1_
  184.4 1.6 apply.12
  186.0 14.5 %all_to_all.43.x_ref = bf16[16,32,256]{2,1,0:T(8,128)(2,1)S(1)} all-to-all(bf16[16,32,256]{2,1,0:T(8,128)(2,1)S(1)} %get-tuple-element.39), channel_id=1, replica_groups=mesh['zl'=2,'core'=2,'zh'=4,'y'=4,'x'=4] {'zh','y'}, dimensions={0} | all-to-all | bytes 524288 | tf_op jit(solution)/shard_map/all_to_all | solution.py:252
  202.0 2.5 collective-permute-start.18
  208.3 2.4 apply.13
  210.7 5.3 %all-to-all-start.6 = ((bf16[16,32,256]{2,1,0:T(8,128)(2,1)}), bf16[16,32,256]{2,1,0:T(8,128)(2,1)S(1)}, u32[]{:S(2)}, u32[]{:S(2)}) async-start(bf16[16,32,256]{2,1,0:T(8,128)(2,1)} %get-tuple-element.41), calls=%async_computation.6 | async-start | bytes 524288 | tf_op jit(solution)/shard_map/all_to_all | solution.py:252
  215.9 14.5 %collective-permute-start.27 = (bf16[2,512,256]{2,1,0:T(8,128)(2,1)}, bf16[2,512,256]{2,1,0:T(8,128)(2,1)}, u32[]{:S(2)}, u32[]{:S(2)}) collective-permute-start(bf16[2,512,256]{2,1,0:T(8,128)(2,1)} %param.12), channel_id=1, source_target_pairs={{0,64},{64,0},{1,65},{65,1},{2,66},{66,2},{3,67},{67,3},{4,68},{68... | collective-permute-start | bytes 1572872 | tf_op jit(solution)/shard_map/ppermute | solution.py:193
  233.1 1.6 collective-permute-start.20
  234.7 2.4 collective-permute-start.21
  238.3 1.9 collective-permute-done.21.refs_2_
  240.7 2.4 apply.14
  243.0 8.1 %all-to-all-start.7 = ((bf16[16,32,256]{2,1,0:T(8,128)(2,1)}), bf16[16,32,256]{2,1,0:T(8,128)(2,1)S(1)}, u32[]{:S(2)}, u32[]{:S(2)}) async-start(bf16[16,32,256]{2,1,0:T(8,128)(2,1)} %get-tuple-element.43), calls=%async_computation.7 | async-start | bytes 524288 | tf_op jit(solution)/shard_map/all_to_all | solution.py:252
  251.2 2.2 broadcast_select_fusion.1
  254.4 6.8 %all-to-all-done.7.x_ref = bf16[16,32,256]{2,1,0:T(8,128)(2,1)S(1)} async-done(((bf16[16,32,256]{2,1,0:T(8,128)(2,1)}), bf16[16,32,256]{2,1,0:T(8,128)(2,1)S(1)}, u32[]{:S(2)}, u32[]{:S(2)}) %all-to-all-start.7) | async-done | bytes 262176 | tf_op jit(solution)/shard_map/all_to_all | solution.py:252
  263.8 1.9 collective-permute-start.24
  269.7 1.6 apply.15
  272.7 2.6 collective-permute-start.29
  276.1 3.2 collective-permute-done.29
  280.7 1.8 collective-permute-start.32
  282.5 2.0 collective-permute-start.33
  284.5 12.4 %collective-permute-start.26 = (bf16[2,32,256]{2,1,0:T(8,128)(2,1)S(1)}, bf16[2,32,256]{2,1,0:T(8,128)(2,1)S(1)}, u32[]{:S(2)}, u32[]{:S(2)}) collective-permute-start(bf16[2,32,256]{2,1,0:T(8,128)(2,1)S(1)} %broadcast_select_fusion.7), channel_id=1, source_target_pairs={{0,64},{64,0},{1,65},{65,1},{2,66},{66,2},{3,67},{67,3},{4,68},{68... | collective-permute-start | bytes 98312 | tf_op jit(solution)/shard_map/ppermute | solution.py:193
  297.8 3.5 %collective-permute-done.34 = f32[32,512]{1,0:T(8,128)S(1)} collective-permute-done((f32[32,512]{1,0:T(8,128)S(1)}, f32[32,512]{1,0:T(8,128)S(1)}, u32[]{:S(2)}, u32[]{:S(2)}) %collective-permute-start.34) | collective-permute-done | bytes 65568 | tf_op jit(solution)/shard_map/ppermute | solution.py:186
  301.6 4.9 %collective-permute-start.35 = (f32[32,512]{1,0:T(8,128)S(1)}, f32[32,512]{1,0:T(8,128)S(1)}, u32[]{:S(2)}, u32[]{:S(2)}) collective-permute-start(f32[32,512]{1,0:T(8,128)S(1)} %fusion.9), channel_id=1, source_target_pairs={{0,64},{64,0},{1,65},{65,1},{2,66},{66,2},{3,67},{67,3},{4,68},{68... | collective-permute-start | bytes 196616 | tf_op jit(solution)/shard_map/ppermute | solution.py:193
  308.0 8.3 %all-reduce.1 = (f32[2,256]{1,0:T(2,128)S(1)}, f32[512]{0:T(512)S(1)}) all-reduce(f32[2,256]{1,0:T(2,128)S(1)} %multiply_reduce_fusion.1, f32[512]{0:T(512)S(1)} %get-tuple-element.54), channel_id=1, replica_groups=mesh['zl'=2,'core'=2,'zh'=4,'y'=4,'x'=4] {'x'}, use_global_device_ids=true, to_apply=%region_1.2 | all-reduce | flops 1024 | bytes 8192 | tf_op jit(solution)/shard_map/psum | solution.py:278
  (144 shorter events, 59.7 us)
Async XLA Ops:
  7.2 294.2 %copy-start = (bf16[512,512]{1,0:T(8,128)(2,1)S(1)}, bf16[512,512]{1,0:T(8,128)(2,1)}, u32[]{:S(2)}) copy-start(bf16[512,512]{1,0:T(8,128)(2,1)} %param.13) | copy-start | bytes 1572868
  7.2 66.0 %all-gather.3.cloned.1.call-start = ((), (), s32[]{:S(2)}) async-start(), calls=%async_computation.8 | async-start | bytes 2969600 | tf_op jit(solution)/shard_map/all_gather | solution.py:224
  8.2 5.5 %collective-permute-start = (bf16[2,32,256]{2,1,0:T(8,128)(2,1)S(1)}, bf16[2,32,256]{2,1,0:T(8,128)(2,1)S(1)}, u32[]{:S(2)}, u32[]{:S(2)}) collective-permute-start(bf16[2,32,256]{2,1,0:T(8,128)(2,1)S(1)} %select_bitcast_fusion), channel_id=1, source_target_pairs={{0,64},{64,0},{1,65},{65,1},{2,66},{66,2},{3,67},{67,3},{4,68},{68... | collective-permute-start | bytes 98312 | tf_op jit(solution)/shard_map/ppermute | solution.py:193
  11.6 1.4 collective-permute-start.1
  11.7 14.0 %collective-permute-start.2 = (bf16[2,256,4096]{2,1,0:T(8,128)(2,1)}, bf16[2,256,4096]{2,1,0:T(8,128)(2,1)}, u32[]{:S(2)}, u32[]{:S(2)}) collective-permute-start(bf16[2,256,4096]{2,1,0:T(8,128)(2,1)} %own_ref.1), channel_id=1, source_target_pairs={{0,64},{64,0},{1,65},{65,1},{2,66},{66,2},{3,67},{67,3},{4,68},{68... | collective-permute-start | bytes 12582920 | tf_op jit(solution)/shard_map/ppermute | solution.py:193
  16.4 20.0 %all-to-all-start = ((bf16[16,32,256]{2,1,0:T(8,128)(2,1)}), bf16[16,32,256]{2,1,0:T(8,128)(2,1)S(1)}, u32[]{:S(2)}, u32[]{:S(2)}) async-start(bf16[16,32,256]{2,1,0:T(8,128)(2,1)} %broadcast_in_dim.14), calls=%async_computation | async-start | bytes 524288 | tf_op jit(solution)/shard_map/all_to_all | solution.py:216
  73.2 11.1 %collective-permute-start.3 = (bf16[4,2320,128]{2,1,0:T(8,128)(2,1)}, bf16[4,2320,128]{2,1,0:T(8,128)(2,1)}, u32[]{:S(2)}, u32[]{:S(2)}) collective-permute-start(bf16[4,2320,128]{2,1,0:T(8,128)(2,1)} %bitcast.43), channel_id=1, source_target_pairs={{0,64},{64,0},{1,65},{65,1},{2,66},{66,2},{3,67},{67,3},{4,68},{68... | collective-permute-start | bytes 7127048 | tf_op jit(solution)/shard_map/ppermute | solution.py:193
  73.6 19.8 %all-to-all-start.1 = ((bf16[16,32,256]{2,1,0:T(8,128)(2,1)}), bf16[16,32,256]{2,1,0:T(8,128)(2,1)S(1)}, u32[]{:S(2)}, u32[]{:S(2)}) async-start(bf16[16,32,256]{2,1,0:T(8,128)(2,1)} %get-tuple-element.27), calls=%async_computation.1 | async-start | bytes 524288 | tf_op jit(solution)/shard_map/all_to_all | solution.py:252
  94.6 29.8 %copy-start.14 = (bf16[4,1024,128]{2,1,0:T(8,128)(2,1)S(1)}, bf16[4,1024,128]{2,1,0:T(8,128)(2,1)}, u32[]{:S(2)}) copy-start(bf16[4,1024,128]{2,1,0:T(8,128)(2,1)} %copy-done.13) | copy-start | bytes 3145732
  96.0 5.1 %collective-permute-start.4 = (bf16[32,1024]{1,0:T(8,128)(2,1)S(1)}, bf16[32,1024]{1,0:T(8,128)(2,1)S(1)}, u32[]{:S(2)}, u32[]{:S(2)}) collective-permute-start(bf16[32,1024]{1,0:T(8,128)(2,1)S(1)} %couple.7.refs_0_), channel_id=1, source_target_pairs={{0,4},{4,8},{8,12},{12,0},{1,5},{5,9},{9,13},{13,1},{2,6},{6,10},{... | collective-permute-start | bytes 196616 | tf_op jit(solution)/shard_map/ppermute | solution.py:186
  96.3 4.8 %collective-permute-start.5 = (bf16[32,1024]{1,0:T(8,128)(2,1)S(1)}, bf16[32,1024]{1,0:T(8,128)(2,1)S(1)}, u32[]{:S(2)}, u32[]{:S(2)}) collective-permute-start(bf16[32,1024]{1,0:T(8,128)(2,1)S(1)} %couple.7.refs_0_), channel_id=1, source_target_pairs={{0,8},{4,12},{8,0},{12,4},{1,9},{5,13},{9,1},{13,5},{2,10},{6,14},... | collective-permute-start | bytes 196616 | tf_op jit(solution)/shard_map/ppermute | solution.py:186
  98.6 3.1 collective-permute-start.6
  124.4 24.5 %copy-start.11 = (bf16[4,1024,128]{2,1,0:T(8,128)(2,1)S(1)}, bf16[4,1024,128]{2,1,0:T(8,128)(2,1)}, u32[]{:S(2)}) copy-start(bf16[4,1024,128]{2,1,0:T(8,128)(2,1)} %copy-done.10) | copy-start | bytes 3145732
  125.8 5.1 %collective-permute-start.7 = (bf16[32,1024]{1,0:T(8,128)(2,1)S(1)}, bf16[32,1024]{1,0:T(8,128)(2,1)S(1)}, u32[]{:S(2)}, u32[]{:S(2)}) collective-permute-start(bf16[32,1024]{1,0:T(8,128)(2,1)S(1)} %couple.8.refs_0_), channel_id=1, source_target_pairs={{0,4},{4,8},{8,12},{12,0},{1,5},{5,9},{9,13},{13,1},{2,6},{6,10},{... | collective-permute-start | bytes 196616 | tf_op jit(solution)/shard_map/ppermute | solution.py:186
  125.8 5.0 %collective-permute-start.8 = (bf16[32,1024]{1,0:T(8,128)(2,1)S(1)}, bf16[32,1024]{1,0:T(8,128)(2,1)S(1)}, u32[]{:S(2)}, u32[]{:S(2)}) collective-permute-start(bf16[32,1024]{1,0:T(8,128)(2,1)S(1)} %couple.8.refs_0_), channel_id=1, source_target_pairs={{0,8},{4,12},{8,0},{12,4},{1,9},{5,13},{9,1},{13,5},{2,10},{6,14},... | collective-permute-start | bytes 196616 | tf_op jit(solution)/shard_map/ppermute | solution.py:186
  128.4 3.1 collective-permute-start.9
  148.9 27.8 %copy-start.22 = (bf16[4,1024,128]{2,1,0:T(8,128)(2,1)S(1)}, bf16[4,1024,128]{2,1,0:T(8,128)(2,1)}, u32[]{:S(2)}) copy-start(bf16[4,1024,128]{2,1,0:T(8,128)(2,1)} %copy-done.21) | copy-start | bytes 3145732
  150.3 5.3 %collective-permute-start.10 = (bf16[32,1024]{1,0:T(8,128)(2,1)S(1)}, bf16[32,1024]{1,0:T(8,128)(2,1)S(1)}, u32[]{:S(2)}, u32[]{:S(2)}) collective-permute-start(bf16[32,1024]{1,0:T(8,128)(2,1)S(1)} %couple.9.refs_0_), channel_id=1, source_target_pairs={{0,4},{4,8},{8,12},{12,0},{1,5},{5,9},{9,13},{13,1},{2,6},{6,10},{... | collective-permute-start | bytes 196616 | tf_op jit(solution)/shard_map/ppermute | solution.py:186
  150.4 5.1 %collective-permute-start.11 = (bf16[32,1024]{1,0:T(8,128)(2,1)S(1)}, bf16[32,1024]{1,0:T(8,128)(2,1)S(1)}, u32[]{:S(2)}, u32[]{:S(2)}) collective-permute-start(bf16[32,1024]{1,0:T(8,128)(2,1)S(1)} %couple.9.refs_0_), channel_id=1, source_target_pairs={{0,8},{4,12},{8,0},{12,4},{1,9},{5,13},{9,1},{13,5},{2,10},{6,14},... | collective-permute-start | bytes 196616 | tf_op jit(solution)/shard_map/ppermute | solution.py:186
  152.7 3.2 %collective-permute-start.12 = (bf16[32,1024]{1,0:T(8,128)(2,1)S(1)}, bf16[32,1024]{1,0:T(8,128)(2,1)S(1)}, u32[]{:S(2)}, u32[]{:S(2)}) collective-permute-start(bf16[32,1024]{1,0:T(8,128)(2,1)S(1)} %couple.9.refs_0_), channel_id=1, source_target_pairs={{0,12},{4,0},{8,4},{12,8},{1,13},{5,1},{9,5},{13,9},{2,14},{6,2},{... | collective-permute-start | bytes 196616 | tf_op jit(solution)/shard_map/ppermute | solution.py:186
  155.9 28.5 %copy-start.6 = (bf16[256,4096]{1,0:T(8,128)(2,1)S(1)}, bf16[256,4096]{1,0:T(8,128)(2,1)}, u32[]{:S(2)}) copy-start(bf16[256,4096]{1,0:T(8,128)(2,1)} %copy-done.4) | copy-start | bytes 6291460
  157.6 3.5 %collective-permute-start.13 = (bf16[32,256]{1,0:T(8,128)(2,1)S(1)}, bf16[32,256]{1,0:T(8,128)(2,1)S(1)}, u32[]{:S(2)}, u32[]{:S(2)}) collective-permute-start(bf16[32,256]{1,0:T(8,128)(2,1)S(1)} %apply.11), channel_id=1, source_target_pairs={{0,128},{1,129},{2,130},{3,131},{4,132},{5,133},{6,134},{7,135},{8... | collective-permute-start | bytes 49160 | tf_op jit(solution)/shard_map/ppermute | solution.py:254
  178.0 30.3 %copy-start.3 = (bf16[256,4096]{1,0:T(8,128)(2,1)S(1)}, bf16[256,4096]{1,0:T(8,128)(2,1)}, u32[]{:S(2)}) copy-start(bf16[256,4096]{1,0:T(8,128)(2,1)} %copy-done.1) | copy-start | bytes 6291460
  178.1 5.8 %collective-permute-start.14 = (bf16[32,1024]{1,0:T(8,128)(2,1)S(1)}, bf16[32,1024]{1,0:T(8,128)(2,1)S(1)}, u32[]{:S(2)}, u32[]{:S(2)}) collective-permute-start(bf16[32,1024]{1,0:T(8,128)(2,1)S(1)} %couple.10.refs_0_), channel_id=1, source_target_pairs={{0,4},{4,8},{8,12},{12,0},{1,5},{5,9},{9,13},{13,1},{2,6},{6,10},{... | collective-permute-start | bytes 196616 | tf_op jit(solution)/shard_map/ppermute | solution.py:186
  178.3 5.5 %collective-permute-start.15 = (bf16[32,1024]{1,0:T(8,128)(2,1)S(1)}, bf16[32,1024]{1,0:T(8,128)(2,1)S(1)}, u32[]{:S(2)}, u32[]{:S(2)}) collective-permute-start(bf16[32,1024]{1,0:T(8,128)(2,1)S(1)} %couple.10.refs_0_), channel_id=1, source_target_pairs={{0,8},{4,12},{8,0},{12,4},{1,9},{5,13},{9,1},{13,5},{2,10},{6,14},... | collective-permute-start | bytes 196616 | tf_op jit(solution)/shard_map/ppermute | solution.py:186
  180.3 4.1 %collective-permute-start.16 = (bf16[32,1024]{1,0:T(8,128)(2,1)S(1)}, bf16[32,1024]{1,0:T(8,128)(2,1)S(1)}, u32[]{:S(2)}, u32[]{:S(2)}) collective-permute-start(bf16[32,1024]{1,0:T(8,128)(2,1)S(1)} %couple.10.refs_0_), channel_id=1, source_target_pairs={{0,12},{4,0},{8,4},{12,8},{1,13},{5,1},{9,5},{13,9},{2,14},{6,2},{... | collective-permute-start | bytes 196616 | tf_op jit(solution)/shard_map/ppermute | solution.py:186
  201.9 5.6 %collective-permute-start.17 = (bf16[32,1024]{1,0:T(8,128)(2,1)S(1)}, bf16[32,1024]{1,0:T(8,128)(2,1)S(1)}, u32[]{:S(2)}, u32[]{:S(2)}) collective-permute-start(bf16[32,1024]{1,0:T(8,128)(2,1)S(1)} %couple.11.refs_0_), channel_id=1, source_target_pairs={{0,4},{4,8},{8,12},{12,0},{1,5},{5,9},{9,13},{13,1},{2,6},{6,10},{... | collective-permute-start | bytes 196616 | tf_op jit(solution)/shard_map/ppermute | solution.py:186
  202.0 5.5 %collective-permute-start.18 = (bf16[32,1024]{1,0:T(8,128)(2,1)S(1)}, bf16[32,1024]{1,0:T(8,128)(2,1)S(1)}, u32[]{:S(2)}, u32[]{:S(2)}) collective-permute-start(bf16[32,1024]{1,0:T(8,128)(2,1)S(1)} %couple.11.refs_0_), channel_id=1, source_target_pairs={{0,8},{4,12},{8,0},{12,4},{1,9},{5,13},{9,1},{13,5},{2,10},{6,14},... | collective-permute-start | bytes 196616 | tf_op jit(solution)/shard_map/ppermute | solution.py:186
  204.6 3.8 %collective-permute-start.19 = (bf16[32,1024]{1,0:T(8,128)(2,1)S(1)}, bf16[32,1024]{1,0:T(8,128)(2,1)S(1)}, u32[]{:S(2)}, u32[]{:S(2)}) collective-permute-start(bf16[32,1024]{1,0:T(8,128)(2,1)S(1)} %couple.11.refs_0_), channel_id=1, source_target_pairs={{0,12},{4,0},{8,4},{12,8},{1,13},{5,1},{9,5},{13,9},{2,14},{6,2},{... | collective-permute-start | bytes 196616 | tf_op jit(solution)/shard_map/ppermute | solution.py:186
  210.7 19.8 %all-to-all-start.6 = ((bf16[16,32,256]{2,1,0:T(8,128)(2,1)}), bf16[16,32,256]{2,1,0:T(8,128)(2,1)S(1)}, u32[]{:S(2)}, u32[]{:S(2)}) async-start(bf16[16,32,256]{2,1,0:T(8,128)(2,1)} %get-tuple-element.41), calls=%async_computation.6 | async-start | bytes 524288 | tf_op jit(solution)/shard_map/all_to_all | solution.py:252
  215.9 35.2 %collective-permute-start.27 = (bf16[2,512,256]{2,1,0:T(8,128)(2,1)}, bf16[2,512,256]{2,1,0:T(8,128)(2,1)}, u32[]{:S(2)}, u32[]{:S(2)}) collective-permute-start(bf16[2,512,256]{2,1,0:T(8,128)(2,1)} %param.12), channel_id=1, source_target_pairs={{0,64},{64,0},{1,65},{65,1},{2,66},{66,2},{3,67},{67,3},{4,68},{68... | collective-permute-start | bytes 1572872 | tf_op jit(solution)/shard_map/ppermute | solution.py:193
  233.1 5.2 %collective-permute-start.20 = (bf16[32,1024]{1,0:T(8,128)(2,1)S(1)}, bf16[32,1024]{1,0:T(8,128)(2,1)S(1)}, u32[]{:S(2)}, u32[]{:S(2)}) collective-permute-start(bf16[32,1024]{1,0:T(8,128)(2,1)S(1)} %couple.12.refs_0_), channel_id=1, source_target_pairs={{0,4},{4,8},{8,12},{12,0},{1,5},{5,9},{9,13},{13,1},{2,6},{6,10},{... | collective-permute-start | bytes 196616 | tf_op jit(solution)/shard_map/ppermute | solution.py:186
  234.7 5.4 %collective-permute-start.21 = (bf16[32,1024]{1,0:T(8,128)(2,1)S(1)}, bf16[32,1024]{1,0:T(8,128)(2,1)S(1)}, u32[]{:S(2)}, u32[]{:S(2)}) collective-permute-start(bf16[32,1024]{1,0:T(8,128)(2,1)S(1)} %couple.12.refs_0_), channel_id=1, source_target_pairs={{0,8},{4,12},{8,0},{12,4},{1,9},{5,13},{9,1},{13,5},{2,10},{6,14},... | collective-permute-start | bytes 196616 | tf_op jit(solution)/shard_map/ppermute | solution.py:186
  237.1 3.6 %collective-permute-start.22 = (bf16[32,1024]{1,0:T(8,128)(2,1)S(1)}, bf16[32,1024]{1,0:T(8,128)(2,1)S(1)}, u32[]{:S(2)}, u32[]{:S(2)}) collective-permute-start(bf16[32,1024]{1,0:T(8,128)(2,1)S(1)} %couple.12.refs_0_), channel_id=1, source_target_pairs={{0,12},{4,0},{8,4},{12,8},{1,13},{5,1},{9,5},{13,9},{2,14},{6,2},{... | collective-permute-start | bytes 196616 | tf_op jit(solution)/shard_map/ppermute | solution.py:186
  243.0 18.2 %all-to-all-start.7 = ((bf16[16,32,256]{2,1,0:T(8,128)(2,1)}), bf16[16,32,256]{2,1,0:T(8,128)(2,1)S(1)}, u32[]{:S(2)}, u32[]{:S(2)}) async-start(bf16[16,32,256]{2,1,0:T(8,128)(2,1)} %get-tuple-element.43), calls=%async_computation.7 | async-start | bytes 524288 | tf_op jit(solution)/shard_map/all_to_all | solution.py:252
  263.8 5.9 %collective-permute-start.23 = (bf16[32,1024]{1,0:T(8,128)(2,1)S(1)}, bf16[32,1024]{1,0:T(8,128)(2,1)S(1)}, u32[]{:S(2)}, u32[]{:S(2)}) collective-permute-start(bf16[32,1024]{1,0:T(8,128)(2,1)S(1)} %couple.13.refs_0_), channel_id=1, source_target_pairs={{0,4},{4,8},{8,12},{12,0},{1,5},{5,9},{9,13},{13,1},{2,6},{6,10},{... | collective-permute-start | bytes 196616 | tf_op jit(solution)/shard_map/ppermute | solution.py:186
  263.8 5.8 %collective-permute-start.24 = (bf16[32,1024]{1,0:T(8,128)(2,1)S(1)}, bf16[32,1024]{1,0:T(8,128)(2,1)S(1)}, u32[]{:S(2)}, u32[]{:S(2)}) collective-permute-start(bf16[32,1024]{1,0:T(8,128)(2,1)S(1)} %couple.13.refs_0_), channel_id=1, source_target_pairs={{0,8},{4,12},{8,0},{12,4},{1,9},{5,13},{9,1},{13,5},{2,10},{6,14},... | collective-permute-start | bytes 196616 | tf_op jit(solution)/shard_map/ppermute | solution.py:186
  265.8 3.9 %collective-permute-start.25 = (bf16[32,1024]{1,0:T(8,128)(2,1)S(1)}, bf16[32,1024]{1,0:T(8,128)(2,1)S(1)}, u32[]{:S(2)}, u32[]{:S(2)}) collective-permute-start(bf16[32,1024]{1,0:T(8,128)(2,1)S(1)} %couple.13.refs_0_), channel_id=1, source_target_pairs={{0,12},{4,0},{8,4},{12,8},{1,13},{5,1},{9,5},{13,9},{2,14},{6,2},{... | collective-permute-start | bytes 196616 | tf_op jit(solution)/shard_map/ppermute | solution.py:186
  268.4 32.9 %copy-start.26 = (s32[64,512]{1,0:T(8,128)S(1)}, s32[64,512]{1,0:T(8,128)}, u32[]{:S(2)}) copy-start(s32[64,512]{1,0:T(8,128)} %param.8) | copy-start | bytes 393220
  271.7 4.4 %collective-permute-start.28 = (f32[32,512]{1,0:T(8,128)S(1)}, f32[32,512]{1,0:T(8,128)S(1)}, u32[]{:S(2)}, u32[]{:S(2)}) collective-permute-start(f32[32,512]{1,0:T(8,128)S(1)} %fusion.2), channel_id=1, source_target_pairs={{0,4},{4,8},{8,12},{12,0},{1,5},{5,9},{9,13},{13,1},{2,6},{6,10},{... | collective-permute-start | bytes 196616 | tf_op jit(solution)/shard_map/ppermute | solution.py:186
  272.7 6.6 %collective-permute-start.29 = (f32[32,512]{1,0:T(8,128)S(1)}, f32[32,512]{1,0:T(8,128)S(1)}, u32[]{:S(2)}, u32[]{:S(2)}) collective-permute-start(f32[32,512]{1,0:T(8,128)S(1)} %fusion.2), channel_id=1, source_target_pairs={{0,8},{4,12},{8,0},{12,4},{1,9},{5,13},{9,1},{13,5},{2,10},{6,14},... | collective-permute-start | bytes 196616 | tf_op jit(solution)/shard_map/ppermute | solution.py:186
  275.3 4.1 %collective-permute-start.30 = (f32[32,512]{1,0:T(8,128)S(1)}, f32[32,512]{1,0:T(8,128)S(1)}, u32[]{:S(2)}, u32[]{:S(2)}) collective-permute-start(f32[32,512]{1,0:T(8,128)S(1)} %fusion.2), channel_id=1, source_target_pairs={{0,12},{4,0},{8,4},{12,8},{1,13},{5,1},{9,5},{13,9},{2,14},{6,2},{... | collective-permute-start | bytes 196616 | tf_op jit(solution)/shard_map/ppermute | solution.py:186
  279.4 17.5 %collective-permute-start.31 = (f32[32,512]{1,0:T(8,128)S(1)}, f32[32,512]{1,0:T(8,128)S(1)}, u32[]{:S(2)}, u32[]{:S(2)}) collective-permute-start(f32[32,512]{1,0:T(8,128)S(1)} %add_add_fusion.1), channel_id=1, source_target_pairs={{0,16},{16,32},{32,48},{48,0},{1,17},{17,33},{33,49},{49,1},{2,18}... | collective-permute-start | bytes 196616 | tf_op jit(solution)/shard_map/ppermute | solution.py:186
  280.7 16.2 %collective-permute-start.32 = (f32[32,512]{1,0:T(8,128)S(1)}, f32[32,512]{1,0:T(8,128)S(1)}, u32[]{:S(2)}, u32[]{:S(2)}) collective-permute-start(f32[32,512]{1,0:T(8,128)S(1)} %add_add_fusion.1), channel_id=1, source_target_pairs={{0,32},{16,48},{32,0},{48,16},{1,33},{17,49},{33,1},{49,17},{2,34}... | collective-permute-start | bytes 196616 | tf_op jit(solution)/shard_map/ppermute | solution.py:186
  282.5 14.4 %collective-permute-start.33 = (f32[32,512]{1,0:T(8,128)S(1)}, f32[32,512]{1,0:T(8,128)S(1)}, u32[]{:S(2)}, u32[]{:S(2)}) collective-permute-start(f32[32,512]{1,0:T(8,128)S(1)} %add_add_fusion.1), channel_id=1, source_target_pairs={{0,48},{16,0},{32,16},{48,32},{1,49},{17,1},{33,17},{49,33},{2,50}... | collective-permute-start | bytes 196616 | tf_op jit(solution)/shard_map/ppermute | solution.py:186
  284.5 13.3 %collective-permute-start.26 = (bf16[2,32,256]{2,1,0:T(8,128)(2,1)S(1)}, bf16[2,32,256]{2,1,0:T(8,128)(2,1)S(1)}, u32[]{:S(2)}, u32[]{:S(2)}) collective-permute-start(bf16[2,32,256]{2,1,0:T(8,128)(2,1)S(1)} %broadcast_select_fusion.7), channel_id=1, source_target_pairs={{0,64},{64,0},{1,65},{65,1},{2,66},{66,2},{3,67},{67,3},{4,68},{68... | collective-permute-start | bytes 98312 | tf_op jit(solution)/shard_map/ppermute | solution.py:193
  297.0 4.4 %collective-permute-start.34 = (f32[32,512]{1,0:T(8,128)S(1)}, f32[32,512]{1,0:T(8,128)S(1)}, u32[]{:S(2)}, u32[]{:S(2)}) collective-permute-start(f32[32,512]{1,0:T(8,128)S(1)} %add_add_fusion), channel_id=1, source_target_pairs={{0,128},{128,0},{1,129},{129,1},{2,130},{130,2},{3,131},{131,3},{4... | collective-permute-start | bytes 196616 | tf_op jit(solution)/shard_map/ppermute | solution.py:186
  301.6 5.8 %collective-permute-start.35 = (f32[32,512]{1,0:T(8,128)S(1)}, f32[32,512]{1,0:T(8,128)S(1)}, u32[]{:S(2)}, u32[]{:S(2)}) collective-permute-start(f32[32,512]{1,0:T(8,128)S(1)} %fusion.9), channel_id=1, source_target_pairs={{0,64},{64,0},{1,65},{65,1},{2,66},{66,2},{3,67},{67,3},{4,68},{68... | collective-permute-start | bytes 196616 | tf_op jit(solution)/shard_map/ppermute | solution.py:193
  (20 other events, 104.3 us)
Sparse Core Ops, SparseCore 0:
  15.8 57.3 all-gather.2
where the time goes:
time: 326 us; the launch traced here: 324 us
  starting transfers between devices  108 us (33%)
  blocking collectives  72.4 us (22%)
  waiting for transfers between devices  66.5 us (20%)
  Pallas kernels  30.5 us (9%)
  local copies, waits for them, and re-layouts  22.1 us (7%)
  between operations  14.4 us (4%)
  other arithmetic  8.54 us (3%)
    all_to_all x3, blocking collectives, shards(): pieces = lax.all_to_all(outs[1], NODES, 0, 0)  48.6 us
    ppermute x28, starting transfers between devices, line(): lax.ppermute(value, axis, [(i, (i + k) % size) for i in range(size)])  37.6 us
    ppermute x7, starting transfers between devices, swap(): return lax.ppermute(value, 'core', [(0, 1), (1, 0)])  36.1 us
    all_gather x1, waiting for transfers between devices, shards(): shared = lax.all_gather(bundle, 'zh', axis=0)  33.4 us
    all_to_all x3, starting transfers between devices, shards(): pieces = lax.all_to_all(outs[1], NODES, 0, 0)  22.4 us
    ppermute x28, waiting for transfers between devices, line(): lax.ppermute(value, axis, [(i, (i + k) % size) for i in range(size)])  21.4 us
    unnamed x55, local copies, waits for them, and re-layouts  20.3 us
    pallas_call x8, Pallas kernels, apply_factor(): pl.pallas_call(kernel, out_shape=tuple(shapes), in_specs=[VMEM, VMEM] if...  15.9 us
  transfers between devices with their start and end apart: 41, of which 25 were waited for; matrix products, arithmetic and copies ran while one was open for 3% of the time, Pallas kernels for 3%

commit v1 on v0

--- a/solution.py
+++ b/solution.py
@@ -24,37 +24,35 @@
             copy.start()
 
 
-def arrange_kernel(place, own_ref, other_ref, *refs, per_core):
-    outs, sems = refs[:-1], refs[-1]
-
-    def copies(source, step):
-        return [pltpu.make_async_copy(source(step % per_core), outs[step], sems.at[step])]
+def arrange_kernel(place, *refs, per_core, steps, pieces, slices):
+    own_refs, other_refs = refs[:pieces], refs[pieces : 2 * pieces]
+    outs, sems = refs[-1 - steps : -1], refs[-1]
+
+    def copies(refs, step):
+        return [
+            pltpu.make_async_copy(*slices(ref, k, outs[step], step % per_core), sems.at[step, k])
+            for k, ref in enumerate(refs)
+        ]
 
     waits = []
-    for step in range(len(outs)):
-        own, other = copies(own_ref, step), copies(other_ref, step)
+    for step in range(steps):
+        own, other = copies(own_refs, step), copies(other_refs, step)
         start_one_of(place[0] == step // per_core, own, other)
         waits += own
     for copy in waits:
         copy.wait()
 
 
-def factor_kernel(place, own_ref, other_ref, *refs, per_core):
-    arrange_kernel(place, lambda i: own_ref.at[i], lambda i: other_ref.at[i], *refs, per_core=per_core)
-
-
-def coupling_kernel(place, own_ref, other_ref, after, *refs, per_core):
-    size = refs[0].shape[1]
-    arrange_kernel(
-        place,
-        lambda i: own_ref.at[:, pl.ds(i * size, size)],
-        lambda i: other_ref.at[:, pl.ds(i * size, size)],
-        *refs,
-        per_core=per_core,
-    )
-
-
-def couple_kernel(cols, x_ref, s_ref, c_ref, out_ref, *, step, slots):
+def factor_slices(ref, k, out, i):
+    return ref.at[i], out
+
+
+def coupling_slices(ref, k, out, i):
+    size = out.shape[1]
+    return ref.at[pl.ds(i * size, size)], out.at[k]
+
+
+def couple_kernel(place, cols, x_ref, s_ref, c_ref, out_ref, *, step, slots):
     lines, tall, block = c_ref.shape
     rows = tall // (slots * block)
     per = x_ref.shape[2] // block
@@ -80,7 +78,8 @@
                 total = term if total is None else total + term
             at = (row * s_ref.shape[1]) // rows + step * probes
             source = s_ref[k, at : at + probes, :].astype(jnp.float32)
-            lanes = pl.ds(pl.multiple_of((k * rows + row) * block, block), block)
+            home = lax.rem(place[1] + lines - k, lines)
+            lanes = pl.ds(pl.multiple_of((home * rows + row) * block, block), block)
             out_ref[:, lanes] = (source - total).astype(jnp.bfloat16)
         return carry
 
@@ -95,19 +94,50 @@
             outs[1][peer] = result
 
 
-def first_kernel(r_ref, l_ref, *outs):
+def early_kernel(place, r_ref, own_ref, other_ref, *refs, step, per_core):
+    outs, (l_buf, sems) = refs[:-2], refs[-2:]
+    chunks, _, wide = l_buf.shape
+    own, other = (
+        [
+            pltpu.make_async_copy(
+                source.at[step % per_core, :, pl.ds(i * wide, wide)], l_buf.at[i], sems.at[i]
+            )
+            for i in range(chunks)
+        ]
+        for source in (own_ref, other_ref)
+    )
+    start_one_of(place[0] == step // per_core, own, other)
     width = r_ref.shape[2]
-
-    def body(i, total):
-        for j in range(4):
-            lanes = pl.ds(pl.multiple_of((i * 4 + j) * width, width), width)
-            total = total + lax.dot_general(
-                r_ref[i * 4 + j], l_ref[:, lanes], NT, preferred_element_type=jnp.float32
+    per = wide // width
+    total = jnp.zeros((r_ref.shape[1], l_buf.shape[1]), jnp.float32)
+    for i in range(chunks):
+        own[i].wait()
+        left = jnp.concatenate([r_ref[i * per + j] for j in range(per)], axis=1)
+        total = total + lax.dot_general(left, l_buf[i], NT, preferred_element_type=jnp.float32)
+    finish(total, outs)
+
+
+def early_couple_kernel(place, cols, x_ref, s_ref, own_ref, other_ref, out_ref, c_buf, sem, *, step, per_core):
+    rows, slots, block, _ = c_buf.shape
+    own, other = (
+        [pltpu.make_async_copy(source.at[step % per_core], c_buf, sem)] for source in (own_ref, other_ref)
+    )
+    start_one_of(place[0] == step // per_core, own, other)
+    own[0].wait()
+    per = x_ref.shape[2] // block
+    for row in range(rows):
+        total = None
+        for slot in range(slots):
+            col = cols[(step * rows + row) * slots + slot]
+            lanes = pl.ds(pl.multiple_of((col % per) * block, block), block)
+            term = lax.dot_general(
+                x_ref[col // per, :, lanes], c_buf[row, slot], NT, preferred_element_type=jnp.float32
             )
-        return total
-
-    start = jnp.zeros((r_ref.shape[1], l_ref.shape[0]), jnp.float32)
-    finish(lax.fori_loop(0, r_ref.shape[0] // 4, body, start), outs)
+            total = term if total is None else total + term
+        span = slice(row * block, (row + 1) * block)
+        resid = (s_ref[:, span].astype(jnp.float32) - total).astype(jnp.bfloat16)
+        for peer in range(out_ref.shape[0]):
+            out_ref[peer, :, span] = resid
 
 
 def apply_kernel(place, *refs, lines):
@@ -134,50 +164,83 @@
 PARAMS = pltpu.CompilerParams(vmem_limit_bytes=16 << 20)
 
 
-def arrange(kernel, place, own, other, steps, shape, name, *after):
-    return pl.pallas_call(
-        functools.partial(kernel, per_core=steps // 2),
+def arrange(slices, place, own, other, steps, shape, name, after):
+    pieces = len(own)
+    return pl.pallas_call(
+        functools.partial(
+            arrange_kernel, per_core=steps // 2, steps=steps, pieces=pieces, slices=slices
+        ),
         out_shape=tuple([jax.ShapeDtypeStruct(shape, jnp.bfloat16)] * steps),
-        in_specs=[SMEM] + [HBM] * (2 + len(after)),
+        in_specs=[SMEM] + [HBM] * (2 * pieces + 1),
         out_specs=tuple([HBM] * steps),
-        scratch_shapes=[pltpu.SemaphoreType.DMA((steps,))],
+        scratch_shapes=[pltpu.SemaphoreType.DMA((steps, pieces))],
         compiler_params=PARAMS,
         cost_estimate=pl.CostEstimate(
             flops=0, transcendentals=0, bytes_accessed=4 * steps * shape[0] * shape[1]
         ),
         name=name,
-    )(place, own, other, *after)
-
-
-def couple(cols, pieces, source, c, step, slots):
+    )(place, *own, *other, after)
+
+
+def couple(place, cols, pieces, source, c, step, slots):
     lines, tall, block = c.shape
     return pl.pallas_call(
         functools.partial(couple_kernel, step=step, slots=slots),
         out_shape=jax.ShapeDtypeStruct((pieces.shape[1], lines * tall // slots), jnp.bfloat16),
-        in_specs=[SMEM, VMEM, VMEM, VMEM],
+        in_specs=[SMEM, SMEM, VMEM, VMEM, VMEM],
         out_specs=VMEM,
         compiler_params=PARAMS,
         name="couple",
-    )(cols, pieces, source, c)
-
-
-def apply_factor(place, pieces, factor, peers):
-    first = not isinstance(pieces, list)
-    probes = pieces.shape[1] if first else pieces[0].shape[0]
-    rows = factor.shape[0]
+    )(place, cols, pieces, source, c)
+
+
+def solved_shapes(probes, rows, peers):
     shapes = [jax.ShapeDtypeStruct((probes, rows), jnp.bfloat16)]
     if peers:
         shapes.append(jax.ShapeDtypeStruct((peers, probes, rows), jnp.bfloat16))
-    kernel = first_kernel if first else functools.partial(apply_kernel, lines=len(pieces))
-    operands = (pieces, factor) if first else (place, *pieces, factor)
-    return pl.pallas_call(
-        kernel,
-        out_shape=tuple(shapes),
-        in_specs=[VMEM, VMEM] if first else [SMEM] + [VMEM] * (len(pieces) + 1),
+    return tuple(shapes)
+
+
+def apply_factor(place, pieces, factor, peers):
+    shapes = solved_shapes(pieces[0].shape[0], factor.shape[0], peers)
+    return pl.pallas_call(
+        functools.partial(apply_kernel, lines=len(pieces)),
+        out_shape=shapes,
+        in_specs=[SMEM] + [VMEM] * (len(pieces) + 1),
         out_specs=tuple([VMEM] * len(shapes)),
         compiler_params=PARAMS,
         name="apply",
-    )(*operands)
+    )(place, *pieces, factor)
+
+
+def apply_early(place, pieces, own, other, step):
+    peers, probes, _ = pieces.shape
+    per_core, rows, width = own.shape
+    shapes = solved_shapes(probes, rows, peers)
+    return pl.pallas_call(
+        functools.partial(early_kernel, step=step, per_core=per_core),
+        out_shape=shapes,
+        in_specs=[SMEM, VMEM, HBM, HBM],
+        out_specs=tuple([VMEM] * len(shapes)),
+        scratch_shapes=[
+            pltpu.VMEM((4, rows, width // 4), own.dtype),
+            pltpu.SemaphoreType.DMA((4,)),
+        ],
+        compiler_params=PARAMS,
+        name="apply_early",
+    )(place, pieces, own, other)
+
+
+def couple_early(place, cols, pieces, source, own, other, step):
+    return pl.pallas_call(
+        functools.partial(early_couple_kernel, step=step, per_core=own.shape[0]),
+        out_shape=jax.ShapeDtypeStruct(pieces.shape, jnp.bfloat16),
+        in_specs=[SMEM, SMEM, VMEM, VMEM, HBM, HBM],
+        out_specs=VMEM,
+        scratch_shapes=[pltpu.VMEM(own.shape[1:], own.dtype), pltpu.SemaphoreType.DMA],
+        compiler_params=PARAMS,
+        name="couple_early",
+    )(place, cols, pieces, source, own, other)
 
 
 def line(value, axis):
@@ -211,48 +274,54 @@
     source = (2 * signs - 1).astype(jnp.bfloat16).reshape(cores, probes, own_steps, local)
     source = source.transpose(0, 2, 1, 3)
     other_half = swap(jnp.where(first, source[1], source[0]))
-    source = in_order(jnp.where(first, source[0], source[1]), other_half)
-    spread = jnp.broadcast_to(source[0][None], (peers, probes, local))
-    begin = lax.all_to_all(spread, NODES, 0, 0)
+    own_source = in_order(jnp.where(first, source[0], source[1]), other_half)
+    spread = jnp.broadcast_to(own_source[0][None], (peers, probes, local))
+    own_cols = in_order(coupling_cols, swap(coupling_cols)).reshape(-1)
+    other_factors, other_couplings = swap(inverse_factors), swap(couplings)
+
+    def everywhere(value):
+        return lax.all_to_all(value, NODES, 0, 0)
+
+    solved0 = apply_early(place, everywhere(spread), inverse_factors, other_factors, 0)
     slots, block = couplings.shape[2:4]
-    cols = in_order(coupling_cols, swap(coupling_cols)).reshape(1, -1).astype(jnp.bfloat16)
+    cols = own_cols.reshape(1, -1).astype(jnp.bfloat16)
     width = cols.shape[1]
     cols = jnp.pad(cols, ((0, 15), (0, block - width)))
-    flat = source.reshape(steps * probes, local)
+    flat = own_source.reshape(steps * probes, local)
     halves = [flat[:, i : i + block] for i in range(0, local, block)]
     bundle = jnp.concatenate([couplings.reshape(-1, block)] + halves + [cols], axis=0)
-    shared = lax.all_gather(bundle, "zh", axis=0)
+    shared = line(bundle, "zh")
     at = couplings.size // block
     until = at + steps * probes * local // block
     tall = at // own_steps
-
+    resid = couple_early(
+        place, own_cols, everywhere(solved0[1]), own_source[1], couplings, other_couplings, 1
+    )
+    solved1 = apply_early(place, everywhere(resid), inverse_factors, other_factors, 1)
+    pieces = everywhere(solved1[1])
+    shared, after = lax.optimization_barrier((shared, solved1[0]))
+    source = jnp.stack([s[at:until] for s in shared])
+    cols = jnp.concatenate([s[until : until + 1, :width] for s in shared], axis=0).astype(jnp.int32)
+    shape = (len(shared), tall, block)
+    blocks = arrange(
+        coupling_slices, place, shared, [swap(s) for s in shared], steps, shape, "couplings", after
+    )
     factors = arrange(
-        factor_kernel, place, inverse_factors, swap(inverse_factors), steps, inverse_factors.shape[1:], "factors"
-    )
-
-    pieces = None
+        factor_slices, place, [inverse_factors], [other_factors], steps, inverse_factors.shape[1:], "factors", after
+    )
+
     for turn in range(turns):
         results = []
-        for step in range(steps):
-            if pieces is None:
-                resid = begin
-            else:
-                resid = line(couple(cols, pieces, source, blocks[step], step, slots), "y")
+        for step in range(2 if turn == 0 else 0, steps):
+            resid = line(couple(place, cols, pieces, source, blocks[step], step, slots), "y")
             more = step + 1 < steps
             outs = apply_factor(place, resid, factors[step], peers if more else 0)
             results.append(outs[0])
-            if turn + step == 0:
-                shared, after = lax.optimization_barrier((shared, outs[0]))
-                source = shared[:, at:until]
-                cols = shared[:, until, :width].astype(jnp.int32)
-                blocks = arrange(
-                    coupling_kernel, place, shared, swap(shared), steps, (shared.shape[0], tall, block), "couplings", after
-                )
             if more:
-                pieces = lax.all_to_all(outs[1], NODES, 0, 0)
+                pieces = everywhere(outs[1])
         if turn + 1 < turns:
             moved = lax.ppermute(outs[0], "zl", [(turn, turn + 1)])
-            pieces = lax.all_to_all(jnp.broadcast_to(moved[None], (peers, probes, local)), NODES, 0, 0)
+            pieces = everywhere(jnp.broadcast_to(moved[None], (peers, probes, local)))
 
     rows4 = in_order(border_rows, swap(border_rows))
     partial = jnp.zeros((probes, border_rows.shape[1]), jnp.float32)

time: 326 us -> 328 us (level)
  blocking collectives: 72.4 us -> 112 us
  waiting for transfers between devices: 66.5 us -> 43.6 us
  between operations: 14.4 us -> 1.14 us
  local copies, waits for them, and re-layouts: 22.1 us -> 16.9 us
  starting transfers between devices: 108 us -> 113 us
  other arithmetic: 8.54 us -> 5.14 us
    all_to_all x4, blocking collectives: 64.2 us -> 104 us  [everywhere(): return lax.all_to_all(value, NODES, 0, 0)]
    all_gather x1 -> x0, waiting for transfers between devices: 33.4 us -> none  [shards(): shared = lax.all_gather(bundle, 'zh', axis=0)]
    all_to_all x4 -> x5, waiting for transfers between devices: 9.52 us -> 19.3 us  [everywhere(): return lax.all_to_all(value, NODES, 0, 0)]
    unnamed x55 -> x43, local copies, waits for them, and re-layouts: 20.3 us -> 13.7 us
    ppermute x7 -> x11, waiting for transfers between devices: 1.33 us -> 6.84 us  [swap(): return lax.ppermute(value, 'core', [(0, 1), (1, 0)])]
    ppermute x28, starting transfers between devices: 37.6 us -> 43 us  [line(): lax.ppermute(value, axis, [(i, (i + k) % size) for i in range(size)])]
    ppermute x28, waiting for transfers between devices: 21.4 us -> 16.6 us  [line(): lax.ppermute(value, axis, [(i, (i + k) % size) for i in range(size)])]
    pallas_call x10 -> x11, Pallas kernels: 21.1 us -> 25.3 us  [the longest x6 11.8 us: apply_factor(): pl.pallas_call(functools.partial(apply_kernel, lines=len(pieces)), out_sh...]
  transfers between devices with their start and end apart: 41 -> 45, of which waited for: 25 -> 25; matrix products, arithmetic and copies ran while one was open for 3% -> 3% of each run, Pallas kernels for 3% -> 5%
where the time goes in v1:
time: 328 us; the launch traced here: 327 us
  starting transfers between devices  113 us (34%)
  blocking collectives  112 us (34%)
  waiting for transfers between devices  43.6 us (13%)
  Pallas kernels  33.4 us (10%)
  local copies, waits for them, and re-layouts  16.9 us (5%)
  other arithmetic  5.14 us (2%)
    all_to_all x4, blocking collectives, everywhere(): return lax.all_to_all(value, NODES, 0, 0)  104 us
    ppermute x28, starting transfers between devices, line(): lax.ppermute(value, axis, [(i, (i + k) % size) for i in range(size)])  43 us
    ppermute x11, starting transfers between devices, swap(): return lax.ppermute(value, 'core', [(0, 1), (1, 0)])  35.7 us
    all_to_all x5, starting transfers between devices, everywhere(): return lax.all_to_all(value, NODES, 0, 0)  32.5 us
    all_to_all x5, waiting for transfers between devices, everywhere(): return lax.all_to_all(value, NODES, 0, 0)  19.3 us
    ppermute x28, waiting for transfers between devices, line(): lax.ppermute(value, axis, [(i, (i + k) % size) for i in range(size)])  16.6 us
    unnamed x43, local copies, waits for them, and re-layouts  13.7 us
    pallas_call x6, Pallas kernels, apply_factor(): pl.pallas_call(functools.partial(apply_kernel, lines=len(pieces)), out_sh...  11.8 us
  transfers between devices with their start and end apart: 45, of which 25 were waited for; matrix products, arithmetic and copies ran while one was open for 3% of the time, Pallas kernels for 5%

profile of v1, /device:TPU:1, one launch (start us, length us, event | category | flops | bytes accessed | tf_op | source)
XLA Modules:
  0.0 327.0 jit_solution(10136420279664856825)
XLA Ops:
  0.7 3.3 %collective-permute-start.5 = (bf16[2,256,4096]{2,1,0:T(8,128)(2,1)}, bf16[2,256,4096]{2,1,0:T(8,128)(2,1)}, u32[]{:S(2)}, u32[]{:S(2)}) collective-permute-start(bf16[2,256,4096]{2,1,0:T(8,128)(2,1)} %refs_0_.1), channel_id=1, source_target_pairs={{0,64},{64,0},{1,65},{65,1},{2,66},{66,2},{3,67},{67,3},{4,68},{68... | collective-permute-start | bytes 12582920 | tf_op jit(solution)/shard_map/ppermute | solution.py:256
  5.6 5.2 %collective-permute-done = bf16[2,32,256]{2,1,0:T(8,128)(2,1)S(1)} collective-permute-done((bf16[2,32,256]{2,1,0:T(8,128)(2,1)S(1)}, bf16[2,32,256]{2,1,0:T(8,128)(2,1)S(1)}, u32[]{:S(2)}, u32[]{:S(2)}) %collective-permute-start) | collective-permute-done | bytes 32800 | tf_op jit(solution)/shard_map/ppermute | solution.py:256
  11.7 9.2 %all-to-all-start = ((bf16[16,32,256]{2,1,0:T(8,128)(2,1)}), bf16[16,32,256]{2,1,0:T(8,128)(2,1)S(1)}, u32[]{:S(2)}, u32[]{:S(2)}) async-start(bf16[16,32,256]{2,1,0:T(8,128)(2,1)} %broadcast_in_dim.14), calls=%async_computation | async-start | bytes 524288 | tf_op jit(solution)/shard_map/all_to_all | solution.py:283
  21.1 10.5 %all-to-all-done.r_ref = bf16[16,32,256]{2,1,0:T(8,128)(2,1)S(1)} async-done(((bf16[16,32,256]{2,1,0:T(8,128)(2,1)}), bf16[16,32,256]{2,1,0:T(8,128)(2,1)S(1)}, u32[]{:S(2)}, u32[]{:S(2)}) %all-to-all-start) | async-done | bytes 262176 | tf_op jit(solution)/shard_map/all_to_all | solution.py:283
  31.6 2.2 copy-done.1
  33.8 3.8 %apply_early.2 = (bf16[32,256]{1,0:T(8,128)(2,1)}, bf16[16,32,256]{2,1,0:T(8,128)(2,1)}) custom-call(s32[3]{0:T(128)S(1)} %pad_add_fusion.1.place, bf16[16,32,256]{2,1,0:T(8,128)(2,1)S(1)} %all-to-all-done.r_ref, bf16[2,256,4096]{2,1,0:T(8,128)(2,1)S(1)} %copy-done.1, bf16[2,256,4096]{2,1,0:T(8,128)(2,1)} %collective-permute-done.5.other_ref.refs_1_), custom_call_target="tpu_custom_call" | custom-call | tf_op jit(solution)/shard_map/apply_early/pallas_call | solution.py:220
  37.6 5.1 %all-to-all-start.1 = ((bf16[16,32,256]{2,1,0:T(8,128)(2,1)}), bf16[16,32,256]{2,1,0:T(8,128)(2,1)S(1)}, u32[]{:S(2)}, u32[]{:S(2)}) async-start(bf16[16,32,256]{2,1,0:T(8,128)(2,1)} %get-tuple-element.27), calls=%async_computation.1 | async-start | bytes 524288 | tf_op jit(solution)/shard_map/all_to_all | solution.py:283
  42.8 2.3 collective-permute-start.2
  45.2 3.3 %collective-permute-start.3 = (bf16[2320,128]{1,0:T(8,128)(2,1)S(1)}, bf16[2320,128]{1,0:T(8,128)(2,1)}, u32[]{:S(2)}, u32[]{:S(2)}) collective-permute-start(bf16[2320,128]{1,0:T(8,128)(2,1)S(1)} %fusion.3.refs_0_), channel_id=1, source_target_pairs={{0,32},{16,48},{32,0},{48,16},{1,33},{17,49},{33,1},{49,17},{2,34}... | collective-permute-start | bytes 1781768 | tf_op jit(solution)/shard_map/ppermute | solution.py:249
  48.5 3.3 %collective-permute-start.4 = (bf16[2320,128]{1,0:T(8,128)(2,1)S(1)}, bf16[2320,128]{1,0:T(8,128)(2,1)}, u32[]{:S(2)}, u32[]{:S(2)}) collective-permute-start(bf16[2320,128]{1,0:T(8,128)(2,1)S(1)} %fusion.3.refs_0_), channel_id=1, source_target_pairs={{0,48},{16,0},{32,16},{48,32},{1,49},{17,1},{33,17},{49,33},{2,50}... | collective-permute-start | bytes 1781768 | tf_op jit(solution)/shard_map/ppermute | solution.py:249
  53.8 56.6 %all_to_all.45.r_ref = bf16[16,32,256]{2,1,0:T(8,128)(2,1)S(1)} all-to-all(bf16[16,32,256]{2,1,0:T(8,128)(2,1)S(1)} %couple_early.1), channel_id=1, replica_groups=mesh['zl'=2,'core'=2,'zh'=4,'y'=4,'x'=4] {'zh','y'}, dimensions={0} | all-to-all | bytes 524288 | tf_op jit(solution)/shard_map/all_to_all | solution.py:283
  110.5 2.2 copy-done.2
  112.6 3.8 %apply_early.3 = (bf16[32,256]{1,0:T(8,128)(2,1)S(1)}, bf16[16,32,256]{2,1,0:T(8,128)(2,1)}) custom-call(s32[3]{0:T(128)S(1)} %pad_add_fusion.1.place, bf16[16,32,256]{2,1,0:T(8,128)(2,1)S(1)} %all_to_all.45.r_ref, bf16[2,256,4096]{2,1,0:T(8,128)(2,1)S(1)} %copy-done.2, bf16[2,256,4096]{2,1,0:T(8,128)(2,1)} %collective-permute-done.5.other_ref.refs_1_), custom_call_target="tpu_custom_call" | custom-call | tf_op jit(solution)/shard_map/apply_early/pallas_call | solution.py:220
  116.5 5.3 %all-to-all-start.3 = ((bf16[16,32,256]{2,1,0:T(8,128)(2,1)}), bf16[16,32,256]{2,1,0:T(8,128)(2,1)S(1)}, u32[]{:S(2)}, u32[]{:S(2)}) async-start(bf16[16,32,256]{2,1,0:T(8,128)(2,1)} %get-tuple-element.33), calls=%async_computation.3 | async-start | bytes 524288 | tf_op jit(solution)/shard_map/all_to_all | solution.py:283
  126.7 2.1 couplings.1
  134.8 2.4 collective-permute-start.12
  138.4 2.2 copy-done.3
  140.5 2.8 factors.1
  143.4 2.3 apply.6
  145.7 16.3 %all_to_all.46.x_ref = bf16[16,32,256]{2,1,0:T(8,128)(2,1)S(1)} all-to-all(bf16[16,32,256]{2,1,0:T(8,128)(2,1)S(1)} %get-tuple-element.37), channel_id=1, replica_groups=mesh['zl'=2,'core'=2,'zh'=4,'y'=4,'x'=4] {'zh','y'}, dimensions={0} | all-to-all | bytes 524288 | tf_op jit(solution)/shard_map/all_to_all | solution.py:283
  163.5 2.5 collective-permute-start.15
  166.0 1.8 collective-permute-start.16
  169.2 1.6 apply.7
  173.0 16.1 %all_to_all.47.x_ref = bf16[16,32,256]{2,1,0:T(8,128)(2,1)S(1)} all-to-all(bf16[16,32,256]{2,1,0:T(8,128)(2,1)S(1)} %broadcast_in_dim.15), channel_id=1, replica_groups=mesh['zl'=2,'core'=2,'zh'=4,'y'=4,'x'=4] {'zh','y'}, dimensions={0} | all-to-all | bytes 524288 | tf_op jit(solution)/shard_map/all_to_all | solution.py:283
  190.6 2.6 collective-permute-start.19
  196.3 1.6 apply.8
  197.9 14.9 %all_to_all.48.x_ref = bf16[16,32,256]{2,1,0:T(8,128)(2,1)S(1)} all-to-all(bf16[16,32,256]{2,1,0:T(8,128)(2,1)S(1)} %get-tuple-element.43), channel_id=1, replica_groups=mesh['zl'=2,'core'=2,'zh'=4,'y'=4,'x'=4] {'zh','y'}, dimensions={0} | all-to-all | bytes 524288 | tf_op jit(solution)/shard_map/all_to_all | solution.py:283
  214.3 2.1 collective-permute-start.22
  217.9 2.1 collective-permute-done.21.refs_1_
  220.4 2.4 apply.9
  222.7 4.7 %all-to-all-start.7 = ((bf16[16,32,256]{2,1,0:T(8,128)(2,1)}), bf16[16,32,256]{2,1,0:T(8,128)(2,1)S(1)}, u32[]{:S(2)}, u32[]{:S(2)}) async-start(bf16[16,32,256]{2,1,0:T(8,128)(2,1)} %get-tuple-element.47), calls=%async_computation.7 | async-start | bytes 524288 | tf_op jit(solution)/shard_map/all_to_all | solution.py:283
  227.4 10.7 %collective-permute-start.31 = (bf16[2,512,256]{2,1,0:T(8,128)(2,1)}, bf16[2,512,256]{2,1,0:T(8,128)(2,1)}, u32[]{:S(2)}, u32[]{:S(2)}) collective-permute-start(bf16[2,512,256]{2,1,0:T(8,128)(2,1)} %param.12), channel_id=1, source_target_pairs={{0,64},{64,0},{1,65},{65,1},{2,66},{66,2},{3,67},{67,3},{4,68},{68... | collective-permute-start | bytes 1572872 | tf_op jit(solution)/shard_map/ppermute | solution.py:256
  240.7 1.6 collective-permute-start.24
  242.3 2.4 collective-permute-start.25
  245.9 1.9 collective-permute-done.25.refs_2_
  248.3 2.4 apply.10
  250.7 8.1 %all-to-all-start.8 = ((bf16[16,32,256]{2,1,0:T(8,128)(2,1)}), bf16[16,32,256]{2,1,0:T(8,128)(2,1)S(1)}, u32[]{:S(2)}, u32[]{:S(2)}) async-start(bf16[16,32,256]{2,1,0:T(8,128)(2,1)} %get-tuple-element.49), calls=%async_computation.8 | async-start | bytes 524288 | tf_op jit(solution)/shard_map/all_to_all | solution.py:283
  258.8 2.1 broadcast_select_fusion.1
  261.8 7.0 %all-to-all-done.8.x_ref = bf16[16,32,256]{2,1,0:T(8,128)(2,1)S(1)} async-done(((bf16[16,32,256]{2,1,0:T(8,128)(2,1)}), bf16[16,32,256]{2,1,0:T(8,128)(2,1)S(1)}, u32[]{:S(2)}, u32[]{:S(2)}) %all-to-all-start.8) | async-done | bytes 262176 | tf_op jit(solution)/shard_map/all_to_all | solution.py:283
  271.7 2.1 collective-permute-start.28
  277.4 1.6 apply.11
  279.4 2.5 collective-permute-start.34
  283.2 3.7 %collective-permute-done.33 = f32[32,512]{1,0:T(8,128)S(1)} collective-permute-done((f32[32,512]{1,0:T(8,128)S(1)}, f32[32,512]{1,0:T(8,128)S(1)}, u32[]{:S(2)}, u32[]{:S(2)}) %collective-permute-start.33) | collective-permute-done | bytes 65568 | tf_op jit(solution)/shard_map/ppermute | solution.py:249
  289.0 2.7 collective-permute-start.36
  291.8 12.1 %collective-permute-start.30 = (bf16[2,32,256]{2,1,0:T(8,128)(2,1)S(1)}, bf16[2,32,256]{2,1,0:T(8,128)(2,1)S(1)}, u32[]{:S(2)}, u32[]{:S(2)}) collective-permute-start(bf16[2,32,256]{2,1,0:T(8,128)(2,1)S(1)} %broadcast_select_fusion.7), channel_id=1, source_target_pairs={{0,64},{64,0},{1,65},{65,1},{2,66},{66,2},{3,67},{67,3},{4,68},{68... | collective-permute-start | bytes 98312 | tf_op jit(solution)/shard_map/ppermute | solution.py:256
  305.0 2.8 collective-permute-done.38
  308.0 7.8 %collective-permute-start.39 = (f32[32,512]{1,0:T(8,128)S(1)}, f32[32,512]{1,0:T(8,128)S(1)}, u32[]{:S(2)}, u32[]{:S(2)}) collective-permute-start(f32[32,512]{1,0:T(8,128)S(1)} %fusion.9), channel_id=1, source_target_pairs={{0,64},{64,0},{1,65},{65,1},{2,66},{66,2},{3,67},{67,3},{4,68},{68... | collective-permute-start | bytes 196616 | tf_op jit(solution)/shard_map/ppermute | solution.py:256
  317.4 8.4 %all-reduce.1 = (f32[2,256]{1,0:T(2,128)S(1)}, f32[512]{0:T(512)S(1)}) all-reduce(f32[2,256]{1,0:T(2,128)S(1)} %multiply_reduce_fusion.1, f32[512]{0:T(512)S(1)} %get-tuple-element.60), channel_id=1, replica_groups=mesh['zl'=2,'core'=2,'zh'=4,'y'=4,'x'=4] {'x'}, use_global_device_ids=true, to_apply=%region_1.2 | all-reduce | flops 1024 | bytes 8192 | tf_op jit(solution)/shard_map/psum | solution.py:347
  (146 shorter events, 49.2 us)
Async XLA Ops:
  0.6 307.1 %copy-start = (bf16[512,512]{1,0:T(8,128)(2,1)S(1)}, bf16[512,512]{1,0:T(8,128)(2,1)}, u32[]{:S(2)}) copy-start(bf16[512,512]{1,0:T(8,128)(2,1)} %param.13) | copy-start | bytes 1572868
  0.7 30.9 %collective-permute-start.5 = (bf16[2,256,4096]{2,1,0:T(8,128)(2,1)}, bf16[2,256,4096]{2,1,0:T(8,128)(2,1)}, u32[]{:S(2)}, u32[]{:S(2)}) collective-permute-start(bf16[2,256,4096]{2,1,0:T(8,128)(2,1)} %refs_0_.1), channel_id=1, source_target_pairs={{0,64},{64,0},{1,65},{65,1},{2,66},{66,2},{3,67},{67,3},{4,68},{68... | collective-permute-start | bytes 12582920 | tf_op jit(solution)/shard_map/ppermute | solution.py:256
  4.9 5.9 %collective-permute-start = (bf16[2,32,256]{2,1,0:T(8,128)(2,1)S(1)}, bf16[2,32,256]{2,1,0:T(8,128)(2,1)S(1)}, u32[]{:S(2)}, u32[]{:S(2)}) collective-permute-start(bf16[2,32,256]{2,1,0:T(8,128)(2,1)S(1)} %select_bitcast_fusion), channel_id=1, source_target_pairs={{0,64},{64,0},{1,65},{65,1},{2,66},{66,2},{3,67},{67,3},{4,68},{68... | collective-permute-start | bytes 98312 | tf_op jit(solution)/shard_map/ppermute | solution.py:256
  5.1 15.9 %collective-permute-start.1 = (s32[2,2,4]{2,1,0:T(2,128)}, s32[2,2,4]{2,1,0:T(2,128)S(1)}, u32[]{:S(2)}, u32[]{:S(2)}) collective-permute-start(s32[2,2,4]{2,1,0:T(2,128)} %param.11), channel_id=1, source_target_pairs={{0,64},{64,0},{1,65},{65,1},{2,66},{66,2},{3,67},{67,3},{4,68},{68... | collective-permute-start | bytes 200 | tf_op jit(solution)/shard_map/ppermute | solution.py:256
  5.5 46.3 %collective-permute-start.6 = (bf16[2,2,4,128,128]{4,3,2,1,0:T(8,128)(2,1)}, bf16[2,2,4,128,128]{4,3,2,1,0:T(8,128)(2,1)S(1)}, u32[]{:S(2)}, u32[]{:S(2)}) collective-permute-start(bf16[2,2,4,128,128]{4,3,2,1,0:T(8,128)(2,1)} %own_ref.4), channel_id=1, source_target_pairs={{0,64},{64,0},{1,65},{65,1},{2,66},{66,2},{3,67},{67,3},{4,68},{68... | collective-permute-start | bytes 1572872 | tf_op jit(solution)/shard_map/ppermute | solution.py:256
  11.7 19.9 %all-to-all-start = ((bf16[16,32,256]{2,1,0:T(8,128)(2,1)}), bf16[16,32,256]{2,1,0:T(8,128)(2,1)S(1)}, u32[]{:S(2)}, u32[]{:S(2)}) async-start(bf16[16,32,256]{2,1,0:T(8,128)(2,1)} %broadcast_in_dim.14), calls=%async_computation | async-start | bytes 524288 | tf_op jit(solution)/shard_map/all_to_all | solution.py:283
  37.6 15.3 %all-to-all-start.1 = ((bf16[16,32,256]{2,1,0:T(8,128)(2,1)}), bf16[16,32,256]{2,1,0:T(8,128)(2,1)S(1)}, u32[]{:S(2)}, u32[]{:S(2)}) async-start(bf16[16,32,256]{2,1,0:T(8,128)(2,1)} %get-tuple-element.27), calls=%async_computation.1 | async-start | bytes 524288 | tf_op jit(solution)/shard_map/all_to_all | solution.py:283
  42.8 73.7 %collective-permute-start.2 = (bf16[2320,128]{1,0:T(8,128)(2,1)S(1)}, bf16[2320,128]{1,0:T(8,128)(2,1)S(1)}, u32[]{:S(2)}, u32[]{:S(2)}) collective-permute-start(bf16[2320,128]{1,0:T(8,128)(2,1)S(1)} %fusion.3.refs_0_), channel_id=1, source_target_pairs={{0,16},{16,32},{32,48},{48,0},{1,17},{17,33},{33,49},{49,1},{2,18}... | collective-permute-start | bytes 1781768 | tf_op jit(solution)/shard_map/ppermute | solution.py:249
  45.2 71.3 %collective-permute-start.3 = (bf16[2320,128]{1,0:T(8,128)(2,1)S(1)}, bf16[2320,128]{1,0:T(8,128)(2,1)}, u32[]{:S(2)}, u32[]{:S(2)}) collective-permute-start(bf16[2320,128]{1,0:T(8,128)(2,1)S(1)} %fusion.3.refs_0_), channel_id=1, source_target_pairs={{0,32},{16,48},{32,0},{48,16},{1,33},{17,49},{33,1},{49,17},{2,34}... | collective-permute-start | bytes 1781768 | tf_op jit(solution)/shard_map/ppermute | solution.py:249
  48.5 68.1 %collective-permute-start.4 = (bf16[2320,128]{1,0:T(8,128)(2,1)S(1)}, bf16[2320,128]{1,0:T(8,128)(2,1)}, u32[]{:S(2)}, u32[]{:S(2)}) collective-permute-start(bf16[2320,128]{1,0:T(8,128)(2,1)S(1)} %fusion.3.refs_0_), channel_id=1, source_target_pairs={{0,48},{16,0},{32,16},{48,32},{1,49},{17,1},{33,17},{49,33},{2,50}... | collective-permute-start | bytes 1781768 | tf_op jit(solution)/shard_map/ppermute | solution.py:249
  116.5 16.1 %all-to-all-start.3 = ((bf16[16,32,256]{2,1,0:T(8,128)(2,1)}), bf16[16,32,256]{2,1,0:T(8,128)(2,1)S(1)}, u32[]{:S(2)}, u32[]{:S(2)}) async-start(bf16[16,32,256]{2,1,0:T(8,128)(2,1)} %get-tuple-element.33), calls=%async_computation.3 | async-start | bytes 524288 | tf_op jit(solution)/shard_map/all_to_all | solution.py:283
  121.9 3.4 %collective-permute-start.7 = (bf16[2320,128]{1,0:T(8,128)(2,1)S(1)}, bf16[2320,128]{1,0:T(8,128)(2,1)S(1)}, u32[]{:S(2)}, u32[]{:S(2)}) collective-permute-start(bf16[2320,128]{1,0:T(8,128)(2,1)S(1)} %fusion.3.refs_0_), channel_id=1, source_target_pairs={{0,64},{64,0},{1,65},{65,1},{2,66},{66,2},{3,67},{67,3},{4,68},{68... | collective-permute-start | bytes 1781768 | tf_op jit(solution)/shard_map/ppermute | solution.py:256
  122.2 3.5 %collective-permute-start.8 = (bf16[2320,128]{1,0:T(8,128)(2,1)S(1)}, bf16[2320,128]{1,0:T(8,128)(2,1)S(1)}, u32[]{:S(2)}, u32[]{:S(2)}) collective-permute-start(bf16[2320,128]{1,0:T(8,128)(2,1)S(1)} %collective-permute-done.2.refs_1_), channel_id=1, source_target_pairs={{0,64},{64,0},{1,65},{65,1},{2,66},{66,2},{3,67},{67,3},{4,68},{68... | collective-permute-start | bytes 1781768 | tf_op jit(solution)/shard_map/ppermute | solution.py:256
  122.5 3.4 %collective-permute-start.9 = (bf16[2320,128]{1,0:T(8,128)(2,1)}, bf16[2320,128]{1,0:T(8,128)(2,1)S(1)}, u32[]{:S(2)}, u32[]{:S(2)}) collective-permute-start(bf16[2320,128]{1,0:T(8,128)(2,1)} %collective-permute-done.3.refs_2_), channel_id=1, source_target_pairs={{0,64},{64,0},{1,65},{65,1},{2,66},{66,2},{3,67},{67,3},{4,68},{68... | collective-permute-start | bytes 1781768 | tf_op jit(solution)/shard_map/ppermute | solution.py:256
  122.7 4.0 %collective-permute-start.10 = (bf16[2320,128]{1,0:T(8,128)(2,1)}, bf16[2320,128]{1,0:T(8,128)(2,1)S(1)}, u32[]{:S(2)}, u32[]{:S(2)}) collective-permute-start(bf16[2320,128]{1,0:T(8,128)(2,1)} %collective-permute-done.4.refs_3_), channel_id=1, source_target_pairs={{0,64},{64,0},{1,65},{65,1},{2,66},{66,2},{3,67},{67,3},{4,68},{68... | collective-permute-start | bytes 1781768 | tf_op jit(solution)/shard_map/ppermute | solution.py:256
  134.0 9.4 %collective-permute-start.11 = (bf16[32,1024]{1,0:T(8,128)(2,1)S(1)}, bf16[32,1024]{1,0:T(8,128)(2,1)S(1)}, u32[]{:S(2)}, u32[]{:S(2)}) collective-permute-start(bf16[32,1024]{1,0:T(8,128)(2,1)S(1)} %couple.6.refs_0_), channel_id=1, source_target_pairs={{0,4},{4,8},{8,12},{12,0},{1,5},{5,9},{9,13},{13,1},{2,6},{6,10},{... | collective-permute-start | bytes 196616 | tf_op jit(solution)/shard_map/ppermute | solution.py:249
  134.8 8.6 %collective-permute-start.12 = (bf16[32,1024]{1,0:T(8,128)(2,1)S(1)}, bf16[32,1024]{1,0:T(8,128)(2,1)S(1)}, u32[]{:S(2)}, u32[]{:S(2)}) collective-permute-start(bf16[32,1024]{1,0:T(8,128)(2,1)S(1)} %couple.6.refs_0_), channel_id=1, source_target_pairs={{0,8},{4,12},{8,0},{12,4},{1,9},{5,13},{9,1},{13,5},{2,10},{6,14},... | collective-permute-start | bytes 196616 | tf_op jit(solution)/shard_map/ppermute | solution.py:249
  137.2 6.2 %collective-permute-start.13 = (bf16[32,1024]{1,0:T(8,128)(2,1)S(1)}, bf16[32,1024]{1,0:T(8,128)(2,1)S(1)}, u32[]{:S(2)}, u32[]{:S(2)}) collective-permute-start(bf16[32,1024]{1,0:T(8,128)(2,1)S(1)} %couple.6.refs_0_), channel_id=1, source_target_pairs={{0,12},{4,0},{8,4},{12,8},{1,13},{5,1},{9,5},{13,9},{2,14},{6,2},{... | collective-permute-start | bytes 196616 | tf_op jit(solution)/shard_map/ppermute | solution.py:249
  143.4 25.8 %copy-start.4 = (bf16[256,4096]{1,0:T(8,128)(2,1)}, bf16[256,4096]{1,0:T(8,128)(2,1)S(1)}, u32[]{:S(2)}) copy-start(bf16[256,4096]{1,0:T(8,128)(2,1)S(1)} %get-tuple-element.39.refs_4_) | copy-start | bytes 6291460
  163.3 4.5 %collective-permute-start.14 = (bf16[32,1024]{1,0:T(8,128)(2,1)S(1)}, bf16[32,1024]{1,0:T(8,128)(2,1)S(1)}, u32[]{:S(2)}, u32[]{:S(2)}) collective-permute-start(bf16[32,1024]{1,0:T(8,128)(2,1)S(1)} %couple.7.refs_0_), channel_id=1, source_target_pairs={{0,4},{4,8},{8,12},{12,0},{1,5},{5,9},{9,13},{13,1},{2,6},{6,10},{... | collective-permute-start | bytes 196616 | tf_op jit(solution)/shard_map/ppermute | solution.py:249
  163.5 4.9 %collective-permute-start.15 = (bf16[32,1024]{1,0:T(8,128)(2,1)S(1)}, bf16[32,1024]{1,0:T(8,128)(2,1)S(1)}, u32[]{:S(2)}, u32[]{:S(2)}) collective-permute-start(bf16[32,1024]{1,0:T(8,128)(2,1)S(1)} %couple.7.refs_0_), channel_id=1, source_target_pairs={{0,8},{4,12},{8,0},{12,4},{1,9},{5,13},{9,1},{13,5},{2,10},{6,14},... | collective-permute-start | bytes 196616 | tf_op jit(solution)/shard_map/ppermute | solution.py:249
  166.0 3.1 collective-permute-start.16
  170.8 2.2 collective-permute-start.17
  190.5 5.0 %collective-permute-start.18 = (bf16[32,1024]{1,0:T(8,128)(2,1)S(1)}, bf16[32,1024]{1,0:T(8,128)(2,1)S(1)}, u32[]{:S(2)}, u32[]{:S(2)}) collective-permute-start(bf16[32,1024]{1,0:T(8,128)(2,1)S(1)} %couple.8.refs_0_), channel_id=1, source_target_pairs={{0,4},{4,8},{8,12},{12,0},{1,5},{5,9},{9,13},{13,1},{2,6},{6,10},{... | collective-permute-start | bytes 196616 | tf_op jit(solution)/shard_map/ppermute | solution.py:249
  190.6 5.1 %collective-permute-start.19 = (bf16[32,1024]{1,0:T(8,128)(2,1)S(1)}, bf16[32,1024]{1,0:T(8,128)(2,1)S(1)}, u32[]{:S(2)}, u32[]{:S(2)}) collective-permute-start(bf16[32,1024]{1,0:T(8,128)(2,1)S(1)} %couple.8.refs_0_), channel_id=1, source_target_pairs={{0,8},{4,12},{8,0},{12,4},{1,9},{5,13},{9,1},{13,5},{2,10},{6,14},... | collective-permute-start | bytes 196616 | tf_op jit(solution)/shard_map/ppermute | solution.py:249
  193.1 3.1 collective-permute-start.20
  214.2 5.8 %collective-permute-start.21 = (bf16[32,1024]{1,0:T(8,128)(2,1)S(1)}, bf16[32,1024]{1,0:T(8,128)(2,1)S(1)}, u32[]{:S(2)}, u32[]{:S(2)}) collective-permute-start(bf16[32,1024]{1,0:T(8,128)(2,1)S(1)} %couple.9.refs_0_), channel_id=1, source_target_pairs={{0,4},{4,8},{8,12},{12,0},{1,5},{5,9},{9,13},{13,1},{2,6},{6,10},{... | collective-permute-start | bytes 196616 | tf_op jit(solution)/shard_map/ppermute | solution.py:249
  214.3 5.7 %collective-permute-start.22 = (bf16[32,1024]{1,0:T(8,128)(2,1)S(1)}, bf16[32,1024]{1,0:T(8,128)(2,1)S(1)}, u32[]{:S(2)}, u32[]{:S(2)}) collective-permute-start(bf16[32,1024]{1,0:T(8,128)(2,1)S(1)} %couple.9.refs_0_), channel_id=1, source_target_pairs={{0,8},{4,12},{8,0},{12,4},{1,9},{5,13},{9,1},{13,5},{2,10},{6,14},... | collective-permute-start | bytes 196616 | tf_op jit(solution)/shard_map/ppermute | solution.py:249
  216.4 4.0 %collective-permute-start.23 = (bf16[32,1024]{1,0:T(8,128)(2,1)S(1)}, bf16[32,1024]{1,0:T(8,128)(2,1)S(1)}, u32[]{:S(2)}, u32[]{:S(2)}) collective-permute-start(bf16[32,1024]{1,0:T(8,128)(2,1)S(1)} %couple.9.refs_0_), channel_id=1, source_target_pairs={{0,12},{4,0},{8,4},{12,8},{1,13},{5,1},{9,5},{13,9},{2,14},{6,2},{... | collective-permute-start | bytes 196616 | tf_op jit(solution)/shard_map/ppermute | solution.py:249
  222.7 15.4 %all-to-all-start.7 = ((bf16[16,32,256]{2,1,0:T(8,128)(2,1)}), bf16[16,32,256]{2,1,0:T(8,128)(2,1)S(1)}, u32[]{:S(2)}, u32[]{:S(2)}) async-start(bf16[16,32,256]{2,1,0:T(8,128)(2,1)} %get-tuple-element.47), calls=%async_computation.7 | async-start | bytes 524288 | tf_op jit(solution)/shard_map/all_to_all | solution.py:283
  227.4 31.4 %collective-permute-start.31 = (bf16[2,512,256]{2,1,0:T(8,128)(2,1)}, bf16[2,512,256]{2,1,0:T(8,128)(2,1)}, u32[]{:S(2)}, u32[]{:S(2)}) collective-permute-start(bf16[2,512,256]{2,1,0:T(8,128)(2,1)} %param.12), channel_id=1, source_target_pairs={{0,64},{64,0},{1,65},{65,1},{2,66},{66,2},{3,67},{67,3},{4,68},{68... | collective-permute-start | bytes 1572872 | tf_op jit(solution)/shard_map/ppermute | solution.py:256
  240.7 5.2 %collective-permute-start.24 = (bf16[32,1024]{1,0:T(8,128)(2,1)S(1)}, bf16[32,1024]{1,0:T(8,128)(2,1)S(1)}, u32[]{:S(2)}, u32[]{:S(2)}) collective-permute-start(bf16[32,1024]{1,0:T(8,128)(2,1)S(1)} %couple.10.refs_0_), channel_id=1, source_target_pairs={{0,4},{4,8},{8,12},{12,0},{1,5},{5,9},{9,13},{13,1},{2,6},{6,10},{... | collective-permute-start | bytes 196616 | tf_op jit(solution)/shard_map/ppermute | solution.py:249
  242.3 5.5 %collective-permute-start.25 = (bf16[32,1024]{1,0:T(8,128)(2,1)S(1)}, bf16[32,1024]{1,0:T(8,128)(2,1)S(1)}, u32[]{:S(2)}, u32[]{:S(2)}) collective-permute-start(bf16[32,1024]{1,0:T(8,128)(2,1)S(1)} %couple.10.refs_0_), channel_id=1, source_target_pairs={{0,8},{4,12},{8,0},{12,4},{1,9},{5,13},{9,1},{13,5},{2,10},{6,14},... | collective-permute-start | bytes 196616 | tf_op jit(solution)/shard_map/ppermute | solution.py:249
  244.7 3.6 %collective-permute-start.26 = (bf16[32,1024]{1,0:T(8,128)(2,1)S(1)}, bf16[32,1024]{1,0:T(8,128)(2,1)S(1)}, u32[]{:S(2)}, u32[]{:S(2)}) collective-permute-start(bf16[32,1024]{1,0:T(8,128)(2,1)S(1)} %couple.10.refs_0_), channel_id=1, source_target_pairs={{0,12},{4,0},{8,4},{12,8},{1,13},{5,1},{9,5},{13,9},{2,14},{6,2},{... | collective-permute-start | bytes 196616 | tf_op jit(solution)/shard_map/ppermute | solution.py:249
  250.7 18.2 %all-to-all-start.8 = ((bf16[16,32,256]{2,1,0:T(8,128)(2,1)}), bf16[16,32,256]{2,1,0:T(8,128)(2,1)S(1)}, u32[]{:S(2)}, u32[]{:S(2)}) async-start(bf16[16,32,256]{2,1,0:T(8,128)(2,1)} %get-tuple-element.49), calls=%async_computation.8 | async-start | bytes 524288 | tf_op jit(solution)/shard_map/all_to_all | solution.py:283
  271.4 5.9 %collective-permute-start.27 = (bf16[32,1024]{1,0:T(8,128)(2,1)S(1)}, bf16[32,1024]{1,0:T(8,128)(2,1)S(1)}, u32[]{:S(2)}, u32[]{:S(2)}) collective-permute-start(bf16[32,1024]{1,0:T(8,128)(2,1)S(1)} %couple.11.refs_0_), channel_id=1, source_target_pairs={{0,4},{4,8},{8,12},{12,0},{1,5},{5,9},{9,13},{13,1},{2,6},{6,10},{... | collective-permute-start | bytes 196616 | tf_op jit(solution)/shard_map/ppermute | solution.py:249
  271.7 5.6 %collective-permute-start.28 = (bf16[32,1024]{1,0:T(8,128)(2,1)S(1)}, bf16[32,1024]{1,0:T(8,128)(2,1)S(1)}, u32[]{:S(2)}, u32[]{:S(2)}) collective-permute-start(bf16[32,1024]{1,0:T(8,128)(2,1)S(1)} %couple.11.refs_0_), channel_id=1, source_target_pairs={{0,8},{4,12},{8,0},{12,4},{1,9},{5,13},{9,1},{13,5},{2,10},{6,14},... | collective-permute-start | bytes 196616 | tf_op jit(solution)/shard_map/ppermute | solution.py:249
  273.8 3.5 %collective-permute-start.29 = (bf16[32,1024]{1,0:T(8,128)(2,1)S(1)}, bf16[32,1024]{1,0:T(8,128)(2,1)S(1)}, u32[]{:S(2)}, u32[]{:S(2)}) collective-permute-start(bf16[32,1024]{1,0:T(8,128)(2,1)S(1)} %couple.11.refs_0_), channel_id=1, source_target_pairs={{0,12},{4,0},{8,4},{12,8},{1,13},{5,1},{9,5},{13,9},{2,14},{6,2},{... | collective-permute-start | bytes 196616 | tf_op jit(solution)/shard_map/ppermute | solution.py:249
  279.0 28.7 %copy-start.19 = (s32[64,512]{1,0:T(8,128)S(1)}, s32[64,512]{1,0:T(8,128)}, u32[]{:S(2)}) copy-start(s32[64,512]{1,0:T(8,128)} %param.8) | copy-start | bytes 393220
  279.4 3.8 %collective-permute-start.34 = (f32[32,512]{1,0:T(8,128)S(1)}, f32[32,512]{1,0:T(8,128)S(1)}, u32[]{:S(2)}, u32[]{:S(2)}) collective-permute-start(f32[32,512]{1,0:T(8,128)S(1)} %fusion.2), channel_id=1, source_target_pairs={{0,12},{4,0},{8,4},{12,8},{1,13},{5,1},{9,5},{13,9},{2,14},{6,2},{... | collective-permute-start | bytes 196616 | tf_op jit(solution)/shard_map/ppermute | solution.py:249
  281.9 5.0 %collective-permute-start.33 = (f32[32,512]{1,0:T(8,128)S(1)}, f32[32,512]{1,0:T(8,128)S(1)}, u32[]{:S(2)}, u32[]{:S(2)}) collective-permute-start(f32[32,512]{1,0:T(8,128)S(1)} %fusion.2), channel_id=1, source_target_pairs={{0,8},{4,12},{8,0},{12,4},{1,9},{5,13},{9,1},{13,5},{2,10},{6,14},... | collective-permute-start | bytes 196616 | tf_op jit(solution)/shard_map/ppermute | solution.py:249
  282.3 5.3 %collective-permute-start.32 = (f32[32,512]{1,0:T(8,128)S(1)}, f32[32,512]{1,0:T(8,128)S(1)}, u32[]{:S(2)}, u32[]{:S(2)}) collective-permute-start(f32[32,512]{1,0:T(8,128)S(1)} %fusion.2), channel_id=1, source_target_pairs={{0,4},{4,8},{8,12},{12,0},{1,5},{5,9},{9,13},{13,1},{2,6},{6,10},{... | collective-permute-start | bytes 196616 | tf_op jit(solution)/shard_map/ppermute | solution.py:249
  287.7 16.2 %collective-permute-start.37 = (f32[32,512]{1,0:T(8,128)S(1)}, f32[32,512]{1,0:T(8,128)S(1)}, u32[]{:S(2)}, u32[]{:S(2)}) collective-permute-start(f32[32,512]{1,0:T(8,128)S(1)} %add_add_fusion.1), channel_id=1, source_target_pairs={{0,48},{16,0},{32,16},{48,32},{1,49},{17,1},{33,17},{49,33},{2,50}... | collective-permute-start | bytes 196616 | tf_op jit(solution)/shard_map/ppermute | solution.py:249
  289.0 14.9 %collective-permute-start.36 = (f32[32,512]{1,0:T(8,128)S(1)}, f32[32,512]{1,0:T(8,128)S(1)}, u32[]{:S(2)}, u32[]{:S(2)}) collective-permute-start(f32[32,512]{1,0:T(8,128)S(1)} %add_add_fusion.1), channel_id=1, source_target_pairs={{0,32},{16,48},{32,0},{48,16},{1,33},{17,49},{33,1},{49,17},{2,34}... | collective-permute-start | bytes 196616 | tf_op jit(solution)/shard_map/ppermute | solution.py:249
  291.8 12.1 %collective-permute-start.35 = (f32[32,512]{1,0:T(8,128)S(1)}, f32[32,512]{1,0:T(8,128)S(1)}, u32[]{:S(2)}, u32[]{:S(2)}) collective-permute-start(f32[32,512]{1,0:T(8,128)S(1)} %add_add_fusion.1), channel_id=1, source_target_pairs={{0,16},{16,32},{32,48},{48,0},{1,17},{17,33},{33,49},{49,1},{2,18}... | collective-permute-start | bytes 196616 | tf_op jit(solution)/shard_map/ppermute | solution.py:249
  291.8 13.2 %collective-permute-start.30 = (bf16[2,32,256]{2,1,0:T(8,128)(2,1)S(1)}, bf16[2,32,256]{2,1,0:T(8,128)(2,1)S(1)}, u32[]{:S(2)}, u32[]{:S(2)}) collective-permute-start(bf16[2,32,256]{2,1,0:T(8,128)(2,1)S(1)} %broadcast_select_fusion.7), channel_id=1, source_target_pairs={{0,64},{64,0},{1,65},{65,1},{2,66},{66,2},{3,67},{67,3},{4,68},{68... | collective-permute-start | bytes 98312 | tf_op jit(solution)/shard_map/ppermute | solution.py:256
  303.9 3.8 %collective-permute-start.38 = (f32[32,512]{1,0:T(8,128)S(1)}, f32[32,512]{1,0:T(8,128)S(1)}, u32[]{:S(2)}, u32[]{:S(2)}) collective-permute-start(f32[32,512]{1,0:T(8,128)S(1)} %add_add_fusion), channel_id=1, source_target_pairs={{0,128},{128,0},{1,129},{129,1},{2,130},{130,2},{3,131},{131,3},{4... | collective-permute-start | bytes 196616 | tf_op jit(solution)/shard_map/ppermute | solution.py:249
  308.0 8.7 %collective-permute-start.39 = (f32[32,512]{1,0:T(8,128)S(1)}, f32[32,512]{1,0:T(8,128)S(1)}, u32[]{:S(2)}, u32[]{:S(2)}) collective-permute-start(f32[32,512]{1,0:T(8,128)S(1)} %fusion.9), channel_id=1, source_target_pairs={{0,64},{64,0},{1,65},{65,1},{2,66},{66,2},{3,67},{67,3},{4,68},{68... | collective-permute-start | bytes 196616 | tf_op jit(solution)/shard_map/ppermute | solution.py:256
  (18 other events, 124.4 us)

commit v2 on v1

--- a/solution.py
+++ b/solution.py
@@ -47,27 +47,23 @@
     return ref.at[i], out
 
 
-def coupling_slices(ref, k, out, i):
-    size = out.shape[1]
-    return ref.at[pl.ds(i * size, size)], out.at[k]
-
-
-def couple_kernel(place, cols, x_ref, s_ref, c_ref, out_ref, *, step, slots):
-    lines, tall, block = c_ref.shape
-    rows = tall // (slots * block)
+def couple_kernel(place, cols, x_ref, own_ref, other_ref, out_ref):
+    lines, tall, block = other_ref.shape
+    slots = tall // block
     per = x_ref.shape[2] // block
     probes = x_ref.shape[1]
 
     def body(k, carry):
-        for row in range(rows):
+        home = lax.rem(place[1] + lines - k, lines)
+        for c_ref, row in ((own_ref, place[0]), (other_ref, 1 - place[0])):
             total = None
             for slot in range(0, slots, 2):
                 left, right = [], []
                 for pair in range(2):
-                    col = cols[k, (step * rows + row) * slots + slot + pair]
+                    col = cols[k, row * slots + slot + pair]
                     lanes = pl.ds(pl.multiple_of((col % per) * block, block), block)
                     left.append(x_ref[col // per, :, lanes])
-                    at = (row * slots + slot + pair) * block
+                    at = (slot + pair) * block
                     right.append(c_ref[k, at : at + block, :])
                 term = lax.dot_general(
                     jnp.concatenate(left, axis=1),
@@ -76,11 +72,12 @@
                     preferred_element_type=jnp.float32,
                 )
                 total = term if total is None else total + term
-            at = (row * s_ref.shape[1]) // rows + step * probes
-            source = s_ref[k, at : at + probes, :].astype(jnp.float32)
-            home = lax.rem(place[1] + lines - k, lines)
-            lanes = pl.ds(pl.multiple_of((home * rows + row) * block, block), block)
-            out_ref[:, lanes] = (source - total).astype(jnp.bfloat16)
+            at = pl.multiple_of(tall + row * probes, probes)
+            source = own_ref[k, pl.ds(at, probes), :].astype(jnp.float32)
+            lanes = pl.ds(pl.multiple_of((home * per + row) * block, block), block)
+            resid = (source - total).astype(jnp.bfloat16)
+            for peer in range(out_ref.shape[0]):
+                out_ref[peer, :, lanes] = resid
         return carry
 
     lax.fori_loop(0, lines, body, 0)
@@ -117,45 +114,21 @@
     finish(total, outs)
 
 
-def early_couple_kernel(place, cols, x_ref, s_ref, own_ref, other_ref, out_ref, c_buf, sem, *, step, per_core):
-    rows, slots, block, _ = c_buf.shape
-    own, other = (
-        [pltpu.make_async_copy(source.at[step % per_core], c_buf, sem)] for source in (own_ref, other_ref)
-    )
-    start_one_of(place[0] == step // per_core, own, other)
-    own[0].wait()
-    per = x_ref.shape[2] // block
-    for row in range(rows):
-        total = None
-        for slot in range(slots):
-            col = cols[(step * rows + row) * slots + slot]
-            lanes = pl.ds(pl.multiple_of((col % per) * block, block), block)
-            term = lax.dot_general(
-                x_ref[col // per, :, lanes], c_buf[row, slot], NT, preferred_element_type=jnp.float32
-            )
-            total = term if total is None else total + term
-        span = slice(row * block, (row + 1) * block)
-        resid = (s_ref[:, span].astype(jnp.float32) - total).astype(jnp.bfloat16)
-        for peer in range(out_ref.shape[0]):
-            out_ref[peer, :, span] = resid
-
-
-def apply_kernel(place, *refs, lines):
-    pieces, l_ref, outs = refs[:lines], refs[lines], refs[lines + 1 :]
+def apply_kernel(r_ref, l_ref, *outs):
     width = l_ref.shape[0]
+    lines = r_ref.shape[0]
 
     def body(zh, total):
-        for k in range(lines):
-            y = lax.rem(place[2] + lines - k, lines)
+        for y in range(lines):
             lanes = pl.ds(pl.multiple_of((zh * lines + y) * width, width), width)
             here = pl.ds(pl.multiple_of(zh * width, width), width)
             total = total + lax.dot_general(
-                pieces[k][:, here], l_ref[:, lanes], NT, preferred_element_type=jnp.float32
+                r_ref[y, :, here], l_ref[:, lanes], NT, preferred_element_type=jnp.float32
             )
         return total
 
-    start = jnp.zeros((pieces[0].shape[0], width), jnp.float32)
-    finish(lax.fori_loop(0, pieces[0].shape[1] // width, body, start), outs)
+    start = jnp.zeros((r_ref.shape[1], width), jnp.float32)
+    finish(lax.fori_loop(0, r_ref.shape[2] // width, body, start), outs)
 
 
 VMEM = pl.BlockSpec(memory_space=pltpu.VMEM)
@@ -182,16 +155,18 @@
     )(place, *own, *other, after)
 
 
-def couple(place, cols, pieces, source, c, step, slots):
-    lines, tall, block = c.shape
+def couple(place, pieces, shared, receivers):
+    cols, own, other = shared
+    lines, tall, block = other.shape
+    per = pieces.shape[2] // block
     return pl.pallas_call(
-        functools.partial(couple_kernel, step=step, slots=slots),
-        out_shape=jax.ShapeDtypeStruct((pieces.shape[1], lines * tall // slots), jnp.bfloat16),
+        couple_kernel,
+        out_shape=jax.ShapeDtypeStruct((receivers, pieces.shape[1], lines * per * block), jnp.bfloat16),
         in_specs=[SMEM, SMEM, VMEM, VMEM, VMEM],
         out_specs=VMEM,
         compiler_params=PARAMS,
         name="couple",
-    )(place, cols, pieces, source, c)
+    )(place, cols, pieces, own, other)
 
 
 def solved_shapes(probes, rows, peers):
@@ -201,16 +176,16 @@
     return tuple(shapes)
 
 
-def apply_factor(place, pieces, factor, peers):
-    shapes = solved_shapes(pieces[0].shape[0], factor.shape[0], peers)
+def apply_factor(pieces, factor, peers):
+    shapes = solved_shapes(pieces.shape[1], factor.shape[0], peers)
     return pl.pallas_call(
-        functools.partial(apply_kernel, lines=len(pieces)),
+        apply_kernel,
         out_shape=shapes,
-        in_specs=[SMEM] + [VMEM] * (len(pieces) + 1),
+        in_specs=[VMEM, VMEM],
         out_specs=tuple([VMEM] * len(shapes)),
         compiler_params=PARAMS,
         name="apply",
-    )(place, *pieces, factor)
+    )(pieces, factor)
 
 
 def apply_early(place, pieces, own, other, step):
@@ -231,18 +206,6 @@
     )(place, pieces, own, other)
 
 
-def couple_early(place, cols, pieces, source, own, other, step):
-    return pl.pallas_call(
-        functools.partial(early_couple_kernel, step=step, per_core=own.shape[0]),
-        out_shape=jax.ShapeDtypeStruct(pieces.shape, jnp.bfloat16),
-        in_specs=[SMEM, SMEM, VMEM, VMEM, HBM, HBM],
-        out_specs=VMEM,
-        scratch_shapes=[pltpu.VMEM(own.shape[1:], own.dtype), pltpu.SemaphoreType.DMA],
-        compiler_params=PARAMS,
-        name="couple_early",
-    )(place, cols, pieces, source, own, other)
-
-
 def line(value, axis):
     size = lax.axis_size(axis)
     moved = {
@@ -273,50 +236,61 @@
 
     source = (2 * signs - 1).astype(jnp.bfloat16).reshape(cores, probes, own_steps, local)
     source = source.transpose(0, 2, 1, 3)
-    other_half = swap(jnp.where(first, source[1], source[0]))
-    own_source = in_order(jnp.where(first, source[0], source[1]), other_half)
+    own_cols = jnp.pad(coupling_cols.reshape(own_steps, 1, -1), ((0, 0), (0, 15), (0, local - coupling_cols[0].size)))
+
+    def packed(half):
+        return jnp.concatenate([half, own_cols.astype(jnp.bfloat16)], axis=1)
+
+    other_half = swap(packed(jnp.where(first, source[1], source[0])))
+    both = in_order(packed(jnp.where(first, source[0], source[1])), other_half)
+    own_source = both[:, :probes]
     spread = jnp.broadcast_to(own_source[0][None], (peers, probes, local))
-    own_cols = in_order(coupling_cols, swap(coupling_cols)).reshape(-1)
     other_factors, other_couplings = swap(inverse_factors), swap(couplings)
+    slots, block = couplings.shape[2:4]
+    tall, width = slots * block, 2 * slots
 
     def everywhere(value):
         return lax.all_to_all(value, NODES, 0, 0)
 
-    solved0 = apply_early(place, everywhere(spread), inverse_factors, other_factors, 0)
-    slots, block = couplings.shape[2:4]
-    cols = own_cols.reshape(1, -1).astype(jnp.bfloat16)
-    width = cols.shape[1]
-    cols = jnp.pad(cols, ((0, 15), (0, block - width)))
-    flat = own_source.reshape(steps * probes, local)
-    halves = [flat[:, i : i + block] for i in range(0, local, block)]
-    bundle = jnp.concatenate([couplings.reshape(-1, block)] + halves + [cols], axis=0)
-    shared = line(bundle, "zh")
-    at = couplings.size // block
-    until = at + steps * probes * local // block
-    tall = at // own_steps
-    resid = couple_early(
-        place, own_cols, everywhere(solved0[1]), own_source[1], couplings, other_couplings, 1
+    def send(step, after):
+        i = step % own_steps
+        own_c, other_c, _ = lax.optimization_barrier((couplings[i], other_couplings[i], after))
+        low = first if step < own_steps else jnp.logical_not(first)
+        rows = jnp.where(low, own_c, other_c).reshape(2, tall, block)
+        mine, theirs = jnp.where(first, rows[0], rows[1]), jnp.where(first, rows[1], rows[0])
+        tail = both[step, probes:, :block]
+        halves = [own_source[step, :, j : j + block] for j in range(0, local, block)]
+        return line(jnp.concatenate([mine] + halves + [tail], axis=0), "zh"), theirs
+
+    def receive(sent, after):
+        bundles, theirs = sent
+        bundles, theirs, _ = lax.optimization_barrier((bundles, theirs, after))
+        own = jnp.stack(bundles)
+        other = jnp.concatenate([theirs[None], swap(own[1:, :tall])], axis=0)
+        cols = own[:, -16, :width].astype(jnp.int32)
+        return cols, own, other
+
+    sent, shared = {}, {}
+    sent[1] = send(1, spread)
+    outs = apply_early(place, everywhere(spread), inverse_factors, other_factors, 0)
+    factors = arrange(
+        factor_slices, place, [inverse_factors], [other_factors], steps, inverse_factors.shape[1:], "factors", outs[0]
     )
-    solved1 = apply_early(place, everywhere(resid), inverse_factors, other_factors, 1)
-    pieces = everywhere(solved1[1])
-    shared, after = lax.optimization_barrier((shared, solved1[0]))
-    source = jnp.stack([s[at:until] for s in shared])
-    cols = jnp.concatenate([s[until : until + 1, :width] for s in shared], axis=0).astype(jnp.int32)
-    shape = (len(shared), tall, block)
-    blocks = arrange(
-        coupling_slices, place, shared, [swap(s) for s in shared], steps, shape, "couplings", after
-    )
-    factors = arrange(
-        factor_slices, place, [inverse_factors], [other_factors], steps, inverse_factors.shape[1:], "factors", after
-    )
-
+    shared[1] = receive(sent[1], outs[0])
+    sent[2] = send(2, outs[0])
+    pieces = everywhere(outs[1])
     for turn in range(turns):
         results = []
-        for step in range(2 if turn == 0 else 0, steps):
-            resid = line(couple(place, cols, pieces, source, blocks[step], step, slots), "y")
+        for step in range(1 if turn == 0 else 0, steps):
+            resid = lax.all_to_all(couple(place, pieces, shared[step], lax.axis_size("y")), "y", 0, 0)
             more = step + 1 < steps
-            outs = apply_factor(place, resid, factors[step], peers if more else 0)
+            outs = apply_factor(resid, factors[step], peers if more else 0)
             results.append(outs[0])
+            if turn == 0:
+                later, following = (step + 1) % steps, (step + 2) % steps
+                shared[later] = receive(sent[later], outs[0])
+                if following != 1:
+                    sent[following] = send(following, outs[0])
             if more:
                 pieces = everywhere(outs[1])
         if turn + 1 < turns:

time: 328 us -> 355 us (1.082)
  blocking collectives: 112 us -> 48.9 us
  waiting for transfers between devices: 43.6 us -> 84.9 us
  other arithmetic: 5.14 us -> 33.4 us
  local copies, waits for them, and re-layouts: 16.9 us -> 29.7 us
  starting transfers between devices: 113 us -> 124 us
  Pallas kernels: 33.4 us -> 26 us
    all_to_all x4 -> x1, blocking collectives: 104 us -> 14.9 us  [everywhere(): return lax.all_to_all(value, NODES, 0, 0)]
    all_to_all x0 -> x3, blocking collectives: none -> 25.6 us  [shards(): lax.all_to_all(couple(place, pieces, shared[step], lax.axis_size('y')), '...]
    all_to_all x5 -> x7, waiting for transfers between devices: 19.3 us -> 41.8 us  [everywhere(): return lax.all_to_all(value, NODES, 0, 0)]
    ppermute x28 -> x19, waiting for transfers between devices: 16.6 us -> 34.6 us  [line(): lax.ppermute(value, axis, [(i, (i + k) % size) for i in range(size)])]
    all_to_all x0 -> x4, starting transfers between devices: none -> 13.8 us  [shards(): lax.all_to_all(couple(place, pieces, shared[step], lax.axis_size('y')), '...]
    unnamed x43 -> x85, local copies, waits for them, and re-layouts: 13.7 us -> 25.9 us
    another operation x1 -> x9, other arithmetic: 0.04 us -> 12.3 us  [the longest x8 11.6 us: receive(): own = jnp.stack(bundles)]
    all_to_all x5 -> x7, starting transfers between devices: 32.5 us -> 43.1 us  [everywhere(): return lax.all_to_all(value, NODES, 0, 0)]
  transfers between devices with their start and end apart: 45 -> 41, of which waited for: 25 -> 23; matrix products, arithmetic and copies ran while one was open for 3% -> 9% of each run, Pallas kernels for 5% -> 4%
where the time goes in v2:
time: 355 us; the launch traced here: 352 us
  starting transfers between devices  124 us (35%)
  waiting for transfers between devices  84.9 us (24%)
  blocking collectives  48.9 us (14%)
  other arithmetic  33.4 us (9%)
  local copies, waits for them, and re-layouts  29.7 us (8%)
  Pallas kernels  26 us (7%)
  matrix products  4.04 us (1%)
    all_to_all x7, starting transfers between devices, everywhere(): return lax.all_to_all(value, NODES, 0, 0)  43.1 us
    all_to_all x7, waiting for transfers between devices, everywhere(): return lax.all_to_all(value, NODES, 0, 0)  41.8 us
    ppermute x19, waiting for transfers between devices, line(): lax.ppermute(value, axis, [(i, (i + k) % size) for i in range(size)])  34.6 us
    ppermute x19, starting transfers between devices, line(): lax.ppermute(value, axis, [(i, (i + k) % size) for i in range(size)])  33.2 us
    ppermute x10, starting transfers between devices, swap(): return lax.ppermute(value, 'core', [(0, 1), (1, 0)])  32.7 us
    unnamed x85, local copies, waits for them, and re-layouts  25.9 us
    all_to_all x3, blocking collectives, shards(): lax.all_to_all(couple(place, pieces, shared[step], lax.axis_size('y')), '...  25.6 us
    all_to_all x1, blocking collectives, everywhere(): return lax.all_to_all(value, NODES, 0, 0)  14.9 us
  transfers between devices with their start and end apart: 41, of which 23 were waited for; matrix products, arithmetic and copies ran while one was open for 9% of the time, Pallas kernels for 4%

profile of v2, /device:TPU:1, one launch (start us, length us, event | category | flops | bytes accessed | tf_op | source)
XLA Modules:
  0.0 352.5 jit_solution(7919958395750055040)
XLA Ops:
  0.6 3.3 collective-permute-start.2
  7.4 3.5 collective-permute-done.1
  11.7 9.2 %all-to-all-start = ((bf16[16,32,256]{2,1,0:T(8,128)(2,1)}), bf16[16,32,256]{2,1,0:T(8,128)(2,1)S(1)}, u32[]{:S(2)}, u32[]{:S(2)}) async-start(bf16[16,32,256]{2,1,0:T(8,128)(2,1)} %broadcast_in_dim.26), calls=%async_computation | async-start | bytes 524288 | tf_op jit(solution)/shard_map/all_to_all | solution.py:253
  22.2 2.3 collective-permute-start.6
  24.5 3.3 collective-permute-start.7
  27.8 3.3 collective-permute-start.8
  31.6 2.2 copy-done.1
  33.8 3.8 %apply_early.1 = (bf16[32,256]{1,0:T(8,128)(2,1)S(1)}, bf16[16,32,256]{2,1,0:T(8,128)(2,1)}) custom-call(s32[3]{0:T(128)S(1)} %pad_add_fusion.place, bf16[16,32,256]{2,1,0:T(8,128)(2,1)S(1)} %all-to-all-done.r_ref, bf16[2,256,4096]{2,1,0:T(8,128)(2,1)S(1)} %copy-done.1, bf16[2,256,4096]{2,1,0:T(8,128)(2,1)} %collective-permute-done.2.other_ref.refs_1_), custom_call_target="tpu_custom_call" | custom-call | tf_op jit(solution)/shard_map/apply_early/pallas_call | solution.py:195
  37.6 3.8 %collective-permute-done.7 = bf16[592,128]{1,0:T(8,128)(2,1)S(1)} collective-permute-done((bf16[592,128]{1,0:T(8,128)(2,1)S(1)}, bf16[592,128]{1,0:T(8,128)(2,1)S(1)}, u32[]{:S(2)}, u32[]{:S(2)}) %collective-permute-start.7) | collective-permute-done | bytes 151584 | tf_op jit(solution)/shard_map/ppermute | solution.py:212
  43.4 3.6 %collective-permute-start.9 = (bf16[3,512,128]{2,1,0:T(8,128)(2,1)}, bf16[3,512,128]{2,1,0:T(8,128)(2,1)}, u32[]{:S(2)}, u32[]{:S(2)}) collective-permute-start(bf16[3,512,128]{2,1,0:T(8,128)(2,1)} %pad_maximum_fusion.14), channel_id=1, source_target_pairs={{0,64},{64,0},{1,65},{65,1},{2,66},{66,2},{3,67},{67,3},{4,68},{68... | collective-permute-start | bytes 1179656 | tf_op jit(solution)/shard_map/ppermute | solution.py:219
  47.0 5.5 %all-to-all-start.1 = ((bf16[16,32,256]{2,1,0:T(8,128)(2,1)}), bf16[16,32,256]{2,1,0:T(8,128)(2,1)S(1)}, u32[]{:S(2)}, u32[]{:S(2)}) async-start(bf16[16,32,256]{2,1,0:T(8,128)(2,1)} %get-tuple-element.57), calls=%async_computation.1 | async-start | bytes 524288 | tf_op jit(solution)/shard_map/all_to_all | solution.py:253
  54.3 10.6 %all-to-all-done.1.x_ref = bf16[16,32,256]{2,1,0:T(8,128)(2,1)S(1)} async-done(((bf16[16,32,256]{2,1,0:T(8,128)(2,1)}), bf16[16,32,256]{2,1,0:T(8,128)(2,1)S(1)}, u32[]{:S(2)}, u32[]{:S(2)}) %all-to-all-start.1) | async-done | bytes 262176 | tf_op jit(solution)/shard_map/all_to_all | solution.py:253
  65.0 2.1 couple.7
  67.1 3.4 all-to-all-start.2
  73.7 2.1 collective-permute-start.5
  75.8 2.2 copy-done.2
  78.0 2.8 factors.1
  93.9 8.7 %all-to-all-start.3 = ((bf16[16,32,256]{2,1,0:T(8,128)(2,1)}), bf16[16,32,256]{2,1,0:T(8,128)(2,1)S(1)}, u32[]{:S(2)}, u32[]{:S(2)}) async-start(bf16[16,32,256]{2,1,0:T(8,128)(2,1)} %copy-done.27), calls=%async_computation.3 | async-start | bytes 524288 | tf_op jit(solution)/shard_map/all_to_all | solution.py:253
  106.9 7.9 %all-to-all-done.3.x_ref = bf16[16,32,256]{2,1,0:T(8,128)(2,1)S(1)} async-done(((bf16[16,32,256]{2,1,0:T(8,128)(2,1)}), bf16[16,32,256]{2,1,0:T(8,128)(2,1)S(1)}, u32[]{:S(2)}, u32[]{:S(2)}) %all-to-all-start.3) | async-done | bytes 262176 | tf_op jit(solution)/shard_map/all_to_all | solution.py:253
  119.0 3.4 all-to-all-start.4
  131.8 7.2 %collective-permute-done.15 = bf16[592,128]{1,0:T(8,128)(2,1)} collective-permute-done((bf16[592,128]{1,0:T(8,128)(2,1)}, bf16[592,128]{1,0:T(8,128)(2,1)}, u32[]{:S(2)}, u32[]{:S(2)}) %collective-permute-start.15) | collective-permute-done | bytes 151584 | tf_op jit(solution)/shard_map/ppermute | solution.py:212
  139.1 2.4 collective-permute-done.16
  145.8 5.7 %all-to-all-start.5 = ((bf16[16,32,256]{2,1,0:T(8,128)(2,1)}), bf16[16,32,256]{2,1,0:T(8,128)(2,1)S(1)}, u32[]{:S(2)}, u32[]{:S(2)}) async-start(bf16[16,32,256]{2,1,0:T(8,128)(2,1)} %copy-done.28), calls=%async_computation.5 | async-start | bytes 524288 | tf_op jit(solution)/shard_map/all_to_all | solution.py:253
  155.8 6.6 %all-to-all-done.5.x_ref = bf16[16,32,256]{2,1,0:T(8,128)(2,1)S(1)} async-done(((bf16[16,32,256]{2,1,0:T(8,128)(2,1)}), bf16[16,32,256]{2,1,0:T(8,128)(2,1)S(1)}, u32[]{:S(2)}, u32[]{:S(2)}) %all-to-all-start.5) | async-done | bytes 262176 | tf_op jit(solution)/shard_map/all_to_all | solution.py:253
  166.6 3.5 all-to-all-start.6
  171.7 3.3 collective-permute-start.11
  176.1 2.5 collective-permute-start.13
  180.5 9.6 %collective-permute-done.12 = bf16[592,128]{1,0:T(8,128)(2,1)} collective-permute-done((bf16[592,128]{1,0:T(8,128)(2,1)}, bf16[592,128]{1,0:T(8,128)(2,1)}, u32[]{:S(2)}, u32[]{:S(2)}) %collective-permute-start.12) | collective-permute-done | bytes 151584 | tf_op jit(solution)/shard_map/ppermute | solution.py:212
  197.0 6.3 %all-to-all-start.7 = ((bf16[16,32,256]{2,1,0:T(8,128)(2,1)}), bf16[16,32,256]{2,1,0:T(8,128)(2,1)S(1)}, u32[]{:S(2)}, u32[]{:S(2)}) async-start(bf16[16,32,256]{2,1,0:T(8,128)(2,1)} %broadcast_in_dim.30), calls=%async_computation.7 | async-start | bytes 524288 | tf_op jit(solution)/shard_map/all_to_all | solution.py:253
  207.3 6.1 %all-to-all-done.7.x_ref = bf16[16,32,256]{2,1,0:T(8,128)(2,1)S(1)} async-done(((bf16[16,32,256]{2,1,0:T(8,128)(2,1)}), bf16[16,32,256]{2,1,0:T(8,128)(2,1)S(1)}, u32[]{:S(2)}, u32[]{:S(2)}) %all-to-all-start.7) | async-done | bytes 262176 | tf_op jit(solution)/shard_map/all_to_all | solution.py:253
  217.0 8.6 %all_to_all.75.r_ref = bf16[4,32,1024]{2,1,0:T(8,128)(2,1)S(1)} all-to-all(bf16[4,32,1024]{2,1,0:T(8,128)(2,1)S(1)} %couple.10), channel_id=1, replica_groups=mesh['zl'=2,'core'=2,'zh'=4,'y'=4,'x'=4] {'y'}, dimensions={0} | all-to-all | bytes 524288 | tf_op jit(solution)/shard_map/all_to_all | solution.py:285
  226.7 14.9 %all_to_all.76.x_ref = bf16[16,32,256]{2,1,0:T(8,128)(2,1)S(1)} all-to-all(bf16[16,32,256]{2,1,0:T(8,128)(2,1)S(1)} %get-tuple-element.87), channel_id=1, replica_groups=mesh['zl'=2,'core'=2,'zh'=4,'y'=4,'x'=4] {'zh','y'}, dimensions={0} | all-to-all | bytes 524288 | tf_op jit(solution)/shard_map/all_to_all | solution.py:253
  243.0 8.4 %all_to_all.77.r_ref = bf16[4,32,1024]{2,1,0:T(8,128)(2,1)S(1)} all-to-all(bf16[4,32,1024]{2,1,0:T(8,128)(2,1)S(1)} %couple.11), channel_id=1, replica_groups=mesh['zl'=2,'core'=2,'zh'=4,'y'=4,'x'=4] {'y'}, dimensions={0} | all-to-all | bytes 524288 | tf_op jit(solution)/shard_map/all_to_all | solution.py:285
  253.2 3.5 %all-to-all-start.11 = ((bf16[16,32,256]{2,1,0:T(8,128)(2,1)}), bf16[16,32,256]{2,1,0:T(8,128)(2,1)S(1)}, u32[]{:S(2)}, u32[]{:S(2)}) async-start(bf16[16,32,256]{2,1,0:T(8,128)(2,1)} %copy-done.30), calls=%async_computation.11 | async-start | bytes 524288 | tf_op jit(solution)/shard_map/all_to_all | solution.py:253
  256.8 6.1 %collective-permute-start.21 = (bf16[2,512,256]{2,1,0:T(8,128)(2,1)}, bf16[2,512,256]{2,1,0:T(8,128)(2,1)}, u32[]{:S(2)}, u32[]{:S(2)}) collective-permute-start(bf16[2,512,256]{2,1,0:T(8,128)(2,1)} %param.12), channel_id=1, source_target_pairs={{0,64},{64,0},{1,65},{65,1},{2,66},{66,2},{3,67},{67,3},{4,68},{68... | collective-permute-start | bytes 1572872 | tf_op jit(solution)/shard_map/ppermute | solution.py:219
  262.9 3.9 %all-to-all-done.11.x_ref = bf16[16,32,256]{2,1,0:T(8,128)(2,1)S(1)} async-done(((bf16[16,32,256]{2,1,0:T(8,128)(2,1)}), bf16[16,32,256]{2,1,0:T(8,128)(2,1)S(1)}, u32[]{:S(2)}, u32[]{:S(2)}) %all-to-all-start.11) | async-done | bytes 262176 | tf_op jit(solution)/shard_map/all_to_all | solution.py:253
  269.2 8.6 %all_to_all.78.r_ref = bf16[4,32,1024]{2,1,0:T(8,128)(2,1)S(1)} all-to-all(bf16[4,32,1024]{2,1,0:T(8,128)(2,1)S(1)} %couple.12), channel_id=1, replica_groups=mesh['zl'=2,'core'=2,'zh'=4,'y'=4,'x'=4] {'y'}, dimensions={0} | all-to-all | bytes 524288 | tf_op jit(solution)/shard_map/all_to_all | solution.py:285
  279.6 4.2 %all-to-all-start.13 = ((bf16[16,32,256]{2,1,0:T(8,128)(2,1)}), bf16[16,32,256]{2,1,0:T(8,128)(2,1)S(1)}, u32[]{:S(2)}, u32[]{:S(2)}) async-start(bf16[16,32,256]{2,1,0:T(8,128)(2,1)} %copy-done.29), calls=%async_computation.13 | async-start | bytes 524288 | tf_op jit(solution)/shard_map/all_to_all | solution.py:253
  283.8 2.1 broadcast_select_fusion.1
  287.5 6.3 %all-to-all-done.13.x_ref = bf16[16,32,256]{2,1,0:T(8,128)(2,1)S(1)} async-done(((bf16[16,32,256]{2,1,0:T(8,128)(2,1)}), bf16[16,32,256]{2,1,0:T(8,128)(2,1)S(1)}, u32[]{:S(2)}, u32[]{:S(2)}) %all-to-all-start.13) | async-done | bytes 262176 | tf_op jit(solution)/shard_map/all_to_all | solution.py:253
  296.9 3.5 %all-to-all-start.14 = ((bf16[4,32,1024]{2,1,0:T(8,128)(2,1)}), bf16[4,32,1024]{2,1,0:T(8,128)(2,1)S(1)}, u32[]{:S(2)}, u32[]{:S(2)}) async-start(bf16[4,32,1024]{2,1,0:T(8,128)(2,1)} %copy-done.26), calls=%async_computation.14 | async-start | bytes 524288 | tf_op jit(solution)/shard_map/all_to_all | solution.py:285
  302.2 3.7 %all-to-all-done.14.r_ref = bf16[4,32,1024]{2,1,0:T(8,128)(2,1)S(1)} async-done(((bf16[4,32,1024]{2,1,0:T(8,128)(2,1)}), bf16[4,32,1024]{2,1,0:T(8,128)(2,1)S(1)}, u32[]{:S(2)}, u32[]{:S(2)}) %all-to-all-start.14) | async-done | bytes 262176 | tf_op jit(solution)/shard_map/all_to_all | solution.py:285
  311.2 2.2 collective-permute-done.22
  316.4 2.3 collective-permute-start.26
  320.2 11.6 %collective-permute-start.20 = (bf16[2,32,256]{2,1,0:T(8,128)(2,1)S(1)}, bf16[2,32,256]{2,1,0:T(8,128)(2,1)S(1)}, u32[]{:S(2)}, u32[]{:S(2)}) collective-permute-start(bf16[2,32,256]{2,1,0:T(8,128)(2,1)S(1)} %broadcast_select_fusion.20), channel_id=1, source_target_pairs={{0,64},{64,0},{1,65},{65,1},{2,66},{66,2},{3,67},{67,3},{4,68},{68... | collective-permute-start | bytes 98312 | tf_op jit(solution)/shard_map/ppermute | solution.py:219
  332.7 3.2 collective-permute-done.28
  336.1 5.2 %collective-permute-start.29 = (f32[32,512]{1,0:T(8,128)S(1)}, f32[32,512]{1,0:T(8,128)S(1)}, u32[]{:S(2)}, u32[]{:S(2)}) collective-permute-start(f32[32,512]{1,0:T(8,128)S(1)} %fusion.10), channel_id=1, source_target_pairs={{0,64},{64,0},{1,65},{65,1},{2,66},{66,2},{3,67},{67,3},{4,68},{68... | collective-permute-start | bytes 196616 | tf_op jit(solution)/shard_map/ppermute | solution.py:219
  342.9 8.4 %all-reduce.1 = (f32[2,256]{1,0:T(2,128)S(1)}, f32[512]{0:T(512)S(1)}) all-reduce(f32[2,256]{1,0:T(2,128)S(1)} %multiply_reduce_fusion.1, f32[512]{0:T(512)S(1)} %get-tuple-element.102), channel_id=1, replica_groups=mesh['zl'=2,'core'=2,'zh'=4,'y'=4,'x'=4] {'x'}, use_global_device_ids=true, to_apply=%region_1.2 | all-reduce | flops 1024 | bytes 8192 | tf_op jit(solution)/shard_map/psum | solution.py:321
  (199 shorter events, 104.2 us)
Async XLA Ops:
  0.6 335.2 %copy-start = (bf16[512,512]{1,0:T(8,128)(2,1)S(1)}, bf16[512,512]{1,0:T(8,128)(2,1)}, u32[]{:S(2)}) copy-start(bf16[512,512]{1,0:T(8,128)(2,1)} %param.13) | copy-start | bytes 1572868
  0.6 30.9 %collective-permute-start.2 = (bf16[2,256,4096]{2,1,0:T(8,128)(2,1)}, bf16[2,256,4096]{2,1,0:T(8,128)(2,1)}, u32[]{:S(2)}, u32[]{:S(2)}) collective-permute-start(bf16[2,256,4096]{2,1,0:T(8,128)(2,1)} %refs_0_.1), channel_id=1, source_target_pairs={{0,64},{64,0},{1,65},{65,1},{2,66},{66,2},{3,67},{67,3},{4,68},{68... | collective-permute-start | bytes 12582920 | tf_op jit(solution)/shard_map/ppermute | solution.py:219
  5.7 5.2 %collective-permute-start.1 = (bf16[2,48,256]{2,1,0:T(8,128)(2,1)S(1)}, bf16[2,48,256]{2,1,0:T(8,128)(2,1)S(1)}, u32[]{:S(2)}, u32[]{:S(2)}) collective-permute-start(bf16[2,48,256]{2,1,0:T(8,128)(2,1)S(1)} %fusion.9), channel_id=1, source_target_pairs={{0,64},{64,0},{1,65},{65,1},{2,66},{66,2},{3,67},{67,3},{4,68},{68... | collective-permute-start | bytes 147464 | tf_op jit(solution)/shard_map/ppermute | solution.py:219
  5.9 16.2 %collective-permute-start = (bf16[2,2,4,128,128]{4,3,2,1,0:T(8,128)(2,1)}, bf16[2,2,4,128,128]{4,3,2,1,0:T(8,128)(2,1)S(1)}, u32[]{:S(2)}, u32[]{:S(2)}) collective-permute-start(bf16[2,2,4,128,128]{4,3,2,1,0:T(8,128)(2,1)} %param.10), channel_id=1, source_target_pairs={{0,64},{64,0},{1,65},{65,1},{2,66},{66,2},{3,67},{67,3},{4,68},{68... | collective-permute-start | bytes 1572872 | tf_op jit(solution)/shard_map/ppermute | solution.py:219
  7.4 30.2 %copy-start.33 = (bf16[2,4,128,128]{3,2,1,0:T(8,128)(2,1)}, bf16[2,4,128,128]{3,2,1,0:T(8,128)(2,1)S(1)}, u32[]{:S(2)}) copy-start(bf16[2,4,128,128]{3,2,1,0:T(8,128)(2,1)S(1)} %get-tuple-element.71) | copy-start | bytes 786436
  7.4 45.1 %copy-start.31 = (bf16[2,4,128,128]{3,2,1,0:T(8,128)(2,1)}, bf16[2,4,128,128]{3,2,1,0:T(8,128)(2,1)S(1)}, u32[]{:S(2)}) copy-start(bf16[2,4,128,128]{3,2,1,0:T(8,128)(2,1)S(1)} %get-tuple-element.69) | copy-start | bytes 786436
  11.7 19.9 %all-to-all-start = ((bf16[16,32,256]{2,1,0:T(8,128)(2,1)}), bf16[16,32,256]{2,1,0:T(8,128)(2,1)S(1)}, u32[]{:S(2)}, u32[]{:S(2)}) async-start(bf16[16,32,256]{2,1,0:T(8,128)(2,1)} %broadcast_in_dim.26), calls=%async_computation | async-start | bytes 524288 | tf_op jit(solution)/shard_map/all_to_all | solution.py:253
  22.1 30.4 %copy-start.32 = (bf16[2,4,128,128]{3,2,1,0:T(8,128)(2,1)}, bf16[2,4,128,128]{3,2,1,0:T(8,128)(2,1)S(1)}, u32[]{:S(2)}) copy-start(bf16[2,4,128,128]{3,2,1,0:T(8,128)(2,1)S(1)} %get-tuple-element.70) | copy-start | bytes 786436
  22.2 15.4 %collective-permute-start.6 = (bf16[592,128]{1,0:T(8,128)(2,1)S(1)}, bf16[592,128]{1,0:T(8,128)(2,1)S(1)}, u32[]{:S(2)}, u32[]{:S(2)}) collective-permute-start(bf16[592,128]{1,0:T(8,128)(2,1)S(1)} %pad_maximum_fusion.17), channel_id=1, source_target_pairs={{0,16},{16,32},{32,48},{48,0},{1,17},{17,33},{33,49},{49,1},{2,18}... | collective-permute-start | bytes 454664 | tf_op jit(solution)/shard_map/ppermute | solution.py:212
  24.5 16.9 %collective-permute-start.7 = (bf16[592,128]{1,0:T(8,128)(2,1)S(1)}, bf16[592,128]{1,0:T(8,128)(2,1)S(1)}, u32[]{:S(2)}, u32[]{:S(2)}) collective-permute-start(bf16[592,128]{1,0:T(8,128)(2,1)S(1)} %pad_maximum_fusion.17), channel_id=1, source_target_pairs={{0,32},{16,48},{32,0},{48,16},{1,33},{17,49},{33,1},{49,17},{2,34}... | collective-permute-start | bytes 454664 | tf_op jit(solution)/shard_map/ppermute | solution.py:212
  27.8 14.8 %collective-permute-start.8 = (bf16[592,128]{1,0:T(8,128)(2,1)S(1)}, bf16[592,128]{1,0:T(8,128)(2,1)S(1)}, u32[]{:S(2)}, u32[]{:S(2)}) collective-permute-start(bf16[592,128]{1,0:T(8,128)(2,1)S(1)} %pad_maximum_fusion.17), channel_id=1, source_target_pairs={{0,48},{16,0},{32,16},{48,32},{1,49},{17,1},{33,17},{49,33},{2,50}... | collective-permute-start | bytes 454664 | tf_op jit(solution)/shard_map/ppermute | solution.py:212
  43.4 9.9 %collective-permute-start.9 = (bf16[3,512,128]{2,1,0:T(8,128)(2,1)}, bf16[3,512,128]{2,1,0:T(8,128)(2,1)}, u32[]{:S(2)}, u32[]{:S(2)}) collective-permute-start(bf16[3,512,128]{2,1,0:T(8,128)(2,1)} %pad_maximum_fusion.14), channel_id=1, source_target_pairs={{0,64},{64,0},{1,65},{65,1},{2,66},{66,2},{3,67},{67,3},{4,68},{68... | collective-permute-start | bytes 1179656 | tf_op jit(solution)/shard_map/ppermute | solution.py:219
  47.0 17.9 %all-to-all-start.1 = ((bf16[16,32,256]{2,1,0:T(8,128)(2,1)}), bf16[16,32,256]{2,1,0:T(8,128)(2,1)S(1)}, u32[]{:S(2)}, u32[]{:S(2)}) async-start(bf16[16,32,256]{2,1,0:T(8,128)(2,1)} %get-tuple-element.57), calls=%async_computation.1 | async-start | bytes 524288 | tf_op jit(solution)/shard_map/all_to_all | solution.py:253
  67.1 17.7 %all-to-all-start.2 = ((bf16[4,32,1024]{2,1,0:T(8,128)(2,1)}), bf16[4,32,1024]{2,1,0:T(8,128)(2,1)S(1)}, u32[]{:S(2)}, u32[]{:S(2)}) async-start(bf16[4,32,1024]{2,1,0:T(8,128)(2,1)} %couple.7), calls=%async_computation.2 | async-start | bytes 524288 | tf_op jit(solution)/shard_map/all_to_all | solution.py:285
  71.2 16.9 %collective-permute-start.3 = (bf16[592,128]{1,0:T(8,128)(2,1)}, bf16[592,128]{1,0:T(8,128)(2,1)}, u32[]{:S(2)}, u32[]{:S(2)}) collective-permute-start(bf16[592,128]{1,0:T(8,128)(2,1)} %pad_maximum_fusion.16), channel_id=1, source_target_pairs={{0,16},{16,32},{32,48},{48,0},{1,17},{17,33},{33,49},{49,1},{2,18}... | collective-permute-start | bytes 454664 | tf_op jit(solution)/shard_map/ppermute | solution.py:212
  72.2 15.9 %collective-permute-start.4 = (bf16[592,128]{1,0:T(8,128)(2,1)}, bf16[592,128]{1,0:T(8,128)(2,1)}, u32[]{:S(2)}, u32[]{:S(2)}) collective-permute-start(bf16[592,128]{1,0:T(8,128)(2,1)} %pad_maximum_fusion.16), channel_id=1, source_target_pairs={{0,32},{16,48},{32,0},{48,16},{1,33},{17,49},{33,1},{49,17},{2,34}... | collective-permute-start | bytes 454664 | tf_op jit(solution)/shard_map/ppermute | solution.py:212
  73.7 15.0 %collective-permute-start.5 = (bf16[592,128]{1,0:T(8,128)(2,1)}, bf16[592,128]{1,0:T(8,128)(2,1)}, u32[]{:S(2)}, u32[]{:S(2)}) collective-permute-start(bf16[592,128]{1,0:T(8,128)(2,1)} %pad_maximum_fusion.16), channel_id=1, source_target_pairs={{0,48},{16,0},{32,16},{48,32},{1,49},{17,1},{33,17},{49,33},{2,50}... | collective-permute-start | bytes 454664 | tf_op jit(solution)/shard_map/ppermute | solution.py:212
  90.5 14.6 %collective-permute-start.10 = (bf16[3,512,128]{2,1,0:T(8,128)(2,1)}, bf16[3,512,128]{2,1,0:T(8,128)(2,1)}, u32[]{:S(2)}, u32[]{:S(2)}) collective-permute-start(bf16[3,512,128]{2,1,0:T(8,128)(2,1)} %pad_maximum_fusion.12), channel_id=1, source_target_pairs={{0,64},{64,0},{1,65},{65,1},{2,66},{66,2},{3,67},{67,3},{4,68},{68... | collective-permute-start | bytes 1179656 | tf_op jit(solution)/shard_map/ppermute | solution.py:219
  93.9 20.9 %all-to-all-start.3 = ((bf16[16,32,256]{2,1,0:T(8,128)(2,1)}), bf16[16,32,256]{2,1,0:T(8,128)(2,1)S(1)}, u32[]{:S(2)}, u32[]{:S(2)}) async-start(bf16[16,32,256]{2,1,0:T(8,128)(2,1)} %copy-done.27), calls=%async_computation.3 | async-start | bytes 524288 | tf_op jit(solution)/shard_map/all_to_all | solution.py:253
  119.0 9.5 %all-to-all-start.4 = ((bf16[4,32,1024]{2,1,0:T(8,128)(2,1)}), bf16[4,32,1024]{2,1,0:T(8,128)(2,1)S(1)}, u32[]{:S(2)}, u32[]{:S(2)}) async-start(bf16[4,32,1024]{2,1,0:T(8,128)(2,1)} %copy-done.25), calls=%async_computation.4 | async-start | bytes 524288 | tf_op jit(solution)/shard_map/all_to_all | solution.py:285
  124.0 7.8 %collective-permute-start.14 = (bf16[592,128]{1,0:T(8,128)(2,1)}, bf16[592,128]{1,0:T(8,128)(2,1)}, u32[]{:S(2)}, u32[]{:S(2)}) collective-permute-start(bf16[592,128]{1,0:T(8,128)(2,1)} %pad_maximum_fusion.19), channel_id=1, source_target_pairs={{0,16},{16,32},{32,48},{48,0},{1,17},{17,33},{33,49},{49,1},{2,18}... | collective-permute-start | bytes 454664 | tf_op jit(solution)/shard_map/ppermute | solution.py:212
  124.9 14.1 %collective-permute-start.15 = (bf16[592,128]{1,0:T(8,128)(2,1)}, bf16[592,128]{1,0:T(8,128)(2,1)}, u32[]{:S(2)}, u32[]{:S(2)}) collective-permute-start(bf16[592,128]{1,0:T(8,128)(2,1)} %pad_maximum_fusion.19), channel_id=1, source_target_pairs={{0,32},{16,48},{32,0},{48,16},{1,33},{17,49},{33,1},{49,17},{2,34}... | collective-permute-start | bytes 454664 | tf_op jit(solution)/shard_map/ppermute | solution.py:212
  126.6 14.8 %collective-permute-start.16 = (bf16[592,128]{1,0:T(8,128)(2,1)}, bf16[592,128]{1,0:T(8,128)(2,1)}, u32[]{:S(2)}, u32[]{:S(2)}) collective-permute-start(bf16[592,128]{1,0:T(8,128)(2,1)} %pad_maximum_fusion.19), channel_id=1, source_target_pairs={{0,48},{16,0},{32,16},{48,32},{1,49},{17,1},{33,17},{49,33},{2,50}... | collective-permute-start | bytes 454664 | tf_op jit(solution)/shard_map/ppermute | solution.py:212
  143.2 10.7 %collective-permute-start.17 = (bf16[3,512,128]{2,1,0:T(8,128)(2,1)}, bf16[3,512,128]{2,1,0:T(8,128)(2,1)}, u32[]{:S(2)}, u32[]{:S(2)}) collective-permute-start(bf16[3,512,128]{2,1,0:T(8,128)(2,1)} %pad_maximum_fusion.10), channel_id=1, source_target_pairs={{0,64},{64,0},{1,65},{65,1},{2,66},{66,2},{3,67},{67,3},{4,68},{68... | collective-permute-start | bytes 1179656 | tf_op jit(solution)/shard_map/ppermute | solution.py:219
  145.8 16.6 %all-to-all-start.5 = ((bf16[16,32,256]{2,1,0:T(8,128)(2,1)}), bf16[16,32,256]{2,1,0:T(8,128)(2,1)S(1)}, u32[]{:S(2)}, u32[]{:S(2)}) async-start(bf16[16,32,256]{2,1,0:T(8,128)(2,1)} %copy-done.28), calls=%async_computation.5 | async-start | bytes 524288 | tf_op jit(solution)/shard_map/all_to_all | solution.py:253
  166.6 12.0 %all-to-all-start.6 = ((bf16[4,32,1024]{2,1,0:T(8,128)(2,1)}), bf16[4,32,1024]{2,1,0:T(8,128)(2,1)S(1)}, u32[]{:S(2)}, u32[]{:S(2)}) async-start(bf16[4,32,1024]{2,1,0:T(8,128)(2,1)} %copy-done.24), calls=%async_computation.6 | async-start | bytes 524288 | tf_op jit(solution)/shard_map/all_to_all | solution.py:285
  171.7 8.8 %collective-permute-start.11 = (bf16[592,128]{1,0:T(8,128)(2,1)}, bf16[592,128]{1,0:T(8,128)(2,1)}, u32[]{:S(2)}, u32[]{:S(2)}) collective-permute-start(bf16[592,128]{1,0:T(8,128)(2,1)} %pad_maximum_fusion.18), channel_id=1, source_target_pairs={{0,16},{16,32},{32,48},{48,0},{1,17},{17,33},{33,49},{49,1},{2,18}... | collective-permute-start | bytes 454664 | tf_op jit(solution)/shard_map/ppermute | solution.py:212
  175.0 15.1 %collective-permute-start.12 = (bf16[592,128]{1,0:T(8,128)(2,1)}, bf16[592,128]{1,0:T(8,128)(2,1)}, u32[]{:S(2)}, u32[]{:S(2)}) collective-permute-start(bf16[592,128]{1,0:T(8,128)(2,1)} %pad_maximum_fusion.18), channel_id=1, source_target_pairs={{0,32},{16,48},{32,0},{48,16},{1,33},{17,49},{33,1},{49,17},{2,34}... | collective-permute-start | bytes 454664 | tf_op jit(solution)/shard_map/ppermute | solution.py:212
  176.1 15.8 %collective-permute-start.13 = (bf16[592,128]{1,0:T(8,128)(2,1)}, bf16[592,128]{1,0:T(8,128)(2,1)}, u32[]{:S(2)}, u32[]{:S(2)}) collective-permute-start(bf16[592,128]{1,0:T(8,128)(2,1)} %pad_maximum_fusion.18), channel_id=1, source_target_pairs={{0,48},{16,0},{32,16},{48,32},{1,49},{17,1},{33,17},{49,33},{2,50}... | collective-permute-start | bytes 454664 | tf_op jit(solution)/shard_map/ppermute | solution.py:212
  193.7 11.8 %collective-permute-start.19 = (bf16[3,512,128]{2,1,0:T(8,128)(2,1)}, bf16[3,512,128]{2,1,0:T(8,128)(2,1)}, u32[]{:S(2)}, u32[]{:S(2)}) collective-permute-start(bf16[3,512,128]{2,1,0:T(8,128)(2,1)} %pad_maximum_fusion.8), channel_id=1, source_target_pairs={{0,64},{64,0},{1,65},{65,1},{2,66},{66,2},{3,67},{67,3},{4,68},{68... | collective-permute-start | bytes 1179656 | tf_op jit(solution)/shard_map/ppermute | solution.py:219
  194.2 2.1 collective-permute-start.18
  197.0 16.4 %all-to-all-start.7 = ((bf16[16,32,256]{2,1,0:T(8,128)(2,1)}), bf16[16,32,256]{2,1,0:T(8,128)(2,1)S(1)}, u32[]{:S(2)}, u32[]{:S(2)}) async-start(bf16[16,32,256]{2,1,0:T(8,128)(2,1)} %broadcast_in_dim.30), calls=%async_computation.7 | async-start | bytes 524288 | tf_op jit(solution)/shard_map/all_to_all | solution.py:253
  217.0 24.6 %copy-start.14 = (bf16[4,512,128]{2,1,0:T(8,128)(2,1)S(1)}, bf16[4,512,128]{2,1,0:T(8,128)(2,1)}, u32[]{:S(2)}) copy-start(bf16[4,512,128]{2,1,0:T(8,128)(2,1)} %copy-done.13) | copy-start | bytes 1572868
  225.6 25.9 %copy-start.8 = (bf16[256,4096]{1,0:T(8,128)(2,1)S(1)}, bf16[256,4096]{1,0:T(8,128)(2,1)}, u32[]{:S(2)}) copy-start(bf16[256,4096]{1,0:T(8,128)(2,1)} %copy-done.6) | copy-start | bytes 6291460
  253.2 13.6 %all-to-all-start.11 = ((bf16[16,32,256]{2,1,0:T(8,128)(2,1)}), bf16[16,32,256]{2,1,0:T(8,128)(2,1)S(1)}, u32[]{:S(2)}, u32[]{:S(2)}) async-start(bf16[16,32,256]{2,1,0:T(8,128)(2,1)} %copy-done.30), calls=%async_computation.11 | async-start | bytes 524288 | tf_op jit(solution)/shard_map/all_to_all | solution.py:253
  256.8 27.0 %collective-permute-start.21 = (bf16[2,512,256]{2,1,0:T(8,128)(2,1)}, bf16[2,512,256]{2,1,0:T(8,128)(2,1)}, u32[]{:S(2)}, u32[]{:S(2)}) collective-permute-start(bf16[2,512,256]{2,1,0:T(8,128)(2,1)} %param.12), channel_id=1, source_target_pairs={{0,64},{64,0},{1,65},{65,1},{2,66},{66,2},{3,67},{67,3},{4,68},{68... | collective-permute-start | bytes 1572872 | tf_op jit(solution)/shard_map/ppermute | solution.py:219
  279.6 14.1 %all-to-all-start.13 = ((bf16[16,32,256]{2,1,0:T(8,128)(2,1)}), bf16[16,32,256]{2,1,0:T(8,128)(2,1)S(1)}, u32[]{:S(2)}, u32[]{:S(2)}) async-start(bf16[16,32,256]{2,1,0:T(8,128)(2,1)} %copy-done.29), calls=%async_computation.13 | async-start | bytes 524288 | tf_op jit(solution)/shard_map/all_to_all | solution.py:253
  296.9 9.0 %all-to-all-start.14 = ((bf16[4,32,1024]{2,1,0:T(8,128)(2,1)}), bf16[4,32,1024]{2,1,0:T(8,128)(2,1)S(1)}, u32[]{:S(2)}, u32[]{:S(2)}) async-start(bf16[4,32,1024]{2,1,0:T(8,128)(2,1)} %copy-done.26), calls=%async_computation.14 | async-start | bytes 524288 | tf_op jit(solution)/shard_map/all_to_all | solution.py:285
  306.0 29.9 %copy-start.40 = (s32[64,512]{1,0:T(8,128)S(1)}, s32[64,512]{1,0:T(8,128)}, u32[]{:S(2)}) copy-start(s32[64,512]{1,0:T(8,128)} %param.8) | copy-start | bytes 393220
  308.3 5.1 %collective-permute-start.22 = (f32[32,512]{1,0:T(8,128)S(1)}, f32[32,512]{1,0:T(8,128)S(1)}, u32[]{:S(2)}, u32[]{:S(2)}) collective-permute-start(f32[32,512]{1,0:T(8,128)S(1)} %fusion.1), channel_id=1, source_target_pairs={{0,4},{4,8},{8,12},{12,0},{1,5},{5,9},{9,13},{13,1},{2,6},{6,10},{... | collective-permute-start | bytes 196616 | tf_op jit(solution)/shard_map/ppermute | solution.py:212
  308.7 4.7 %collective-permute-start.23 = (f32[32,512]{1,0:T(8,128)S(1)}, f32[32,512]{1,0:T(8,128)S(1)}, u32[]{:S(2)}, u32[]{:S(2)}) collective-permute-start(f32[32,512]{1,0:T(8,128)S(1)} %fusion.1), channel_id=1, source_target_pairs={{0,8},{4,12},{8,0},{12,4},{1,9},{5,13},{9,1},{13,5},{2,10},{6,14},... | collective-permute-start | bytes 196616 | tf_op jit(solution)/shard_map/ppermute | solution.py:212
  310.4 4.8 %collective-permute-start.24 = (f32[32,512]{1,0:T(8,128)S(1)}, f32[32,512]{1,0:T(8,128)S(1)}, u32[]{:S(2)}, u32[]{:S(2)}) collective-permute-start(f32[32,512]{1,0:T(8,128)S(1)} %fusion.1), channel_id=1, source_target_pairs={{0,12},{4,0},{8,4},{12,8},{1,13},{5,1},{9,5},{13,9},{2,14},{6,2},{... | collective-permute-start | bytes 196616 | tf_op jit(solution)/shard_map/ppermute | solution.py:212
  315.3 16.6 %collective-permute-start.25 = (f32[32,512]{1,0:T(8,128)S(1)}, f32[32,512]{1,0:T(8,128)S(1)}, u32[]{:S(2)}, u32[]{:S(2)}) collective-permute-start(f32[32,512]{1,0:T(8,128)S(1)} %add_add_fusion.1), channel_id=1, source_target_pairs={{0,16},{16,32},{32,48},{48,0},{1,17},{17,33},{33,49},{49,1},{2,18}... | collective-permute-start | bytes 196616 | tf_op jit(solution)/shard_map/ppermute | solution.py:212
  316.4 15.4 %collective-permute-start.26 = (f32[32,512]{1,0:T(8,128)S(1)}, f32[32,512]{1,0:T(8,128)S(1)}, u32[]{:S(2)}, u32[]{:S(2)}) collective-permute-start(f32[32,512]{1,0:T(8,128)S(1)} %add_add_fusion.1), channel_id=1, source_target_pairs={{0,32},{16,48},{32,0},{48,16},{1,33},{17,49},{33,1},{49,17},{2,34}... | collective-permute-start | bytes 196616 | tf_op jit(solution)/shard_map/ppermute | solution.py:212
  318.7 13.1 %collective-permute-start.27 = (f32[32,512]{1,0:T(8,128)S(1)}, f32[32,512]{1,0:T(8,128)S(1)}, u32[]{:S(2)}, u32[]{:S(2)}) collective-permute-start(f32[32,512]{1,0:T(8,128)S(1)} %add_add_fusion.1), channel_id=1, source_target_pairs={{0,48},{16,0},{32,16},{48,32},{1,49},{17,1},{33,17},{49,33},{2,50}... | collective-permute-start | bytes 196616 | tf_op jit(solution)/shard_map/ppermute | solution.py:212
  320.2 12.5 %collective-permute-start.20 = (bf16[2,32,256]{2,1,0:T(8,128)(2,1)S(1)}, bf16[2,32,256]{2,1,0:T(8,128)(2,1)S(1)}, u32[]{:S(2)}, u32[]{:S(2)}) collective-permute-start(bf16[2,32,256]{2,1,0:T(8,128)(2,1)S(1)} %broadcast_select_fusion.20), channel_id=1, source_target_pairs={{0,64},{64,0},{1,65},{65,1},{2,66},{66,2},{3,67},{67,3},{4,68},{68... | collective-permute-start | bytes 98312 | tf_op jit(solution)/shard_map/ppermute | solution.py:219
  331.9 4.0 %collective-permute-start.28 = (f32[32,512]{1,0:T(8,128)S(1)}, f32[32,512]{1,0:T(8,128)S(1)}, u32[]{:S(2)}, u32[]{:S(2)}) collective-permute-start(f32[32,512]{1,0:T(8,128)S(1)} %add_add_fusion), channel_id=1, source_target_pairs={{0,128},{128,0},{1,129},{129,1},{2,130},{130,2},{3,131},{131,3},{4... | collective-permute-start | bytes 196616 | tf_op jit(solution)/shard_map/ppermute | solution.py:212
  336.1 6.1 %collective-permute-start.29 = (f32[32,512]{1,0:T(8,128)S(1)}, f32[32,512]{1,0:T(8,128)S(1)}, u32[]{:S(2)}, u32[]{:S(2)}) collective-permute-start(f32[32,512]{1,0:T(8,128)S(1)} %fusion.10), channel_id=1, source_target_pairs={{0,64},{64,0},{1,65},{65,1},{2,66},{66,2},{3,67},{67,3},{4,68},{68... | collective-permute-start | bytes 196616 | tf_op jit(solution)/shard_map/ppermute | solution.py:219
  (35 other events, 191.9 us)

commit v3 on v1

--- a/solution.py
+++ b/solution.py
@@ -24,51 +24,46 @@
             copy.start()
 
 
-def arrange_kernel(place, *refs, per_core, steps, pieces, slices):
-    own_refs, other_refs = refs[:pieces], refs[pieces : 2 * pieces]
-    outs, sems = refs[-1 - steps : -1], refs[-1]
-
-    def copies(refs, step):
-        return [
-            pltpu.make_async_copy(*slices(ref, k, outs[step], step % per_core), sems.at[step, k])
-            for k, ref in enumerate(refs)
-        ]
-
-    waits = []
-    for step in range(steps):
-        own, other = copies(own_refs, step), copies(other_refs, step)
-        start_one_of(place[0] == step // per_core, own, other)
-        waits += own
-    for copy in waits:
+def full_kernel(
+    place, cols, x_ref, own_c, other_c, own_l, other_l, *refs, step, per_core, slots
+):
+    outs, (c_buf, s_buf, r_buf, l_buf, c_sems, s_sems, l_sems) = refs[:-7], refs[-7:]
+    peers, tall, block = c_buf.shape
+    probes, width = x_ref.shape[1:]
+    per = width // block
+    chunks, _, wide = l_buf.shape
+    i = step % per_core
+    own, other = (
+        [pltpu.make_async_copy(c.at[m, pl.ds(i * tall, tall)], c_buf.at[m], c_sems.at[m]) for m in range(peers)]
+        + [pltpu.make_async_copy(f.at[i, :, pl.ds(j * wide, wide)], l_buf.at[j], l_sems.at[j]) for j in range(chunks)]
+        for c, f in ((own_c, own_l), (other_c, other_l))
+    )
+    begin, steps = per_core * tall, 2 * per_core
+    sources = [
+        pltpu.make_async_copy(
+            own_c.at[:, pl.ds(begin + (half * steps + step) * probes, probes)], s_buf.at[half], s_sems.at[half]
+        )
+        for half in range(per)
+    ]
+    for copy in sources:
+        copy.start()
+    start_one_of(place[0] == step // per_core, own, other)
+    for copy in sources:
         copy.wait()
-
-
-def factor_slices(ref, k, out, i):
-    return ref.at[i], out
-
-
-def coupling_slices(ref, k, out, i):
-    size = out.shape[1]
-    return ref.at[pl.ds(i * size, size)], out.at[k]
-
-
-def couple_kernel(place, cols, x_ref, s_ref, c_ref, out_ref, *, step, slots):
-    lines, tall, block = c_ref.shape
-    rows = tall // (slots * block)
-    per = x_ref.shape[2] // block
-    probes = x_ref.shape[1]
-
-    def body(k, carry):
-        for row in range(rows):
+    for m in range(peers):
+        own[m].wait()
+
+    def body(m, carry):
+        for row in range(per):
             total = None
             for slot in range(0, slots, 2):
                 left, right = [], []
                 for pair in range(2):
-                    col = cols[k, (step * rows + row) * slots + slot + pair]
+                    col = cols[m, (step * per + row) * slots + slot + pair]
                     lanes = pl.ds(pl.multiple_of((col % per) * block, block), block)
                     left.append(x_ref[col // per, :, lanes])
                     at = (row * slots + slot + pair) * block
-                    right.append(c_ref[k, at : at + block, :])
+                    right.append(c_buf[m, at : at + block, :])
                 term = lax.dot_general(
                     jnp.concatenate(left, axis=1),
                     jnp.concatenate(right, axis=1),
@@ -76,14 +71,18 @@
                     preferred_element_type=jnp.float32,
                 )
                 total = term if total is None else total + term
-            at = (row * s_ref.shape[1]) // rows + step * probes
-            source = s_ref[k, at : at + probes, :].astype(jnp.float32)
-            home = lax.rem(place[1] + lines - k, lines)
-            lanes = pl.ds(pl.multiple_of((home * rows + row) * block, block), block)
-            out_ref[:, lanes] = (source - total).astype(jnp.bfloat16)
+            resid = s_buf[row, m].astype(jnp.float32) - total
+            r_buf[m, :, row * block : (row + 1) * block] = resid.astype(jnp.bfloat16)
         return carry
 
-    lax.fori_loop(0, lines, body, 0)
+    lax.fori_loop(0, peers, body, 0, unroll=2)
+    group = peers // chunks
+    total = jnp.zeros((probes, l_buf.shape[1]), jnp.float32)
+    for j in range(chunks):
+        own[peers + j].wait()
+        left = jnp.concatenate([r_buf[j * group + n] for n in range(group)], axis=1)
+        total = total + lax.dot_general(left, l_buf[j], NT, preferred_element_type=jnp.float32)
+    finish(total, outs)
 
 
 def finish(total, outs):
@@ -140,58 +139,10 @@
             out_ref[peer, :, span] = resid
 
 
-def apply_kernel(place, *refs, lines):
-    pieces, l_ref, outs = refs[:lines], refs[lines], refs[lines + 1 :]
-    width = l_ref.shape[0]
-
-    def body(zh, total):
-        for k in range(lines):
-            y = lax.rem(place[2] + lines - k, lines)
-            lanes = pl.ds(pl.multiple_of((zh * lines + y) * width, width), width)
-            here = pl.ds(pl.multiple_of(zh * width, width), width)
-            total = total + lax.dot_general(
-                pieces[k][:, here], l_ref[:, lanes], NT, preferred_element_type=jnp.float32
-            )
-        return total
-
-    start = jnp.zeros((pieces[0].shape[0], width), jnp.float32)
-    finish(lax.fori_loop(0, pieces[0].shape[1] // width, body, start), outs)
-
-
 VMEM = pl.BlockSpec(memory_space=pltpu.VMEM)
 SMEM = pl.BlockSpec(memory_space=pltpu.SMEM)
 HBM = pl.BlockSpec(memory_space=pltpu.HBM)
-PARAMS = pltpu.CompilerParams(vmem_limit_bytes=16 << 20)
-
-
-def arrange(slices, place, own, other, steps, shape, name, after):
-    pieces = len(own)
-    return pl.pallas_call(
-        functools.partial(
-            arrange_kernel, per_core=steps // 2, steps=steps, pieces=pieces, slices=slices
-        ),
-        out_shape=tuple([jax.ShapeDtypeStruct(shape, jnp.bfloat16)] * steps),
-        in_specs=[SMEM] + [HBM] * (2 * pieces + 1),
-        out_specs=tuple([HBM] * steps),
-        scratch_shapes=[pltpu.SemaphoreType.DMA((steps, pieces))],
-        compiler_params=PARAMS,
-        cost_estimate=pl.CostEstimate(
-            flops=0, transcendentals=0, bytes_accessed=4 * steps * shape[0] * shape[1]
-        ),
-        name=name,
-    )(place, *own, *other, after)
-
-
-def couple(place, cols, pieces, source, c, step, slots):
-    lines, tall, block = c.shape
-    return pl.pallas_call(
-        functools.partial(couple_kernel, step=step, slots=slots),
-        out_shape=jax.ShapeDtypeStruct((pieces.shape[1], lines * tall // slots), jnp.bfloat16),
-        in_specs=[SMEM, SMEM, VMEM, VMEM, VMEM],
-        out_specs=VMEM,
-        compiler_params=PARAMS,
-        name="couple",
-    )(place, cols, pieces, source, c)
+PARAMS = pltpu.CompilerParams(vmem_limit_bytes=50 << 20)
 
 
 def solved_shapes(probes, rows, peers):
@@ -201,16 +152,28 @@
     return tuple(shapes)
 
 
-def apply_factor(place, pieces, factor, peers):
-    shapes = solved_shapes(pieces[0].shape[0], factor.shape[0], peers)
+def apply_full(place, cols, pieces, shared, factors, step, slots, block, spread):
+    peers, probes, width = pieces.shape
+    per_core, rows, whole = factors[0].shape
+    per = width // block
+    shapes = solved_shapes(probes, rows, peers if spread else 0)
     return pl.pallas_call(
-        functools.partial(apply_kernel, lines=len(pieces)),
+        functools.partial(full_kernel, step=step, per_core=per_core, slots=slots),
         out_shape=shapes,
-        in_specs=[SMEM] + [VMEM] * (len(pieces) + 1),
+        in_specs=[SMEM, SMEM, VMEM] + [HBM] * 4,
         out_specs=tuple([VMEM] * len(shapes)),
+        scratch_shapes=[
+            pltpu.VMEM((peers, per * slots * block, block), jnp.bfloat16),
+            pltpu.VMEM((per, peers, probes, block), jnp.bfloat16),
+            pltpu.VMEM((peers, probes, width), jnp.bfloat16),
+            pltpu.VMEM((4, rows, whole // 4), jnp.bfloat16),
+            pltpu.SemaphoreType.DMA((peers,)),
+            pltpu.SemaphoreType.DMA((per,)),
+            pltpu.SemaphoreType.DMA((4,)),
+        ],
         compiler_params=PARAMS,
-        name="apply",
-    )(place, *pieces, factor)
+        name="apply_full",
+    )(place, cols, pieces, *shared, *factors)
 
 
 def apply_early(place, pieces, own, other, step):
@@ -282,7 +245,6 @@
     def everywhere(value):
         return lax.all_to_all(value, NODES, 0, 0)
 
-    solved0 = apply_early(place, everywhere(spread), inverse_factors, other_factors, 0)
     slots, block = couplings.shape[2:4]
     cols = own_cols.reshape(1, -1).astype(jnp.bfloat16)
     width = cols.shape[1]
@@ -290,38 +252,33 @@
     flat = own_source.reshape(steps * probes, local)
     halves = [flat[:, i : i + block] for i in range(0, local, block)]
     bundle = jnp.concatenate([couplings.reshape(-1, block)] + halves + [cols], axis=0)
-    shared = line(bundle, "zh")
-    at = couplings.size // block
-    until = at + steps * probes * local // block
-    tall = at // own_steps
-    resid = couple_early(
-        place, own_cols, everywhere(solved0[1]), own_source[1], couplings, other_couplings, 1
-    )
-    solved1 = apply_early(place, everywhere(resid), inverse_factors, other_factors, 1)
-    pieces = everywhere(solved1[1])
-    shared, after = lax.optimization_barrier((shared, solved1[0]))
-    source = jnp.stack([s[at:until] for s in shared])
-    cols = jnp.concatenate([s[until : until + 1, :width] for s in shared], axis=0).astype(jnp.int32)
-    shape = (len(shared), tall, block)
-    blocks = arrange(
-        coupling_slices, place, shared, [swap(s) for s in shared], steps, shape, "couplings", after
-    )
-    factors = arrange(
-        factor_slices, place, [inverse_factors], [other_factors], steps, inverse_factors.shape[1:], "factors", after
-    )
-
-    for turn in range(turns):
+    shared = lax.all_gather(bundle, NODES, axis=0)
+    factors = (inverse_factors, other_factors)
+
+    results = []
+    resid = spread
+    for step in range(steps):
+        outs = apply_early(place, everywhere(resid), *factors, step)
+        if step + 1 < steps:
+            pieces = everywhere(outs[1])
+            resid = couple_early(
+                place, own_cols, pieces, own_source[step + 1], couplings, other_couplings, step + 1
+            )
+        if step == 2:
+            shared, _, resid = lax.optimization_barrier((shared, outs[0], resid))
+            full = (shared, swap(shared))
+    until = couplings.size // block + steps * probes * local // block
+    cols = shared[:, until, :width].astype(jnp.int32)
+    for turn in range(1, turns):
+        moved = lax.ppermute(outs[0], "zl", [(turn - 1, turn)])
+        pieces = everywhere(jnp.broadcast_to(moved[None], (peers, probes, local)))
         results = []
-        for step in range(2 if turn == 0 else 0, steps):
-            resid = line(couple(place, cols, pieces, source, blocks[step], step, slots), "y")
+        for step in range(steps):
             more = step + 1 < steps
-            outs = apply_factor(place, resid, factors[step], peers if more else 0)
+            outs = apply_full(place, cols, pieces, full, factors, step, slots, block, more)
             results.append(outs[0])
             if more:
                 pieces = everywhere(outs[1])
-        if turn + 1 < turns:
-            moved = lax.ppermute(outs[0], "zl", [(turn, turn + 1)])
-            pieces = everywhere(jnp.broadcast_to(moved[None], (peers, probes, local)))
 
     rows4 = in_order(border_rows, swap(border_rows))
     partial = jnp.zeros((probes, border_rows.shape[1]), jnp.float32)

time: 328 us -> 333 us (1.015)
  starting transfers between devices: 113 us -> 66.3 us
  waiting for transfers between devices: 43.6 us -> 86.3 us
  Pallas kernels: 33.4 us -> 48.6 us
  local copies, waits for them, and re-layouts: 16.9 us -> 2.38 us
  between operations: 1.14 us -> 14.3 us
  blocking collectives: 112 us -> 108 us
    all_to_all x5 -> x6, waiting for transfers between devices: 19.3 us -> 65.4 us  [everywhere(): return lax.all_to_all(value, NODES, 0, 0)]
    ppermute x28 -> x7, starting transfers between devices: 43 us -> 8.47 us  [line(): lax.ppermute(value, axis, [(i, (i + k) % size) for i in range(size)])]
    ppermute x11 -> x8, starting transfers between devices: 35.7 us -> 22.2 us  [swap(): return lax.ppermute(value, 'core', [(0, 1), (1, 0)])]
    unnamed x43 -> x9, local copies, waits for them, and re-layouts: 13.7 us -> 0.72 us
    all_gather x0 -> x1, waiting for transfers between devices: none -> 12.6 us  [shards(): shared = lax.all_gather(bundle, NODES, axis=0)]
    ppermute x28 -> x7, waiting for transfers between devices: 16.6 us -> 6.69 us  [line(): lax.ppermute(value, axis, [(i, (i + k) % size) for i in range(size)])]
    pallas_call x2 -> x4, Pallas kernels: 7.68 us -> 15.3 us  [apply_early(): pl.pallas_call(functools.partial(early_kernel, step=step, per_core=per_co...]
    ppermute x11 -> x8, waiting for transfers between devices: 6.84 us -> 0.82 us  [swap(): return lax.ppermute(value, 'core', [(0, 1), (1, 0)])]
  transfers between devices with their start and end apart: 45 -> 23, of which waited for: 25 -> 15; matrix products, arithmetic and copies ran while one was open for 3% -> 2% of each run, Pallas kernels for 5% -> 10%
where the time goes in v3:
time: 333 us; the launch traced here: 332 us
  blocking collectives  108 us (32%)
  waiting for transfers between devices  86.3 us (26%)
  starting transfers between devices  66.3 us (20%)
  Pallas kernels  48.6 us (15%)
  between operations  14.3 us (4%)
  other arithmetic  5.39 us (2%)
    all_to_all x5, blocking collectives, everywhere(): return lax.all_to_all(value, NODES, 0, 0)  98.8 us
    all_to_all x6, waiting for transfers between devices, everywhere(): return lax.all_to_all(value, NODES, 0, 0)  65.4 us
    all_to_all x6, starting transfers between devices, everywhere(): return lax.all_to_all(value, NODES, 0, 0)  32.9 us
    pallas_call x4, Pallas kernels, apply_full(): pl.pallas_call(functools.partial(full_kernel, step=step, per_core=per_cor...  30.7 us
    ppermute x8, starting transfers between devices, swap(): return lax.ppermute(value, 'core', [(0, 1), (1, 0)])  22.2 us
    pallas_call x4, Pallas kernels, apply_early(): pl.pallas_call(functools.partial(early_kernel, step=step, per_core=per_co...  15.3 us
    all_gather x1, waiting for transfers between devices, shards(): shared = lax.all_gather(bundle, NODES, axis=0)  12.6 us
    psum x1, blocking collectives, shards(): node_sums, border_sums = lax.psum((node_sums, border_sums), 'x')  9.06 us
  transfers between devices with their start and end apart: 23, of which 15 were waited for; matrix products, arithmetic and copies ran while one was open for 2% of the time, Pallas kernels for 10%

profile of v3, /device:TPU:1, one launch (start us, length us, event | category | flops | bytes accessed | tf_op | source)
XLA Modules:
  0.0 332.1 jit_solution(4340616044715980563)
XLA Ops:
  7.2 3.3 %collective-permute-start.1 = (s32[2,2,4]{2,1,0:T(2,128)}, s32[2,2,4]{2,1,0:T(2,128)S(1)}, u32[]{:S(2)}, u32[]{:S(2)}) collective-permute-start(s32[2,2,4]{2,1,0:T(2,128)} %param.11), channel_id=1, source_target_pairs={{0,64},{64,0},{1,65},{65,1},{2,66},{66,2},{3,67},{67,3},{4,68},{68... | collective-permute-start | bytes 200 | tf_op jit(solution)/shard_map/ppermute | solution.py:219
  10.6 0.9 fusion.8
  12.9 0.9 fusion.3
  14.8 9.2 %all-to-all-start = ((bf16[16,32,256]{2,1,0:T(8,128)(2,1)}), bf16[16,32,256]{2,1,0:T(8,128)(2,1)S(1)}, u32[]{:S(2)}, u32[]{:S(2)}) async-start(bf16[16,32,256]{2,1,0:T(8,128)(2,1)} %broadcast_in_dim.14), calls=%async_computation | async-start | bytes 524288 | tf_op jit(solution)/shard_map/all_to_all | solution.py:246
  24.8 10.0 %all-to-all-done.r_ref = bf16[16,32,256]{2,1,0:T(8,128)(2,1)S(1)} async-done(((bf16[16,32,256]{2,1,0:T(8,128)(2,1)}), bf16[16,32,256]{2,1,0:T(8,128)(2,1)S(1)}, u32[]{:S(2)}, u32[]{:S(2)}) %all-to-all-start) | async-done | bytes 262176 | tf_op jit(solution)/shard_map/all_to_all | solution.py:246
  34.7 3.8 %apply_early.4 = (bf16[32,256]{1,0:T(8,128)(2,1)}, bf16[16,32,256]{2,1,0:T(8,128)(2,1)}) custom-call(s32[3]{0:T(128)S(1)} %pad_add_fusion.1.place, bf16[16,32,256]{2,1,0:T(8,128)(2,1)S(1)} %all-to-all-done.r_ref, bf16[2,256,4096]{2,1,0:T(8,128)(2,1)} %own_l.7, bf16[2,256,4096]{2,1,0:T(8,128)(2,1)} %collective-permute-done.2.other_ref.other_l), custom_call_target="tpu_custom_call" | custom-call | tf_op jit(solution)/shard_map/apply_early/pallas_call | solution.py:183
  38.6 6.0 %all-to-all-start.1 = ((bf16[16,32,256]{2,1,0:T(8,128)(2,1)}), bf16[16,32,256]{2,1,0:T(8,128)(2,1)S(1)}, u32[]{:S(2)}, u32[]{:S(2)}) async-start(bf16[16,32,256]{2,1,0:T(8,128)(2,1)} %get-tuple-element.16), calls=%async_computation.1 | async-start | bytes 524288 | tf_op jit(solution)/shard_map/all_to_all | solution.py:246
  44.6 16.1 %all-to-all-done.1.x_ref = bf16[16,32,256]{2,1,0:T(8,128)(2,1)S(1)} async-done(((bf16[16,32,256]{2,1,0:T(8,128)(2,1)}), bf16[16,32,256]{2,1,0:T(8,128)(2,1)S(1)}, u32[]{:S(2)}, u32[]{:S(2)}) %all-to-all-start.1) | async-done | bytes 262176 | tf_op jit(solution)/shard_map/all_to_all | solution.py:246
  60.8 0.9 couple_early.3
  61.7 15.8 %all_to_all.55.r_ref = bf16[16,32,256]{2,1,0:T(8,128)(2,1)S(1)} all-to-all(bf16[16,32,256]{2,1,0:T(8,128)(2,1)S(1)} %couple_early.3), channel_id=1, replica_groups=mesh['zl'=2,'core'=2,'zh'=4,'y'=4,'x'=4] {'zh','y'}, dimensions={0} | all-to-all | bytes 524288 | tf_op jit(solution)/shard_map/all_to_all | solution.py:246
  77.4 3.8 %apply_early.5 = (bf16[32,256]{1,0:T(8,128)(2,1)}, bf16[16,32,256]{2,1,0:T(8,128)(2,1)}) custom-call(s32[3]{0:T(128)S(1)} %pad_add_fusion.1.place, bf16[16,32,256]{2,1,0:T(8,128)(2,1)S(1)} %all_to_all.55.r_ref, bf16[2,256,4096]{2,1,0:T(8,128)(2,1)} %own_l.7, bf16[2,256,4096]{2,1,0:T(8,128)(2,1)} %collective-permute-done.2.other_ref.other_l), custom_call_target="tpu_custom_call" | custom-call | tf_op jit(solution)/shard_map/apply_early/pallas_call | solution.py:183
  81.3 4.5 %all-to-all-start.3 = ((bf16[16,32,256]{2,1,0:T(8,128)(2,1)}), bf16[16,32,256]{2,1,0:T(8,128)(2,1)S(1)}, u32[]{:S(2)}, u32[]{:S(2)}) async-start(bf16[16,32,256]{2,1,0:T(8,128)(2,1)} %get-tuple-element.17), calls=%async_computation.3 | async-start | bytes 524288 | tf_op jit(solution)/shard_map/all_to_all | solution.py:246
  85.8 13.3 %all-to-all-done.3.x_ref = bf16[16,32,256]{2,1,0:T(8,128)(2,1)S(1)} async-done(((bf16[16,32,256]{2,1,0:T(8,128)(2,1)}), bf16[16,32,256]{2,1,0:T(8,128)(2,1)S(1)}, u32[]{:S(2)}, u32[]{:S(2)}) %all-to-all-start.3) | async-done | bytes 262176 | tf_op jit(solution)/shard_map/all_to_all | solution.py:246
  99.1 0.9 couple_early.4
  100.0 18.2 %all_to_all.56.r_ref = bf16[16,32,256]{2,1,0:T(8,128)(2,1)S(1)} all-to-all(bf16[16,32,256]{2,1,0:T(8,128)(2,1)S(1)} %couple_early.4), channel_id=1, replica_groups=mesh['zl'=2,'core'=2,'zh'=4,'y'=4,'x'=4] {'zh','y'}, dimensions={0} | all-to-all | bytes 524288 | tf_op jit(solution)/shard_map/all_to_all | solution.py:246
  118.2 3.7 %apply_early.6 = (bf16[32,256]{1,0:T(8,128)(2,1)}, bf16[16,32,256]{2,1,0:T(8,128)(2,1)S(1)}) custom-call(s32[3]{0:T(128)S(1)} %pad_add_fusion.1.place, bf16[16,32,256]{2,1,0:T(8,128)(2,1)S(1)} %all_to_all.56.r_ref, bf16[2,256,4096]{2,1,0:T(8,128)(2,1)} %own_l.7, bf16[2,256,4096]{2,1,0:T(8,128)(2,1)} %collective-permute-done.2.other_ref.other_l), custom_call_target="tpu_custom_call" | custom-call | tf_op jit(solution)/shard_map/apply_early/pallas_call | solution.py:183
  121.9 17.5 %all_to_all.57.x_ref = bf16[16,32,256]{2,1,0:T(8,128)(2,1)S(1)} all-to-all(bf16[16,32,256]{2,1,0:T(8,128)(2,1)S(1)} %get-tuple-element.18), channel_id=1, replica_groups=mesh['zl'=2,'core'=2,'zh'=4,'y'=4,'x'=4] {'zh','y'}, dimensions={0} | all-to-all | bytes 524288 | tf_op jit(solution)/shard_map/all_to_all | solution.py:246
  139.4 0.9 couple_early.5
  140.3 12.6 %all-gather.3.cloned.1.call-done = bf16[37120,128]{1,0:T(8,128)(2,1)} async-done(((bf16[2320,128]{1,0:T(8,128)(2,1)}), bf16[37120,128]{1,0:T(8,128)(2,1)}) %all-gather.3.cloned.1.call-update) | async-done | bytes 9502736 | tf_op jit(solution)/shard_map/all_gather | solution.py:255
  153.3 33.5 %all_to_all.58.r_ref = bf16[16,32,256]{2,1,0:T(8,128)(2,1)S(1)} all-to-all(bf16[16,32,256]{2,1,0:T(8,128)(2,1)S(1)} %couple_early.5), channel_id=1, replica_groups=mesh['zl'=2,'core'=2,'zh'=4,'y'=4,'x'=4] {'zh','y'}, dimensions={0} | all-to-all | bytes 524288 | tf_op jit(solution)/shard_map/all_to_all | solution.py:246
  186.8 3.8 %apply_early.7 = (bf16[32,256]{1,0:T(8,128)(2,1)S(1)}, bf16[16,32,256]{2,1,0:T(8,128)(2,1)}) custom-call(s32[3]{0:T(128)S(1)} %pad_add_fusion.1.place, bf16[16,32,256]{2,1,0:T(8,128)(2,1)S(1)} %all_to_all.58.r_ref, bf16[2,256,4096]{2,1,0:T(8,128)(2,1)} %own_l.7, bf16[2,256,4096]{2,1,0:T(8,128)(2,1)} %collective-permute-done.2.other_ref.other_l), custom_call_target="tpu_custom_call" | custom-call | tf_op jit(solution)/shard_map/apply_early/pallas_call | solution.py:183
  190.7 2.7 collective-permute-start.4
  193.4 0.9 collective-permute-done.4
  194.2 0.7 broadcast_in_dim.15
  195.0 4.5 %all-to-all-start.7 = ((bf16[16,32,256]{2,1,0:T(8,128)(2,1)}), bf16[16,32,256]{2,1,0:T(8,128)(2,1)S(1)}, u32[]{:S(2)}, u32[]{:S(2)}) async-start(bf16[16,32,256]{2,1,0:T(8,128)(2,1)} %broadcast_in_dim.15), calls=%async_computation.7 | async-start | bytes 524288 | tf_op jit(solution)/shard_map/all_to_all | solution.py:246
  199.5 0.8 slice_convert_fusion
  200.3 9.4 %all-to-all-done.7.x_ref = bf16[16,32,256]{2,1,0:T(8,128)(2,1)S(1)} async-done(((bf16[16,32,256]{2,1,0:T(8,128)(2,1)}), bf16[16,32,256]{2,1,0:T(8,128)(2,1)S(1)}, u32[]{:S(2)}, u32[]{:S(2)}) %all-to-all-start.7) | async-done | bytes 262176 | tf_op jit(solution)/shard_map/all_to_all | solution.py:246
  209.6 7.9 %apply_full.4 = (bf16[32,256]{1,0:T(8,128)(2,1)S(1)}, bf16[16,32,256]{2,1,0:T(8,128)(2,1)}) custom-call(s32[3]{0:T(128)S(1)} %pad_add_fusion.1.place, s32[16,32]{1,0:T(8,128)S(1)} %bitcast.52, bf16[16,32,256]{2,1,0:T(8,128)(2,1)S(1)} %all-to-all-done.7.x_ref, bf16[16,2320,128]{2,1,0:T(8,128)(2,1)} %bitcast.64, ...), custom_call_target="tpu_custom_call" | custom-call | tf_op jit(solution)/shard_map/apply_full/pallas_call | solution.py:160
  217.6 4.8 %all-to-all-start.8 = ((bf16[16,32,256]{2,1,0:T(8,128)(2,1)}), bf16[16,32,256]{2,1,0:T(8,128)(2,1)S(1)}, u32[]{:S(2)}, u32[]{:S(2)}) async-start(bf16[16,32,256]{2,1,0:T(8,128)(2,1)} %get-tuple-element.23), calls=%async_computation.8 | async-start | bytes 524288 | tf_op jit(solution)/shard_map/all_to_all | solution.py:246
  222.5 3.2 collective-permute-start.7
  225.6 7.0 %all-to-all-done.8.x_ref = bf16[16,32,256]{2,1,0:T(8,128)(2,1)S(1)} async-done(((bf16[16,32,256]{2,1,0:T(8,128)(2,1)}), bf16[16,32,256]{2,1,0:T(8,128)(2,1)S(1)}, u32[]{:S(2)}, u32[]{:S(2)}) %all-to-all-start.8) | async-done | bytes 262176 | tf_op jit(solution)/shard_map/all_to_all | solution.py:246
  232.6 7.2 %apply_full.5 = (bf16[32,256]{1,0:T(8,128)(2,1)S(1)}, bf16[16,32,256]{2,1,0:T(8,128)(2,1)S(1)}) custom-call(s32[3]{0:T(128)S(1)} %pad_add_fusion.1.place, s32[16,32]{1,0:T(8,128)S(1)} %bitcast.53, bf16[16,32,256]{2,1,0:T(8,128)(2,1)S(1)} %all-to-all-done.8.x_ref, bf16[16,2320,128]{2,1,0:T(8,128)(2,1)} %bitcast.65, ...), custom_call_target="tpu_custom_call" | custom-call | tf_op jit(solution)/shard_map/apply_full/pallas_call | solution.py:160
  239.8 13.8 %all_to_all.59.x_ref = bf16[16,32,256]{2,1,0:T(8,128)(2,1)S(1)} all-to-all(bf16[16,32,256]{2,1,0:T(8,128)(2,1)S(1)} %get-tuple-element.25), channel_id=1, replica_groups=mesh['zl'=2,'core'=2,'zh'=4,'y'=4,'x'=4] {'zh','y'}, dimensions={0} | all-to-all | bytes 524288 | tf_op jit(solution)/shard_map/all_to_all | solution.py:246
  253.6 8.1 %apply_full.6 = (bf16[32,256]{1,0:T(8,128)(2,1)S(1)}, bf16[16,32,256]{2,1,0:T(8,128)(2,1)}) custom-call(s32[3]{0:T(128)S(1)} %pad_add_fusion.1.place, s32[16,32]{1,0:T(8,128)S(1)} %bitcast.54, bf16[16,32,256]{2,1,0:T(8,128)(2,1)S(1)} %all_to_all.59.x_ref, bf16[16,2320,128]{2,1,0:T(8,128)(2,1)} %bitcast.66, ...), custom_call_target="tpu_custom_call" | custom-call | tf_op jit(solution)/shard_map/apply_full/pallas_call | solution.py:160
  261.8 3.9 %all-to-all-start.10 = ((bf16[16,32,256]{2,1,0:T(8,128)(2,1)}), bf16[16,32,256]{2,1,0:T(8,128)(2,1)S(1)}, u32[]{:S(2)}, u32[]{:S(2)}) async-start(bf16[16,32,256]{2,1,0:T(8,128)(2,1)} %get-tuple-element.27), calls=%async_computation.10 | async-start | bytes 524288 | tf_op jit(solution)/shard_map/all_to_all | solution.py:246
  266.1 9.6 %all-to-all-done.10.x_ref = bf16[16,32,256]{2,1,0:T(8,128)(2,1)S(1)} async-done(((bf16[16,32,256]{2,1,0:T(8,128)(2,1)}), bf16[16,32,256]{2,1,0:T(8,128)(2,1)S(1)}, u32[]{:S(2)}, u32[]{:S(2)}) %all-to-all-start.10) | async-done | bytes 262176 | tf_op jit(solution)/shard_map/all_to_all | solution.py:246
  275.8 7.4 %apply_full.7 = bf16[32,256]{1,0:T(8,128)(2,1)S(1)} custom-call(s32[3]{0:T(128)S(1)} %pad_add_fusion.1.place, s32[16,32]{1,0:T(8,128)S(1)} %bitcast.55, bf16[16,32,256]{2,1,0:T(8,128)(2,1)S(1)} %all-to-all-done.10.x_ref, bf16[16,2320,128]{2,1,0:T(8,128)(2,1)} %bitcast.67, bf16[16,2320,128]{2,1,0:T(8,128)(2,1)} %collective-permute-done.5.other_c, ...), custom_call_target="tpu_custom_call" | custom-call | tf_op jit(solution)/shard_map/apply_full/pallas_call | solution.py:160
  283.6 0.8 collective-permute-start.10
  285.1 1.4 collective-permute-start.9
  286.8 2.0 collective-permute-done.8
  288.7 1.0 collective-permute-done.9
  289.7 0.8 collective-permute-start.11
  290.6 2.6 collective-permute-start.12
  293.2 1.6 collective-permute-start.13
  294.8 9.0 %collective-permute-start.6 = (bf16[2,32,256]{2,1,0:T(8,128)(2,1)S(1)}, bf16[2,32,256]{2,1,0:T(8,128)(2,1)S(1)}, u32[]{:S(2)}, u32[]{:S(2)}) collective-permute-start(bf16[2,32,256]{2,1,0:T(8,128)(2,1)S(1)} %broadcast_select_fusion.7), channel_id=1, source_target_pairs={{0,64},{64,0},{1,65},{65,1},{2,66},{66,2},{3,67},{67,3},{4,68},{68... | collective-permute-start | bytes 98312 | tf_op jit(solution)/shard_map/ppermute | solution.py:219
  304.7 3.4 %collective-permute-done.14 = f32[32,512]{1,0:T(8,128)S(1)} collective-permute-done((f32[32,512]{1,0:T(8,128)S(1)}, f32[32,512]{1,0:T(8,128)S(1)}, u32[]{:S(2)}, u32[]{:S(2)}) %collective-permute-start.14) | collective-permute-done | bytes 65568 | tf_op jit(solution)/shard_map/ppermute | solution.py:212
  308.3 5.1 %collective-permute-start.15 = (f32[32,512]{1,0:T(8,128)S(1)}, f32[32,512]{1,0:T(8,128)S(1)}, u32[]{:S(2)}, u32[]{:S(2)}) collective-permute-start(f32[32,512]{1,0:T(8,128)S(1)} %fusion.9), channel_id=1, source_target_pairs={{0,64},{64,0},{1,65},{65,1},{2,66},{66,2},{3,67},{67,3},{4,68},{68... | collective-permute-start | bytes 196616 | tf_op jit(solution)/shard_map/ppermute | solution.py:219
  315.1 9.1 %all-reduce.1 = (f32[2,256]{1,0:T(2,128)S(1)}, f32[512]{0:T(512)S(1)}) all-reduce(f32[2,256]{1,0:T(2,128)S(1)} %multiply_reduce_fusion.1, f32[512]{0:T(512)S(1)} %get-tuple-element.38), channel_id=1, replica_groups=mesh['zl'=2,'core'=2,'zh'=4,'y'=4,'x'=4] {'x'}, use_global_device_ids=true, to_apply=%region_1.2 | all-reduce | flops 1024 | bytes 8192 | tf_op jit(solution)/shard_map/psum | solution.py:304
  (58 shorter events, 9.4 us)
Async XLA Ops:
  7.2 300.9 %copy-start = (bf16[512,512]{1,0:T(8,128)(2,1)S(1)}, bf16[512,512]{1,0:T(8,128)(2,1)}, u32[]{:S(2)}) copy-start(bf16[512,512]{1,0:T(8,128)(2,1)} %param.13) | copy-start | bytes 1572868
  7.2 5.7 %copy-start.1 = (bf16[2,2,4,128,128]{4,3,2,1,0:T(8,128)(2,1)S(1)}, bf16[2,2,4,128,128]{4,3,2,1,0:T(8,128)(2,1)}, u32[]{:S(2)}) copy-start(bf16[2,2,4,128,128]{4,3,2,1,0:T(8,128)(2,1)} %own_ref.12) | copy-start | bytes 1572868
  7.2 145.6 %all-gather.3.cloned.1.call-start = ((), (), s32[]{:S(2)}) async-start(), calls=%async_computation.11 | async-start | bytes 10096640 | tf_op jit(solution)/shard_map/all_gather | solution.py:255
  7.2 4.5 %collective-permute-start.1 = (s32[2,2,4]{2,1,0:T(2,128)}, s32[2,2,4]{2,1,0:T(2,128)S(1)}, u32[]{:S(2)}, u32[]{:S(2)}) collective-permute-start(s32[2,2,4]{2,1,0:T(2,128)} %param.11), channel_id=1, source_target_pairs={{0,64},{64,0},{1,65},{65,1},{2,66},{66,2},{3,67},{67,3},{4,68},{68... | collective-permute-start | bytes 200 | tf_op jit(solution)/shard_map/ppermute | solution.py:219
  11.5 1.3 collective-permute-start
  13.8 20.9 %collective-permute-start.2 = (bf16[2,256,4096]{2,1,0:T(8,128)(2,1)}, bf16[2,256,4096]{2,1,0:T(8,128)(2,1)}, u32[]{:S(2)}, u32[]{:S(2)}) collective-permute-start(bf16[2,256,4096]{2,1,0:T(8,128)(2,1)} %own_l.7), channel_id=1, source_target_pairs={{0,64},{64,0},{1,65},{65,1},{2,66},{66,2},{3,67},{67,3},{4,68},{68... | collective-permute-start | bytes 12582920 | tf_op jit(solution)/shard_map/ppermute | solution.py:219
  14.8 19.9 %all-to-all-start = ((bf16[16,32,256]{2,1,0:T(8,128)(2,1)}), bf16[16,32,256]{2,1,0:T(8,128)(2,1)S(1)}, u32[]{:S(2)}, u32[]{:S(2)}) async-start(bf16[16,32,256]{2,1,0:T(8,128)(2,1)} %broadcast_in_dim.14), calls=%async_computation | async-start | bytes 524288 | tf_op jit(solution)/shard_map/all_to_all | solution.py:246
  24.0 20.7 %collective-permute-start.3 = (bf16[2,2,4,128,128]{4,3,2,1,0:T(8,128)(2,1)S(1)}, bf16[2,2,4,128,128]{4,3,2,1,0:T(8,128)(2,1)S(1)}, u32[]{:S(2)}, u32[]{:S(2)}) collective-permute-start(bf16[2,2,4,128,128]{4,3,2,1,0:T(8,128)(2,1)S(1)} %copy-done.1), channel_id=1, source_target_pairs={{0,64},{64,0},{1,65},{65,1},{2,66},{66,2},{3,67},{67,3},{4,68},{68... | collective-permute-start | bytes 1572872 | tf_op jit(solution)/shard_map/ppermute | solution.py:219
  38.6 22.2 %all-to-all-start.1 = ((bf16[16,32,256]{2,1,0:T(8,128)(2,1)}), bf16[16,32,256]{2,1,0:T(8,128)(2,1)S(1)}, u32[]{:S(2)}, u32[]{:S(2)}) async-start(bf16[16,32,256]{2,1,0:T(8,128)(2,1)} %get-tuple-element.16), calls=%async_computation.1 | async-start | bytes 524288 | tf_op jit(solution)/shard_map/all_to_all | solution.py:246
  81.3 17.8 %all-to-all-start.3 = ((bf16[16,32,256]{2,1,0:T(8,128)(2,1)}), bf16[16,32,256]{2,1,0:T(8,128)(2,1)S(1)}, u32[]{:S(2)}, u32[]{:S(2)}) async-start(bf16[16,32,256]{2,1,0:T(8,128)(2,1)} %get-tuple-element.17), calls=%async_computation.3 | async-start | bytes 524288 | tf_op jit(solution)/shard_map/all_to_all | solution.py:246
  152.8 56.8 %collective-permute-start.5 = (bf16[16,2320,128]{2,1,0:T(8,128)(2,1)}, bf16[16,2320,128]{2,1,0:T(8,128)(2,1)}, u32[]{:S(2)}, u32[]{:S(2)}) collective-permute-start(bf16[16,2320,128]{2,1,0:T(8,128)(2,1)} %bitcast.62), channel_id=1, source_target_pairs={{0,64},{64,0},{1,65},{65,1},{2,66},{66,2},{3,67},{67,3},{4,68},{68... | collective-permute-start | bytes 28508168 | tf_op jit(solution)/shard_map/ppermute | solution.py:219
  190.7 3.5 %collective-permute-start.4 = (bf16[32,256]{1,0:T(8,128)(2,1)S(1)}, bf16[32,256]{1,0:T(8,128)(2,1)S(1)}, u32[]{:S(2)}, u32[]{:S(2)}) collective-permute-start(bf16[32,256]{1,0:T(8,128)(2,1)S(1)} %get-tuple-element.21), channel_id=1, source_target_pairs={{0,128},{1,129},{2,130},{3,131},{4,132},{5,133},{6,134},{7,135},{8... | collective-permute-start | bytes 49160 | tf_op jit(solution)/shard_map/ppermute | solution.py:273
  195.0 14.7 %all-to-all-start.7 = ((bf16[16,32,256]{2,1,0:T(8,128)(2,1)}), bf16[16,32,256]{2,1,0:T(8,128)(2,1)S(1)}, u32[]{:S(2)}, u32[]{:S(2)}) async-start(bf16[16,32,256]{2,1,0:T(8,128)(2,1)} %broadcast_in_dim.15), calls=%async_computation.7 | async-start | bytes 524288 | tf_op jit(solution)/shard_map/all_to_all | solution.py:246
  209.6 12.8 %copy-start.2 = (bf16[2,512,256]{2,1,0:T(8,128)(2,1)S(1)}, bf16[2,512,256]{2,1,0:T(8,128)(2,1)}, u32[]{:S(2)}) copy-start(bf16[2,512,256]{2,1,0:T(8,128)(2,1)} %param.12) | copy-start | bytes 1572868
  217.6 15.0 %all-to-all-start.8 = ((bf16[16,32,256]{2,1,0:T(8,128)(2,1)}), bf16[16,32,256]{2,1,0:T(8,128)(2,1)S(1)}, u32[]{:S(2)}, u32[]{:S(2)}) async-start(bf16[16,32,256]{2,1,0:T(8,128)(2,1)} %get-tuple-element.23), calls=%async_computation.8 | async-start | bytes 524288 | tf_op jit(solution)/shard_map/all_to_all | solution.py:246
  222.5 43.2 %collective-permute-start.7 = (bf16[2,512,256]{2,1,0:T(8,128)(2,1)S(1)}, bf16[2,512,256]{2,1,0:T(8,128)(2,1)S(1)}, u32[]{:S(2)}, u32[]{:S(2)}) collective-permute-start(bf16[2,512,256]{2,1,0:T(8,128)(2,1)S(1)} %copy-done.2), channel_id=1, source_target_pairs={{0,64},{64,0},{1,65},{65,1},{2,66},{66,2},{3,67},{67,3},{4,68},{68... | collective-permute-start | bytes 1572872 | tf_op jit(solution)/shard_map/ppermute | solution.py:219
  261.8 14.0 %all-to-all-start.10 = ((bf16[16,32,256]{2,1,0:T(8,128)(2,1)}), bf16[16,32,256]{2,1,0:T(8,128)(2,1)S(1)}, u32[]{:S(2)}, u32[]{:S(2)}) async-start(bf16[16,32,256]{2,1,0:T(8,128)(2,1)} %get-tuple-element.27), calls=%async_computation.10 | async-start | bytes 524288 | tf_op jit(solution)/shard_map/all_to_all | solution.py:246
  283.2 24.9 %copy-start.3 = (s32[64,512]{1,0:T(8,128)S(1)}, s32[64,512]{1,0:T(8,128)}, u32[]{:S(2)}) copy-start(s32[64,512]{1,0:T(8,128)} %param.8) | copy-start | bytes 393220
  283.6 3.2 collective-permute-start.10
  284.4 4.3 %collective-permute-start.8 = (f32[32,512]{1,0:T(8,128)S(1)}, f32[32,512]{1,0:T(8,128)S(1)}, u32[]{:S(2)}, u32[]{:S(2)}) collective-permute-start(f32[32,512]{1,0:T(8,128)S(1)} %fusion.2), channel_id=1, source_target_pairs={{0,4},{4,8},{8,12},{12,0},{1,5},{5,9},{9,13},{13,1},{2,6},{6,10},{... | collective-permute-start | bytes 196616 | tf_op jit(solution)/shard_map/ppermute | solution.py:212
  285.1 4.6 %collective-permute-start.9 = (f32[32,512]{1,0:T(8,128)S(1)}, f32[32,512]{1,0:T(8,128)S(1)}, u32[]{:S(2)}, u32[]{:S(2)}) collective-permute-start(f32[32,512]{1,0:T(8,128)S(1)} %fusion.2), channel_id=1, source_target_pairs={{0,8},{4,12},{8,0},{12,4},{1,9},{5,13},{9,1},{13,5},{2,10},{6,14},... | collective-permute-start | bytes 196616 | tf_op jit(solution)/shard_map/ppermute | solution.py:212
  289.7 14.1 %collective-permute-start.11 = (f32[32,512]{1,0:T(8,128)S(1)}, f32[32,512]{1,0:T(8,128)S(1)}, u32[]{:S(2)}, u32[]{:S(2)}) collective-permute-start(f32[32,512]{1,0:T(8,128)S(1)} %add_add_fusion.1), channel_id=1, source_target_pairs={{0,16},{16,32},{32,48},{48,0},{1,17},{17,33},{33,49},{49,1},{2,18}... | collective-permute-start | bytes 196616 | tf_op jit(solution)/shard_map/ppermute | solution.py:212
  290.6 13.2 %collective-permute-start.12 = (f32[32,512]{1,0:T(8,128)S(1)}, f32[32,512]{1,0:T(8,128)S(1)}, u32[]{:S(2)}, u32[]{:S(2)}) collective-permute-start(f32[32,512]{1,0:T(8,128)S(1)} %add_add_fusion.1), channel_id=1, source_target_pairs={{0,32},{16,48},{32,0},{48,16},{1,33},{17,49},{33,1},{49,17},{2,34}... | collective-permute-start | bytes 196616 | tf_op jit(solution)/shard_map/ppermute | solution.py:212
  293.2 10.6 %collective-permute-start.13 = (f32[32,512]{1,0:T(8,128)S(1)}, f32[32,512]{1,0:T(8,128)S(1)}, u32[]{:S(2)}, u32[]{:S(2)}) collective-permute-start(f32[32,512]{1,0:T(8,128)S(1)} %add_add_fusion.1), channel_id=1, source_target_pairs={{0,48},{16,0},{32,16},{48,32},{1,49},{17,1},{33,17},{49,33},{2,50}... | collective-permute-start | bytes 196616 | tf_op jit(solution)/shard_map/ppermute | solution.py:212
  294.8 9.9 %collective-permute-start.6 = (bf16[2,32,256]{2,1,0:T(8,128)(2,1)S(1)}, bf16[2,32,256]{2,1,0:T(8,128)(2,1)S(1)}, u32[]{:S(2)}, u32[]{:S(2)}) collective-permute-start(bf16[2,32,256]{2,1,0:T(8,128)(2,1)S(1)} %broadcast_select_fusion.7), channel_id=1, source_target_pairs={{0,64},{64,0},{1,65},{65,1},{2,66},{66,2},{3,67},{67,3},{4,68},{68... | collective-permute-start | bytes 98312 | tf_op jit(solution)/shard_map/ppermute | solution.py:219
  303.8 4.2 %collective-permute-start.14 = (f32[32,512]{1,0:T(8,128)S(1)}, f32[32,512]{1,0:T(8,128)S(1)}, u32[]{:S(2)}, u32[]{:S(2)}) collective-permute-start(f32[32,512]{1,0:T(8,128)S(1)} %add_add_fusion), channel_id=1, source_target_pairs={{0,128},{128,0},{1,129},{129,1},{2,130},{130,2},{3,131},{131,3},{4... | collective-permute-start | bytes 196616 | tf_op jit(solution)/shard_map/ppermute | solution.py:212
  308.3 6.0 %collective-permute-start.15 = (f32[32,512]{1,0:T(8,128)S(1)}, f32[32,512]{1,0:T(8,128)S(1)}, u32[]{:S(2)}, u32[]{:S(2)}) collective-permute-start(f32[32,512]{1,0:T(8,128)S(1)} %fusion.9), channel_id=1, source_target_pairs={{0,64},{64,0},{1,65},{65,1},{2,66},{66,2},{3,67},{67,3},{4,68},{68... | collective-permute-start | bytes 196616 | tf_op jit(solution)/shard_map/ppermute | solution.py:219
Sparse Core Ops, SparseCore 0:
  13.9 138.8 all-gather.2

commit v4 on v1

--- a/solution.py
+++ b/solution.py
@@ -45,45 +45,6 @@
 
 def factor_slices(ref, k, out, i):
     return ref.at[i], out
-
-
-def coupling_slices(ref, k, out, i):
-    size = out.shape[1]
-    return ref.at[pl.ds(i * size, size)], out.at[k]
-
-
-def couple_kernel(place, cols, x_ref, s_ref, c_ref, out_ref, *, step, slots):
-    lines, tall, block = c_ref.shape
-    rows = tall // (slots * block)
-    per = x_ref.shape[2] // block
-    probes = x_ref.shape[1]
-
-    def body(k, carry):
-        for row in range(rows):
-            total = None
-            for slot in range(0, slots, 2):
-                left, right = [], []
-                for pair in range(2):
-                    col = cols[k, (step * rows + row) * slots + slot + pair]
-                    lanes = pl.ds(pl.multiple_of((col % per) * block, block), block)
-                    left.append(x_ref[col // per, :, lanes])
-                    at = (row * slots + slot + pair) * block
-                    right.append(c_ref[k, at : at + block, :])
-                term = lax.dot_general(
-                    jnp.concatenate(left, axis=1),
-                    jnp.concatenate(right, axis=1),
-                    NT,
-                    preferred_element_type=jnp.float32,
-                )
-                total = term if total is None else total + term
-            at = (row * s_ref.shape[1]) // rows + step * probes
-            source = s_ref[k, at : at + probes, :].astype(jnp.float32)
-            home = lax.rem(place[1] + lines - k, lines)
-            lanes = pl.ds(pl.multiple_of((home * rows + row) * block, block), block)
-            out_ref[:, lanes] = (source - total).astype(jnp.bfloat16)
-        return carry
-
-    lax.fori_loop(0, lines, body, 0)
 
 
 def finish(total, outs):
@@ -140,28 +101,27 @@
             out_ref[peer, :, span] = resid
 
 
-def apply_kernel(place, *refs, lines):
-    pieces, l_ref, outs = refs[:lines], refs[lines], refs[lines + 1 :]
-    width = l_ref.shape[0]
-
-    def body(zh, total):
-        for k in range(lines):
-            y = lax.rem(place[2] + lines - k, lines)
-            lanes = pl.ds(pl.multiple_of((zh * lines + y) * width, width), width)
-            here = pl.ds(pl.multiple_of(zh * width, width), width)
+def apply_kernel(r_ref, l_ref, *outs):
+    peers, probes, width = r_ref.shape
+    group = 4
+
+    def body(i, total):
+        for j in range(group):
+            lanes = pl.ds(pl.multiple_of((i * group + j) * width, width), width)
             total = total + lax.dot_general(
-                pieces[k][:, here], l_ref[:, lanes], NT, preferred_element_type=jnp.float32
+                r_ref[i * group + j], l_ref[:, lanes], NT, preferred_element_type=jnp.float32
             )
         return total
 
-    start = jnp.zeros((pieces[0].shape[0], width), jnp.float32)
-    finish(lax.fori_loop(0, pieces[0].shape[1] // width, body, start), outs)
+    start = jnp.zeros((probes, l_ref.shape[0]), jnp.float32)
+    finish(lax.fori_loop(0, peers // group, body, start), outs)
 
 
 VMEM = pl.BlockSpec(memory_space=pltpu.VMEM)
 SMEM = pl.BlockSpec(memory_space=pltpu.SMEM)
 HBM = pl.BlockSpec(memory_space=pltpu.HBM)
 PARAMS = pltpu.CompilerParams(vmem_limit_bytes=16 << 20)
+LARGE = pltpu.CompilerParams(vmem_limit_bytes=50 << 20)
 
 
 def arrange(slices, place, own, other, steps, shape, name, after):
@@ -174,7 +134,7 @@
         in_specs=[SMEM] + [HBM] * (2 * pieces + 1),
         out_specs=tuple([HBM] * steps),
         scratch_shapes=[pltpu.SemaphoreType.DMA((steps, pieces))],
-        compiler_params=PARAMS,
+        compiler_params=LARGE,
         cost_estimate=pl.CostEstimate(
             flops=0, transcendentals=0, bytes_accessed=4 * steps * shape[0] * shape[1]
         ),
@@ -182,18 +142,6 @@
     )(place, *own, *other, after)
 
 
-def couple(place, cols, pieces, source, c, step, slots):
-    lines, tall, block = c.shape
-    return pl.pallas_call(
-        functools.partial(couple_kernel, step=step, slots=slots),
-        out_shape=jax.ShapeDtypeStruct((pieces.shape[1], lines * tall // slots), jnp.bfloat16),
-        in_specs=[SMEM, SMEM, VMEM, VMEM, VMEM],
-        out_specs=VMEM,
-        compiler_params=PARAMS,
-        name="couple",
-    )(place, cols, pieces, source, c)
-
-
 def solved_shapes(probes, rows, peers):
     shapes = [jax.ShapeDtypeStruct((probes, rows), jnp.bfloat16)]
     if peers:
@@ -201,16 +149,17 @@
     return tuple(shapes)
 
 
-def apply_factor(place, pieces, factor, peers):
-    shapes = solved_shapes(pieces[0].shape[0], factor.shape[0], peers)
-    return pl.pallas_call(
-        functools.partial(apply_kernel, lines=len(pieces)),
+def apply_factor(pieces, factor, spread):
+    peers, probes, _ = pieces.shape
+    shapes = solved_shapes(probes, factor.shape[0], peers if spread else 0)
+    return pl.pallas_call(
+        apply_kernel,
         out_shape=shapes,
-        in_specs=[SMEM] + [VMEM] * (len(pieces) + 1),
+        in_specs=[VMEM, VMEM],
         out_specs=tuple([VMEM] * len(shapes)),
         compiler_params=PARAMS,
         name="apply",
-    )(place, *pieces, factor)
+    )(pieces, factor)
 
 
 def apply_early(place, pieces, own, other, step):
@@ -226,7 +175,7 @@
             pltpu.VMEM((4, rows, width // 4), own.dtype),
             pltpu.SemaphoreType.DMA((4,)),
         ],
-        compiler_params=PARAMS,
+        compiler_params=LARGE,
         name="apply_early",
     )(place, pieces, own, other)
 
@@ -238,7 +187,7 @@
         in_specs=[SMEM, SMEM, VMEM, VMEM, HBM, HBM],
         out_specs=VMEM,
         scratch_shapes=[pltpu.VMEM(own.shape[1:], own.dtype), pltpu.SemaphoreType.DMA],
-        compiler_params=PARAMS,
+        compiler_params=LARGE,
         name="couple_early",
     )(place, cols, pieces, source, own, other)
 
@@ -282,46 +231,24 @@
     def everywhere(value):
         return lax.all_to_all(value, NODES, 0, 0)
 
-    solved0 = apply_early(place, everywhere(spread), inverse_factors, other_factors, 0)
-    slots, block = couplings.shape[2:4]
-    cols = own_cols.reshape(1, -1).astype(jnp.bfloat16)
-    width = cols.shape[1]
-    cols = jnp.pad(cols, ((0, 15), (0, block - width)))
-    flat = own_source.reshape(steps * probes, local)
-    halves = [flat[:, i : i + block] for i in range(0, local, block)]
-    bundle = jnp.concatenate([couplings.reshape(-1, block)] + halves + [cols], axis=0)
-    shared = line(bundle, "zh")
-    at = couplings.size // block
-    until = at + steps * probes * local // block
-    tall = at // own_steps
-    resid = couple_early(
-        place, own_cols, everywhere(solved0[1]), own_source[1], couplings, other_couplings, 1
-    )
-    solved1 = apply_early(place, everywhere(resid), inverse_factors, other_factors, 1)
-    pieces = everywhere(solved1[1])
-    shared, after = lax.optimization_barrier((shared, solved1[0]))
-    source = jnp.stack([s[at:until] for s in shared])
-    cols = jnp.concatenate([s[until : until + 1, :width] for s in shared], axis=0).astype(jnp.int32)
-    shape = (len(shared), tall, block)
-    blocks = arrange(
-        coupling_slices, place, shared, [swap(s) for s in shared], steps, shape, "couplings", after
-    )
+    outs = apply_early(place, everywhere(spread), inverse_factors, other_factors, 0)
     factors = arrange(
-        factor_slices, place, [inverse_factors], [other_factors], steps, inverse_factors.shape[1:], "factors", after
-    )
-
+        factor_slices, place, [inverse_factors], [other_factors], steps, inverse_factors.shape[1:], "factors", outs[0]
+    )
+    results = [outs[0]]
     for turn in range(turns):
-        results = []
-        for step in range(2 if turn == 0 else 0, steps):
-            resid = line(couple(place, cols, pieces, source, blocks[step], step, slots), "y")
-            more = step + 1 < steps
-            outs = apply_factor(place, resid, factors[step], peers if more else 0)
+        for step in range(1 if turn == 0 else 0, steps):
+            if step > 0:
+                pieces = everywhere(outs[1])
+            resid = couple_early(
+                place, own_cols, pieces, own_source[step], couplings, other_couplings, step
+            )
+            outs = apply_factor(everywhere(resid), factors[step], step + 1 < steps)
             results.append(outs[0])
-            if more:
-                pieces = everywhere(outs[1])
         if turn + 1 < turns:
             moved = lax.ppermute(outs[0], "zl", [(turn, turn + 1)])
             pieces = everywhere(jnp.broadcast_to(moved[None], (peers, probes, local)))
+            results = []
 
     rows4 = in_order(border_rows, swap(border_rows))
     partial = jnp.zeros((probes, border_rows.shape[1]), jnp.float32)

time: 328 us -> 506 us (1.54)
  Pallas kernels: 33.4 us -> 213 us
  blocking collectives: 112 us -> 140 us
  starting transfers between devices: 113 us -> 89.1 us
  local copies, waits for them, and re-layouts: 16.9 us -> 6.74 us
    pallas_call x2 -> x1, Pallas kernels: 4.9 us -> 192 us  [arrange(): pl.pallas_call(functools.partial(arrange_kernel, per_core=steps // 2, ste...]
    ppermute x28 -> x7, starting transfers between devices: 43 us -> 9.2 us  [line(): lax.ppermute(value, axis, [(i, (i + k) % size) for i in range(size)])]
    all_to_all x4 -> x9, blocking collectives: 104 us -> 131 us  [everywhere(): return lax.all_to_all(value, NODES, 0, 0)]
    all_to_all x5 -> x6, waiting for transfers between devices: 19.3 us -> 34.3 us  [everywhere(): return lax.all_to_all(value, NODES, 0, 0)]
    pallas_call x12 -> x7, Pallas kernels: 20 us -> 8.96 us  [apply_factor(): pl.pallas_call(apply_kernel, out_shape=shapes, in_specs=[VMEM, VMEM], out...]
    ppermute x28 -> x7, waiting for transfers between devices: 16.6 us -> 5.84 us  [line(): lax.ppermute(value, axis, [(i, (i + k) % size) for i in range(size)])]
    unnamed x43 -> x33, local copies, waits for them, and re-layouts: 13.7 us -> 5.89 us
    pallas_call x1 -> x7, Pallas kernels: 0.88 us -> 8.3 us  [couple_early(): pl.pallas_call(functools.partial(early_couple_kernel, step=step, per_core...]
  transfers between devices with their start and end apart: 45 -> 21, of which waited for: 25 -> 12; matrix products, arithmetic and copies ran while one was open for 3% -> 1% of each run, Pallas kernels for 5% -> 39%
where the time goes in v4:
time: 506 us; the launch traced here: 504 us
  Pallas kernels  213 us (42%)
  blocking collectives  140 us (28%)
  starting transfers between devices  89.1 us (18%)
  waiting for transfers between devices  48 us (9%)
  local copies, waits for them, and re-layouts  6.74 us (1%)
    pallas_call x1, Pallas kernels, arrange(): pl.pallas_call(functools.partial(arrange_kernel, per_core=steps // 2, ste...  192 us
    all_to_all x9, blocking collectives, everywhere(): return lax.all_to_all(value, NODES, 0, 0)  131 us
    ppermute x7, starting transfers between devices, swap(): return lax.ppermute(value, 'core', [(0, 1), (1, 0)])  41.1 us
    all_to_all x6, starting transfers between devices, everywhere(): return lax.all_to_all(value, NODES, 0, 0)  36.5 us
    all_to_all x6, waiting for transfers between devices, everywhere(): return lax.all_to_all(value, NODES, 0, 0)  34.3 us
  transfers between devices with their start and end apart: 21, of which 12 were waited for; matrix products, arithmetic and copies ran while one was open for 1% of the time, Pallas kernels for 39%

profile of v4, /device:TPU:1, one launch (start us, length us, event | category | flops | bytes accessed | tf_op | source)
XLA Modules:
  0.0 504.0 jit_solution(17767064896814807152)
XLA Ops:
  0.6 3.3 collective-permute-start.2
  5.1 5.7 %collective-permute-done.1 = bf16[2,32,256]{2,1,0:T(8,128)(2,1)S(1)} collective-permute-done((bf16[2,32,256]{2,1,0:T(8,128)(2,1)S(1)}, bf16[2,32,256]{2,1,0:T(8,128)(2,1)S(1)}, u32[]{:S(2)}, u32[]{:S(2)}) %collective-permute-start.1) | collective-permute-done | bytes 32800 | tf_op jit(solution)/shard_map/ppermute | solution.py:205
  11.6 9.2 %all-to-all-start = ((bf16[16,32,256]{2,1,0:T(8,128)(2,1)}), bf16[16,32,256]{2,1,0:T(8,128)(2,1)S(1)}, u32[]{:S(2)}, u32[]{:S(2)}) async-start(bf16[16,32,256]{2,1,0:T(8,128)(2,1)} %broadcast_in_dim.14), calls=%async_computation | async-start | bytes 524288 | tf_op jit(solution)/shard_map/all_to_all | solution.py:232
  21.6 9.9 %all-to-all-done.r_ref = bf16[16,32,256]{2,1,0:T(8,128)(2,1)S(1)} async-done(((bf16[16,32,256]{2,1,0:T(8,128)(2,1)}), bf16[16,32,256]{2,1,0:T(8,128)(2,1)S(1)}, u32[]{:S(2)}, u32[]{:S(2)}) %all-to-all-start) | async-done | bytes 262176 | tf_op jit(solution)/shard_map/all_to_all | solution.py:232
  31.5 3.8 apply_early.1
  35.3 5.1 %all-to-all-start.1 = ((bf16[16,32,256]{2,1,0:T(8,128)(2,1)}), bf16[16,32,256]{2,1,0:T(8,128)(2,1)S(1)}, u32[]{:S(2)}, u32[]{:S(2)}) async-start(bf16[16,32,256]{2,1,0:T(8,128)(2,1)} %get-tuple-element.18), calls=%async_computation.1 | async-start | bytes 524288 | tf_op jit(solution)/shard_map/all_to_all | solution.py:232
  40.5 1.9 collective-permute-start
  43.3 7.3 %all-to-all-done.1.x_ref = bf16[16,32,256]{2,1,0:T(8,128)(2,1)S(1)} async-done(((bf16[16,32,256]{2,1,0:T(8,128)(2,1)}), bf16[16,32,256]{2,1,0:T(8,128)(2,1)S(1)}, u32[]{:S(2)}, u32[]{:S(2)}) %all-to-all-start.1) | async-done | bytes 262176 | tf_op jit(solution)/shard_map/all_to_all | solution.py:232
  50.6 1.6 couple_early.7
  52.2 4.9 all-to-all-start.2
  57.1 192.3 %factors.1 = (bf16[256,4096]{1,0:T(8,128)(2,1)S(1)}, bf16[256,4096]{1,0:T(8,128)(2,1)}, bf16[256,4096]{1,0:T(8,128)(2,1)}, bf16[256,4096]{1,0:T(8,128)(2,1)}) custom-call(s32[3]{0:T(128)S(1)} %pad_add_fusion.1.place, bf16[2,256,4096]{2,1,0:T(8,128)(2,1)} %refs_0_.1, bf16[2,256,4096]{2,1,0:T(8,128)(2,1)} %collective-permute-done.2.other_ref.refs_1_, ...), custom_call_target="tpu_custom_call" | custom-call | bytes 16777216 | tf_op jit(solution)/shard_map/factors/pallas_call | solution.py:129
  249.4 1.3 copy-done.8
  250.8 1.6 copy-done.6
  252.4 1.8 apply.7
  254.2 9.1 %all-to-all-start.3 = ((bf16[16,32,256]{2,1,0:T(8,128)(2,1)}), bf16[16,32,256]{2,1,0:T(8,128)(2,1)S(1)}, u32[]{:S(2)}, u32[]{:S(2)}) async-start(bf16[16,32,256]{2,1,0:T(8,128)(2,1)} %get-tuple-element.21), calls=%async_computation.3 | async-start | bytes 524288 | tf_op jit(solution)/shard_map/all_to_all | solution.py:232
  263.3 10.0 %all-to-all-done.3.x_ref = bf16[16,32,256]{2,1,0:T(8,128)(2,1)S(1)} async-done(((bf16[16,32,256]{2,1,0:T(8,128)(2,1)}), bf16[16,32,256]{2,1,0:T(8,128)(2,1)S(1)}, u32[]{:S(2)}, u32[]{:S(2)}) %all-to-all-start.3) | async-done | bytes 262176 | tf_op jit(solution)/shard_map/all_to_all | solution.py:232
  274.2 13.6 %all_to_all.75.r_ref = bf16[16,32,256]{2,1,0:T(8,128)(2,1)S(1)} all-to-all(bf16[16,32,256]{2,1,0:T(8,128)(2,1)S(1)} %couple_early.8), channel_id=1, replica_groups=mesh['zl'=2,'core'=2,'zh'=4,'y'=4,'x'=4] {'zh','y'}, dimensions={0} | all-to-all | bytes 524288 | tf_op jit(solution)/shard_map/all_to_all | solution.py:232
  287.8 1.7 apply.8
  289.5 13.7 %all_to_all.76.x_ref = bf16[16,32,256]{2,1,0:T(8,128)(2,1)S(1)} all-to-all(bf16[16,32,256]{2,1,0:T(8,128)(2,1)S(1)} %get-tuple-element.23), channel_id=1, replica_groups=mesh['zl'=2,'core'=2,'zh'=4,'y'=4,'x'=4] {'zh','y'}, dimensions={0} | all-to-all | bytes 524288 | tf_op jit(solution)/shard_map/all_to_all | solution.py:232
  304.1 13.6 %all_to_all.77.r_ref = bf16[16,32,256]{2,1,0:T(8,128)(2,1)S(1)} all-to-all(bf16[16,32,256]{2,1,0:T(8,128)(2,1)S(1)} %couple_early.9), channel_id=1, replica_groups=mesh['zl'=2,'core'=2,'zh'=4,'y'=4,'x'=4] {'zh','y'}, dimensions={0} | all-to-all | bytes 524288 | tf_op jit(solution)/shard_map/all_to_all | solution.py:232
  317.7 1.1 apply.9
  318.8 2.3 collective-permute-start.4
  321.9 13.7 %all_to_all.78.x_ref = bf16[16,32,256]{2,1,0:T(8,128)(2,1)S(1)} all-to-all(bf16[16,32,256]{2,1,0:T(8,128)(2,1)S(1)} %broadcast_in_dim.15), channel_id=1, replica_groups=mesh['zl'=2,'core'=2,'zh'=4,'y'=4,'x'=4] {'zh','y'}, dimensions={0} | all-to-all | bytes 524288 | tf_op jit(solution)/shard_map/all_to_all | solution.py:232
  336.5 14.1 %all_to_all.79.r_ref = bf16[16,32,256]{2,1,0:T(8,128)(2,1)S(1)} all-to-all(bf16[16,32,256]{2,1,0:T(8,128)(2,1)S(1)} %couple_early.10), channel_id=1, replica_groups=mesh['zl'=2,'core'=2,'zh'=4,'y'=4,'x'=4] {'zh','y'}, dimensions={0} | all-to-all | bytes 524288 | tf_op jit(solution)/shard_map/all_to_all | solution.py:232
  350.6 1.1 apply.10
  351.7 14.2 %all_to_all.80.x_ref = bf16[16,32,256]{2,1,0:T(8,128)(2,1)S(1)} all-to-all(bf16[16,32,256]{2,1,0:T(8,128)(2,1)S(1)} %get-tuple-element.27), channel_id=1, replica_groups=mesh['zl'=2,'core'=2,'zh'=4,'y'=4,'x'=4] {'zh','y'}, dimensions={0} | all-to-all | bytes 524288 | tf_op jit(solution)/shard_map/all_to_all | solution.py:232
  366.8 13.9 %all_to_all.81.r_ref = bf16[16,32,256]{2,1,0:T(8,128)(2,1)S(1)} all-to-all(bf16[16,32,256]{2,1,0:T(8,128)(2,1)S(1)} %couple_early.11), channel_id=1, replica_groups=mesh['zl'=2,'core'=2,'zh'=4,'y'=4,'x'=4] {'zh','y'}, dimensions={0} | all-to-all | bytes 524288 | tf_op jit(solution)/shard_map/all_to_all | solution.py:232
  380.7 1.1 apply.11
  381.8 15.6 %all_to_all.82.x_ref = bf16[16,32,256]{2,1,0:T(8,128)(2,1)S(1)} all-to-all(bf16[16,32,256]{2,1,0:T(8,128)(2,1)S(1)} %get-tuple-element.29), channel_id=1, replica_groups=mesh['zl'=2,'core'=2,'zh'=4,'y'=4,'x'=4] {'zh','y'}, dimensions={0} | all-to-all | bytes 524288 | tf_op jit(solution)/shard_map/all_to_all | solution.py:232
  397.4 1.6 couple_early.12
  399.0 4.1 all-to-all-start.12
  403.1 19.4 %collective-permute-start.6 = (bf16[2,512,256]{2,1,0:T(8,128)(2,1)S(1)}, bf16[2,512,256]{2,1,0:T(8,128)(2,1)}, u32[]{:S(2)}, u32[]{:S(2)}) collective-permute-start(bf16[2,512,256]{2,1,0:T(8,128)(2,1)S(1)} %copy-done.12), channel_id=1, source_target_pairs={{0,64},{64,0},{1,65},{65,1},{2,66},{66,2},{3,67},{67,3},{4,68},{68... | collective-permute-start | bytes 1572872 | tf_op jit(solution)/shard_map/ppermute | solution.py:205
  422.5 1.6 copy-done.5
  424.1 1.1 apply.12
  425.2 19.1 %all_to_all.83.x_ref = bf16[16,32,256]{2,1,0:T(8,128)(2,1)S(1)} all-to-all(bf16[16,32,256]{2,1,0:T(8,128)(2,1)S(1)} %get-tuple-element.31), channel_id=1, replica_groups=mesh['zl'=2,'core'=2,'zh'=4,'y'=4,'x'=4] {'zh','y'}, dimensions={0} | all-to-all | bytes 524288 | tf_op jit(solution)/shard_map/all_to_all | solution.py:232
  444.3 1.6 couple_early.13
  445.9 4.1 all-to-all-start.14
  450.0 1.3 broadcast_select_fusion.1
  452.9 7.0 %all-to-all-done.14.r_ref = bf16[16,32,256]{2,1,0:T(8,128)(2,1)S(1)} async-done(((bf16[16,32,256]{2,1,0:T(8,128)(2,1)}), bf16[16,32,256]{2,1,0:T(8,128)(2,1)S(1)}, u32[]{:S(2)}, u32[]{:S(2)}) %all-to-all-start.14) | async-done | bytes 262176 | tf_op jit(solution)/shard_map/all_to_all | solution.py:232
  461.6 1.9 collective-permute-start.8
  463.5 1.5 collective-permute-start.9
  465.0 2.2 collective-permute-done.7
  468.6 2.4 collective-permute-start.11
  471.0 1.8 collective-permute-start.12
  472.9 10.0 %collective-permute-start.5 = (bf16[2,32,256]{2,1,0:T(8,128)(2,1)S(1)}, bf16[2,32,256]{2,1,0:T(8,128)(2,1)S(1)}, u32[]{:S(2)}, u32[]{:S(2)}) collective-permute-start(bf16[2,32,256]{2,1,0:T(8,128)(2,1)S(1)} %broadcast_select_fusion.7), channel_id=1, source_target_pairs={{0,64},{64,0},{1,65},{65,1},{2,66},{66,2},{3,67},{67,3},{4,68},{68... | collective-permute-start | bytes 98312 | tf_op jit(solution)/shard_map/ppermute | solution.py:205
  483.8 3.2 collective-permute-done.13
  487.2 5.6 %collective-permute-start.14 = (f32[32,512]{1,0:T(8,128)S(1)}, f32[32,512]{1,0:T(8,128)S(1)}, u32[]{:S(2)}, u32[]{:S(2)}) collective-permute-start(f32[32,512]{1,0:T(8,128)S(1)} %fusion.7), channel_id=1, source_target_pairs={{0,64},{64,0},{1,65},{65,1},{2,66},{66,2},{3,67},{67,3},{4,68},{68... | collective-permute-start | bytes 196616 | tf_op jit(solution)/shard_map/ppermute | solution.py:205
  494.4 8.4 %all-reduce = (f32[2,256]{1,0:T(2,128)S(1)}, f32[512]{0:T(512)S(1)}) all-reduce(f32[2,256]{1,0:T(2,128)S(1)} %multiply_reduce_fusion.1, f32[512]{0:T(512)S(1)} %get-tuple-element.42), channel_id=1, replica_groups=mesh['zl'=2,'core'=2,'zh'=4,'y'=4,'x'=4] {'x'}, use_global_device_ids=true, to_apply=%region_1.2 | all-reduce | flops 1024 | bytes 8192 | tf_op jit(solution)/shard_map/psum | solution.py:274
  (81 shorter events, 16.5 us)
Async XLA Ops:
  0.6 486.3 %copy-start = (bf16[512,512]{1,0:T(8,128)(2,1)S(1)}, bf16[512,512]{1,0:T(8,128)(2,1)}, u32[]{:S(2)}) copy-start(bf16[512,512]{1,0:T(8,128)(2,1)} %param.13) | copy-start | bytes 1572868
  0.6 30.8 %collective-permute-start.2 = (bf16[2,256,4096]{2,1,0:T(8,128)(2,1)}, bf16[2,256,4096]{2,1,0:T(8,128)(2,1)}, u32[]{:S(2)}, u32[]{:S(2)}) collective-permute-start(bf16[2,256,4096]{2,1,0:T(8,128)(2,1)} %refs_0_.1), channel_id=1, source_target_pairs={{0,64},{64,0},{1,65},{65,1},{2,66},{66,2},{3,67},{67,3},{4,68},{68... | collective-permute-start | bytes 12582920 | tf_op jit(solution)/shard_map/ppermute | solution.py:205
  4.9 5.9 %collective-permute-start.1 = (bf16[2,32,256]{2,1,0:T(8,128)(2,1)S(1)}, bf16[2,32,256]{2,1,0:T(8,128)(2,1)S(1)}, u32[]{:S(2)}, u32[]{:S(2)}) collective-permute-start(bf16[2,32,256]{2,1,0:T(8,128)(2,1)S(1)} %select_bitcast_fusion), channel_id=1, source_target_pairs={{0,64},{64,0},{1,65},{65,1},{2,66},{66,2},{3,67},{67,3},{4,68},{68... | collective-permute-start | bytes 98312 | tf_op jit(solution)/shard_map/ppermute | solution.py:205
  11.6 19.9 %all-to-all-start = ((bf16[16,32,256]{2,1,0:T(8,128)(2,1)}), bf16[16,32,256]{2,1,0:T(8,128)(2,1)S(1)}, u32[]{:S(2)}, u32[]{:S(2)}) async-start(bf16[16,32,256]{2,1,0:T(8,128)(2,1)} %broadcast_in_dim.14), calls=%async_computation | async-start | bytes 524288 | tf_op jit(solution)/shard_map/all_to_all | solution.py:232
  20.8 22.6 %collective-permute-start.3 = (bf16[2,2,4,128,128]{4,3,2,1,0:T(8,128)(2,1)}, bf16[2,2,4,128,128]{4,3,2,1,0:T(8,128)(2,1)S(1)}, u32[]{:S(2)}, u32[]{:S(2)}) collective-permute-start(bf16[2,2,4,128,128]{4,3,2,1,0:T(8,128)(2,1)} %own_ref.15), channel_id=1, source_target_pairs={{0,64},{64,0},{1,65},{65,1},{2,66},{66,2},{3,67},{67,3},{4,68},{68... | collective-permute-start | bytes 1572872 | tf_op jit(solution)/shard_map/ppermute | solution.py:205
  21.6 18.9 %copy-start.15 = (s32[2,2,4]{2,1,0:T(2,128)S(1)}, s32[2,2,4]{2,1,0:T(2,128)}, u32[]{:S(2)}) copy-start(s32[2,2,4]{2,1,0:T(2,128)} %param.11) | copy-start | bytes 196
  21.6 29.1 %copy-start.1 = (bf16[2,2,4,128,128]{4,3,2,1,0:T(8,128)(2,1)S(1)}, bf16[2,2,4,128,128]{4,3,2,1,0:T(8,128)(2,1)}, u32[]{:S(2)}) copy-start(bf16[2,2,4,128,128]{4,3,2,1,0:T(8,128)(2,1)} %own_ref.15) | copy-start | bytes 1572868
  35.3 15.3 %all-to-all-start.1 = ((bf16[16,32,256]{2,1,0:T(8,128)(2,1)}), bf16[16,32,256]{2,1,0:T(8,128)(2,1)S(1)}, u32[]{:S(2)}, u32[]{:S(2)}) async-start(bf16[16,32,256]{2,1,0:T(8,128)(2,1)} %get-tuple-element.18), calls=%async_computation.1 | async-start | bytes 524288 | tf_op jit(solution)/shard_map/all_to_all | solution.py:232
  40.5 2.8 collective-permute-start
  52.2 198.6 %all-to-all-start.2 = ((bf16[16,32,256]{2,1,0:T(8,128)(2,1)}), bf16[16,32,256]{2,1,0:T(8,128)(2,1)S(1)}, u32[]{:S(2)}, u32[]{:S(2)}) async-start(bf16[16,32,256]{2,1,0:T(8,128)(2,1)} %couple_early.7), calls=%async_computation.2 | async-start | bytes 524288 | tf_op jit(solution)/shard_map/all_to_all | solution.py:232
  249.4 1.3 copy-start.8
  250.8 1.6 copy-start.6
  254.2 19.1 %all-to-all-start.3 = ((bf16[16,32,256]{2,1,0:T(8,128)(2,1)}), bf16[16,32,256]{2,1,0:T(8,128)(2,1)S(1)}, u32[]{:S(2)}, u32[]{:S(2)}) async-start(bf16[16,32,256]{2,1,0:T(8,128)(2,1)} %get-tuple-element.21), calls=%async_computation.3 | async-start | bytes 524288 | tf_op jit(solution)/shard_map/all_to_all | solution.py:232
  273.3 14.5 %copy-start.4 = (bf16[256,4096]{1,0:T(8,128)(2,1)S(1)}, bf16[256,4096]{1,0:T(8,128)(2,1)}, u32[]{:S(2)}) copy-start(bf16[256,4096]{1,0:T(8,128)(2,1)} %get-tuple-element.22.l_ref) | copy-start | bytes 6291460
  287.8 29.9 %copy-start.2 = (bf16[256,4096]{1,0:T(8,128)(2,1)S(1)}, bf16[256,4096]{1,0:T(8,128)(2,1)}, u32[]{:S(2)}) copy-start(bf16[256,4096]{1,0:T(8,128)(2,1)} %get-tuple-element.24.l_ref) | copy-start | bytes 6291460
  317.7 32.9 %copy-start.9 = (bf16[256,4096]{1,0:T(8,128)(2,1)S(1)}, bf16[256,4096]{1,0:T(8,128)(2,1)}, u32[]{:S(2)}) copy-start(bf16[256,4096]{1,0:T(8,128)(2,1)} %copy-done.8) | copy-start | bytes 6291460
  318.8 3.1 collective-permute-start.4
  350.6 30.1 %copy-start.7 = (bf16[256,4096]{1,0:T(8,128)(2,1)S(1)}, bf16[256,4096]{1,0:T(8,128)(2,1)}, u32[]{:S(2)}) copy-start(bf16[256,4096]{1,0:T(8,128)(2,1)} %get-tuple-element.20.l_ref) | copy-start | bytes 6291460
  380.7 22.4 %copy-start.12 = (bf16[2,512,256]{2,1,0:T(8,128)(2,1)S(1)}, bf16[2,512,256]{2,1,0:T(8,128)(2,1)}, u32[]{:S(2)}) copy-start(bf16[2,512,256]{2,1,0:T(8,128)(2,1)} %param.12) | copy-start | bytes 1572868
  399.0 23.5 %all-to-all-start.12 = ((bf16[16,32,256]{2,1,0:T(8,128)(2,1)}), bf16[16,32,256]{2,1,0:T(8,128)(2,1)S(1)}, u32[]{:S(2)}, u32[]{:S(2)}) async-start(bf16[16,32,256]{2,1,0:T(8,128)(2,1)} %couple_early.12), calls=%async_computation.12 | async-start | bytes 524288 | tf_op jit(solution)/shard_map/all_to_all | solution.py:232
  403.1 46.9 %collective-permute-start.6 = (bf16[2,512,256]{2,1,0:T(8,128)(2,1)S(1)}, bf16[2,512,256]{2,1,0:T(8,128)(2,1)}, u32[]{:S(2)}, u32[]{:S(2)}) collective-permute-start(bf16[2,512,256]{2,1,0:T(8,128)(2,1)S(1)} %copy-done.12), channel_id=1, source_target_pairs={{0,64},{64,0},{1,65},{65,1},{2,66},{66,2},{3,67},{67,3},{4,68},{68... | collective-permute-start | bytes 1572872 | tf_op jit(solution)/shard_map/ppermute | solution.py:205
  422.5 1.6 copy-start.5
  445.9 14.1 %copy-start.3 = (bf16[256,4096]{1,0:T(8,128)(2,1)S(1)}, bf16[256,4096]{1,0:T(8,128)(2,1)}, u32[]{:S(2)}) copy-start(bf16[256,4096]{1,0:T(8,128)(2,1)} %get-tuple-element.24.l_ref) | copy-start | bytes 6291460
  445.9 14.1 %all-to-all-start.14 = ((bf16[16,32,256]{2,1,0:T(8,128)(2,1)}), bf16[16,32,256]{2,1,0:T(8,128)(2,1)S(1)}, u32[]{:S(2)}, u32[]{:S(2)}) async-start(bf16[16,32,256]{2,1,0:T(8,128)(2,1)} %couple_early.13), calls=%async_computation.14 | async-start | bytes 524288 | tf_op jit(solution)/shard_map/all_to_all | solution.py:232
  451.3 0.8 copy-start.10
  460.0 1.1 copy-start.11
  460.0 1.3 copy-start.13
  460.0 27.0 %copy-start.14 = (s32[64,512]{1,0:T(8,128)S(1)}, s32[64,512]{1,0:T(8,128)}, u32[]{:S(2)}) copy-start(s32[64,512]{1,0:T(8,128)} %param.8) | copy-start | bytes 393220
  461.5 5.7 %collective-permute-start.7 = (f32[32,512]{1,0:T(8,128)S(1)}, f32[32,512]{1,0:T(8,128)S(1)}, u32[]{:S(2)}, u32[]{:S(2)}) collective-permute-start(f32[32,512]{1,0:T(8,128)S(1)} %fusion.1), channel_id=1, source_target_pairs={{0,4},{4,8},{8,12},{12,0},{1,5},{5,9},{9,13},{13,1},{2,6},{6,10},{... | collective-permute-start | bytes 196616 | tf_op jit(solution)/shard_map/ppermute | solution.py:198
  461.6 5.6 %collective-permute-start.8 = (f32[32,512]{1,0:T(8,128)S(1)}, f32[32,512]{1,0:T(8,128)S(1)}, u32[]{:S(2)}, u32[]{:S(2)}) collective-permute-start(f32[32,512]{1,0:T(8,128)S(1)} %fusion.1), channel_id=1, source_target_pairs={{0,8},{4,12},{8,0},{12,4},{1,9},{5,13},{9,1},{13,5},{2,10},{6,14},... | collective-permute-start | bytes 196616 | tf_op jit(solution)/shard_map/ppermute | solution.py:198
  463.5 4.1 collective-permute-start.9
  467.6 15.3 %collective-permute-start.10 = (f32[32,512]{1,0:T(8,128)S(1)}, f32[32,512]{1,0:T(8,128)S(1)}, u32[]{:S(2)}, u32[]{:S(2)}) collective-permute-start(f32[32,512]{1,0:T(8,128)S(1)} %add_add_fusion.1), channel_id=1, source_target_pairs={{0,16},{16,32},{32,48},{48,0},{1,17},{17,33},{33,49},{49,1},{2,18}... | collective-permute-start | bytes 196616 | tf_op jit(solution)/shard_map/ppermute | solution.py:198
  468.6 14.3 %collective-permute-start.11 = (f32[32,512]{1,0:T(8,128)S(1)}, f32[32,512]{1,0:T(8,128)S(1)}, u32[]{:S(2)}, u32[]{:S(2)}) collective-permute-start(f32[32,512]{1,0:T(8,128)S(1)} %add_add_fusion.1), channel_id=1, source_target_pairs={{0,32},{16,48},{32,0},{48,16},{1,33},{17,49},{33,1},{49,17},{2,34}... | collective-permute-start | bytes 196616 | tf_op jit(solution)/shard_map/ppermute | solution.py:198
  471.0 11.9 %collective-permute-start.12 = (f32[32,512]{1,0:T(8,128)S(1)}, f32[32,512]{1,0:T(8,128)S(1)}, u32[]{:S(2)}, u32[]{:S(2)}) collective-permute-start(f32[32,512]{1,0:T(8,128)S(1)} %add_add_fusion.1), channel_id=1, source_target_pairs={{0,48},{16,0},{32,16},{48,32},{1,49},{17,1},{33,17},{49,33},{2,50}... | collective-permute-start | bytes 196616 | tf_op jit(solution)/shard_map/ppermute | solution.py:198
  472.9 10.9 %collective-permute-start.5 = (bf16[2,32,256]{2,1,0:T(8,128)(2,1)S(1)}, bf16[2,32,256]{2,1,0:T(8,128)(2,1)S(1)}, u32[]{:S(2)}, u32[]{:S(2)}) collective-permute-start(bf16[2,32,256]{2,1,0:T(8,128)(2,1)S(1)} %broadcast_select_fusion.7), channel_id=1, source_target_pairs={{0,64},{64,0},{1,65},{65,1},{2,66},{66,2},{3,67},{67,3},{4,68},{68... | collective-permute-start | bytes 98312 | tf_op jit(solution)/shard_map/ppermute | solution.py:205
  482.9 4.0 collective-permute-start.13
  487.2 6.5 %collective-permute-start.14 = (f32[32,512]{1,0:T(8,128)S(1)}, f32[32,512]{1,0:T(8,128)S(1)}, u32[]{:S(2)}, u32[]{:S(2)}) collective-permute-start(f32[32,512]{1,0:T(8,128)S(1)} %fusion.7), channel_id=1, source_target_pairs={{0,64},{64,0},{1,65},{65,1},{2,66},{66,2},{3,67},{67,3},{4,68},{68... | collective-permute-start | bytes 196616 | tf_op jit(solution)/shard_map/ppermute | solution.py:205

commit v5 on v4

--- a/solution.py
+++ b/solution.py
@@ -132,9 +132,9 @@
         ),
         out_shape=tuple([jax.ShapeDtypeStruct(shape, jnp.bfloat16)] * steps),
         in_specs=[SMEM] + [HBM] * (2 * pieces + 1),
-        out_specs=tuple([HBM] * steps),
+        out_specs=tuple([VMEM] * steps),
         scratch_shapes=[pltpu.SemaphoreType.DMA((steps, pieces))],
-        compiler_params=LARGE,
+        compiler_params=PARAMS,
         cost_estimate=pl.CostEstimate(
             flops=0, transcendentals=0, bytes_accessed=4 * steps * shape[0] * shape[1]
         ),
@@ -226,7 +226,8 @@
     own_source = in_order(jnp.where(first, source[0], source[1]), other_half)
     spread = jnp.broadcast_to(own_source[0][None], (peers, probes, local))
     own_cols = in_order(coupling_cols, swap(coupling_cols)).reshape(-1)
-    other_factors, other_couplings = swap(inverse_factors), swap(couplings)
+    own_factors, own_couplings, _ = lax.optimization_barrier((inverse_factors, couplings, spread))
+    other_factors, other_couplings = swap(own_factors), swap(own_couplings)
 
     def everywhere(value):
         return lax.all_to_all(value, NODES, 0, 0)

time: 506 us -> 318 us (0.63)
  Pallas kernels: 213 us -> 23.9 us
  local copies, waits for them, and re-layouts: 6.74 us -> 13 us
    pallas_call x1, Pallas kernels: 192 us -> 2.81 us  [arrange(): pl.pallas_call(functools.partial(arrange_kernel, per_core=steps // 2, ste...]
    unnamed x33 -> x41, local copies, waits for them, and re-layouts: 5.89 us -> 12.2 us
  transfers between devices with their start and end apart: 21 -> 21, of which waited for: 12 -> 12; matrix products, arithmetic and copies ran while one was open for 1% -> 1% of each run, Pallas kernels for 39% -> 3%
where the time goes in v5:
time: 318 us; the launch traced here: 317 us
  blocking collectives  140 us (44%)
  starting transfers between devices  88.9 us (28%)
  waiting for transfers between devices  43.4 us (14%)
  Pallas kernels  23.9 us (8%)
  local copies, waits for them, and re-layouts  13 us (4%)
  other arithmetic  4.3 us (1%)
    all_to_all x9, blocking collectives, everywhere(): return lax.all_to_all(value, NODES, 0, 0)  132 us
    ppermute x7, starting transfers between devices, swap(): return lax.ppermute(value, 'core', [(0, 1), (1, 0)])  41.1 us
    all_to_all x6, starting transfers between devices, everywhere(): return lax.all_to_all(value, NODES, 0, 0)  36.5 us
    all_to_all x6, waiting for transfers between devices, everywhere(): return lax.all_to_all(value, NODES, 0, 0)  34.5 us
    unnamed x41, local copies, waits for them, and re-layouts  12.2 us
    ppermute x7, starting transfers between devices, line(): lax.ppermute(value, axis, [(i, (i + k) % size) for i in range(size)])  9.21 us
    pallas_call x7, Pallas kernels, apply_factor(): pl.pallas_call(apply_kernel, out_shape=shapes, in_specs=[VMEM, VMEM], out...  8.96 us
    psum x1, blocking collectives, shards(): node_sums, border_sums = lax.psum((node_sums, border_sums), 'x')  8.47 us
  transfers between devices with their start and end apart: 21, of which 12 were waited for; matrix products, arithmetic and copies ran while one was open for 1% of the time, Pallas kernels for 3%

profile of v5, /device:TPU:1, one launch (start us, length us, event | category | flops | bytes accessed | tf_op | source)
XLA Modules:
  0.0 316.7 jit_solution(1287188695871006249)
XLA Ops:
  1.7 3.3 %collective-permute-start.1 = (bf16[2,32,256]{2,1,0:T(8,128)(2,1)S(1)}, bf16[2,32,256]{2,1,0:T(8,128)(2,1)S(1)}, u32[]{:S(2)}, u32[]{:S(2)}) collective-permute-start(bf16[2,32,256]{2,1,0:T(8,128)(2,1)S(1)} %select_bitcast_fusion), channel_id=1, source_target_pairs={{0,64},{64,0},{1,65},{65,1},{2,66},{66,2},{3,67},{67,3},{4,68},{68... | collective-permute-start | bytes 98312 | tf_op jit(solution)/shard_map/ppermute | solution.py:205
  7.0 9.2 %all-to-all-start = ((bf16[16,32,256]{2,1,0:T(8,128)(2,1)}), bf16[16,32,256]{2,1,0:T(8,128)(2,1)S(1)}, u32[]{:S(2)}, u32[]{:S(2)}) async-start(bf16[16,32,256]{2,1,0:T(8,128)(2,1)} %broadcast_in_dim.14), calls=%async_computation | async-start | bytes 524288 | tf_op jit(solution)/shard_map/all_to_all | solution.py:233
  16.8 10.2 %all-to-all-done.r_ref = bf16[16,32,256]{2,1,0:T(8,128)(2,1)S(1)} async-done(((bf16[16,32,256]{2,1,0:T(8,128)(2,1)}), bf16[16,32,256]{2,1,0:T(8,128)(2,1)S(1)}, u32[]{:S(2)}, u32[]{:S(2)}) %all-to-all-start) | async-done | bytes 262176 | tf_op jit(solution)/shard_map/all_to_all | solution.py:233
  27.0 3.9 %apply_early.1 = (bf16[32,256]{1,0:T(8,128)(2,1)S(1)}, bf16[16,32,256]{2,1,0:T(8,128)(2,1)}) custom-call(s32[3]{0:T(128)S(1)} %pad_add_fusion.1.place, bf16[16,32,256]{2,1,0:T(8,128)(2,1)S(1)} %all-to-all-done.r_ref, bf16[2,256,4096]{2,1,0:T(8,128)(2,1)} %refs_0_.1, bf16[2,256,4096]{2,1,0:T(8,128)(2,1)} %collective-permute-done.2.other_ref.refs_1_), custom_call_target="tpu_custom_call" | custom-call | tf_op jit(solution)/shard_map/apply_early/pallas_call | solution.py:169
  30.8 5.1 %all-to-all-start.1 = ((bf16[16,32,256]{2,1,0:T(8,128)(2,1)}), bf16[16,32,256]{2,1,0:T(8,128)(2,1)S(1)}, u32[]{:S(2)}, u32[]{:S(2)}) async-start(bf16[16,32,256]{2,1,0:T(8,128)(2,1)} %get-tuple-element.21), calls=%async_computation.1 | async-start | bytes 524288 | tf_op jit(solution)/shard_map/all_to_all | solution.py:233
  35.9 1.9 collective-permute-start
  38.8 7.3 %all-to-all-done.1.x_ref = bf16[16,32,256]{2,1,0:T(8,128)(2,1)S(1)} async-done(((bf16[16,32,256]{2,1,0:T(8,128)(2,1)}), bf16[16,32,256]{2,1,0:T(8,128)(2,1)S(1)}, u32[]{:S(2)}, u32[]{:S(2)}) %all-to-all-start.1) | async-done | bytes 262176 | tf_op jit(solution)/shard_map/all_to_all | solution.py:233
  46.0 1.6 couple_early.7
  47.7 5.0 %all-to-all-start.2 = ((bf16[16,32,256]{2,1,0:T(8,128)(2,1)}), bf16[16,32,256]{2,1,0:T(8,128)(2,1)S(1)}, u32[]{:S(2)}, u32[]{:S(2)}) async-start(bf16[16,32,256]{2,1,0:T(8,128)(2,1)} %couple_early.7), calls=%async_computation.2 | async-start | bytes 524288 | tf_op jit(solution)/shard_map/all_to_all | solution.py:233
  52.7 2.2 copy-done.2
  54.9 2.8 factors.1
  57.7 1.3 copy-done.3
  59.0 1.4 copy-done.6
  60.4 1.4 copy-done.9
  61.7 1.4 copy-done.12
  63.1 1.6 copy-done.10
  64.7 1.8 apply.7
  66.5 9.1 %all-to-all-start.3 = ((bf16[16,32,256]{2,1,0:T(8,128)(2,1)}), bf16[16,32,256]{2,1,0:T(8,128)(2,1)S(1)}, u32[]{:S(2)}, u32[]{:S(2)}) async-start(bf16[16,32,256]{2,1,0:T(8,128)(2,1)} %get-tuple-element.25), calls=%async_computation.3 | async-start | bytes 524288 | tf_op jit(solution)/shard_map/all_to_all | solution.py:233
  75.6 10.0 %all-to-all-done.3.x_ref = bf16[16,32,256]{2,1,0:T(8,128)(2,1)S(1)} async-done(((bf16[16,32,256]{2,1,0:T(8,128)(2,1)}), bf16[16,32,256]{2,1,0:T(8,128)(2,1)S(1)}, u32[]{:S(2)}, u32[]{:S(2)}) %all-to-all-start.3) | async-done | bytes 262176 | tf_op jit(solution)/shard_map/all_to_all | solution.py:233
  86.6 13.9 %all_to_all.75.r_ref = bf16[16,32,256]{2,1,0:T(8,128)(2,1)S(1)} all-to-all(bf16[16,32,256]{2,1,0:T(8,128)(2,1)S(1)} %couple_early.8), channel_id=1, replica_groups=mesh['zl'=2,'core'=2,'zh'=4,'y'=4,'x'=4] {'zh','y'}, dimensions={0} | all-to-all | bytes 524288 | tf_op jit(solution)/shard_map/all_to_all | solution.py:233
  100.5 1.7 apply.8
  102.2 13.7 %all_to_all.76.x_ref = bf16[16,32,256]{2,1,0:T(8,128)(2,1)S(1)} all-to-all(bf16[16,32,256]{2,1,0:T(8,128)(2,1)S(1)} %get-tuple-element.27), channel_id=1, replica_groups=mesh['zl'=2,'core'=2,'zh'=4,'y'=4,'x'=4] {'zh','y'}, dimensions={0} | all-to-all | bytes 524288 | tf_op jit(solution)/shard_map/all_to_all | solution.py:233
  116.8 13.6 %all_to_all.77.r_ref = bf16[16,32,256]{2,1,0:T(8,128)(2,1)S(1)} all-to-all(bf16[16,32,256]{2,1,0:T(8,128)(2,1)S(1)} %couple_early.9), channel_id=1, replica_groups=mesh['zl'=2,'core'=2,'zh'=4,'y'=4,'x'=4] {'zh','y'}, dimensions={0} | all-to-all | bytes 524288 | tf_op jit(solution)/shard_map/all_to_all | solution.py:233
  131.5 2.1 collective-permute-start.4
  134.5 13.8 %all_to_all.78.x_ref = bf16[16,32,256]{2,1,0:T(8,128)(2,1)S(1)} all-to-all(bf16[16,32,256]{2,1,0:T(8,128)(2,1)S(1)} %broadcast_in_dim.15), channel_id=1, replica_groups=mesh['zl'=2,'core'=2,'zh'=4,'y'=4,'x'=4] {'zh','y'}, dimensions={0} | all-to-all | bytes 524288 | tf_op jit(solution)/shard_map/all_to_all | solution.py:233
  149.2 14.1 %all_to_all.79.r_ref = bf16[16,32,256]{2,1,0:T(8,128)(2,1)S(1)} all-to-all(bf16[16,32,256]{2,1,0:T(8,128)(2,1)S(1)} %couple_early.10), channel_id=1, replica_groups=mesh['zl'=2,'core'=2,'zh'=4,'y'=4,'x'=4] {'zh','y'}, dimensions={0} | all-to-all | bytes 524288 | tf_op jit(solution)/shard_map/all_to_all | solution.py:233
  163.3 1.1 apply.10
  164.4 14.3 %all_to_all.80.x_ref = bf16[16,32,256]{2,1,0:T(8,128)(2,1)S(1)} all-to-all(bf16[16,32,256]{2,1,0:T(8,128)(2,1)S(1)} %get-tuple-element.31), channel_id=1, replica_groups=mesh['zl'=2,'core'=2,'zh'=4,'y'=4,'x'=4] {'zh','y'}, dimensions={0} | all-to-all | bytes 524288 | tf_op jit(solution)/shard_map/all_to_all | solution.py:233
  179.5 13.9 %all_to_all.81.r_ref = bf16[16,32,256]{2,1,0:T(8,128)(2,1)S(1)} all-to-all(bf16[16,32,256]{2,1,0:T(8,128)(2,1)S(1)} %couple_early.11), channel_id=1, replica_groups=mesh['zl'=2,'core'=2,'zh'=4,'y'=4,'x'=4] {'zh','y'}, dimensions={0} | all-to-all | bytes 524288 | tf_op jit(solution)/shard_map/all_to_all | solution.py:233
  194.5 15.7 %all_to_all.82.x_ref = bf16[16,32,256]{2,1,0:T(8,128)(2,1)S(1)} all-to-all(bf16[16,32,256]{2,1,0:T(8,128)(2,1)S(1)} %get-tuple-element.33), channel_id=1, replica_groups=mesh['zl'=2,'core'=2,'zh'=4,'y'=4,'x'=4] {'zh','y'}, dimensions={0} | all-to-all | bytes 524288 | tf_op jit(solution)/shard_map/all_to_all | solution.py:233
  210.2 1.6 couple_early.12
  211.8 4.0 %all-to-all-start.12 = ((bf16[16,32,256]{2,1,0:T(8,128)(2,1)}), bf16[16,32,256]{2,1,0:T(8,128)(2,1)S(1)}, u32[]{:S(2)}, u32[]{:S(2)}) async-start(bf16[16,32,256]{2,1,0:T(8,128)(2,1)} %couple_early.12), calls=%async_computation.12 | async-start | bytes 524288 | tf_op jit(solution)/shard_map/all_to_all | solution.py:233
  215.8 19.4 %collective-permute-start.6 = (bf16[2,512,256]{2,1,0:T(8,128)(2,1)S(1)}, bf16[2,512,256]{2,1,0:T(8,128)(2,1)}, u32[]{:S(2)}, u32[]{:S(2)}) collective-permute-start(bf16[2,512,256]{2,1,0:T(8,128)(2,1)S(1)} %copy-done.16), channel_id=1, source_target_pairs={{0,64},{64,0},{1,65},{65,1},{2,66},{66,2},{3,67},{67,3},{4,68},{68... | collective-permute-start | bytes 1572872 | tf_op jit(solution)/shard_map/ppermute | solution.py:205
  235.3 1.6 copy-done.8
  237.9 19.1 %all_to_all.83.x_ref = bf16[16,32,256]{2,1,0:T(8,128)(2,1)S(1)} all-to-all(bf16[16,32,256]{2,1,0:T(8,128)(2,1)S(1)} %get-tuple-element.35), channel_id=1, replica_groups=mesh['zl'=2,'core'=2,'zh'=4,'y'=4,'x'=4] {'zh','y'}, dimensions={0} | all-to-all | bytes 524288 | tf_op jit(solution)/shard_map/all_to_all | solution.py:233
  257.0 1.6 couple_early.13
  258.6 4.1 %all-to-all-start.14 = ((bf16[16,32,256]{2,1,0:T(8,128)(2,1)}), bf16[16,32,256]{2,1,0:T(8,128)(2,1)S(1)}, u32[]{:S(2)}, u32[]{:S(2)}) async-start(bf16[16,32,256]{2,1,0:T(8,128)(2,1)} %couple_early.13), calls=%async_computation.14 | async-start | bytes 524288 | tf_op jit(solution)/shard_map/all_to_all | solution.py:233
  262.8 1.3 broadcast_select_fusion.1
  265.6 7.0 %all-to-all-done.14.r_ref = bf16[16,32,256]{2,1,0:T(8,128)(2,1)S(1)} async-done(((bf16[16,32,256]{2,1,0:T(8,128)(2,1)}), bf16[16,32,256]{2,1,0:T(8,128)(2,1)S(1)}, u32[]{:S(2)}, u32[]{:S(2)}) %all-to-all-start.14) | async-done | bytes 262176 | tf_op jit(solution)/shard_map/all_to_all | solution.py:233
  274.3 1.9 collective-permute-start.8
  276.2 1.5 collective-permute-start.9
  277.7 2.2 collective-permute-done.7
  281.3 2.4 collective-permute-start.11
  283.8 1.8 collective-permute-start.12
  285.6 10.0 %collective-permute-start.5 = (bf16[2,32,256]{2,1,0:T(8,128)(2,1)S(1)}, bf16[2,32,256]{2,1,0:T(8,128)(2,1)S(1)}, u32[]{:S(2)}, u32[]{:S(2)}) collective-permute-start(bf16[2,32,256]{2,1,0:T(8,128)(2,1)S(1)} %broadcast_select_fusion.7), channel_id=1, source_target_pairs={{0,64},{64,0},{1,65},{65,1},{2,66},{66,2},{3,67},{67,3},{4,68},{68... | collective-permute-start | bytes 98312 | tf_op jit(solution)/shard_map/ppermute | solution.py:205
  296.5 3.2 %collective-permute-done.13 = f32[32,512]{1,0:T(8,128)S(1)} collective-permute-done((f32[32,512]{1,0:T(8,128)S(1)}, f32[32,512]{1,0:T(8,128)S(1)}, u32[]{:S(2)}, u32[]{:S(2)}) %collective-permute-start.13) | collective-permute-done | bytes 65568 | tf_op jit(solution)/shard_map/ppermute | solution.py:198
  300.0 5.6 %collective-permute-start.14 = (f32[32,512]{1,0:T(8,128)S(1)}, f32[32,512]{1,0:T(8,128)S(1)}, u32[]{:S(2)}, u32[]{:S(2)}) collective-permute-start(f32[32,512]{1,0:T(8,128)S(1)} %fusion.7), channel_id=1, source_target_pairs={{0,64},{64,0},{1,65},{65,1},{2,66},{66,2},{3,67},{67,3},{4,68},{68... | collective-permute-start | bytes 196616 | tf_op jit(solution)/shard_map/ppermute | solution.py:205
  307.1 8.5 %all-reduce = (f32[2,256]{1,0:T(2,128)S(1)}, f32[512]{0:T(512)S(1)}) all-reduce(f32[2,256]{1,0:T(2,128)S(1)} %multiply_reduce_fusion.1, f32[512]{0:T(512)S(1)} %get-tuple-element.46), channel_id=1, replica_groups=mesh['zl'=2,'core'=2,'zh'=4,'y'=4,'x'=4] {'x'}, use_global_device_ids=true, to_apply=%region_1.2 | all-reduce | flops 1024 | bytes 8192 | tf_op jit(solution)/shard_map/psum | solution.py:275
  (89 shorter events, 20.7 us)
Async XLA Ops:
  0.6 299.1 %copy-start = (bf16[512,512]{1,0:T(8,128)(2,1)S(1)}, bf16[512,512]{1,0:T(8,128)(2,1)}, u32[]{:S(2)}) copy-start(bf16[512,512]{1,0:T(8,128)(2,1)} %param.13) | copy-start | bytes 1572868
  1.7 4.2 %collective-permute-start.1 = (bf16[2,32,256]{2,1,0:T(8,128)(2,1)S(1)}, bf16[2,32,256]{2,1,0:T(8,128)(2,1)S(1)}, u32[]{:S(2)}, u32[]{:S(2)}) collective-permute-start(bf16[2,32,256]{2,1,0:T(8,128)(2,1)S(1)} %select_bitcast_fusion), channel_id=1, source_target_pairs={{0,64},{64,0},{1,65},{65,1},{2,66},{66,2},{3,67},{67,3},{4,68},{68... | collective-permute-start | bytes 98312 | tf_op jit(solution)/shard_map/ppermute | solution.py:205
  6.6 20.3 %collective-permute-start.2 = (bf16[2,256,4096]{2,1,0:T(8,128)(2,1)}, bf16[2,256,4096]{2,1,0:T(8,128)(2,1)}, u32[]{:S(2)}, u32[]{:S(2)}) collective-permute-start(bf16[2,256,4096]{2,1,0:T(8,128)(2,1)} %refs_0_.1), channel_id=1, source_target_pairs={{0,64},{64,0},{1,65},{65,1},{2,66},{66,2},{3,67},{67,3},{4,68},{68... | collective-permute-start | bytes 12582920 | tf_op jit(solution)/shard_map/ppermute | solution.py:205
  7.0 20.0 %all-to-all-start = ((bf16[16,32,256]{2,1,0:T(8,128)(2,1)}), bf16[16,32,256]{2,1,0:T(8,128)(2,1)S(1)}, u32[]{:S(2)}, u32[]{:S(2)}) async-start(bf16[16,32,256]{2,1,0:T(8,128)(2,1)} %broadcast_in_dim.14), calls=%async_computation | async-start | bytes 524288 | tf_op jit(solution)/shard_map/all_to_all | solution.py:233
  16.2 22.6 %collective-permute-start.3 = (bf16[2,2,4,128,128]{4,3,2,1,0:T(8,128)(2,1)}, bf16[2,2,4,128,128]{4,3,2,1,0:T(8,128)(2,1)S(1)}, u32[]{:S(2)}, u32[]{:S(2)}) collective-permute-start(bf16[2,2,4,128,128]{4,3,2,1,0:T(8,128)(2,1)} %own_ref.15), channel_id=1, source_target_pairs={{0,64},{64,0},{1,65},{65,1},{2,66},{66,2},{3,67},{67,3},{4,68},{68... | collective-permute-start | bytes 1572872 | tf_op jit(solution)/shard_map/ppermute | solution.py:205
  16.8 19.1 %copy-start.19 = (s32[2,2,4]{2,1,0:T(2,128)S(1)}, s32[2,2,4]{2,1,0:T(2,128)}, u32[]{:S(2)}) copy-start(s32[2,2,4]{2,1,0:T(2,128)} %param.11) | copy-start | bytes 196
  16.8 29.3 %copy-start.1 = (bf16[2,2,4,128,128]{4,3,2,1,0:T(8,128)(2,1)S(1)}, bf16[2,2,4,128,128]{4,3,2,1,0:T(8,128)(2,1)}, u32[]{:S(2)}) copy-start(bf16[2,2,4,128,128]{4,3,2,1,0:T(8,128)(2,1)} %own_ref.15) | copy-start | bytes 1572868
  30.8 15.2 %all-to-all-start.1 = ((bf16[16,32,256]{2,1,0:T(8,128)(2,1)}), bf16[16,32,256]{2,1,0:T(8,128)(2,1)S(1)}, u32[]{:S(2)}, u32[]{:S(2)}) async-start(bf16[16,32,256]{2,1,0:T(8,128)(2,1)} %get-tuple-element.21), calls=%async_computation.1 | async-start | bytes 524288 | tf_op jit(solution)/shard_map/all_to_all | solution.py:233
  35.9 2.8 collective-permute-start
  47.7 15.5 %all-to-all-start.2 = ((bf16[16,32,256]{2,1,0:T(8,128)(2,1)}), bf16[16,32,256]{2,1,0:T(8,128)(2,1)S(1)}, u32[]{:S(2)}, u32[]{:S(2)}) async-start(bf16[16,32,256]{2,1,0:T(8,128)(2,1)} %couple_early.7), calls=%async_computation.2 | async-start | bytes 524288 | tf_op jit(solution)/shard_map/all_to_all | solution.py:233
  52.7 2.2 copy-start.2
  57.7 1.3 copy-start.3
  59.0 1.4 copy-start.6
  60.4 1.4 copy-start.9
  61.7 1.4 copy-start.12
  63.1 1.6 copy-start.10
  66.5 19.1 %all-to-all-start.3 = ((bf16[16,32,256]{2,1,0:T(8,128)(2,1)}), bf16[16,32,256]{2,1,0:T(8,128)(2,1)S(1)}, u32[]{:S(2)}, u32[]{:S(2)}) async-start(bf16[16,32,256]{2,1,0:T(8,128)(2,1)} %get-tuple-element.25), calls=%async_computation.3 | async-start | bytes 524288 | tf_op jit(solution)/shard_map/all_to_all | solution.py:233
  85.7 14.8 %copy-start.7 = (bf16[256,4096]{1,0:T(8,128)(2,1)S(1)}, bf16[256,4096]{1,0:T(8,128)(2,1)}, u32[]{:S(2)}) copy-start(bf16[256,4096]{1,0:T(8,128)(2,1)} %copy-done.6) | copy-start | bytes 6291460
  100.5 30.0 %copy-start.4 = (bf16[256,4096]{1,0:T(8,128)(2,1)S(1)}, bf16[256,4096]{1,0:T(8,128)(2,1)}, u32[]{:S(2)}) copy-start(bf16[256,4096]{1,0:T(8,128)(2,1)} %copy-done.3) | copy-start | bytes 6291460
  130.4 32.9 %copy-start.13 = (bf16[256,4096]{1,0:T(8,128)(2,1)S(1)}, bf16[256,4096]{1,0:T(8,128)(2,1)}, u32[]{:S(2)}) copy-start(bf16[256,4096]{1,0:T(8,128)(2,1)} %copy-done.12) | copy-start | bytes 6291460
  131.5 3.0 collective-permute-start.4
  163.3 30.1 %copy-start.11 = (bf16[256,4096]{1,0:T(8,128)(2,1)S(1)}, bf16[256,4096]{1,0:T(8,128)(2,1)}, u32[]{:S(2)}) copy-start(bf16[256,4096]{1,0:T(8,128)(2,1)} %copy-done.9) | copy-start | bytes 6291460
  193.4 22.4 %copy-start.16 = (bf16[2,512,256]{2,1,0:T(8,128)(2,1)S(1)}, bf16[2,512,256]{2,1,0:T(8,128)(2,1)}, u32[]{:S(2)}) copy-start(bf16[2,512,256]{2,1,0:T(8,128)(2,1)} %param.12) | copy-start | bytes 1572868
  211.8 23.5 %all-to-all-start.12 = ((bf16[16,32,256]{2,1,0:T(8,128)(2,1)}), bf16[16,32,256]{2,1,0:T(8,128)(2,1)S(1)}, u32[]{:S(2)}, u32[]{:S(2)}) async-start(bf16[16,32,256]{2,1,0:T(8,128)(2,1)} %couple_early.12), calls=%async_computation.12 | async-start | bytes 524288 | tf_op jit(solution)/shard_map/all_to_all | solution.py:233
  215.8 46.9 %collective-permute-start.6 = (bf16[2,512,256]{2,1,0:T(8,128)(2,1)S(1)}, bf16[2,512,256]{2,1,0:T(8,128)(2,1)}, u32[]{:S(2)}, u32[]{:S(2)}) collective-permute-start(bf16[2,512,256]{2,1,0:T(8,128)(2,1)S(1)} %copy-done.16), channel_id=1, source_target_pairs={{0,64},{64,0},{1,65},{65,1},{2,66},{66,2},{3,67},{67,3},{4,68},{68... | collective-permute-start | bytes 1572872 | tf_op jit(solution)/shard_map/ppermute | solution.py:205
  235.3 1.6 copy-start.8
  258.6 14.1 %copy-start.5 = (bf16[256,4096]{1,0:T(8,128)(2,1)S(1)}, bf16[256,4096]{1,0:T(8,128)(2,1)}, u32[]{:S(2)}) copy-start(bf16[256,4096]{1,0:T(8,128)(2,1)} %copy-done.3) | copy-start | bytes 6291460
  258.6 14.1 %all-to-all-start.14 = ((bf16[16,32,256]{2,1,0:T(8,128)(2,1)}), bf16[16,32,256]{2,1,0:T(8,128)(2,1)S(1)}, u32[]{:S(2)}, u32[]{:S(2)}) async-start(bf16[16,32,256]{2,1,0:T(8,128)(2,1)} %couple_early.13), calls=%async_computation.14 | async-start | bytes 524288 | tf_op jit(solution)/shard_map/all_to_all | solution.py:233
  264.0 0.8 copy-start.14
  272.7 1.1 copy-start.15
  272.7 1.3 copy-start.17
  272.7 27.0 %copy-start.18 = (s32[64,512]{1,0:T(8,128)S(1)}, s32[64,512]{1,0:T(8,128)}, u32[]{:S(2)}) copy-start(s32[64,512]{1,0:T(8,128)} %param.8) | copy-start | bytes 393220
  274.2 5.7 %collective-permute-start.7 = (f32[32,512]{1,0:T(8,128)S(1)}, f32[32,512]{1,0:T(8,128)S(1)}, u32[]{:S(2)}, u32[]{:S(2)}) collective-permute-start(f32[32,512]{1,0:T(8,128)S(1)} %fusion.1), channel_id=1, source_target_pairs={{0,4},{4,8},{8,12},{12,0},{1,5},{5,9},{9,13},{13,1},{2,6},{6,10},{... | collective-permute-start | bytes 196616 | tf_op jit(solution)/shard_map/ppermute | solution.py:198
  274.3 5.6 %collective-permute-start.8 = (f32[32,512]{1,0:T(8,128)S(1)}, f32[32,512]{1,0:T(8,128)S(1)}, u32[]{:S(2)}, u32[]{:S(2)}) collective-permute-start(f32[32,512]{1,0:T(8,128)S(1)} %fusion.1), channel_id=1, source_target_pairs={{0,8},{4,12},{8,0},{12,4},{1,9},{5,13},{9,1},{13,5},{2,10},{6,14},... | collective-permute-start | bytes 196616 | tf_op jit(solution)/shard_map/ppermute | solution.py:198
  276.2 4.1 %collective-permute-start.9 = (f32[32,512]{1,0:T(8,128)S(1)}, f32[32,512]{1,0:T(8,128)S(1)}, u32[]{:S(2)}, u32[]{:S(2)}) collective-permute-start(f32[32,512]{1,0:T(8,128)S(1)} %fusion.1), channel_id=1, source_target_pairs={{0,12},{4,0},{8,4},{12,8},{1,13},{5,1},{9,5},{13,9},{2,14},{6,2},{... | collective-permute-start | bytes 196616 | tf_op jit(solution)/shard_map/ppermute | solution.py:198
  280.4 15.3 %collective-permute-start.10 = (f32[32,512]{1,0:T(8,128)S(1)}, f32[32,512]{1,0:T(8,128)S(1)}, u32[]{:S(2)}, u32[]{:S(2)}) collective-permute-start(f32[32,512]{1,0:T(8,128)S(1)} %add_add_fusion.1), channel_id=1, source_target_pairs={{0,16},{16,32},{32,48},{48,0},{1,17},{17,33},{33,49},{49,1},{2,18}... | collective-permute-start | bytes 196616 | tf_op jit(solution)/shard_map/ppermute | solution.py:198
  281.3 14.3 %collective-permute-start.11 = (f32[32,512]{1,0:T(8,128)S(1)}, f32[32,512]{1,0:T(8,128)S(1)}, u32[]{:S(2)}, u32[]{:S(2)}) collective-permute-start(f32[32,512]{1,0:T(8,128)S(1)} %add_add_fusion.1), channel_id=1, source_target_pairs={{0,32},{16,48},{32,0},{48,16},{1,33},{17,49},{33,1},{49,17},{2,34}... | collective-permute-start | bytes 196616 | tf_op jit(solution)/shard_map/ppermute | solution.py:198
  283.8 11.9 %collective-permute-start.12 = (f32[32,512]{1,0:T(8,128)S(1)}, f32[32,512]{1,0:T(8,128)S(1)}, u32[]{:S(2)}, u32[]{:S(2)}) collective-permute-start(f32[32,512]{1,0:T(8,128)S(1)} %add_add_fusion.1), channel_id=1, source_target_pairs={{0,48},{16,0},{32,16},{48,32},{1,49},{17,1},{33,17},{49,33},{2,50}... | collective-permute-start | bytes 196616 | tf_op jit(solution)/shard_map/ppermute | solution.py:198
  285.6 10.9 %collective-permute-start.5 = (bf16[2,32,256]{2,1,0:T(8,128)(2,1)S(1)}, bf16[2,32,256]{2,1,0:T(8,128)(2,1)S(1)}, u32[]{:S(2)}, u32[]{:S(2)}) collective-permute-start(bf16[2,32,256]{2,1,0:T(8,128)(2,1)S(1)} %broadcast_select_fusion.7), channel_id=1, source_target_pairs={{0,64},{64,0},{1,65},{65,1},{2,66},{66,2},{3,67},{67,3},{4,68},{68... | collective-permute-start | bytes 98312 | tf_op jit(solution)/shard_map/ppermute | solution.py:205
  295.7 4.0 %collective-permute-start.13 = (f32[32,512]{1,0:T(8,128)S(1)}, f32[32,512]{1,0:T(8,128)S(1)}, u32[]{:S(2)}, u32[]{:S(2)}) collective-permute-start(f32[32,512]{1,0:T(8,128)S(1)} %add_add_fusion), channel_id=1, source_target_pairs={{0,128},{128,0},{1,129},{129,1},{2,130},{130,2},{3,131},{131,3},{4... | collective-permute-start | bytes 196616 | tf_op jit(solution)/shard_map/ppermute | solution.py:198
  300.0 6.5 %collective-permute-start.14 = (f32[32,512]{1,0:T(8,128)S(1)}, f32[32,512]{1,0:T(8,128)S(1)}, u32[]{:S(2)}, u32[]{:S(2)}) collective-permute-start(f32[32,512]{1,0:T(8,128)S(1)} %fusion.7), channel_id=1, source_target_pairs={{0,64},{64,0},{1,65},{65,1},{2,66},{66,2},{3,67},{67,3},{4,68},{68... | collective-permute-start | bytes 196616 | tf_op jit(solution)/shard_map/ppermute | solution.py:205

commit v6 on v5

--- a/solution.py
+++ b/solution.py
@@ -237,10 +237,13 @@
         factor_slices, place, [inverse_factors], [other_factors], steps, inverse_factors.shape[1:], "factors", outs[0]
     )
     results = [outs[0]]
+    other_rows, *outs = lax.optimization_barrier((swap(border_rows), *outs))
     for turn in range(turns):
         for step in range(1 if turn == 0 else 0, steps):
             if step > 0:
                 pieces = everywhere(outs[1])
+            if turn == 0 and step == 1:
+                pieces, *factors = lax.optimization_barrier((pieces, *factors))
             resid = couple_early(
                 place, own_cols, pieces, own_source[step], couplings, other_couplings, step
             )
@@ -251,7 +254,7 @@
             pieces = everywhere(jnp.broadcast_to(moved[None], (peers, probes, local)))
             results = []
 
-    rows4 = in_order(border_rows, swap(border_rows))
+    rows4 = in_order(border_rows, other_rows)
     partial = jnp.zeros((probes, border_rows.shape[1]), jnp.float32)
     for step in range(steps):
         partial = partial + lax.dot_general(results[step], rows4[step], NT, preferred_element_type=jnp.float32)
@@ -272,8 +275,10 @@
     total_probes = local_probes * lax.axis_size("x")
     node_sums = jnp.sum(jnp.square(solved.astype(jnp.float32)), axis=0)
     border_sums = jnp.sum(jnp.square(border_solved), axis=0)
-    node_sums, border_sums = lax.psum((node_sums, border_sums), "x")
-    return solved, border_solved, node_sums / total_probes, border_sums / total_probes
+    sums = jnp.concatenate([node_sums.reshape(-1, 128), border_sums.reshape(-1, 128)], axis=0)
+    sums = functools.reduce(jnp.add, line(sums, "x")) / total_probes
+    split = node_sums.size // 128
+    return solved, border_solved, sums[:split].reshape(node_sums.shape), sums[split:].reshape(-1)
 
 
 def solution(mesh):

time: 318 us -> 315 us (level)
  starting transfers between devices: 88.9 us -> 75.7 us
  waiting for transfers between devices: 43.4 us -> 52.8 us
  blocking collectives: 140 us -> 145 us
    all_to_all x9 -> x10, blocking collectives: 132 us -> 145 us  [everywhere(): return lax.all_to_all(value, NODES, 0, 0)]
    psum x1 -> x0, blocking collectives: 8.47 us -> none  [shards(): node_sums, border_sums = lax.psum((node_sums, border_sums), 'x')]
    ppermute x7, starting transfers between devices: 41.1 us -> 32.8 us  [swap(): return lax.ppermute(value, 'core', [(0, 1), (1, 0)])]
    all_to_all x6 -> x5, starting transfers between devices: 36.5 us -> 28.3 us  [everywhere(): return lax.all_to_all(value, NODES, 0, 0)]
    all_to_all x6 -> x5, waiting for transfers between devices: 34.5 us -> 42.2 us  [everywhere(): return lax.all_to_all(value, NODES, 0, 0)]
    ppermute x7 -> x10, starting transfers between devices: 9.21 us -> 13.4 us  [line(): lax.ppermute(value, axis, [(i, (i + k) % size) for i in range(size)])]
    unnamed x41 -> x35, local copies, waits for them, and re-layouts: 12.2 us -> 9.96 us
    ppermute x7 -> x10, waiting for transfers between devices: 5.85 us -> 7.28 us  [line(): lax.ppermute(value, axis, [(i, (i + k) % size) for i in range(size)])]
  transfers between devices with their start and end apart: 21 -> 23, of which waited for: 12 -> 13; matrix products, arithmetic and copies ran while one was open for 1% -> 1% of each run, Pallas kernels for 3% -> 2%
where the time goes in v6:
time: 315 us; the launch traced here: 314 us
  blocking collectives  145 us (46%)
  starting transfers between devices  75.7 us (24%)
  waiting for transfers between devices  52.8 us (17%)
  Pallas kernels  23.2 us (7%)
  local copies, waits for them, and re-layouts  12 us (4%)
    all_to_all x10, blocking collectives, everywhere(): return lax.all_to_all(value, NODES, 0, 0)  145 us
    all_to_all x5, waiting for transfers between devices, everywhere(): return lax.all_to_all(value, NODES, 0, 0)  42.2 us
    ppermute x7, starting transfers between devices, swap(): return lax.ppermute(value, 'core', [(0, 1), (1, 0)])  32.8 us
    all_to_all x5, starting transfers between devices, everywhere(): return lax.all_to_all(value, NODES, 0, 0)  28.3 us
    ppermute x10, starting transfers between devices, line(): lax.ppermute(value, axis, [(i, (i + k) % size) for i in range(size)])  13.4 us
    unnamed x35, local copies, waits for them, and re-layouts  9.96 us
    pallas_call x7, Pallas kernels, apply_factor(): pl.pallas_call(apply_kernel, out_shape=shapes, in_specs=[VMEM, VMEM], out...  9.65 us
    ppermute x10, waiting for transfers between devices, line(): lax.ppermute(value, axis, [(i, (i + k) % size) for i in range(size)])  7.28 us
  transfers between devices with their start and end apart: 23, of which 13 were waited for; matrix products, arithmetic and copies ran while one was open for 1% of the time, Pallas kernels for 2%

profile of v6, /device:TPU:1, one launch (start us, length us, event | category | flops | bytes accessed | tf_op | source)
XLA Modules:
  0.0 313.7 jit_solution(10561261539179901152)
XLA Ops:
  1.7 3.3 %collective-permute-start.2 = (bf16[2,32,256]{2,1,0:T(8,128)(2,1)S(1)}, bf16[2,32,256]{2,1,0:T(8,128)(2,1)S(1)}, u32[]{:S(2)}, u32[]{:S(2)}) collective-permute-start(bf16[2,32,256]{2,1,0:T(8,128)(2,1)S(1)} %select_bitcast_fusion), channel_id=1, source_target_pairs={{0,64},{64,0},{1,65},{65,1},{2,66},{66,2},{3,67},{67,3},{4,68},{68... | collective-permute-start | bytes 98312 | tf_op jit(solution)/shard_map/ppermute | solution.py:205
  7.1 9.2 %all-to-all-start = ((bf16[16,32,256]{2,1,0:T(8,128)(2,1)}), bf16[16,32,256]{2,1,0:T(8,128)(2,1)S(1)}, u32[]{:S(2)}, u32[]{:S(2)}) async-start(bf16[16,32,256]{2,1,0:T(8,128)(2,1)} %broadcast_in_dim.14), calls=%async_computation | async-start | bytes 524288 | tf_op jit(solution)/shard_map/all_to_all | solution.py:233
  17.1 9.9 %all-to-all-done.r_ref = bf16[16,32,256]{2,1,0:T(8,128)(2,1)S(1)} async-done(((bf16[16,32,256]{2,1,0:T(8,128)(2,1)}), bf16[16,32,256]{2,1,0:T(8,128)(2,1)S(1)}, u32[]{:S(2)}, u32[]{:S(2)}) %all-to-all-start) | async-done | bytes 262176 | tf_op jit(solution)/shard_map/all_to_all | solution.py:233
  27.1 3.8 %apply_early.1 = (bf16[32,256]{1,0:T(8,128)(2,1)S(1)}, bf16[16,32,256]{2,1,0:T(8,128)(2,1)}) custom-call(s32[3]{0:T(128)S(1)} %pad_add_fusion.1.place, bf16[16,32,256]{2,1,0:T(8,128)(2,1)S(1)} %all-to-all-done.r_ref, bf16[2,256,4096]{2,1,0:T(8,128)(2,1)} %refs_0_.1, bf16[2,256,4096]{2,1,0:T(8,128)(2,1)} %collective-permute-done.3.other_ref.refs_1_), custom_call_target="tpu_custom_call" | custom-call | tf_op jit(solution)/shard_map/apply_early/pallas_call | solution.py:169
  30.9 5.1 %all-to-all-start.1 = ((bf16[16,32,256]{2,1,0:T(8,128)(2,1)}), bf16[16,32,256]{2,1,0:T(8,128)(2,1)S(1)}, u32[]{:S(2)}, u32[]{:S(2)}) async-start(bf16[16,32,256]{2,1,0:T(8,128)(2,1)} %get-tuple-element.30), calls=%async_computation.1 | async-start | bytes 524288 | tf_op jit(solution)/shard_map/all_to_all | solution.py:233
  36.1 1.9 collective-permute-start
  38.9 2.2 copy-done.2
  41.1 2.8 factors.1
  43.9 1.3 copy-done.3
  45.3 1.4 copy-done.6
  46.6 1.4 copy-done.8
  48.0 1.4 copy-done.11
  50.3 19.3 %all_to_all.75.r_ref = bf16[16,32,256]{2,1,0:T(8,128)(2,1)S(1)} all-to-all(bf16[16,32,256]{2,1,0:T(8,128)(2,1)S(1)} %couple_early.7), channel_id=1, replica_groups=mesh['zl'=2,'core'=2,'zh'=4,'y'=4,'x'=4] {'zh','y'}, dimensions={0} | all-to-all | bytes 524288 | tf_op jit(solution)/shard_map/all_to_all | solution.py:233
  69.6 1.8 apply.7
  71.4 6.7 %all-to-all-start.3 = ((bf16[16,32,256]{2,1,0:T(8,128)(2,1)}), bf16[16,32,256]{2,1,0:T(8,128)(2,1)S(1)}, u32[]{:S(2)}, u32[]{:S(2)}) async-start(bf16[16,32,256]{2,1,0:T(8,128)(2,1)} %get-tuple-element.38), calls=%async_computation.3 | async-start | bytes 524288 | tf_op jit(solution)/shard_map/all_to_all | solution.py:233
  78.2 11.2 %all-to-all-done.3.x_ref = bf16[16,32,256]{2,1,0:T(8,128)(2,1)S(1)} async-done(((bf16[16,32,256]{2,1,0:T(8,128)(2,1)}), bf16[16,32,256]{2,1,0:T(8,128)(2,1)S(1)}, u32[]{:S(2)}, u32[]{:S(2)}) %all-to-all-start.3) | async-done | bytes 262176 | tf_op jit(solution)/shard_map/all_to_all | solution.py:233
  90.2 13.7 %all_to_all.76.r_ref = bf16[16,32,256]{2,1,0:T(8,128)(2,1)S(1)} all-to-all(bf16[16,32,256]{2,1,0:T(8,128)(2,1)S(1)} %couple_early.8), channel_id=1, replica_groups=mesh['zl'=2,'core'=2,'zh'=4,'y'=4,'x'=4] {'zh','y'}, dimensions={0} | all-to-all | bytes 524288 | tf_op jit(solution)/shard_map/all_to_all | solution.py:233
  103.9 1.7 apply.8
  105.6 14.8 %all_to_all.77.x_ref = bf16[16,32,256]{2,1,0:T(8,128)(2,1)S(1)} all-to-all(bf16[16,32,256]{2,1,0:T(8,128)(2,1)S(1)} %get-tuple-element.40), channel_id=1, replica_groups=mesh['zl'=2,'core'=2,'zh'=4,'y'=4,'x'=4] {'zh','y'}, dimensions={0} | all-to-all | bytes 524288 | tf_op jit(solution)/shard_map/all_to_all | solution.py:233
  121.3 14.3 %all_to_all.78.r_ref = bf16[16,32,256]{2,1,0:T(8,128)(2,1)S(1)} all-to-all(bf16[16,32,256]{2,1,0:T(8,128)(2,1)S(1)} %couple_early.9), channel_id=1, replica_groups=mesh['zl'=2,'core'=2,'zh'=4,'y'=4,'x'=4] {'zh','y'}, dimensions={0} | all-to-all | bytes 524288 | tf_op jit(solution)/shard_map/all_to_all | solution.py:233
  135.6 1.1 apply.9
  136.7 1.3 collective-permute-start.5
  138.8 12.9 %all_to_all.79.x_ref = bf16[16,32,256]{2,1,0:T(8,128)(2,1)S(1)} all-to-all(bf16[16,32,256]{2,1,0:T(8,128)(2,1)S(1)} %broadcast_in_dim.15), channel_id=1, replica_groups=mesh['zl'=2,'core'=2,'zh'=4,'y'=4,'x'=4] {'zh','y'}, dimensions={0} | all-to-all | bytes 524288 | tf_op jit(solution)/shard_map/all_to_all | solution.py:233
  152.7 13.5 %all_to_all.80.r_ref = bf16[16,32,256]{2,1,0:T(8,128)(2,1)S(1)} all-to-all(bf16[16,32,256]{2,1,0:T(8,128)(2,1)S(1)} %couple_early.10), channel_id=1, replica_groups=mesh['zl'=2,'core'=2,'zh'=4,'y'=4,'x'=4] {'zh','y'}, dimensions={0} | all-to-all | bytes 524288 | tf_op jit(solution)/shard_map/all_to_all | solution.py:233
  166.2 1.1 apply.10
  167.3 13.5 %all_to_all.81.x_ref = bf16[16,32,256]{2,1,0:T(8,128)(2,1)S(1)} all-to-all(bf16[16,32,256]{2,1,0:T(8,128)(2,1)S(1)} %get-tuple-element.44), channel_id=1, replica_groups=mesh['zl'=2,'core'=2,'zh'=4,'y'=4,'x'=4] {'zh','y'}, dimensions={0} | all-to-all | bytes 524288 | tf_op jit(solution)/shard_map/all_to_all | solution.py:233
  181.7 13.7 %all_to_all.82.r_ref = bf16[16,32,256]{2,1,0:T(8,128)(2,1)S(1)} all-to-all(bf16[16,32,256]{2,1,0:T(8,128)(2,1)S(1)} %couple_early.11), channel_id=1, replica_groups=mesh['zl'=2,'core'=2,'zh'=4,'y'=4,'x'=4] {'zh','y'}, dimensions={0} | all-to-all | bytes 524288 | tf_op jit(solution)/shard_map/all_to_all | solution.py:233
  195.4 1.1 apply.11
  196.5 13.7 %all_to_all.83.x_ref = bf16[16,32,256]{2,1,0:T(8,128)(2,1)S(1)} all-to-all(bf16[16,32,256]{2,1,0:T(8,128)(2,1)S(1)} %get-tuple-element.46), channel_id=1, replica_groups=mesh['zl'=2,'core'=2,'zh'=4,'y'=4,'x'=4] {'zh','y'}, dimensions={0} | all-to-all | bytes 524288 | tf_op jit(solution)/shard_map/all_to_all | solution.py:233
  211.1 15.5 %all_to_all.84.r_ref = bf16[16,32,256]{2,1,0:T(8,128)(2,1)S(1)} all-to-all(bf16[16,32,256]{2,1,0:T(8,128)(2,1)S(1)} %couple_early.12), channel_id=1, replica_groups=mesh['zl'=2,'core'=2,'zh'=4,'y'=4,'x'=4] {'zh','y'}, dimensions={0} | all-to-all | bytes 524288 | tf_op jit(solution)/shard_map/all_to_all | solution.py:233
  226.6 1.8 apply.12
  228.4 3.5 %all-to-all-start.13 = ((bf16[16,32,256]{2,1,0:T(8,128)(2,1)}), bf16[16,32,256]{2,1,0:T(8,128)(2,1)S(1)}, u32[]{:S(2)}, u32[]{:S(2)}) async-start(bf16[16,32,256]{2,1,0:T(8,128)(2,1)} %get-tuple-element.48), calls=%async_computation.13 | async-start | bytes 524288 | tf_op jit(solution)/shard_map/all_to_all | solution.py:233
  232.0 1.1 broadcast_select_fusion
  233.1 10.4 %all-to-all-done.13.x_ref = bf16[16,32,256]{2,1,0:T(8,128)(2,1)S(1)} async-done(((bf16[16,32,256]{2,1,0:T(8,128)(2,1)}), bf16[16,32,256]{2,1,0:T(8,128)(2,1)S(1)}, u32[]{:S(2)}, u32[]{:S(2)}) %all-to-all-start.13) | async-done | bytes 262176 | tf_op jit(solution)/shard_map/all_to_all | solution.py:233
  243.5 1.6 couple_early.13
  245.2 3.7 %all-to-all-start.14 = ((bf16[16,32,256]{2,1,0:T(8,128)(2,1)}), bf16[16,32,256]{2,1,0:T(8,128)(2,1)S(1)}, u32[]{:S(2)}, u32[]{:S(2)}) async-start(bf16[16,32,256]{2,1,0:T(8,128)(2,1)} %couple_early.13), calls=%async_computation.14 | async-start | bytes 524288 | tf_op jit(solution)/shard_map/all_to_all | solution.py:233
  249.4 10.6 %all-to-all-done.14.r_ref = bf16[16,32,256]{2,1,0:T(8,128)(2,1)S(1)} async-done(((bf16[16,32,256]{2,1,0:T(8,128)(2,1)}), bf16[16,32,256]{2,1,0:T(8,128)(2,1)S(1)}, u32[]{:S(2)}, u32[]{:S(2)}) %all-to-all-start.14) | async-done | bytes 262176 | tf_op jit(solution)/shard_map/all_to_all | solution.py:233
  260.1 1.6 copy-done.5
  261.6 1.1 apply.13
  264.1 1.6 collective-permute-start.9
  265.7 2.2 collective-permute-done.7
  268.6 2.0 collective-permute-start.10
  271.2 2.9 collective-permute-start.12
  274.9 3.1 collective-permute-done.11
  278.1 22.2 %collective-permute-start.6 = (bf16[2,32,256]{2,1,0:T(8,128)(2,1)S(1)}, bf16[2,32,256]{2,1,0:T(8,128)(2,1)S(1)}, u32[]{:S(2)}, u32[]{:S(2)}) collective-permute-start(bf16[2,32,256]{2,1,0:T(8,128)(2,1)S(1)} %broadcast_select_fusion.7), channel_id=1, source_target_pairs={{0,64},{64,0},{1,65},{65,1},{2,66},{66,2},{3,67},{67,3},{4,68},{68... | collective-permute-start | bytes 98312 | tf_op jit(solution)/shard_map/ppermute | solution.py:205
  300.6 4.2 %collective-permute-start.14 = (f32[32,512]{1,0:T(8,128)S(1)}, f32[32,512]{1,0:T(8,128)S(1)}, u32[]{:S(2)}, u32[]{:S(2)}) collective-permute-start(f32[32,512]{1,0:T(8,128)S(1)} %fusion.3), channel_id=1, source_target_pairs={{0,64},{64,0},{1,65},{65,1},{2,66},{66,2},{3,67},{67,3},{4,68},{68... | collective-permute-start | bytes 196616 | tf_op jit(solution)/shard_map/ppermute | solution.py:205
  306.7 3.4 %collective-permute-start.16 = (f32[8,128]{1,0:T(8,128)S(1)}, f32[8,128]{1,0:T(8,128)S(1)}, u32[]{:S(2)}, u32[]{:S(2)}) collective-permute-start(f32[8,128]{1,0:T(8,128)S(1)} %pad_maximum_fusion.3), channel_id=1, source_target_pairs={{0,2},{1,3},{2,0},{3,1},{4,6},{5,7},{6,4},{7,5},{8,10},{9,11},{10,... | collective-permute-start | bytes 12296 | tf_op jit(solution)/shard_map/ppermute | solution.py:198
  310.1 1.1 collective-permute-start.17
  (90 shorter events, 19.8 us)
Async XLA Ops:
  0.6 299.7 %copy-start = (bf16[512,512]{1,0:T(8,128)(2,1)S(1)}, bf16[512,512]{1,0:T(8,128)(2,1)}, u32[]{:S(2)}) copy-start(bf16[512,512]{1,0:T(8,128)(2,1)} %param.13) | copy-start | bytes 1572868
  1.7 4.2 %collective-permute-start.2 = (bf16[2,32,256]{2,1,0:T(8,128)(2,1)S(1)}, bf16[2,32,256]{2,1,0:T(8,128)(2,1)S(1)}, u32[]{:S(2)}, u32[]{:S(2)}) collective-permute-start(bf16[2,32,256]{2,1,0:T(8,128)(2,1)S(1)} %select_bitcast_fusion), channel_id=1, source_target_pairs={{0,64},{64,0},{1,65},{65,1},{2,66},{66,2},{3,67},{67,3},{4,68},{68... | collective-permute-start | bytes 98312 | tf_op jit(solution)/shard_map/ppermute | solution.py:205
  6.6 20.5 %collective-permute-start.3 = (bf16[2,256,4096]{2,1,0:T(8,128)(2,1)}, bf16[2,256,4096]{2,1,0:T(8,128)(2,1)}, u32[]{:S(2)}, u32[]{:S(2)}) collective-permute-start(bf16[2,256,4096]{2,1,0:T(8,128)(2,1)} %refs_0_.1), channel_id=1, source_target_pairs={{0,64},{64,0},{1,65},{65,1},{2,66},{66,2},{3,67},{67,3},{4,68},{68... | collective-permute-start | bytes 12582920 | tf_op jit(solution)/shard_map/ppermute | solution.py:205
  7.0 24.0 %collective-permute-start.1 = (bf16[2,512,256]{2,1,0:T(8,128)(2,1)}, bf16[2,512,256]{2,1,0:T(8,128)(2,1)S(1)}, u32[]{:S(2)}, u32[]{:S(2)}) collective-permute-start(bf16[2,512,256]{2,1,0:T(8,128)(2,1)} %param.12), channel_id=1, source_target_pairs={{0,64},{64,0},{1,65},{65,1},{2,66},{66,2},{3,67},{67,3},{4,68},{68... | collective-permute-start | bytes 1572872 | tf_op jit(solution)/shard_map/ppermute | solution.py:205
  7.1 19.9 %all-to-all-start = ((bf16[16,32,256]{2,1,0:T(8,128)(2,1)}), bf16[16,32,256]{2,1,0:T(8,128)(2,1)S(1)}, u32[]{:S(2)}, u32[]{:S(2)}) async-start(bf16[16,32,256]{2,1,0:T(8,128)(2,1)} %broadcast_in_dim.14), calls=%async_computation | async-start | bytes 524288 | tf_op jit(solution)/shard_map/all_to_all | solution.py:233
  16.3 33.1 %collective-permute-start.4 = (bf16[2,2,4,128,128]{4,3,2,1,0:T(8,128)(2,1)}, bf16[2,2,4,128,128]{4,3,2,1,0:T(8,128)(2,1)S(1)}, u32[]{:S(2)}, u32[]{:S(2)}) collective-permute-start(bf16[2,2,4,128,128]{4,3,2,1,0:T(8,128)(2,1)} %own_ref.15), channel_id=1, source_target_pairs={{0,64},{64,0},{1,65},{65,1},{2,66},{66,2},{3,67},{67,3},{4,68},{68... | collective-permute-start | bytes 1572872 | tf_op jit(solution)/shard_map/ppermute | solution.py:205
  17.1 18.9 %copy-start.16 = (s32[2,2,4]{2,1,0:T(2,128)S(1)}, s32[2,2,4]{2,1,0:T(2,128)}, u32[]{:S(2)}) copy-start(s32[2,2,4]{2,1,0:T(2,128)} %param.11) | copy-start | bytes 196
  30.9 40.5 %copy-start.14 = (bf16[2,512,256]{2,1,0:T(8,128)(2,1)}, bf16[2,512,256]{2,1,0:T(8,128)(2,1)S(1)}, u32[]{:S(2)}) copy-start(bf16[2,512,256]{2,1,0:T(8,128)(2,1)S(1)} %collective-permute-done.1) | copy-start | bytes 1572868
  30.9 18.4 %all-to-all-start.1 = ((bf16[16,32,256]{2,1,0:T(8,128)(2,1)}), bf16[16,32,256]{2,1,0:T(8,128)(2,1)S(1)}, u32[]{:S(2)}, u32[]{:S(2)}) async-start(bf16[16,32,256]{2,1,0:T(8,128)(2,1)} %get-tuple-element.30), calls=%async_computation.1 | async-start | bytes 524288 | tf_op jit(solution)/shard_map/all_to_all | solution.py:233
  36.1 2.8 collective-permute-start
  38.9 2.2 copy-start.2
  41.1 8.3 %copy-start.1 = (bf16[2,2,4,128,128]{4,3,2,1,0:T(8,128)(2,1)S(1)}, bf16[2,2,4,128,128]{4,3,2,1,0:T(8,128)(2,1)}, u32[]{:S(2)}) copy-start(bf16[2,2,4,128,128]{4,3,2,1,0:T(8,128)(2,1)} %own_ref.15) | copy-start | bytes 1572868
  43.9 1.3 copy-start.3
  45.3 1.4 copy-start.6
  46.6 1.4 copy-start.8
  48.0 1.4 copy-start.11
  49.4 20.2 %copy-start.9 = (bf16[256,4096]{1,0:T(8,128)(2,1)S(1)}, bf16[256,4096]{1,0:T(8,128)(2,1)}, u32[]{:S(2)}) copy-start(bf16[256,4096]{1,0:T(8,128)(2,1)} %copy-done.8) | copy-start | bytes 6291460
  71.4 17.9 %all-to-all-start.3 = ((bf16[16,32,256]{2,1,0:T(8,128)(2,1)}), bf16[16,32,256]{2,1,0:T(8,128)(2,1)S(1)}, u32[]{:S(2)}, u32[]{:S(2)}) async-start(bf16[16,32,256]{2,1,0:T(8,128)(2,1)} %get-tuple-element.38), calls=%async_computation.3 | async-start | bytes 524288 | tf_op jit(solution)/shard_map/all_to_all | solution.py:233
  89.3 14.6 %copy-start.7 = (bf16[256,4096]{1,0:T(8,128)(2,1)S(1)}, bf16[256,4096]{1,0:T(8,128)(2,1)}, u32[]{:S(2)}) copy-start(bf16[256,4096]{1,0:T(8,128)(2,1)} %copy-done.6) | copy-start | bytes 6291460
  103.9 31.7 %copy-start.4 = (bf16[256,4096]{1,0:T(8,128)(2,1)S(1)}, bf16[256,4096]{1,0:T(8,128)(2,1)}, u32[]{:S(2)}) copy-start(bf16[256,4096]{1,0:T(8,128)(2,1)} %copy-done.3) | copy-start | bytes 6291460
  135.6 30.6 %copy-start.12 = (bf16[256,4096]{1,0:T(8,128)(2,1)S(1)}, bf16[256,4096]{1,0:T(8,128)(2,1)}, u32[]{:S(2)}) copy-start(bf16[256,4096]{1,0:T(8,128)(2,1)} %copy-done.11) | copy-start | bytes 6291460
  136.7 2.1 collective-permute-start.5
  166.2 29.2 %copy-start.10 = (bf16[256,4096]{1,0:T(8,128)(2,1)S(1)}, bf16[256,4096]{1,0:T(8,128)(2,1)}, u32[]{:S(2)}) copy-start(bf16[256,4096]{1,0:T(8,128)(2,1)} %copy-done.8) | copy-start | bytes 6291460
  211.1 20.9 %copy-start.13 = (bf16[2,512,256]{2,1,0:T(8,128)(2,1)S(1)}, bf16[2,512,256]{2,1,0:T(8,128)(2,1)}, u32[]{:S(2)}) copy-start(bf16[2,512,256]{2,1,0:T(8,128)(2,1)} %param.12) | copy-start | bytes 1572868
  228.4 15.1 %all-to-all-start.13 = ((bf16[16,32,256]{2,1,0:T(8,128)(2,1)}), bf16[16,32,256]{2,1,0:T(8,128)(2,1)S(1)}, u32[]{:S(2)}, u32[]{:S(2)}) async-start(bf16[16,32,256]{2,1,0:T(8,128)(2,1)} %get-tuple-element.48), calls=%async_computation.13 | async-start | bytes 524288 | tf_op jit(solution)/shard_map/all_to_all | solution.py:233
  245.2 14.9 %all-to-all-start.14 = ((bf16[16,32,256]{2,1,0:T(8,128)(2,1)}), bf16[16,32,256]{2,1,0:T(8,128)(2,1)S(1)}, u32[]{:S(2)}, u32[]{:S(2)}) async-start(bf16[16,32,256]{2,1,0:T(8,128)(2,1)} %couple_early.13), calls=%async_computation.14 | async-start | bytes 524288 | tf_op jit(solution)/shard_map/all_to_all | solution.py:233
  249.0 51.3 %copy-start.15 = (s32[64,512]{1,0:T(8,128)S(1)}, s32[64,512]{1,0:T(8,128)}, u32[]{:S(2)}) copy-start(s32[64,512]{1,0:T(8,128)} %param.8) | copy-start | bytes 393220
  260.1 1.6 copy-start.5
  262.9 5.1 %collective-permute-start.7 = (f32[32,512]{1,0:T(8,128)S(1)}, f32[32,512]{1,0:T(8,128)S(1)}, u32[]{:S(2)}, u32[]{:S(2)}) collective-permute-start(f32[32,512]{1,0:T(8,128)S(1)} %convolution_add_fusion), channel_id=1, source_target_pairs={{0,4},{4,8},{8,12},{12,0},{1,5},{5,9},{9,13},{13,1},{2,6},{6,10},{... | collective-permute-start | bytes 196616 | tf_op jit(solution)/shard_map/ppermute | solution.py:198
  263.2 4.7 %collective-permute-start.8 = (f32[32,512]{1,0:T(8,128)S(1)}, f32[32,512]{1,0:T(8,128)S(1)}, u32[]{:S(2)}, u32[]{:S(2)}) collective-permute-start(f32[32,512]{1,0:T(8,128)S(1)} %convolution_add_fusion), channel_id=1, source_target_pairs={{0,8},{4,12},{8,0},{12,4},{1,9},{5,13},{9,1},{13,5},{2,10},{6,14},... | collective-permute-start | bytes 196616 | tf_op jit(solution)/shard_map/ppermute | solution.py:198
  264.1 4.4 %collective-permute-start.9 = (f32[32,512]{1,0:T(8,128)S(1)}, f32[32,512]{1,0:T(8,128)S(1)}, u32[]{:S(2)}, u32[]{:S(2)}) collective-permute-start(f32[32,512]{1,0:T(8,128)S(1)} %convolution_add_fusion), channel_id=1, source_target_pairs={{0,12},{4,0},{8,4},{12,8},{1,13},{5,1},{9,5},{13,9},{2,14},{6,2},{... | collective-permute-start | bytes 196616 | tf_op jit(solution)/shard_map/ppermute | solution.py:198
  268.6 6.3 %collective-permute-start.10 = (f32[32,512]{1,0:T(8,128)S(1)}, f32[32,512]{1,0:T(8,128)S(1)}, u32[]{:S(2)}, u32[]{:S(2)}) collective-permute-start(f32[32,512]{1,0:T(8,128)S(1)} %add_add_fusion.1), channel_id=1, source_target_pairs={{0,16},{16,32},{32,48},{48,0},{1,17},{17,33},{33,49},{49,1},{2,18}... | collective-permute-start | bytes 196616 | tf_op jit(solution)/shard_map/ppermute | solution.py:198
  270.6 7.4 %collective-permute-start.11 = (f32[32,512]{1,0:T(8,128)S(1)}, f32[32,512]{1,0:T(8,128)S(1)}, u32[]{:S(2)}, u32[]{:S(2)}) collective-permute-start(f32[32,512]{1,0:T(8,128)S(1)} %add_add_fusion.1), channel_id=1, source_target_pairs={{0,32},{16,48},{32,0},{48,16},{1,33},{17,49},{33,1},{49,17},{2,34}... | collective-permute-start | bytes 196616 | tf_op jit(solution)/shard_map/ppermute | solution.py:198
  271.2 6.7 %collective-permute-start.12 = (f32[32,512]{1,0:T(8,128)S(1)}, f32[32,512]{1,0:T(8,128)S(1)}, u32[]{:S(2)}, u32[]{:S(2)}) collective-permute-start(f32[32,512]{1,0:T(8,128)S(1)} %add_add_fusion.1), channel_id=1, source_target_pairs={{0,48},{16,0},{32,16},{48,32},{1,49},{17,1},{33,17},{49,33},{2,50}... | collective-permute-start | bytes 196616 | tf_op jit(solution)/shard_map/ppermute | solution.py:198
  278.0 22.3 %collective-permute-start.13 = (f32[32,512]{1,0:T(8,128)S(1)}, f32[32,512]{1,0:T(8,128)S(1)}, u32[]{:S(2)}, u32[]{:S(2)}) collective-permute-start(f32[32,512]{1,0:T(8,128)S(1)} %add_add_fusion), channel_id=1, source_target_pairs={{0,128},{128,0},{1,129},{129,1},{2,130},{130,2},{3,131},{131,3},{4... | collective-permute-start | bytes 196616 | tf_op jit(solution)/shard_map/ppermute | solution.py:198
  278.1 26.6 %collective-permute-start.6 = (bf16[2,32,256]{2,1,0:T(8,128)(2,1)S(1)}, bf16[2,32,256]{2,1,0:T(8,128)(2,1)S(1)}, u32[]{:S(2)}, u32[]{:S(2)}) collective-permute-start(bf16[2,32,256]{2,1,0:T(8,128)(2,1)S(1)} %broadcast_select_fusion.7), channel_id=1, source_target_pairs={{0,64},{64,0},{1,65},{65,1},{2,66},{66,2},{3,67},{67,3},{4,68},{68... | collective-permute-start | bytes 98312 | tf_op jit(solution)/shard_map/ppermute | solution.py:205
  300.6 5.1 %collective-permute-start.14 = (f32[32,512]{1,0:T(8,128)S(1)}, f32[32,512]{1,0:T(8,128)S(1)}, u32[]{:S(2)}, u32[]{:S(2)}) collective-permute-start(f32[32,512]{1,0:T(8,128)S(1)} %fusion.3), channel_id=1, source_target_pairs={{0,64},{64,0},{1,65},{65,1},{2,66},{66,2},{3,67},{67,3},{4,68},{68... | collective-permute-start | bytes 196616 | tf_op jit(solution)/shard_map/ppermute | solution.py:205
  306.3 5.6 %collective-permute-start.15 = (f32[8,128]{1,0:T(8,128)S(1)}, f32[8,128]{1,0:T(8,128)S(1)}, u32[]{:S(2)}, u32[]{:S(2)}) collective-permute-start(f32[8,128]{1,0:T(8,128)S(1)} %pad_maximum_fusion.3), channel_id=1, source_target_pairs={{0,1},{1,2},{2,3},{3,0},{4,5},{5,6},{6,7},{7,4},{8,9},{9,10},{10,1... | collective-permute-start | bytes 12296 | tf_op jit(solution)/shard_map/ppermute | solution.py:198
  306.7 5.2 %collective-permute-start.16 = (f32[8,128]{1,0:T(8,128)S(1)}, f32[8,128]{1,0:T(8,128)S(1)}, u32[]{:S(2)}, u32[]{:S(2)}) collective-permute-start(f32[8,128]{1,0:T(8,128)S(1)} %pad_maximum_fusion.3), channel_id=1, source_target_pairs={{0,2},{1,3},{2,0},{3,1},{4,6},{5,7},{6,4},{7,5},{8,10},{9,11},{10,... | collective-permute-start | bytes 12296 | tf_op jit(solution)/shard_map/ppermute | solution.py:198
  310.1 2.5 collective-permute-start.17

commit v7 on v6

--- a/solution.py
+++ b/solution.py
@@ -22,29 +22,6 @@
     def _():
         for copy in second:
             copy.start()
-
-
-def arrange_kernel(place, *refs, per_core, steps, pieces, slices):
-    own_refs, other_refs = refs[:pieces], refs[pieces : 2 * pieces]
-    outs, sems = refs[-1 - steps : -1], refs[-1]
-
-    def copies(refs, step):
-        return [
-            pltpu.make_async_copy(*slices(ref, k, outs[step], step % per_core), sems.at[step, k])
-            for k, ref in enumerate(refs)
-        ]
-
-    waits = []
-    for step in range(steps):
-        own, other = copies(own_refs, step), copies(other_refs, step)
-        start_one_of(place[0] == step // per_core, own, other)
-        waits += own
-    for copy in waits:
-        copy.wait()
-
-
-def factor_slices(ref, k, out, i):
-    return ref.at[i], out
 
 
 def finish(total, outs):
@@ -78,21 +55,22 @@
     finish(total, outs)
 
 
-def early_couple_kernel(place, cols, x_ref, s_ref, own_ref, other_ref, out_ref, c_buf, sem, *, step, per_core):
-    rows, slots, block, _ = c_buf.shape
-    own, other = (
-        [pltpu.make_async_copy(source.at[step % per_core], c_buf, sem)] for source in (own_ref, other_ref)
-    )
-    start_one_of(place[0] == step // per_core, own, other)
-    own[0].wait()
+def couple_kernel(cols, x_ref, s_ref, c_ref, out_ref, *, step):
+    rows, slots, block, _ = c_ref.shape
     per = x_ref.shape[2] // block
     for row in range(rows):
         total = None
-        for slot in range(slots):
-            col = cols[(step * rows + row) * slots + slot]
-            lanes = pl.ds(pl.multiple_of((col % per) * block, block), block)
+        for slot in range(0, slots, 2):
+            left = []
+            for pair in range(2):
+                col = cols[(step * rows + row) * slots + slot + pair]
+                lanes = pl.ds(pl.multiple_of((col % per) * block, block), block)
+                left.append(x_ref[col // per, :, lanes])
             term = lax.dot_general(
-                x_ref[col // per, :, lanes], c_buf[row, slot], NT, preferred_element_type=jnp.float32
+                jnp.concatenate(left, axis=1),
+                jnp.concatenate([c_ref[row, slot], c_ref[row, slot + 1]], axis=1),
+                NT,
+                preferred_element_type=jnp.float32,
             )
             total = term if total is None else total + term
         span = slice(row * block, (row + 1) * block)
@@ -122,24 +100,6 @@
 HBM = pl.BlockSpec(memory_space=pltpu.HBM)
 PARAMS = pltpu.CompilerParams(vmem_limit_bytes=16 << 20)
 LARGE = pltpu.CompilerParams(vmem_limit_bytes=50 << 20)
-
-
-def arrange(slices, place, own, other, steps, shape, name, after):
-    pieces = len(own)
-    return pl.pallas_call(
-        functools.partial(
-            arrange_kernel, per_core=steps // 2, steps=steps, pieces=pieces, slices=slices
-        ),
-        out_shape=tuple([jax.ShapeDtypeStruct(shape, jnp.bfloat16)] * steps),
-        in_specs=[SMEM] + [HBM] * (2 * pieces + 1),
-        out_specs=tuple([VMEM] * steps),
-        scratch_shapes=[pltpu.SemaphoreType.DMA((steps, pieces))],
-        compiler_params=PARAMS,
-        cost_estimate=pl.CostEstimate(
-            flops=0, transcendentals=0, bytes_accessed=4 * steps * shape[0] * shape[1]
-        ),
-        name=name,
-    )(place, *own, *other, after)
 
 
 def solved_shapes(probes, rows, peers):
@@ -180,16 +140,15 @@
     )(place, pieces, own, other)
 
 
-def couple_early(place, cols, pieces, source, own, other, step):
+def couple(cols, pieces, source, c, step):
     return pl.pallas_call(
-        functools.partial(early_couple_kernel, step=step, per_core=own.shape[0]),
+        functools.partial(couple_kernel, step=step),
         out_shape=jax.ShapeDtypeStruct(pieces.shape, jnp.bfloat16),
-        in_specs=[SMEM, SMEM, VMEM, VMEM, HBM, HBM],
+        in_specs=[SMEM, VMEM, VMEM, VMEM],
         out_specs=VMEM,
-        scratch_shapes=[pltpu.VMEM(own.shape[1:], own.dtype), pltpu.SemaphoreType.DMA],
-        compiler_params=LARGE,
-        name="couple_early",
-    )(place, cols, pieces, source, own, other)
+        compiler_params=PARAMS,
+        name="couple",
+    )(cols, pieces, source, c)
 
 
 def line(value, axis):
@@ -233,21 +192,23 @@
         return lax.all_to_all(value, NODES, 0, 0)
 
     outs = apply_early(place, everywhere(spread), inverse_factors, other_factors, 0)
-    factors = arrange(
-        factor_slices, place, [inverse_factors], [other_factors], steps, inverse_factors.shape[1:], "factors", outs[0]
-    )
+    other_rows, *outs = lax.optimization_barrier((swap(border_rows), *outs))
+    factor_pair, coupling_pair = (inverse_factors, other_factors), (couplings, other_couplings)
+
+    def slice_of(pair, step, after):
+        own, other, _ = lax.optimization_barrier((*pair, after))
+        mine = first if step < own_steps else jnp.logical_not(first)
+        return jnp.where(mine, own[step % own_steps], other[step % own_steps])
+
     results = [outs[0]]
-    other_rows, *outs = lax.optimization_barrier((swap(border_rows), *outs))
     for turn in range(turns):
         for step in range(1 if turn == 0 else 0, steps):
             if step > 0:
                 pieces = everywhere(outs[1])
-            if turn == 0 and step == 1:
-                pieces, *factors = lax.optimization_barrier((pieces, *factors))
-            resid = couple_early(
-                place, own_cols, pieces, own_source[step], couplings, other_couplings, step
-            )
-            outs = apply_factor(everywhere(resid), factors[step], step + 1 < steps)
+            block = slice_of(coupling_pair, step, outs[0])
+            resid = couple(own_cols, pieces, own_source[step], block, step)
+            factor = slice_of(factor_pair, step, resid)
+            outs = apply_factor(everywhere(resid), factor, step + 1 < steps)
             results.append(outs[0])
         if turn + 1 < turns:
             moved = lax.ppermute(outs[0], "zl", [(turn, turn + 1)])

time: 315 us -> 317 us (level)
  blocking collectives: 145 us -> 13.5 us
  waiting for transfers between devices: 52.8 us -> 133 us
  starting transfers between devices: 75.7 us -> 109 us
  other arithmetic: 3.01 us -> 24.1 us
  local copies, waits for them, and re-layouts: 12 us -> 5.57 us
    all_to_all x10 -> x1, blocking collectives: 145 us -> 13.5 us  [everywhere(): return lax.all_to_all(value, NODES, 0, 0)]
    all_to_all x5 -> x14, waiting for transfers between devices: 42.2 us -> 120 us  [everywhere(): return lax.all_to_all(value, NODES, 0, 0)]
    all_to_all x5 -> x14, starting transfers between devices: 28.3 us -> 62.5 us  [everywhere(): return lax.all_to_all(value, NODES, 0, 0)]
    select_n x0 -> x12, other arithmetic: none -> 20.2 us  [slice_of(): return jnp.where(mine, own[step % own_steps], other[step % own_steps])]
    unnamed x35 -> x23, local copies, waits for them, and re-layouts: 9.96 us -> 2.84 us
    pallas_call x8 -> x7, Pallas kernels: 9.71 us -> 10.4 us  [couple(): pl.pallas_call(functools.partial(couple_kernel, step=step), out_shape=jax...]
  transfers between devices with their start and end apart: 23 -> 32, of which waited for: 13 -> 23; matrix products, arithmetic and copies ran while one was open for 1% -> 8% of each run, Pallas kernels for 2% -> 1%
where the time goes in v7:
time: 317 us; the launch traced here: 315 us
  waiting for transfers between devices  133 us (42%)
  starting transfers between devices  109 us (34%)
  Pallas kernels  25.2 us (8%)
  other arithmetic  24.1 us (8%)
  blocking collectives  13.5 us (4%)
  local copies, waits for them, and re-layouts  5.57 us (2%)
    all_to_all x14, waiting for transfers between devices, everywhere(): return lax.all_to_all(value, NODES, 0, 0)  120 us
    all_to_all x14, starting transfers between devices, everywhere(): return lax.all_to_all(value, NODES, 0, 0)  62.5 us
    ppermute x7, starting transfers between devices, swap(): return lax.ppermute(value, 'core', [(0, 1), (1, 0)])  31.2 us
    select_n x12, other arithmetic, slice_of(): return jnp.where(mine, own[step % own_steps], other[step % own_steps])  20.2 us
    all_to_all x1, blocking collectives, everywhere(): return lax.all_to_all(value, NODES, 0, 0)  13.5 us
    ppermute x10, starting transfers between devices, line(): lax.ppermute(value, axis, [(i, (i + k) % size) for i in range(size)])  13.5 us
    pallas_call x7, Pallas kernels, apply_factor(): pl.pallas_call(apply_kernel, out_shape=shapes, in_specs=[VMEM, VMEM], out...  11 us
    pallas_call x7, Pallas kernels, couple(): pl.pallas_call(functools.partial(couple_kernel, step=step), out_shape=jax...  10.4 us
  transfers between devices with their start and end apart: 32, of which 23 were waited for; matrix products, arithmetic and copies ran while one was open for 8% of the time, Pallas kernels for 1%

profile of v7, /device:TPU:1, one launch (start us, length us, event | category | flops | bytes accessed | tf_op | source)
XLA Modules:
  0.0 314.6 jit_solution(6143922623922583413)
XLA Ops:
  1.7 3.3 %collective-permute-start.2 = (bf16[2,32,256]{2,1,0:T(8,128)(2,1)S(1)}, bf16[2,32,256]{2,1,0:T(8,128)(2,1)S(1)}, u32[]{:S(2)}, u32[]{:S(2)}) collective-permute-start(bf16[2,32,256]{2,1,0:T(8,128)(2,1)S(1)} %select_bitcast_fusion.14), channel_id=1, source_target_pairs={{0,64},{64,0},{1,65},{65,1},{2,66},{66,2},{3,67},{67,3},{4,68},{68... | collective-permute-start | bytes 98312 | tf_op jit(solution)/shard_map/ppermute | solution.py:164
  7.1 9.2 %all-to-all-start = ((bf16[16,32,256]{2,1,0:T(8,128)(2,1)}), bf16[16,32,256]{2,1,0:T(8,128)(2,1)S(1)}, u32[]{:S(2)}, u32[]{:S(2)}) async-start(bf16[16,32,256]{2,1,0:T(8,128)(2,1)} %broadcast_in_dim.14), calls=%async_computation | async-start | bytes 524288 | tf_op jit(solution)/shard_map/all_to_all | solution.py:192
  17.2 9.8 %all-to-all-done.r_ref = bf16[16,32,256]{2,1,0:T(8,128)(2,1)S(1)} async-done(((bf16[16,32,256]{2,1,0:T(8,128)(2,1)}), bf16[16,32,256]{2,1,0:T(8,128)(2,1)S(1)}, u32[]{:S(2)}, u32[]{:S(2)}) %all-to-all-start) | async-done | bytes 262176 | tf_op jit(solution)/shard_map/all_to_all | solution.py:192
  27.1 3.9 %apply_early.1 = (bf16[32,256]{1,0:T(8,128)(2,1)}, bf16[16,32,256]{2,1,0:T(8,128)(2,1)}) custom-call(s32[3]{0:T(128)S(1)} %pad_add_fusion.1.place, bf16[16,32,256]{2,1,0:T(8,128)(2,1)S(1)} %all-to-all-done.r_ref, bf16[2,256,4096]{2,1,0:T(8,128)(2,1)} %own_ref.1, bf16[2,256,4096]{2,1,0:T(8,128)(2,1)} %collective-permute-done.3.other_ref), custom_call_target="tpu_custom_call" | custom-call | tf_op jit(solution)/shard_map/apply_early/pallas_call | solution.py:129
  31.7 5.1 %all-to-all-start.1 = ((bf16[16,32,256]{2,1,0:T(8,128)(2,1)}), bf16[16,32,256]{2,1,0:T(8,128)(2,1)S(1)}, u32[]{:S(2)}, u32[]{:S(2)}) async-start(bf16[16,32,256]{2,1,0:T(8,128)(2,1)} %get-tuple-element.43), calls=%async_computation.1 | async-start | bytes 524288 | tf_op jit(solution)/shard_map/all_to_all | solution.py:192
  37.0 9.9 %all-to-all-done.1.x_ref = bf16[16,32,256]{2,1,0:T(8,128)(2,1)S(1)} async-done(((bf16[16,32,256]{2,1,0:T(8,128)(2,1)}), bf16[16,32,256]{2,1,0:T(8,128)(2,1)S(1)}, u32[]{:S(2)}, u32[]{:S(2)}) %all-to-all-start.1) | async-done | bytes 262176 | tf_op jit(solution)/shard_map/all_to_all | solution.py:192
  48.5 4.9 %all-to-all-start.2 = ((bf16[16,32,256]{2,1,0:T(8,128)(2,1)}), bf16[16,32,256]{2,1,0:T(8,128)(2,1)S(1)}, u32[]{:S(2)}, u32[]{:S(2)}) async-start(bf16[16,32,256]{2,1,0:T(8,128)(2,1)} %couple.7), calls=%async_computation.2 | async-start | bytes 524288 | tf_op jit(solution)/shard_map/all_to_all | solution.py:192
  53.4 2.4 select_bitcast_fusion.6.l_ref
  55.8 7.5 %all-to-all-done.2.r_ref = bf16[16,32,256]{2,1,0:T(8,128)(2,1)S(1)} async-done(((bf16[16,32,256]{2,1,0:T(8,128)(2,1)}), bf16[16,32,256]{2,1,0:T(8,128)(2,1)S(1)}, u32[]{:S(2)}, u32[]{:S(2)}) %all-to-all-start.2) | async-done | bytes 262176 | tf_op jit(solution)/shard_map/all_to_all | solution.py:192
  65.8 3.8 %all-to-all-start.3 = ((bf16[16,32,256]{2,1,0:T(8,128)(2,1)}), bf16[16,32,256]{2,1,0:T(8,128)(2,1)S(1)}, u32[]{:S(2)}, u32[]{:S(2)}) async-start(bf16[16,32,256]{2,1,0:T(8,128)(2,1)} %copy-done.1), calls=%async_computation.3 | async-start | bytes 524288 | tf_op jit(solution)/shard_map/all_to_all | solution.py:192
  69.6 10.0 %all-to-all-done.3.x_ref = bf16[16,32,256]{2,1,0:T(8,128)(2,1)S(1)} async-done(((bf16[16,32,256]{2,1,0:T(8,128)(2,1)}), bf16[16,32,256]{2,1,0:T(8,128)(2,1)S(1)}, u32[]{:S(2)}, u32[]{:S(2)}) %all-to-all-start.3) | async-done | bytes 262176 | tf_op jit(solution)/shard_map/all_to_all | solution.py:192
  81.1 4.2 %all-to-all-start.4 = ((bf16[16,32,256]{2,1,0:T(8,128)(2,1)}), bf16[16,32,256]{2,1,0:T(8,128)(2,1)S(1)}, u32[]{:S(2)}, u32[]{:S(2)}) async-start(bf16[16,32,256]{2,1,0:T(8,128)(2,1)} %couple.8), calls=%async_computation.4 | async-start | bytes 524288 | tf_op jit(solution)/shard_map/all_to_all | solution.py:192
  85.3 2.4 select_bitcast_fusion.5.l_ref
  87.7 7.5 %all-to-all-done.4.r_ref = bf16[16,32,256]{2,1,0:T(8,128)(2,1)S(1)} async-done(((bf16[16,32,256]{2,1,0:T(8,128)(2,1)}), bf16[16,32,256]{2,1,0:T(8,128)(2,1)S(1)}, u32[]{:S(2)}, u32[]{:S(2)}) %all-to-all-start.4) | async-done | bytes 262176 | tf_op jit(solution)/shard_map/all_to_all | solution.py:192
  96.9 13.5 %all_to_all.75.x_ref = bf16[16,32,256]{2,1,0:T(8,128)(2,1)S(1)} all-to-all(bf16[16,32,256]{2,1,0:T(8,128)(2,1)S(1)} %get-tuple-element.52), channel_id=1, replica_groups=mesh['zl'=2,'core'=2,'zh'=4,'y'=4,'x'=4] {'zh','y'}, dimensions={0} | all-to-all | bytes 524288 | tf_op jit(solution)/shard_map/all_to_all | solution.py:192
  112.0 3.9 %all-to-all-start.6 = ((bf16[16,32,256]{2,1,0:T(8,128)(2,1)}), bf16[16,32,256]{2,1,0:T(8,128)(2,1)S(1)}, u32[]{:S(2)}, u32[]{:S(2)}) async-start(bf16[16,32,256]{2,1,0:T(8,128)(2,1)} %couple.9), calls=%async_computation.6 | async-start | bytes 524288 | tf_op jit(solution)/shard_map/all_to_all | solution.py:192
  115.8 2.4 select_bitcast_fusion.4.l_ref
  118.3 7.5 %all-to-all-done.6.r_ref = bf16[16,32,256]{2,1,0:T(8,128)(2,1)S(1)} async-done(((bf16[16,32,256]{2,1,0:T(8,128)(2,1)}), bf16[16,32,256]{2,1,0:T(8,128)(2,1)S(1)}, u32[]{:S(2)}, u32[]{:S(2)}) %all-to-all-start.6) | async-done | bytes 262176 | tf_op jit(solution)/shard_map/all_to_all | solution.py:192
  126.9 2.2 collective-permute-start.5
  130.7 3.9 %all-to-all-start.7 = ((bf16[16,32,256]{2,1,0:T(8,128)(2,1)}), bf16[16,32,256]{2,1,0:T(8,128)(2,1)S(1)}, u32[]{:S(2)}, u32[]{:S(2)}) async-start(bf16[16,32,256]{2,1,0:T(8,128)(2,1)} %broadcast_in_dim.15), calls=%async_computation.7 | async-start | bytes 524288 | tf_op jit(solution)/shard_map/all_to_all | solution.py:192
  135.6 9.7 %all-to-all-done.7.x_ref = bf16[16,32,256]{2,1,0:T(8,128)(2,1)S(1)} async-done(((bf16[16,32,256]{2,1,0:T(8,128)(2,1)}), bf16[16,32,256]{2,1,0:T(8,128)(2,1)S(1)}, u32[]{:S(2)}, u32[]{:S(2)}) %all-to-all-start.7) | async-done | bytes 262176 | tf_op jit(solution)/shard_map/all_to_all | solution.py:192
  146.8 3.5 %all-to-all-start.8 = ((bf16[16,32,256]{2,1,0:T(8,128)(2,1)}), bf16[16,32,256]{2,1,0:T(8,128)(2,1)S(1)}, u32[]{:S(2)}, u32[]{:S(2)}) async-start(bf16[16,32,256]{2,1,0:T(8,128)(2,1)} %couple.10), calls=%async_computation.8 | async-start | bytes 524288 | tf_op jit(solution)/shard_map/all_to_all | solution.py:192
  150.3 2.4 select_bitcast_fusion.3.l_ref
  152.7 7.8 %all-to-all-done.8.r_ref = bf16[16,32,256]{2,1,0:T(8,128)(2,1)S(1)} async-done(((bf16[16,32,256]{2,1,0:T(8,128)(2,1)}), bf16[16,32,256]{2,1,0:T(8,128)(2,1)S(1)}, u32[]{:S(2)}, u32[]{:S(2)}) %all-to-all-start.8) | async-done | bytes 262176 | tf_op jit(solution)/shard_map/all_to_all | solution.py:192
  162.4 3.5 %all-to-all-start.9 = ((bf16[16,32,256]{2,1,0:T(8,128)(2,1)}), bf16[16,32,256]{2,1,0:T(8,128)(2,1)S(1)}, u32[]{:S(2)}, u32[]{:S(2)}) async-start(bf16[16,32,256]{2,1,0:T(8,128)(2,1)} %get-tuple-element.60), calls=%async_computation.9 | async-start | bytes 524288 | tf_op jit(solution)/shard_map/all_to_all | solution.py:192
  166.9 9.7 %all-to-all-done.9.x_ref = bf16[16,32,256]{2,1,0:T(8,128)(2,1)S(1)} async-done(((bf16[16,32,256]{2,1,0:T(8,128)(2,1)}), bf16[16,32,256]{2,1,0:T(8,128)(2,1)S(1)}, u32[]{:S(2)}, u32[]{:S(2)}) %all-to-all-start.9) | async-done | bytes 262176 | tf_op jit(solution)/shard_map/all_to_all | solution.py:192
  178.1 3.5 %all-to-all-start.10 = ((bf16[16,32,256]{2,1,0:T(8,128)(2,1)}), bf16[16,32,256]{2,1,0:T(8,128)(2,1)S(1)}, u32[]{:S(2)}, u32[]{:S(2)}) async-start(bf16[16,32,256]{2,1,0:T(8,128)(2,1)} %couple.11), calls=%async_computation.10 | async-start | bytes 524288 | tf_op jit(solution)/shard_map/all_to_all | solution.py:192
  181.6 2.4 select_bitcast_fusion.2.l_ref
  184.1 8.3 %all-to-all-done.10.r_ref = bf16[16,32,256]{2,1,0:T(8,128)(2,1)S(1)} async-done(((bf16[16,32,256]{2,1,0:T(8,128)(2,1)}), bf16[16,32,256]{2,1,0:T(8,128)(2,1)S(1)}, u32[]{:S(2)}, u32[]{:S(2)}) %all-to-all-start.10) | async-done | bytes 262176 | tf_op jit(solution)/shard_map/all_to_all | solution.py:192
  192.4 1.8 apply.11
  194.2 4.2 %all-to-all-start.11 = ((bf16[16,32,256]{2,1,0:T(8,128)(2,1)}), bf16[16,32,256]{2,1,0:T(8,128)(2,1)S(1)}, u32[]{:S(2)}, u32[]{:S(2)}) async-start(bf16[16,32,256]{2,1,0:T(8,128)(2,1)} %get-tuple-element.66), calls=%async_computation.11 | async-start | bytes 524288 | tf_op jit(solution)/shard_map/all_to_all | solution.py:192
  198.3 2.1 broadcast_select_fusion
  201.2 9.4 %all-to-all-done.11.x_ref = bf16[16,32,256]{2,1,0:T(8,128)(2,1)S(1)} async-done(((bf16[16,32,256]{2,1,0:T(8,128)(2,1)}), bf16[16,32,256]{2,1,0:T(8,128)(2,1)S(1)}, u32[]{:S(2)}, u32[]{:S(2)}) %all-to-all-start.11) | async-done | bytes 262176 | tf_op jit(solution)/shard_map/all_to_all | solution.py:192
  212.2 3.5 %all-to-all-start.12 = ((bf16[16,32,256]{2,1,0:T(8,128)(2,1)}), bf16[16,32,256]{2,1,0:T(8,128)(2,1)S(1)}, u32[]{:S(2)}, u32[]{:S(2)}) async-start(bf16[16,32,256]{2,1,0:T(8,128)(2,1)} %couple.12), calls=%async_computation.12 | async-start | bytes 524288 | tf_op jit(solution)/shard_map/all_to_all | solution.py:192
  215.7 2.4 select_bitcast_fusion.1.l_ref
  218.2 8.3 %all-to-all-done.12.r_ref = bf16[16,32,256]{2,1,0:T(8,128)(2,1)S(1)} async-done(((bf16[16,32,256]{2,1,0:T(8,128)(2,1)}), bf16[16,32,256]{2,1,0:T(8,128)(2,1)S(1)}, u32[]{:S(2)}, u32[]{:S(2)}) %all-to-all-start.12) | async-done | bytes 262176 | tf_op jit(solution)/shard_map/all_to_all | solution.py:192
  228.3 4.7 %all-to-all-start.13 = ((bf16[16,32,256]{2,1,0:T(8,128)(2,1)}), bf16[16,32,256]{2,1,0:T(8,128)(2,1)S(1)}, u32[]{:S(2)}, u32[]{:S(2)}) async-start(bf16[16,32,256]{2,1,0:T(8,128)(2,1)} %get-tuple-element.72), calls=%async_computation.13 | async-start | bytes 524288 | tf_op jit(solution)/shard_map/all_to_all | solution.py:192
  236.3 6.9 %all-to-all-done.13.x_ref = bf16[16,32,256]{2,1,0:T(8,128)(2,1)S(1)} async-done(((bf16[16,32,256]{2,1,0:T(8,128)(2,1)}), bf16[16,32,256]{2,1,0:T(8,128)(2,1)S(1)}, u32[]{:S(2)}, u32[]{:S(2)}) %all-to-all-start.13) | async-done | bytes 262176 | tf_op jit(solution)/shard_map/all_to_all | solution.py:192
  244.6 4.6 %all-to-all-start.14 = ((bf16[16,32,256]{2,1,0:T(8,128)(2,1)}), bf16[16,32,256]{2,1,0:T(8,128)(2,1)S(1)}, u32[]{:S(2)}, u32[]{:S(2)}) async-start(bf16[16,32,256]{2,1,0:T(8,128)(2,1)} %couple.13), calls=%async_computation.14 | async-start | bytes 524288 | tf_op jit(solution)/shard_map/all_to_all | solution.py:192
  249.2 2.4 select_bitcast_fusion.l_ref
  251.7 7.6 %all-to-all-done.14.r_ref = bf16[16,32,256]{2,1,0:T(8,128)(2,1)S(1)} async-done(((bf16[16,32,256]{2,1,0:T(8,128)(2,1)}), bf16[16,32,256]{2,1,0:T(8,128)(2,1)S(1)}, u32[]{:S(2)}, u32[]{:S(2)}) %all-to-all-start.14) | async-done | bytes 262176 | tf_op jit(solution)/shard_map/all_to_all | solution.py:192
  260.7 1.9 collective-permute-start.8
  267.3 2.8 collective-permute-start.11
  271.8 2.5 collective-permute-done.11
  274.3 4.5 %collective-permute-done.12 = f32[32,512]{1,0:T(8,128)S(1)} collective-permute-done((f32[32,512]{1,0:T(8,128)S(1)}, f32[32,512]{1,0:T(8,128)S(1)}, u32[]{:S(2)}, u32[]{:S(2)}) %collective-permute-start.12) | collective-permute-done | bytes 65568 | tf_op jit(solution)/shard_map/ppermute | solution.py:157
  278.9 22.4 %collective-permute-start.6 = (bf16[2,32,256]{2,1,0:T(8,128)(2,1)S(1)}, bf16[2,32,256]{2,1,0:T(8,128)(2,1)S(1)}, u32[]{:S(2)}, u32[]{:S(2)}) collective-permute-start(bf16[2,32,256]{2,1,0:T(8,128)(2,1)S(1)} %broadcast_select_fusion.7), channel_id=1, source_target_pairs={{0,64},{64,0},{1,65},{65,1},{2,66},{66,2},{3,67},{67,3},{4,68},{68... | collective-permute-start | bytes 98312 | tf_op jit(solution)/shard_map/ppermute | solution.py:164
  301.6 4.2 %collective-permute-start.14 = (f32[32,512]{1,0:T(8,128)S(1)}, f32[32,512]{1,0:T(8,128)S(1)}, u32[]{:S(2)}, u32[]{:S(2)}) collective-permute-start(f32[32,512]{1,0:T(8,128)S(1)} %fusion.3), channel_id=1, source_target_pairs={{0,64},{64,0},{1,65},{65,1},{2,66},{66,2},{3,67},{67,3},{4,68},{68... | collective-permute-start | bytes 196616 | tf_op jit(solution)/shard_map/ppermute | solution.py:164
  308.3 2.4 collective-permute-start.16
  (98 shorter events, 46.4 us)
Async XLA Ops:
  0.6 300.7 %copy-start = (bf16[512,512]{1,0:T(8,128)(2,1)S(1)}, bf16[512,512]{1,0:T(8,128)(2,1)}, u32[]{:S(2)}) copy-start(bf16[512,512]{1,0:T(8,128)(2,1)} %param.13) | copy-start | bytes 1572868
  1.7 4.2 %collective-permute-start.2 = (bf16[2,32,256]{2,1,0:T(8,128)(2,1)S(1)}, bf16[2,32,256]{2,1,0:T(8,128)(2,1)S(1)}, u32[]{:S(2)}, u32[]{:S(2)}) collective-permute-start(bf16[2,32,256]{2,1,0:T(8,128)(2,1)S(1)} %select_bitcast_fusion.14), channel_id=1, source_target_pairs={{0,64},{64,0},{1,65},{65,1},{2,66},{66,2},{3,67},{67,3},{4,68},{68... | collective-permute-start | bytes 98312 | tf_op jit(solution)/shard_map/ppermute | solution.py:164
  6.6 20.5 %collective-permute-start.3 = (bf16[2,256,4096]{2,1,0:T(8,128)(2,1)}, bf16[2,256,4096]{2,1,0:T(8,128)(2,1)}, u32[]{:S(2)}, u32[]{:S(2)}) collective-permute-start(bf16[2,256,4096]{2,1,0:T(8,128)(2,1)} %own_ref.1), channel_id=1, source_target_pairs={{0,64},{64,0},{1,65},{65,1},{2,66},{66,2},{3,67},{67,3},{4,68},{68... | collective-permute-start | bytes 12582920 | tf_op jit(solution)/shard_map/ppermute | solution.py:164
  6.9 24.0 %collective-permute-start.1 = (bf16[2,512,256]{2,1,0:T(8,128)(2,1)}, bf16[2,512,256]{2,1,0:T(8,128)(2,1)S(1)}, u32[]{:S(2)}, u32[]{:S(2)}) collective-permute-start(bf16[2,512,256]{2,1,0:T(8,128)(2,1)} %param.12), channel_id=1, source_target_pairs={{0,64},{64,0},{1,65},{65,1},{2,66},{66,2},{3,67},{67,3},{4,68},{68... | collective-permute-start | bytes 1572872 | tf_op jit(solution)/shard_map/ppermute | solution.py:164
  7.1 19.9 %all-to-all-start = ((bf16[16,32,256]{2,1,0:T(8,128)(2,1)}), bf16[16,32,256]{2,1,0:T(8,128)(2,1)S(1)}, u32[]{:S(2)}, u32[]{:S(2)}) async-start(bf16[16,32,256]{2,1,0:T(8,128)(2,1)} %broadcast_in_dim.14), calls=%async_computation | async-start | bytes 524288 | tf_op jit(solution)/shard_map/all_to_all | solution.py:192
  16.3 20.6 %collective-permute-start.4 = (bf16[2,2,4,128,128]{4,3,2,1,0:T(8,128)(2,1)}, bf16[2,2,4,128,128]{4,3,2,1,0:T(8,128)(2,1)S(1)}, u32[]{:S(2)}, u32[]{:S(2)}) collective-permute-start(bf16[2,2,4,128,128]{4,3,2,1,0:T(8,128)(2,1)} %param.10), channel_id=1, source_target_pairs={{0,64},{64,0},{1,65},{65,1},{2,66},{66,2},{3,67},{67,3},{4,68},{68... | collective-permute-start | bytes 1572872 | tf_op jit(solution)/shard_map/ppermute | solution.py:164
  17.0 19.8 %collective-permute-start = (s32[2,2,4]{2,1,0:T(2,128)}, s32[2,2,4]{2,1,0:T(2,128)S(1)}, u32[]{:S(2)}, u32[]{:S(2)}) collective-permute-start(s32[2,2,4]{2,1,0:T(2,128)} %param.11), channel_id=1, source_target_pairs={{0,64},{64,0},{1,65},{65,1},{2,66},{66,2},{3,67},{67,3},{4,68},{68... | collective-permute-start | bytes 200 | tf_op jit(solution)/shard_map/ppermute | solution.py:164
  17.2 19.6 %copy-start.10 = (s32[2,2,4]{2,1,0:T(2,128)S(1)}, s32[2,2,4]{2,1,0:T(2,128)}, u32[]{:S(2)}) copy-start(s32[2,2,4]{2,1,0:T(2,128)} %param.11) | copy-start | bytes 196
  17.2 19.8 %copy-start.2 = (bf16[2,2,4,128,128]{4,3,2,1,0:T(8,128)(2,1)S(1)}, bf16[2,2,4,128,128]{4,3,2,1,0:T(8,128)(2,1)}, u32[]{:S(2)}) copy-start(bf16[2,2,4,128,128]{4,3,2,1,0:T(8,128)(2,1)} %param.10) | copy-start | bytes 1572868
  30.9 0.8 copy-start.8
  31.7 15.3 %all-to-all-start.1 = ((bf16[16,32,256]{2,1,0:T(8,128)(2,1)}), bf16[16,32,256]{2,1,0:T(8,128)(2,1)S(1)}, u32[]{:S(2)}, u32[]{:S(2)}) async-start(bf16[16,32,256]{2,1,0:T(8,128)(2,1)} %get-tuple-element.43), calls=%async_computation.1 | async-start | bytes 524288 | tf_op jit(solution)/shard_map/all_to_all | solution.py:192
  37.0 11.5 %copy-start.4 = (bf16[2,2,4,128,128]{4,3,2,1,0:T(8,128)(2,1)}, bf16[2,2,4,128,128]{4,3,2,1,0:T(8,128)(2,1)S(1)}, u32[]{:S(2)}) copy-start(bf16[2,2,4,128,128]{4,3,2,1,0:T(8,128)(2,1)S(1)} %collective-permute-done.4) | copy-start | bytes 1572868
  48.5 14.9 %all-to-all-start.2 = ((bf16[16,32,256]{2,1,0:T(8,128)(2,1)}), bf16[16,32,256]{2,1,0:T(8,128)(2,1)S(1)}, u32[]{:S(2)}, u32[]{:S(2)}) async-start(bf16[16,32,256]{2,1,0:T(8,128)(2,1)} %couple.7), calls=%async_computation.2 | async-start | bytes 524288 | tf_op jit(solution)/shard_map/all_to_all | solution.py:192
  65.0 0.7 copy-start.1
  65.8 13.9 %all-to-all-start.3 = ((bf16[16,32,256]{2,1,0:T(8,128)(2,1)}), bf16[16,32,256]{2,1,0:T(8,128)(2,1)S(1)}, u32[]{:S(2)}, u32[]{:S(2)}) async-start(bf16[16,32,256]{2,1,0:T(8,128)(2,1)} %copy-done.1), calls=%async_computation.3 | async-start | bytes 524288 | tf_op jit(solution)/shard_map/all_to_all | solution.py:192
  81.1 14.1 %all-to-all-start.4 = ((bf16[16,32,256]{2,1,0:T(8,128)(2,1)}), bf16[16,32,256]{2,1,0:T(8,128)(2,1)S(1)}, u32[]{:S(2)}, u32[]{:S(2)}) async-start(bf16[16,32,256]{2,1,0:T(8,128)(2,1)} %couple.8), calls=%async_computation.4 | async-start | bytes 524288 | tf_op jit(solution)/shard_map/all_to_all | solution.py:192
  112.0 13.8 %all-to-all-start.6 = ((bf16[16,32,256]{2,1,0:T(8,128)(2,1)}), bf16[16,32,256]{2,1,0:T(8,128)(2,1)S(1)}, u32[]{:S(2)}, u32[]{:S(2)}) async-start(bf16[16,32,256]{2,1,0:T(8,128)(2,1)} %couple.9), calls=%async_computation.6 | async-start | bytes 524288 | tf_op jit(solution)/shard_map/all_to_all | solution.py:192
  118.3 16.3 %copy-start.3 = (bf16[2,2,4,128,128]{4,3,2,1,0:T(8,128)(2,1)S(1)}, bf16[2,2,4,128,128]{4,3,2,1,0:T(8,128)(2,1)}, u32[]{:S(2)}) copy-start(bf16[2,2,4,128,128]{4,3,2,1,0:T(8,128)(2,1)} %param.10) | copy-start | bytes 1572868
  126.9 3.1 collective-permute-start.5
  130.7 14.6 %all-to-all-start.7 = ((bf16[16,32,256]{2,1,0:T(8,128)(2,1)}), bf16[16,32,256]{2,1,0:T(8,128)(2,1)S(1)}, u32[]{:S(2)}, u32[]{:S(2)}) async-start(bf16[16,32,256]{2,1,0:T(8,128)(2,1)} %broadcast_in_dim.15), calls=%async_computation.7 | async-start | bytes 524288 | tf_op jit(solution)/shard_map/all_to_all | solution.py:192
  146.8 13.8 %all-to-all-start.8 = ((bf16[16,32,256]{2,1,0:T(8,128)(2,1)}), bf16[16,32,256]{2,1,0:T(8,128)(2,1)S(1)}, u32[]{:S(2)}, u32[]{:S(2)}) async-start(bf16[16,32,256]{2,1,0:T(8,128)(2,1)} %couple.10), calls=%async_computation.8 | async-start | bytes 524288 | tf_op jit(solution)/shard_map/all_to_all | solution.py:192
  162.4 14.2 %all-to-all-start.9 = ((bf16[16,32,256]{2,1,0:T(8,128)(2,1)}), bf16[16,32,256]{2,1,0:T(8,128)(2,1)S(1)}, u32[]{:S(2)}, u32[]{:S(2)}) async-start(bf16[16,32,256]{2,1,0:T(8,128)(2,1)} %get-tuple-element.60), calls=%async_computation.9 | async-start | bytes 524288 | tf_op jit(solution)/shard_map/all_to_all | solution.py:192
  178.1 14.3 %all-to-all-start.10 = ((bf16[16,32,256]{2,1,0:T(8,128)(2,1)}), bf16[16,32,256]{2,1,0:T(8,128)(2,1)S(1)}, u32[]{:S(2)}, u32[]{:S(2)}) async-start(bf16[16,32,256]{2,1,0:T(8,128)(2,1)} %couple.11), calls=%async_computation.10 | async-start | bytes 524288 | tf_op jit(solution)/shard_map/all_to_all | solution.py:192
  194.2 7.0 %copy-start.5 = (bf16[2,2,4,128,128]{4,3,2,1,0:T(8,128)(2,1)S(1)}, bf16[2,2,4,128,128]{4,3,2,1,0:T(8,128)(2,1)}, u32[]{:S(2)}) copy-start(bf16[2,2,4,128,128]{4,3,2,1,0:T(8,128)(2,1)} %copy-done.4) | copy-start | bytes 1572868
  194.2 16.5 %all-to-all-start.11 = ((bf16[16,32,256]{2,1,0:T(8,128)(2,1)}), bf16[16,32,256]{2,1,0:T(8,128)(2,1)S(1)}, u32[]{:S(2)}, u32[]{:S(2)}) async-start(bf16[16,32,256]{2,1,0:T(8,128)(2,1)} %get-tuple-element.66), calls=%async_computation.11 | async-start | bytes 524288 | tf_op jit(solution)/shard_map/all_to_all | solution.py:192
  200.4 0.8 copy-start.7
  212.2 14.3 %all-to-all-start.12 = ((bf16[16,32,256]{2,1,0:T(8,128)(2,1)}), bf16[16,32,256]{2,1,0:T(8,128)(2,1)S(1)}, u32[]{:S(2)}, u32[]{:S(2)}) async-start(bf16[16,32,256]{2,1,0:T(8,128)(2,1)} %couple.12), calls=%async_computation.12 | async-start | bytes 524288 | tf_op jit(solution)/shard_map/all_to_all | solution.py:192
  228.3 14.9 %all-to-all-start.13 = ((bf16[16,32,256]{2,1,0:T(8,128)(2,1)}), bf16[16,32,256]{2,1,0:T(8,128)(2,1)S(1)}, u32[]{:S(2)}, u32[]{:S(2)}) async-start(bf16[16,32,256]{2,1,0:T(8,128)(2,1)} %get-tuple-element.72), calls=%async_computation.13 | async-start | bytes 524288 | tf_op jit(solution)/shard_map/all_to_all | solution.py:192
  244.6 14.6 %all-to-all-start.14 = ((bf16[16,32,256]{2,1,0:T(8,128)(2,1)}), bf16[16,32,256]{2,1,0:T(8,128)(2,1)S(1)}, u32[]{:S(2)}, u32[]{:S(2)}) async-start(bf16[16,32,256]{2,1,0:T(8,128)(2,1)} %couple.13), calls=%async_computation.14 | async-start | bytes 524288 | tf_op jit(solution)/shard_map/all_to_all | solution.py:192
  251.7 8.6 %copy-start.6 = (bf16[2,512,256]{2,1,0:T(8,128)(2,1)S(1)}, bf16[2,512,256]{2,1,0:T(8,128)(2,1)}, u32[]{:S(2)}) copy-start(bf16[2,512,256]{2,1,0:T(8,128)(2,1)} %get-tuple-element.88) | copy-start | bytes 1572868
  259.2 42.1 %copy-start.9 = (s32[64,512]{1,0:T(8,128)S(1)}, s32[64,512]{1,0:T(8,128)}, u32[]{:S(2)}) copy-start(s32[64,512]{1,0:T(8,128)} %param.8) | copy-start | bytes 393220
  260.5 5.2 %collective-permute-start.7 = (f32[32,512]{1,0:T(8,128)S(1)}, f32[32,512]{1,0:T(8,128)S(1)}, u32[]{:S(2)}, u32[]{:S(2)}) collective-permute-start(f32[32,512]{1,0:T(8,128)S(1)} %convolution_add_fusion), channel_id=1, source_target_pairs={{0,4},{4,8},{8,12},{12,0},{1,5},{5,9},{9,13},{13,1},{2,6},{6,10},{... | collective-permute-start | bytes 196616 | tf_op jit(solution)/shard_map/ppermute | solution.py:157
  260.7 5.0 %collective-permute-start.8 = (f32[32,512]{1,0:T(8,128)S(1)}, f32[32,512]{1,0:T(8,128)S(1)}, u32[]{:S(2)}, u32[]{:S(2)}) collective-permute-start(f32[32,512]{1,0:T(8,128)S(1)} %convolution_add_fusion), channel_id=1, source_target_pairs={{0,8},{4,12},{8,0},{12,4},{1,9},{5,13},{9,1},{13,5},{2,10},{6,14},... | collective-permute-start | bytes 196616 | tf_op jit(solution)/shard_map/ppermute | solution.py:157
  262.6 3.7 %collective-permute-start.9 = (f32[32,512]{1,0:T(8,128)S(1)}, f32[32,512]{1,0:T(8,128)S(1)}, u32[]{:S(2)}, u32[]{:S(2)}) collective-permute-start(f32[32,512]{1,0:T(8,128)S(1)} %convolution_add_fusion), channel_id=1, source_target_pairs={{0,12},{4,0},{8,4},{12,8},{1,13},{5,1},{9,5},{13,9},{2,14},{6,2},{... | collective-permute-start | bytes 196616 | tf_op jit(solution)/shard_map/ppermute | solution.py:157
  266.3 5.4 %collective-permute-start.10 = (f32[32,512]{1,0:T(8,128)S(1)}, f32[32,512]{1,0:T(8,128)S(1)}, u32[]{:S(2)}, u32[]{:S(2)}) collective-permute-start(f32[32,512]{1,0:T(8,128)S(1)} %add_add_fusion.1), channel_id=1, source_target_pairs={{0,16},{16,32},{32,48},{48,0},{1,17},{17,33},{33,49},{49,1},{2,18}... | collective-permute-start | bytes 196616 | tf_op jit(solution)/shard_map/ppermute | solution.py:157
  267.3 7.0 %collective-permute-start.11 = (f32[32,512]{1,0:T(8,128)S(1)}, f32[32,512]{1,0:T(8,128)S(1)}, u32[]{:S(2)}, u32[]{:S(2)}) collective-permute-start(f32[32,512]{1,0:T(8,128)S(1)} %add_add_fusion.1), channel_id=1, source_target_pairs={{0,32},{16,48},{32,0},{48,16},{1,33},{17,49},{33,1},{49,17},{2,34}... | collective-permute-start | bytes 196616 | tf_op jit(solution)/shard_map/ppermute | solution.py:157
  270.0 8.7 %collective-permute-start.12 = (f32[32,512]{1,0:T(8,128)S(1)}, f32[32,512]{1,0:T(8,128)S(1)}, u32[]{:S(2)}, u32[]{:S(2)}) collective-permute-start(f32[32,512]{1,0:T(8,128)S(1)} %add_add_fusion.1), channel_id=1, source_target_pairs={{0,48},{16,0},{32,16},{48,32},{1,49},{17,1},{33,17},{49,33},{2,50}... | collective-permute-start | bytes 196616 | tf_op jit(solution)/shard_map/ppermute | solution.py:157
  278.8 22.5 %collective-permute-start.13 = (f32[32,512]{1,0:T(8,128)S(1)}, f32[32,512]{1,0:T(8,128)S(1)}, u32[]{:S(2)}, u32[]{:S(2)}) collective-permute-start(f32[32,512]{1,0:T(8,128)S(1)} %add_add_fusion), channel_id=1, source_target_pairs={{0,128},{128,0},{1,129},{129,1},{2,130},{130,2},{3,131},{131,3},{4... | collective-permute-start | bytes 196616 | tf_op jit(solution)/shard_map/ppermute | solution.py:157
  278.9 26.8 %collective-permute-start.6 = (bf16[2,32,256]{2,1,0:T(8,128)(2,1)S(1)}, bf16[2,32,256]{2,1,0:T(8,128)(2,1)S(1)}, u32[]{:S(2)}, u32[]{:S(2)}) collective-permute-start(bf16[2,32,256]{2,1,0:T(8,128)(2,1)S(1)} %broadcast_select_fusion.7), channel_id=1, source_target_pairs={{0,64},{64,0},{1,65},{65,1},{2,66},{66,2},{3,67},{67,3},{4,68},{68... | collective-permute-start | bytes 98312 | tf_op jit(solution)/shard_map/ppermute | solution.py:164
  301.6 5.1 %collective-permute-start.14 = (f32[32,512]{1,0:T(8,128)S(1)}, f32[32,512]{1,0:T(8,128)S(1)}, u32[]{:S(2)}, u32[]{:S(2)}) collective-permute-start(f32[32,512]{1,0:T(8,128)S(1)} %fusion.3), channel_id=1, source_target_pairs={{0,64},{64,0},{1,65},{65,1},{2,66},{66,2},{3,67},{67,3},{4,68},{68... | collective-permute-start | bytes 196616 | tf_op jit(solution)/shard_map/ppermute | solution.py:164
  307.3 5.4 %collective-permute-start.15 = (f32[8,128]{1,0:T(8,128)S(1)}, f32[8,128]{1,0:T(8,128)S(1)}, u32[]{:S(2)}, u32[]{:S(2)}) collective-permute-start(f32[8,128]{1,0:T(8,128)S(1)} %pad_maximum_fusion.3), channel_id=1, source_target_pairs={{0,1},{1,2},{2,3},{3,0},{4,5},{5,6},{6,7},{7,4},{8,9},{9,10},{10,1... | collective-permute-start | bytes 12296 | tf_op jit(solution)/shard_map/ppermute | solution.py:157
  308.3 4.5 %collective-permute-start.16 = (f32[8,128]{1,0:T(8,128)S(1)}, f32[8,128]{1,0:T(8,128)S(1)}, u32[]{:S(2)}, u32[]{:S(2)}) collective-permute-start(f32[8,128]{1,0:T(8,128)S(1)} %pad_maximum_fusion.3), channel_id=1, source_target_pairs={{0,2},{1,3},{2,0},{3,1},{4,6},{5,7},{6,4},{7,5},{8,10},{9,11},{10,... | collective-permute-start | bytes 12296 | tf_op jit(solution)/shard_map/ppermute | solution.py:157
  310.7 2.8 collective-permute-start.17

commit v8 on v6

--- a/solution.py
+++ b/solution.py
@@ -24,19 +24,19 @@
             copy.start()
 
 
-def arrange_kernel(place, *refs, per_core, steps, pieces, slices):
+def arrange_kernel(place, *refs, per_core, which, pieces, slices):
     own_refs, other_refs = refs[:pieces], refs[pieces : 2 * pieces]
-    outs, sems = refs[-1 - steps : -1], refs[-1]
-
-    def copies(refs, step):
+    outs, sems = refs[-1 - len(which) : -1], refs[-1]
+
+    def copies(refs, n, step):
         return [
-            pltpu.make_async_copy(*slices(ref, k, outs[step], step % per_core), sems.at[step, k])
+            pltpu.make_async_copy(*slices(ref, k, outs[n], step % per_core), sems.at[n, k])
             for k, ref in enumerate(refs)
         ]
 
     waits = []
-    for step in range(steps):
-        own, other = copies(own_refs, step), copies(other_refs, step)
+    for n, step in enumerate(which):
+        own, other = copies(own_refs, n, step), copies(other_refs, n, step)
         start_one_of(place[0] == step // per_core, own, other)
         waits += own
     for copy in waits:
@@ -124,19 +124,19 @@
 LARGE = pltpu.CompilerParams(vmem_limit_bytes=50 << 20)
 
 
-def arrange(slices, place, own, other, steps, shape, name, after):
+def arrange(slices, place, own, other, which, per_core, shape, name, after):
     pieces = len(own)
     return pl.pallas_call(
         functools.partial(
-            arrange_kernel, per_core=steps // 2, steps=steps, pieces=pieces, slices=slices
+            arrange_kernel, per_core=per_core, which=which, pieces=pieces, slices=slices
         ),
-        out_shape=tuple([jax.ShapeDtypeStruct(shape, jnp.bfloat16)] * steps),
+        out_shape=tuple([jax.ShapeDtypeStruct(shape, jnp.bfloat16)] * len(which)),
         in_specs=[SMEM] + [HBM] * (2 * pieces + 1),
-        out_specs=tuple([VMEM] * steps),
-        scratch_shapes=[pltpu.SemaphoreType.DMA((steps, pieces))],
+        out_specs=tuple([VMEM] * len(which)),
+        scratch_shapes=[pltpu.SemaphoreType.DMA((len(which), pieces))],
         compiler_params=PARAMS,
         cost_estimate=pl.CostEstimate(
-            flops=0, transcendentals=0, bytes_accessed=4 * steps * shape[0] * shape[1]
+            flops=0, transcendentals=0, bytes_accessed=8 * len(which) * shape[0] * shape[1]
         ),
         name=name,
     )(place, *own, *other, after)
@@ -233,22 +233,35 @@
         return lax.all_to_all(value, NODES, 0, 0)
 
     outs = apply_early(place, everywhere(spread), inverse_factors, other_factors, 0)
-    factors = arrange(
-        factor_slices, place, [inverse_factors], [other_factors], steps, inverse_factors.shape[1:], "factors", outs[0]
-    )
+    factors = {}
+
+    def arranged(which, after):
+        slices = arrange(
+            factor_slices, place, [inverse_factors], [other_factors], which, own_steps, inverse_factors.shape[1:], "factors", after
+        )
+        factors.update(zip(which, slices))
+
     results = [outs[0]]
     other_rows, *outs = lax.optimization_barrier((swap(border_rows), *outs))
     for turn in range(turns):
         for step in range(1 if turn == 0 else 0, steps):
             if step > 0:
                 pieces = everywhere(outs[1])
-            if turn == 0 and step == 1:
-                pieces, *factors = lax.optimization_barrier((pieces, *factors))
             resid = couple_early(
                 place, own_cols, pieces, own_source[step], couplings, other_couplings, step
             )
-            outs = apply_factor(everywhere(resid), factors[step], step + 1 < steps)
+            if turn == 0 and step == 1:
+                own, other, _ = lax.optimization_barrier((inverse_factors, other_factors, resid))
+                low = first if step < own_steps else jnp.logical_not(first)
+                factor = jnp.where(low, own[step % own_steps], other[step % own_steps])
+            else:
+                factor = factors[step]
+            outs = apply_factor(everywhere(resid), factor, step + 1 < steps)
             results.append(outs[0])
+            if turn == 0 and step == 1:
+                arranged(tuple(range(2, steps)), outs[0])
+            if turn == 0 and step == 2:
+                arranged((0, 1), outs[0])
         if turn + 1 < turns:
             moved = lax.ppermute(outs[0], "zl", [(turn, turn + 1)])
             pieces = everywhere(jnp.broadcast_to(moved[None], (peers, probes, local)))

time: 315 us -> 324 us (1.029)
  blocking collectives: 145 us -> 103 us
  waiting for transfers between devices: 52.8 us -> 78.1 us
  starting transfers between devices: 75.7 us -> 87.3 us
  local copies, waits for them, and re-layouts: 12 us -> 19.8 us
  other arithmetic: 3.01 us -> 6.81 us
    all_to_all x10 -> x7, blocking collectives: 145 us -> 103 us  [everywhere(): return lax.all_to_all(value, NODES, 0, 0)]
    all_to_all x5 -> x8, waiting for transfers between devices: 42.2 us -> 62.7 us  [everywhere(): return lax.all_to_all(value, NODES, 0, 0)]
    all_to_all x5 -> x8, starting transfers between devices: 28.3 us -> 40 us  [everywhere(): return lax.all_to_all(value, NODES, 0, 0)]
    unnamed x35 -> x39, local copies, waits for them, and re-layouts: 9.96 us -> 17.7 us
    ppermute x10, waiting for transfers between devices: 7.28 us -> 12.1 us  [line(): lax.ppermute(value, axis, [(i, (i + k) % size) for i in range(size)])]
    select_n x0 -> x1, other arithmetic: none -> 3.8 us  [shards(): factor = jnp.where(low, own[step % own_steps], other[step % own_steps])]
  transfers between devices with their start and end apart: 23 -> 26, of which waited for: 13 -> 20; matrix products, arithmetic and copies ran while one was open for 1% -> 2% of each run, Pallas kernels for 2% -> 2%
where the time goes in v8:
time: 324 us; the launch traced here: 322 us
  blocking collectives  103 us (32%)
  starting transfers between devices  87.3 us (27%)
  waiting for transfers between devices  78.1 us (24%)
  Pallas kernels  25.6 us (8%)
  local copies, waits for them, and re-layouts  19.8 us (6%)
  other arithmetic  6.81 us (2%)
    all_to_all x7, blocking collectives, everywhere(): return lax.all_to_all(value, NODES, 0, 0)  103 us
    all_to_all x8, waiting for transfers between devices, everywhere(): return lax.all_to_all(value, NODES, 0, 0)  62.7 us
    all_to_all x8, starting transfers between devices, everywhere(): return lax.all_to_all(value, NODES, 0, 0)  40 us
    ppermute x7, starting transfers between devices, swap(): return lax.ppermute(value, 'core', [(0, 1), (1, 0)])  33.6 us
    unnamed x39, local copies, waits for them, and re-layouts  17.7 us
    ppermute x10, waiting for transfers between devices, line(): lax.ppermute(value, axis, [(i, (i + k) % size) for i in range(size)])  12.1 us
    ppermute x10, starting transfers between devices, line(): lax.ppermute(value, axis, [(i, (i + k) % size) for i in range(size)])  11.4 us
    pallas_call x7, Pallas kernels, apply_factor(): pl.pallas_call(apply_kernel, out_shape=shapes, in_specs=[VMEM, VMEM], out...  9.05 us
  transfers between devices with their start and end apart: 26, of which 20 were waited for; matrix products, arithmetic and copies ran while one was open for 2% of the time, Pallas kernels for 2%

profile of v8, /device:TPU:1, one launch (start us, length us, event | category | flops | bytes accessed | tf_op | source)
XLA Modules:
  0.0 322.2 jit_solution(6102134931270393694)
XLA Ops:
  1.7 3.3 %collective-permute-start.2 = (bf16[2,32,256]{2,1,0:T(8,128)(2,1)S(1)}, bf16[2,32,256]{2,1,0:T(8,128)(2,1)S(1)}, u32[]{:S(2)}, u32[]{:S(2)}) collective-permute-start(bf16[2,32,256]{2,1,0:T(8,128)(2,1)S(1)} %select_bitcast_fusion.1), channel_id=1, source_target_pairs={{0,64},{64,0},{1,65},{65,1},{2,66},{66,2},{3,67},{67,3},{4,68},{68... | collective-permute-start | bytes 98312 | tf_op jit(solution)/shard_map/ppermute | solution.py:205
  7.1 9.2 %all-to-all-start = ((bf16[16,32,256]{2,1,0:T(8,128)(2,1)}), bf16[16,32,256]{2,1,0:T(8,128)(2,1)S(1)}, u32[]{:S(2)}, u32[]{:S(2)}) async-start(bf16[16,32,256]{2,1,0:T(8,128)(2,1)} %broadcast_in_dim.14), calls=%async_computation | async-start | bytes 524288 | tf_op jit(solution)/shard_map/all_to_all | solution.py:233
  17.1 9.9 %all-to-all-done.r_ref = bf16[16,32,256]{2,1,0:T(8,128)(2,1)S(1)} async-done(((bf16[16,32,256]{2,1,0:T(8,128)(2,1)}), bf16[16,32,256]{2,1,0:T(8,128)(2,1)S(1)}, u32[]{:S(2)}, u32[]{:S(2)}) %all-to-all-start) | async-done | bytes 262176 | tf_op jit(solution)/shard_map/all_to_all | solution.py:233
  27.1 3.9 %apply_early.1 = (bf16[32,256]{1,0:T(8,128)(2,1)}, bf16[16,32,256]{2,1,0:T(8,128)(2,1)}) custom-call(s32[3]{0:T(128)S(1)} %pad_add_fusion.1.place, bf16[16,32,256]{2,1,0:T(8,128)(2,1)S(1)} %all-to-all-done.r_ref, bf16[2,256,4096]{2,1,0:T(8,128)(2,1)} %refs_0_.3, bf16[2,256,4096]{2,1,0:T(8,128)(2,1)} %collective-permute-done.3.other_ref.refs_1_), custom_call_target="tpu_custom_call" | custom-call | tf_op jit(solution)/shard_map/apply_early/pallas_call | solution.py:169
  31.8 5.1 %all-to-all-start.1 = ((bf16[16,32,256]{2,1,0:T(8,128)(2,1)}), bf16[16,32,256]{2,1,0:T(8,128)(2,1)S(1)}, u32[]{:S(2)}, u32[]{:S(2)}) async-start(bf16[16,32,256]{2,1,0:T(8,128)(2,1)} %get-tuple-element.27), calls=%async_computation.1 | async-start | bytes 524288 | tf_op jit(solution)/shard_map/all_to_all | solution.py:233
  36.9 1.9 collective-permute-start
  39.7 7.3 %all-to-all-done.1.x_ref = bf16[16,32,256]{2,1,0:T(8,128)(2,1)S(1)} async-done(((bf16[16,32,256]{2,1,0:T(8,128)(2,1)}), bf16[16,32,256]{2,1,0:T(8,128)(2,1)S(1)}, u32[]{:S(2)}, u32[]{:S(2)}) %all-to-all-start.1) | async-done | bytes 262176 | tf_op jit(solution)/shard_map/all_to_all | solution.py:233
  48.6 4.9 %all-to-all-start.2 = ((bf16[16,32,256]{2,1,0:T(8,128)(2,1)}), bf16[16,32,256]{2,1,0:T(8,128)(2,1)S(1)}, u32[]{:S(2)}, u32[]{:S(2)}) async-start(bf16[16,32,256]{2,1,0:T(8,128)(2,1)} %couple_early.7), calls=%async_computation.2 | async-start | bytes 524288 | tf_op jit(solution)/shard_map/all_to_all | solution.py:233
  53.6 3.8 %select_bitcast_fusion.l_ref = bf16[256,4096]{1,0:T(8,128)(2,1)} fusion(bf16[2,256,4096]{2,1,0:T(8,128)(2,1)} %collective-permute-done.3.other_ref.refs_1_, bf16[2,256,4096]{2,1,0:T(8,128)(2,1)} %refs_0_.3, pred[]{:T(512)S(6)} %eq.3), kind=kLoop, calls=%fused_computation | loop fusion | flops 1048576 | bytes 6291457 | tf_op jit(solution)/shard_map/jit(_where)/select_n | solution.py:256
  57.4 6.2 %all-to-all-done.2.r_ref = bf16[16,32,256]{2,1,0:T(8,128)(2,1)S(1)} async-done(((bf16[16,32,256]{2,1,0:T(8,128)(2,1)}), bf16[16,32,256]{2,1,0:T(8,128)(2,1)S(1)}, u32[]{:S(2)}, u32[]{:S(2)}) %all-to-all-start.2) | async-done | bytes 262176 | tf_op jit(solution)/shard_map/all_to_all | solution.py:233
  63.5 1.6 copy-done.4
  65.1 1.8 apply.7
  66.9 3.8 %all-to-all-start.3 = ((bf16[16,32,256]{2,1,0:T(8,128)(2,1)}), bf16[16,32,256]{2,1,0:T(8,128)(2,1)S(1)}, u32[]{:S(2)}, u32[]{:S(2)}) async-start(bf16[16,32,256]{2,1,0:T(8,128)(2,1)} %get-tuple-element.31), calls=%async_computation.3 | async-start | bytes 524288 | tf_op jit(solution)/shard_map/all_to_all | solution.py:233
  70.8 10.0 %all-to-all-done.3.x_ref = bf16[16,32,256]{2,1,0:T(8,128)(2,1)S(1)} async-done(((bf16[16,32,256]{2,1,0:T(8,128)(2,1)}), bf16[16,32,256]{2,1,0:T(8,128)(2,1)S(1)}, u32[]{:S(2)}, u32[]{:S(2)}) %all-to-all-start.3) | async-done | bytes 262176 | tf_op jit(solution)/shard_map/all_to_all | solution.py:233
  80.8 1.6 couple_early.8
  82.4 4.2 %all-to-all-start.4 = ((bf16[16,32,256]{2,1,0:T(8,128)(2,1)}), bf16[16,32,256]{2,1,0:T(8,128)(2,1)S(1)}, u32[]{:S(2)}, u32[]{:S(2)}) async-start(bf16[16,32,256]{2,1,0:T(8,128)(2,1)} %couple_early.8), calls=%async_computation.4 | async-start | bytes 524288 | tf_op jit(solution)/shard_map/all_to_all | solution.py:233
  86.6 2.2 copy-done.1
  92.4 4.1 %all-to-all-done.4.r_ref = bf16[16,32,256]{2,1,0:T(8,128)(2,1)S(1)} async-done(((bf16[16,32,256]{2,1,0:T(8,128)(2,1)}), bf16[16,32,256]{2,1,0:T(8,128)(2,1)S(1)}, u32[]{:S(2)}, u32[]{:S(2)}) %all-to-all-start.4) | async-done | bytes 262176 | tf_op jit(solution)/shard_map/all_to_all | solution.py:233
  96.5 1.6 copy-done.9
  99.2 14.7 %all_to_all.75.x_ref = bf16[16,32,256]{2,1,0:T(8,128)(2,1)S(1)} all-to-all(bf16[16,32,256]{2,1,0:T(8,128)(2,1)S(1)} %get-tuple-element.34), channel_id=1, replica_groups=mesh['zl'=2,'core'=2,'zh'=4,'y'=4,'x'=4] {'zh','y'}, dimensions={0} | all-to-all | bytes 524288 | tf_op jit(solution)/shard_map/all_to_all | solution.py:233
  114.8 13.5 %all_to_all.76.r_ref = bf16[16,32,256]{2,1,0:T(8,128)(2,1)S(1)} all-to-all(bf16[16,32,256]{2,1,0:T(8,128)(2,1)S(1)} %couple_early.9), channel_id=1, replica_groups=mesh['zl'=2,'core'=2,'zh'=4,'y'=4,'x'=4] {'zh','y'}, dimensions={0} | all-to-all | bytes 524288 | tf_op jit(solution)/shard_map/all_to_all | solution.py:233
  129.4 2.3 collective-permute-start.5
  132.6 14.4 %all_to_all.77.x_ref = bf16[16,32,256]{2,1,0:T(8,128)(2,1)S(1)} all-to-all(bf16[16,32,256]{2,1,0:T(8,128)(2,1)S(1)} %broadcast_in_dim.15), channel_id=1, replica_groups=mesh['zl'=2,'core'=2,'zh'=4,'y'=4,'x'=4] {'zh','y'}, dimensions={0} | all-to-all | bytes 524288 | tf_op jit(solution)/shard_map/all_to_all | solution.py:233
  147.0 1.6 couple_early.10
  148.6 3.5 %all-to-all-start.8 = ((bf16[16,32,256]{2,1,0:T(8,128)(2,1)}), bf16[16,32,256]{2,1,0:T(8,128)(2,1)S(1)}, u32[]{:S(2)}, u32[]{:S(2)}) async-start(bf16[16,32,256]{2,1,0:T(8,128)(2,1)} %couple_early.10), calls=%async_computation.8 | async-start | bytes 524288 | tf_op jit(solution)/shard_map/all_to_all | solution.py:233
  152.2 2.2 copy-done.2
  154.3 2.8 factors.3
  159.9 2.9 all-to-all-done.8.r_ref
  165.4 16.0 %all_to_all.78.x_ref = bf16[16,32,256]{2,1,0:T(8,128)(2,1)S(1)} all-to-all(bf16[16,32,256]{2,1,0:T(8,128)(2,1)S(1)} %get-tuple-element.39), channel_id=1, replica_groups=mesh['zl'=2,'core'=2,'zh'=4,'y'=4,'x'=4] {'zh','y'}, dimensions={0} | all-to-all | bytes 524288 | tf_op jit(solution)/shard_map/all_to_all | solution.py:233
  182.3 14.5 %all_to_all.79.r_ref = bf16[16,32,256]{2,1,0:T(8,128)(2,1)S(1)} all-to-all(bf16[16,32,256]{2,1,0:T(8,128)(2,1)S(1)} %couple_early.11), channel_id=1, replica_groups=mesh['zl'=2,'core'=2,'zh'=4,'y'=4,'x'=4] {'zh','y'}, dimensions={0} | all-to-all | bytes 524288 | tf_op jit(solution)/shard_map/all_to_all | solution.py:233
  197.9 14.0 %all_to_all.80.x_ref = bf16[16,32,256]{2,1,0:T(8,128)(2,1)S(1)} all-to-all(bf16[16,32,256]{2,1,0:T(8,128)(2,1)S(1)} %get-tuple-element.42), channel_id=1, replica_groups=mesh['zl'=2,'core'=2,'zh'=4,'y'=4,'x'=4] {'zh','y'}, dimensions={0} | all-to-all | bytes 524288 | tf_op jit(solution)/shard_map/all_to_all | solution.py:233
  212.8 15.5 %all_to_all.81.r_ref = bf16[16,32,256]{2,1,0:T(8,128)(2,1)S(1)} all-to-all(bf16[16,32,256]{2,1,0:T(8,128)(2,1)S(1)} %couple_early.12), channel_id=1, replica_groups=mesh['zl'=2,'core'=2,'zh'=4,'y'=4,'x'=4] {'zh','y'}, dimensions={0} | all-to-all | bytes 524288 | tf_op jit(solution)/shard_map/all_to_all | solution.py:233
  228.3 1.8 apply.12
  230.1 4.7 %all-to-all-start.13 = ((bf16[16,32,256]{2,1,0:T(8,128)(2,1)}), bf16[16,32,256]{2,1,0:T(8,128)(2,1)S(1)}, u32[]{:S(2)}, u32[]{:S(2)}) async-start(bf16[16,32,256]{2,1,0:T(8,128)(2,1)} %get-tuple-element.44), calls=%async_computation.13 | async-start | bytes 524288 | tf_op jit(solution)/shard_map/all_to_all | solution.py:233
  235.9 11.2 %all-to-all-done.13.x_ref = bf16[16,32,256]{2,1,0:T(8,128)(2,1)S(1)} async-done(((bf16[16,32,256]{2,1,0:T(8,128)(2,1)}), bf16[16,32,256]{2,1,0:T(8,128)(2,1)S(1)}, u32[]{:S(2)}, u32[]{:S(2)}) %all-to-all-start.13) | async-done | bytes 262176 | tf_op jit(solution)/shard_map/all_to_all | solution.py:233
  248.8 4.6 %all-to-all-start.14 = ((bf16[16,32,256]{2,1,0:T(8,128)(2,1)}), bf16[16,32,256]{2,1,0:T(8,128)(2,1)S(1)}, u32[]{:S(2)}, u32[]{:S(2)}) async-start(bf16[16,32,256]{2,1,0:T(8,128)(2,1)} %couple_early.13), calls=%async_computation.14 | async-start | bytes 524288 | tf_op jit(solution)/shard_map/all_to_all | solution.py:233
  253.9 11.0 %all-to-all-done.14.r_ref = bf16[16,32,256]{2,1,0:T(8,128)(2,1)S(1)} async-done(((bf16[16,32,256]{2,1,0:T(8,128)(2,1)}), bf16[16,32,256]{2,1,0:T(8,128)(2,1)S(1)}, u32[]{:S(2)}, u32[]{:S(2)}) %all-to-all-start.14) | async-done | bytes 262176 | tf_op jit(solution)/shard_map/all_to_all | solution.py:233
  264.9 1.6 copy-done.7
  267.8 2.1 collective-permute-start.8
  270.9 1.6 collective-permute-done.8
  272.5 1.7 collective-permute-done.7
  275.5 4.1 %collective-permute-start.11 = (f32[32,512]{1,0:T(8,128)S(1)}, f32[32,512]{1,0:T(8,128)S(1)}, u32[]{:S(2)}, u32[]{:S(2)}) collective-permute-start(f32[32,512]{1,0:T(8,128)S(1)} %add_add_fusion.1), channel_id=1, source_target_pairs={{0,32},{16,48},{32,0},{48,16},{1,33},{17,49},{33,1},{49,17},{2,34}... | collective-permute-start | bytes 196616 | tf_op jit(solution)/shard_map/ppermute | solution.py:198
  280.3 2.6 collective-permute-done.11
  282.8 2.3 collective-permute-done.10
  285.3 23.0 %collective-permute-start.6 = (bf16[2,32,256]{2,1,0:T(8,128)(2,1)S(1)}, bf16[2,32,256]{2,1,0:T(8,128)(2,1)S(1)}, u32[]{:S(2)}, u32[]{:S(2)}) collective-permute-start(bf16[2,32,256]{2,1,0:T(8,128)(2,1)S(1)} %broadcast_select_fusion.7), channel_id=1, source_target_pairs={{0,64},{64,0},{1,65},{65,1},{2,66},{66,2},{3,67},{67,3},{4,68},{68... | collective-permute-start | bytes 98312 | tf_op jit(solution)/shard_map/ppermute | solution.py:205
  308.5 4.2 %collective-permute-start.14 = (f32[32,512]{1,0:T(8,128)S(1)}, f32[32,512]{1,0:T(8,128)S(1)}, u32[]{:S(2)}, u32[]{:S(2)}) collective-permute-start(f32[32,512]{1,0:T(8,128)S(1)} %fusion.3), channel_id=1, source_target_pairs={{0,64},{64,0},{1,65},{65,1},{2,66},{66,2},{3,67},{67,3},{4,68},{68... | collective-permute-start | bytes 196616 | tf_op jit(solution)/shard_map/ppermute | solution.py:205
  314.2 2.7 collective-permute-start.17
  318.7 2.1 collective-permute-done.16
  (99 shorter events, 35.6 us)
Async XLA Ops:
  0.6 307.6 %copy-start = (bf16[512,512]{1,0:T(8,128)(2,1)S(1)}, bf16[512,512]{1,0:T(8,128)(2,1)}, u32[]{:S(2)}) copy-start(bf16[512,512]{1,0:T(8,128)(2,1)} %param.13) | copy-start | bytes 1572868
  1.7 4.2 %collective-permute-start.2 = (bf16[2,32,256]{2,1,0:T(8,128)(2,1)S(1)}, bf16[2,32,256]{2,1,0:T(8,128)(2,1)S(1)}, u32[]{:S(2)}, u32[]{:S(2)}) collective-permute-start(bf16[2,32,256]{2,1,0:T(8,128)(2,1)S(1)} %select_bitcast_fusion.1), channel_id=1, source_target_pairs={{0,64},{64,0},{1,65},{65,1},{2,66},{66,2},{3,67},{67,3},{4,68},{68... | collective-permute-start | bytes 98312 | tf_op jit(solution)/shard_map/ppermute | solution.py:205
  6.6 20.5 %collective-permute-start.3 = (bf16[2,256,4096]{2,1,0:T(8,128)(2,1)}, bf16[2,256,4096]{2,1,0:T(8,128)(2,1)}, u32[]{:S(2)}, u32[]{:S(2)}) collective-permute-start(bf16[2,256,4096]{2,1,0:T(8,128)(2,1)} %refs_0_.3), channel_id=1, source_target_pairs={{0,64},{64,0},{1,65},{65,1},{2,66},{66,2},{3,67},{67,3},{4,68},{68... | collective-permute-start | bytes 12582920 | tf_op jit(solution)/shard_map/ppermute | solution.py:205
  7.0 24.0 %collective-permute-start.1 = (bf16[2,512,256]{2,1,0:T(8,128)(2,1)}, bf16[2,512,256]{2,1,0:T(8,128)(2,1)S(1)}, u32[]{:S(2)}, u32[]{:S(2)}) collective-permute-start(bf16[2,512,256]{2,1,0:T(8,128)(2,1)} %param.12), channel_id=1, source_target_pairs={{0,64},{64,0},{1,65},{65,1},{2,66},{66,2},{3,67},{67,3},{4,68},{68... | collective-permute-start | bytes 1572872 | tf_op jit(solution)/shard_map/ppermute | solution.py:205
  7.1 19.9 %all-to-all-start = ((bf16[16,32,256]{2,1,0:T(8,128)(2,1)}), bf16[16,32,256]{2,1,0:T(8,128)(2,1)S(1)}, u32[]{:S(2)}, u32[]{:S(2)}) async-start(bf16[16,32,256]{2,1,0:T(8,128)(2,1)} %broadcast_in_dim.14), calls=%async_computation | async-start | bytes 524288 | tf_op jit(solution)/shard_map/all_to_all | solution.py:233
  16.3 23.4 %collective-permute-start.4 = (bf16[2,2,4,128,128]{4,3,2,1,0:T(8,128)(2,1)}, bf16[2,2,4,128,128]{4,3,2,1,0:T(8,128)(2,1)S(1)}, u32[]{:S(2)}, u32[]{:S(2)}) collective-permute-start(bf16[2,2,4,128,128]{4,3,2,1,0:T(8,128)(2,1)} %own_ref.15), channel_id=1, source_target_pairs={{0,64},{64,0},{1,65},{65,1},{2,66},{66,2},{3,67},{67,3},{4,68},{68... | collective-permute-start | bytes 1572872 | tf_op jit(solution)/shard_map/ppermute | solution.py:205
  17.1 19.7 %copy-start.18 = (s32[2,2,4]{2,1,0:T(2,128)S(1)}, s32[2,2,4]{2,1,0:T(2,128)}, u32[]{:S(2)}) copy-start(s32[2,2,4]{2,1,0:T(2,128)} %param.11) | copy-start | bytes 196
  17.1 29.9 %copy-start.3 = (bf16[2,2,4,128,128]{4,3,2,1,0:T(8,128)(2,1)S(1)}, bf16[2,2,4,128,128]{4,3,2,1,0:T(8,128)(2,1)}, u32[]{:S(2)}) copy-start(bf16[2,2,4,128,128]{4,3,2,1,0:T(8,128)(2,1)} %own_ref.15) | copy-start | bytes 1572868
  31.0 0.8 copy-start.16
  31.8 15.3 %all-to-all-start.1 = ((bf16[16,32,256]{2,1,0:T(8,128)(2,1)}), bf16[16,32,256]{2,1,0:T(8,128)(2,1)S(1)}, u32[]{:S(2)}, u32[]{:S(2)}) async-start(bf16[16,32,256]{2,1,0:T(8,128)(2,1)} %get-tuple-element.27), calls=%async_computation.1 | async-start | bytes 524288 | tf_op jit(solution)/shard_map/all_to_all | solution.py:233
  36.9 2.8 collective-permute-start
  48.6 14.9 %all-to-all-start.2 = ((bf16[16,32,256]{2,1,0:T(8,128)(2,1)}), bf16[16,32,256]{2,1,0:T(8,128)(2,1)S(1)}, u32[]{:S(2)}, u32[]{:S(2)}) async-start(bf16[16,32,256]{2,1,0:T(8,128)(2,1)} %couple_early.7), calls=%async_computation.2 | async-start | bytes 524288 | tf_op jit(solution)/shard_map/all_to_all | solution.py:233
  63.5 1.6 copy-start.4
  66.9 13.9 %all-to-all-start.3 = ((bf16[16,32,256]{2,1,0:T(8,128)(2,1)}), bf16[16,32,256]{2,1,0:T(8,128)(2,1)S(1)}, u32[]{:S(2)}, u32[]{:S(2)}) async-start(bf16[16,32,256]{2,1,0:T(8,128)(2,1)} %get-tuple-element.31), calls=%async_computation.3 | async-start | bytes 524288 | tf_op jit(solution)/shard_map/all_to_all | solution.py:233
  82.4 14.1 %all-to-all-start.4 = ((bf16[16,32,256]{2,1,0:T(8,128)(2,1)}), bf16[16,32,256]{2,1,0:T(8,128)(2,1)S(1)}, u32[]{:S(2)}, u32[]{:S(2)}) async-start(bf16[16,32,256]{2,1,0:T(8,128)(2,1)} %couple_early.8), calls=%async_computation.4 | async-start | bytes 524288 | tf_op jit(solution)/shard_map/all_to_all | solution.py:233
  86.6 2.2 copy-start.1
  89.6 1.4 copy-start.5
  91.0 1.4 copy-start.8
  96.5 1.6 copy-start.9
  98.1 30.2 %copy-start.6 = (bf16[256,4096]{1,0:T(8,128)(2,1)S(1)}, bf16[256,4096]{1,0:T(8,128)(2,1)}, u32[]{:S(2)}) copy-start(bf16[256,4096]{1,0:T(8,128)(2,1)} %copy-done.5) | copy-start | bytes 6291460
  129.4 3.2 collective-permute-start.5
  148.6 14.1 %all-to-all-start.8 = ((bf16[16,32,256]{2,1,0:T(8,128)(2,1)}), bf16[16,32,256]{2,1,0:T(8,128)(2,1)S(1)}, u32[]{:S(2)}, u32[]{:S(2)}) async-start(bf16[16,32,256]{2,1,0:T(8,128)(2,1)} %couple_early.10), calls=%async_computation.8 | async-start | bytes 524288 | tf_op jit(solution)/shard_map/all_to_all | solution.py:233
  152.2 2.2 copy-start.2
  157.1 1.3 copy-start.11
  158.5 1.4 copy-start.13
  162.7 1.6 copy-start.14
  164.3 32.4 %copy-start.12 = (bf16[256,4096]{1,0:T(8,128)(2,1)S(1)}, bf16[256,4096]{1,0:T(8,128)(2,1)}, u32[]{:S(2)}) copy-start(bf16[256,4096]{1,0:T(8,128)(2,1)} %copy-done.11) | copy-start | bytes 6291460
  196.8 31.6 %copy-start.10 = (bf16[256,4096]{1,0:T(8,128)(2,1)S(1)}, bf16[256,4096]{1,0:T(8,128)(2,1)}, u32[]{:S(2)}) copy-start(bf16[256,4096]{1,0:T(8,128)(2,1)} %copy-done.8) | copy-start | bytes 6291460
  212.8 22.1 %copy-start.15 = (bf16[2,512,256]{2,1,0:T(8,128)(2,1)S(1)}, bf16[2,512,256]{2,1,0:T(8,128)(2,1)}, u32[]{:S(2)}) copy-start(bf16[2,512,256]{2,1,0:T(8,128)(2,1)} %param.12) | copy-start | bytes 1572868
  230.1 17.0 %all-to-all-start.13 = ((bf16[16,32,256]{2,1,0:T(8,128)(2,1)}), bf16[16,32,256]{2,1,0:T(8,128)(2,1)S(1)}, u32[]{:S(2)}, u32[]{:S(2)}) async-start(bf16[16,32,256]{2,1,0:T(8,128)(2,1)} %get-tuple-element.44), calls=%async_computation.13 | async-start | bytes 524288 | tf_op jit(solution)/shard_map/all_to_all | solution.py:233
  248.8 16.2 %all-to-all-start.14 = ((bf16[16,32,256]{2,1,0:T(8,128)(2,1)}), bf16[16,32,256]{2,1,0:T(8,128)(2,1)S(1)}, u32[]{:S(2)}, u32[]{:S(2)}) async-start(bf16[16,32,256]{2,1,0:T(8,128)(2,1)} %couple_early.13), calls=%async_computation.14 | async-start | bytes 524288 | tf_op jit(solution)/shard_map/all_to_all | solution.py:233
  253.6 54.7 %copy-start.17 = (s32[64,512]{1,0:T(8,128)S(1)}, s32[64,512]{1,0:T(8,128)}, u32[]{:S(2)}) copy-start(s32[64,512]{1,0:T(8,128)} %param.8) | copy-start | bytes 393220
  264.9 1.6 copy-start.7
  267.8 3.2 collective-permute-start.9
  267.8 4.7 %collective-permute-start.8 = (f32[32,512]{1,0:T(8,128)S(1)}, f32[32,512]{1,0:T(8,128)S(1)}, u32[]{:S(2)}, u32[]{:S(2)}) collective-permute-start(f32[32,512]{1,0:T(8,128)S(1)} %convolution_add_fusion), channel_id=1, source_target_pairs={{0,8},{4,12},{8,0},{12,4},{1,9},{5,13},{9,1},{13,5},{2,10},{6,14},... | collective-permute-start | bytes 196616 | tf_op jit(solution)/shard_map/ppermute | solution.py:198
  269.9 4.3 %collective-permute-start.7 = (f32[32,512]{1,0:T(8,128)S(1)}, f32[32,512]{1,0:T(8,128)S(1)}, u32[]{:S(2)}, u32[]{:S(2)}) collective-permute-start(f32[32,512]{1,0:T(8,128)S(1)} %convolution_add_fusion), channel_id=1, source_target_pairs={{0,4},{4,8},{8,12},{12,0},{1,5},{5,9},{9,13},{13,1},{2,6},{6,10},{... | collective-permute-start | bytes 196616 | tf_op jit(solution)/shard_map/ppermute | solution.py:198
  274.2 6.0 %collective-permute-start.12 = (f32[32,512]{1,0:T(8,128)S(1)}, f32[32,512]{1,0:T(8,128)S(1)}, u32[]{:S(2)}, u32[]{:S(2)}) collective-permute-start(f32[32,512]{1,0:T(8,128)S(1)} %add_add_fusion.1), channel_id=1, source_target_pairs={{0,48},{16,0},{32,16},{48,32},{1,49},{17,1},{33,17},{49,33},{2,50}... | collective-permute-start | bytes 196616 | tf_op jit(solution)/shard_map/ppermute | solution.py:198
  275.5 7.4 %collective-permute-start.11 = (f32[32,512]{1,0:T(8,128)S(1)}, f32[32,512]{1,0:T(8,128)S(1)}, u32[]{:S(2)}, u32[]{:S(2)}) collective-permute-start(f32[32,512]{1,0:T(8,128)S(1)} %add_add_fusion.1), channel_id=1, source_target_pairs={{0,32},{16,48},{32,0},{48,16},{1,33},{17,49},{33,1},{49,17},{2,34}... | collective-permute-start | bytes 196616 | tf_op jit(solution)/shard_map/ppermute | solution.py:198
  279.6 5.5 %collective-permute-start.10 = (f32[32,512]{1,0:T(8,128)S(1)}, f32[32,512]{1,0:T(8,128)S(1)}, u32[]{:S(2)}, u32[]{:S(2)}) collective-permute-start(f32[32,512]{1,0:T(8,128)S(1)} %add_add_fusion.1), channel_id=1, source_target_pairs={{0,16},{16,32},{32,48},{48,0},{1,17},{17,33},{33,49},{49,1},{2,18}... | collective-permute-start | bytes 196616 | tf_op jit(solution)/shard_map/ppermute | solution.py:198
  285.1 23.1 %collective-permute-start.13 = (f32[32,512]{1,0:T(8,128)S(1)}, f32[32,512]{1,0:T(8,128)S(1)}, u32[]{:S(2)}, u32[]{:S(2)}) collective-permute-start(f32[32,512]{1,0:T(8,128)S(1)} %add_add_fusion), channel_id=1, source_target_pairs={{0,128},{128,0},{1,129},{129,1},{2,130},{130,2},{3,131},{131,3},{4... | collective-permute-start | bytes 196616 | tf_op jit(solution)/shard_map/ppermute | solution.py:198
  285.3 27.4 %collective-permute-start.6 = (bf16[2,32,256]{2,1,0:T(8,128)(2,1)S(1)}, bf16[2,32,256]{2,1,0:T(8,128)(2,1)S(1)}, u32[]{:S(2)}, u32[]{:S(2)}) collective-permute-start(bf16[2,32,256]{2,1,0:T(8,128)(2,1)S(1)} %broadcast_select_fusion.7), channel_id=1, source_target_pairs={{0,64},{64,0},{1,65},{65,1},{2,66},{66,2},{3,67},{67,3},{4,68},{68... | collective-permute-start | bytes 98312 | tf_op jit(solution)/shard_map/ppermute | solution.py:205
  308.5 5.1 %collective-permute-start.14 = (f32[32,512]{1,0:T(8,128)S(1)}, f32[32,512]{1,0:T(8,128)S(1)}, u32[]{:S(2)}, u32[]{:S(2)}) collective-permute-start(f32[32,512]{1,0:T(8,128)S(1)} %fusion.3), channel_id=1, source_target_pairs={{0,64},{64,0},{1,65},{65,1},{2,66},{66,2},{3,67},{67,3},{4,68},{68... | collective-permute-start | bytes 196616 | tf_op jit(solution)/shard_map/ppermute | solution.py:205
  314.2 4.5 %collective-permute-start.17 = (f32[8,128]{1,0:T(8,128)S(1)}, f32[8,128]{1,0:T(8,128)S(1)}, u32[]{:S(2)}, u32[]{:S(2)}) collective-permute-start(f32[8,128]{1,0:T(8,128)S(1)} %pad_maximum_fusion.3), channel_id=1, source_target_pairs={{0,3},{1,0},{2,1},{3,2},{4,7},{5,4},{6,5},{7,6},{8,11},{9,8},{10,9... | collective-permute-start | bytes 12296 | tf_op jit(solution)/shard_map/ppermute | solution.py:198
  316.9 4.0 %collective-permute-start.16 = (f32[8,128]{1,0:T(8,128)S(1)}, f32[8,128]{1,0:T(8,128)S(1)}, u32[]{:S(2)}, u32[]{:S(2)}) collective-permute-start(f32[8,128]{1,0:T(8,128)S(1)} %pad_maximum_fusion.3), channel_id=1, source_target_pairs={{0,2},{1,3},{2,0},{3,1},{4,6},{5,7},{6,4},{7,5},{8,10},{9,11},{10,... | collective-permute-start | bytes 12296 | tf_op jit(solution)/shard_map/ppermute | solution.py:198
  317.3 3.7 %collective-permute-start.15 = (f32[8,128]{1,0:T(8,128)S(1)}, f32[8,128]{1,0:T(8,128)S(1)}, u32[]{:S(2)}, u32[]{:S(2)}) collective-permute-start(f32[8,128]{1,0:T(8,128)S(1)} %pad_maximum_fusion.3), channel_id=1, source_target_pairs={{0,1},{1,2},{2,3},{3,0},{4,5},{5,6},{6,7},{7,4},{8,9},{9,10},{10,1... | collective-permute-start | bytes 12296 | tf_op jit(solution)/shard_map/ppermute | solution.py:198

commit v9 on v7

--- a/solution.py
+++ b/solution.py
@@ -22,6 +22,29 @@
     def _():
         for copy in second:
             copy.start()
+
+
+def arrange_kernel(place, *refs, per_core, steps, pieces, slices):
+    own_refs, other_refs = refs[:pieces], refs[pieces : 2 * pieces]
+    outs, sems = refs[-1 - steps : -1], refs[-1]
+
+    def copies(refs, step):
+        return [
+            pltpu.make_async_copy(*slices(ref, k, outs[step], step % per_core), sems.at[step, k])
+            for k, ref in enumerate(refs)
+        ]
+
+    waits = []
+    for step in range(steps):
+        own, other = copies(own_refs, step), copies(other_refs, step)
+        start_one_of(place[0] == step // per_core, own, other)
+        waits += own
+    for copy in waits:
+        copy.wait()
+
+
+def factor_slices(ref, k, out, i):
+    return ref.at[i], out
 
 
 def finish(total, outs):
@@ -102,6 +125,24 @@
 LARGE = pltpu.CompilerParams(vmem_limit_bytes=50 << 20)
 
 
+def arrange(slices, place, own, other, steps, shape, name, after):
+    pieces = len(own)
+    return pl.pallas_call(
+        functools.partial(
+            arrange_kernel, per_core=steps // 2, steps=steps, pieces=pieces, slices=slices
+        ),
+        out_shape=tuple([jax.ShapeDtypeStruct(shape, jnp.bfloat16)] * steps),
+        in_specs=[SMEM] + [HBM] * (2 * pieces + 1),
+        out_specs=tuple([VMEM] * steps),
+        scratch_shapes=[pltpu.SemaphoreType.DMA((steps, pieces))],
+        compiler_params=PARAMS,
+        cost_estimate=pl.CostEstimate(
+            flops=0, transcendentals=0, bytes_accessed=4 * steps * shape[0] * shape[1]
+        ),
+        name=name,
+    )(place, *own, *other, after)
+
+
 def solved_shapes(probes, rows, peers):
     shapes = [jax.ShapeDtypeStruct((probes, rows), jnp.bfloat16)]
     if peers:
@@ -200,18 +241,25 @@
         mine = first if step < own_steps else jnp.logical_not(first)
         return jnp.where(mine, own[step % own_steps], other[step % own_steps])
 
+    blocks = [slice_of(coupling_pair, step, outs[0]) for step in range(steps)]
     results = [outs[0]]
     for turn in range(turns):
         for step in range(1 if turn == 0 else 0, steps):
             if step > 0:
                 pieces = everywhere(outs[1])
-            block = slice_of(coupling_pair, step, outs[0])
+            block = blocks[step]
             resid = couple(own_cols, pieces, own_source[step], block, step)
-            factor = slice_of(factor_pair, step, resid)
+            if turn == 0:
+                factor = slice_of(factor_pair, step, resid)
+            else:
+                factor = factors[step]
             outs = apply_factor(everywhere(resid), factor, step + 1 < steps)
             results.append(outs[0])
         if turn + 1 < turns:
             moved = lax.ppermute(outs[0], "zl", [(turn, turn + 1)])
+            factors = arrange(
+                factor_slices, place, [inverse_factors], [other_factors], steps, inverse_factors.shape[1:], "factors", moved
+            )
             pieces = everywhere(jnp.broadcast_to(moved[None], (peers, probes, local)))
             results = []
 

time: 317 us -> 325 us (1.025)
  blocking collectives: 13.5 us -> 90.9 us
  waiting for transfers between devices: 133 us -> 83.9 us
  starting transfers between devices: 109 us -> 90.6 us
  other arithmetic: 24.1 us -> 12.3 us
  local copies, waits for them, and re-layouts: 5.57 us -> 11.4 us
  Pallas kernels: 25.2 us -> 29.3 us
    all_to_all x1 -> x6, blocking collectives: 13.5 us -> 90.9 us  [everywhere(): return lax.all_to_all(value, NODES, 0, 0)]
    all_to_all x14 -> x9, waiting for transfers between devices: 120 us -> 69 us  [everywhere(): return lax.all_to_all(value, NODES, 0, 0)]
    all_to_all x14 -> x9, starting transfers between devices: 62.5 us -> 46.7 us  [everywhere(): return lax.all_to_all(value, NODES, 0, 0)]
    select_n x12 -> x4, other arithmetic: 20.2 us -> 8.11 us  [slice_of(): return jnp.where(mine, own[step % own_steps], other[step % own_steps])]
    unnamed x23 -> x31, local copies, waits for them, and re-layouts: 2.84 us -> 9.32 us
  transfers between devices with their start and end apart: 32 -> 27, of which waited for: 23 -> 20; matrix products, arithmetic and copies ran while one was open for 8% -> 5% of each run, Pallas kernels for 1% -> 2%
where the time goes in v9:
time: 325 us; the launch traced here: 323 us
  blocking collectives  90.9 us (28%)
  starting transfers between devices  90.6 us (28%)
  waiting for transfers between devices  83.9 us (26%)
  Pallas kernels  29.3 us (9%)
  other arithmetic  12.3 us (4%)
  local copies, waits for them, and re-layouts  11.4 us (4%)
  matrix products  3.82 us (1%)
    all_to_all x6, blocking collectives, everywhere(): return lax.all_to_all(value, NODES, 0, 0)  90.9 us
    all_to_all x9, waiting for transfers between devices, everywhere(): return lax.all_to_all(value, NODES, 0, 0)  69 us
    all_to_all x9, starting transfers between devices, everywhere(): return lax.all_to_all(value, NODES, 0, 0)  46.7 us
    ppermute x7, starting transfers between devices, swap(): return lax.ppermute(value, 'core', [(0, 1), (1, 0)])  31.2 us
    pallas_call x7, Pallas kernels, apply_factor(): pl.pallas_call(apply_kernel, out_shape=shapes, in_specs=[VMEM, VMEM], out...  13.5 us
    ppermute x10, waiting for transfers between devices, line(): lax.ppermute(value, axis, [(i, (i + k) % size) for i in range(size)])  12.3 us
    ppermute x10, starting transfers between devices, line(): lax.ppermute(value, axis, [(i, (i + k) % size) for i in range(size)])  10.7 us
    unnamed x31, local copies, waits for them, and re-layouts  9.32 us
  transfers between devices with their start and end apart: 27, of which 20 were waited for; matrix products, arithmetic and copies ran while one was open for 5% of the time, Pallas kernels for 2%

profile of v9, /device:TPU:1, one launch (start us, length us, event | category | flops | bytes accessed | tf_op | source)
XLA Modules:
  0.0 323.2 jit_solution(3303194240366801692)
XLA Ops:
  1.7 3.3 %collective-permute-start.2 = (bf16[2,32,256]{2,1,0:T(8,128)(2,1)S(1)}, bf16[2,32,256]{2,1,0:T(8,128)(2,1)S(1)}, u32[]{:S(2)}, u32[]{:S(2)}) collective-permute-start(bf16[2,32,256]{2,1,0:T(8,128)(2,1)S(1)} %select_bitcast_fusion.7), channel_id=1, source_target_pairs={{0,64},{64,0},{1,65},{65,1},{2,66},{66,2},{3,67},{67,3},{4,68},{68... | collective-permute-start | bytes 98312 | tf_op jit(solution)/shard_map/ppermute | solution.py:205
  7.1 9.2 %all-to-all-start = ((bf16[16,32,256]{2,1,0:T(8,128)(2,1)}), bf16[16,32,256]{2,1,0:T(8,128)(2,1)S(1)}, u32[]{:S(2)}, u32[]{:S(2)}) async-start(bf16[16,32,256]{2,1,0:T(8,128)(2,1)} %broadcast_in_dim.14), calls=%async_computation | async-start | bytes 524288 | tf_op jit(solution)/shard_map/all_to_all | solution.py:233
  17.2 9.8 %all-to-all-done.r_ref = bf16[16,32,256]{2,1,0:T(8,128)(2,1)S(1)} async-done(((bf16[16,32,256]{2,1,0:T(8,128)(2,1)}), bf16[16,32,256]{2,1,0:T(8,128)(2,1)S(1)}, u32[]{:S(2)}, u32[]{:S(2)}) %all-to-all-start) | async-done | bytes 262176 | tf_op jit(solution)/shard_map/all_to_all | solution.py:233
  27.1 3.9 %apply_early.1 = (bf16[32,256]{1,0:T(8,128)(2,1)}, bf16[16,32,256]{2,1,0:T(8,128)(2,1)}) custom-call(s32[3]{0:T(128)S(1)} %pad_add_fusion.1.place, bf16[16,32,256]{2,1,0:T(8,128)(2,1)S(1)} %all-to-all-done.r_ref, bf16[2,256,4096]{2,1,0:T(8,128)(2,1)} %refs_0_.1, bf16[2,256,4096]{2,1,0:T(8,128)(2,1)} %collective-permute-done.3.other_ref.refs_1_), custom_call_target="tpu_custom_call" | custom-call | tf_op jit(solution)/shard_map/apply_early/pallas_call | solution.py:170
  31.0 5.1 %all-to-all-start.1 = ((bf16[16,32,256]{2,1,0:T(8,128)(2,1)}), bf16[16,32,256]{2,1,0:T(8,128)(2,1)S(1)}, u32[]{:S(2)}, u32[]{:S(2)}) async-start(bf16[16,32,256]{2,1,0:T(8,128)(2,1)} %get-tuple-element.31), calls=%async_computation.1 | async-start | bytes 524288 | tf_op jit(solution)/shard_map/all_to_all | solution.py:233
  37.0 9.2 %all-to-all-done.1.x_ref = bf16[16,32,256]{2,1,0:T(8,128)(2,1)S(1)} async-done(((bf16[16,32,256]{2,1,0:T(8,128)(2,1)}), bf16[16,32,256]{2,1,0:T(8,128)(2,1)S(1)}, u32[]{:S(2)}, u32[]{:S(2)}) %all-to-all-start.1) | async-done | bytes 262176 | tf_op jit(solution)/shard_map/all_to_all | solution.py:233
  47.7 5.0 %all-to-all-start.2 = ((bf16[16,32,256]{2,1,0:T(8,128)(2,1)}), bf16[16,32,256]{2,1,0:T(8,128)(2,1)}, u32[]{:S(2)}, u32[]{:S(2)}) async-start(bf16[16,32,256]{2,1,0:T(8,128)(2,1)} %couple.7), calls=%async_computation.2 | async-start | bytes 524288 | tf_op jit(solution)/shard_map/all_to_all | solution.py:233
  52.7 2.4 select_bitcast_fusion.2.l_ref
  55.2 7.6 %all-to-all-done.2.r_ref = bf16[16,32,256]{2,1,0:T(8,128)(2,1)} async-done(((bf16[16,32,256]{2,1,0:T(8,128)(2,1)}), bf16[16,32,256]{2,1,0:T(8,128)(2,1)}, u32[]{:S(2)}, u32[]{:S(2)}) %all-to-all-start.2) | async-done | bytes 262176 | tf_op jit(solution)/shard_map/all_to_all | solution.py:233
  62.7 2.7 apply.7
  66.1 3.8 %all-to-all-start.3 = ((bf16[16,32,256]{2,1,0:T(8,128)(2,1)}), bf16[16,32,256]{2,1,0:T(8,128)(2,1)S(1)}, u32[]{:S(2)}, u32[]{:S(2)}) async-start(bf16[16,32,256]{2,1,0:T(8,128)(2,1)} %copy-done.9), calls=%async_computation.3 | async-start | bytes 524288 | tf_op jit(solution)/shard_map/all_to_all | solution.py:233
  69.9 10.0 %all-to-all-done.3.x_ref = bf16[16,32,256]{2,1,0:T(8,128)(2,1)S(1)} async-done(((bf16[16,32,256]{2,1,0:T(8,128)(2,1)}), bf16[16,32,256]{2,1,0:T(8,128)(2,1)S(1)}, u32[]{:S(2)}, u32[]{:S(2)}) %all-to-all-start.3) | async-done | bytes 262176 | tf_op jit(solution)/shard_map/all_to_all | solution.py:233
  81.5 4.2 %all-to-all-start.4 = ((bf16[16,32,256]{2,1,0:T(8,128)(2,1)}), bf16[16,32,256]{2,1,0:T(8,128)(2,1)}, u32[]{:S(2)}, u32[]{:S(2)}) async-start(bf16[16,32,256]{2,1,0:T(8,128)(2,1)} %couple.8), calls=%async_computation.4 | async-start | bytes 524288 | tf_op jit(solution)/shard_map/all_to_all | solution.py:233
  85.7 2.4 select_bitcast_fusion.1.l_ref
  88.1 7.6 %all-to-all-done.4.r_ref = bf16[16,32,256]{2,1,0:T(8,128)(2,1)} async-done(((bf16[16,32,256]{2,1,0:T(8,128)(2,1)}), bf16[16,32,256]{2,1,0:T(8,128)(2,1)}, u32[]{:S(2)}, u32[]{:S(2)}) %all-to-all-start.4) | async-done | bytes 262176 | tf_op jit(solution)/shard_map/all_to_all | solution.py:233
  95.7 2.7 apply.8
  98.4 13.6 %all_to_all.75.x_ref = bf16[16,32,256]{2,1,0:T(8,128)(2,1)S(1)} all-to-all(bf16[16,32,256]{2,1,0:T(8,128)(2,1)S(1)} %get-tuple-element.40), channel_id=1, replica_groups=mesh['zl'=2,'core'=2,'zh'=4,'y'=4,'x'=4] {'zh','y'}, dimensions={0} | all-to-all | bytes 524288 | tf_op jit(solution)/shard_map/all_to_all | solution.py:233
  113.5 4.2 %all-to-all-start.6 = ((bf16[16,32,256]{2,1,0:T(8,128)(2,1)}), bf16[16,32,256]{2,1,0:T(8,128)(2,1)}, u32[]{:S(2)}, u32[]{:S(2)}) async-start(bf16[16,32,256]{2,1,0:T(8,128)(2,1)} %couple.9), calls=%async_computation.6 | async-start | bytes 524288 | tf_op jit(solution)/shard_map/all_to_all | solution.py:233
  117.7 2.4 select_bitcast_fusion.l_ref
  120.2 7.5 %all-to-all-done.6.r_ref = bf16[16,32,256]{2,1,0:T(8,128)(2,1)} async-done(((bf16[16,32,256]{2,1,0:T(8,128)(2,1)}), bf16[16,32,256]{2,1,0:T(8,128)(2,1)}, u32[]{:S(2)}, u32[]{:S(2)}) %all-to-all-start.6) | async-done | bytes 262176 | tf_op jit(solution)/shard_map/all_to_all | solution.py:233
  127.7 2.1 apply.9
  129.7 2.0 collective-permute-start.5
  132.7 13.8 %all_to_all.76.x_ref = bf16[16,32,256]{2,1,0:T(8,128)(2,1)S(1)} all-to-all(bf16[16,32,256]{2,1,0:T(8,128)(2,1)S(1)} %broadcast_in_dim.15), channel_id=1, replica_groups=mesh['zl'=2,'core'=2,'zh'=4,'y'=4,'x'=4] {'zh','y'}, dimensions={0} | all-to-all | bytes 524288 | tf_op jit(solution)/shard_map/all_to_all | solution.py:233
  148.0 4.2 %all-to-all-start.8 = ((bf16[16,32,256]{2,1,0:T(8,128)(2,1)}), bf16[16,32,256]{2,1,0:T(8,128)(2,1)}, u32[]{:S(2)}, u32[]{:S(2)}) async-start(bf16[16,32,256]{2,1,0:T(8,128)(2,1)} %couple.10), calls=%async_computation.8 | async-start | bytes 524288 | tf_op jit(solution)/shard_map/all_to_all | solution.py:233
  152.2 2.2 copy-done.1
  154.4 2.8 factors.1
  162.2 1.6 copy-done.7
  163.8 2.2 apply.10
  166.0 17.9 %all_to_all.77.x_ref = bf16[16,32,256]{2,1,0:T(8,128)(2,1)S(1)} all-to-all(bf16[16,32,256]{2,1,0:T(8,128)(2,1)S(1)} %get-tuple-element.45), channel_id=1, replica_groups=mesh['zl'=2,'core'=2,'zh'=4,'y'=4,'x'=4] {'zh','y'}, dimensions={0} | all-to-all | bytes 524288 | tf_op jit(solution)/shard_map/all_to_all | solution.py:233
  184.6 14.6 %all_to_all.78.r_ref = bf16[16,32,256]{2,1,0:T(8,128)(2,1)S(1)} all-to-all(bf16[16,32,256]{2,1,0:T(8,128)(2,1)S(1)} %couple.11), channel_id=1, replica_groups=mesh['zl'=2,'core'=2,'zh'=4,'y'=4,'x'=4] {'zh','y'}, dimensions={0} | all-to-all | bytes 524288 | tf_op jit(solution)/shard_map/all_to_all | solution.py:233
  200.4 16.0 %all_to_all.79.x_ref = bf16[16,32,256]{2,1,0:T(8,128)(2,1)S(1)} all-to-all(bf16[16,32,256]{2,1,0:T(8,128)(2,1)S(1)} %get-tuple-element.48), channel_id=1, replica_groups=mesh['zl'=2,'core'=2,'zh'=4,'y'=4,'x'=4] {'zh','y'}, dimensions={0} | all-to-all | bytes 524288 | tf_op jit(solution)/shard_map/all_to_all | solution.py:233
  217.1 14.9 %all_to_all.80.r_ref = bf16[16,32,256]{2,1,0:T(8,128)(2,1)S(1)} all-to-all(bf16[16,32,256]{2,1,0:T(8,128)(2,1)S(1)} %couple.12), channel_id=1, replica_groups=mesh['zl'=2,'core'=2,'zh'=4,'y'=4,'x'=4] {'zh','y'}, dimensions={0} | all-to-all | bytes 524288 | tf_op jit(solution)/shard_map/all_to_all | solution.py:233
  232.1 1.8 apply.12
  233.9 4.8 %all-to-all-start.13 = ((bf16[16,32,256]{2,1,0:T(8,128)(2,1)}), bf16[16,32,256]{2,1,0:T(8,128)(2,1)S(1)}, u32[]{:S(2)}, u32[]{:S(2)}) async-start(bf16[16,32,256]{2,1,0:T(8,128)(2,1)} %get-tuple-element.51), calls=%async_computation.13 | async-start | bytes 524288 | tf_op jit(solution)/shard_map/all_to_all | solution.py:233
  238.7 2.3 broadcast_select_fusion
  241.0 8.5 %all-to-all-done.13.x_ref = bf16[16,32,256]{2,1,0:T(8,128)(2,1)S(1)} async-done(((bf16[16,32,256]{2,1,0:T(8,128)(2,1)}), bf16[16,32,256]{2,1,0:T(8,128)(2,1)S(1)}, u32[]{:S(2)}, u32[]{:S(2)}) %all-to-all-start.13) | async-done | bytes 262176 | tf_op jit(solution)/shard_map/all_to_all | solution.py:233
  249.5 1.5 couple.13
  251.0 6.2 %all-to-all-start.14 = ((bf16[16,32,256]{2,1,0:T(8,128)(2,1)}), bf16[16,32,256]{2,1,0:T(8,128)(2,1)S(1)}, u32[]{:S(2)}, u32[]{:S(2)}) async-start(bf16[16,32,256]{2,1,0:T(8,128)(2,1)} %couple.13), calls=%async_computation.14 | async-start | bytes 524288 | tf_op jit(solution)/shard_map/all_to_all | solution.py:233
  260.6 7.9 %all-to-all-done.14.r_ref = bf16[16,32,256]{2,1,0:T(8,128)(2,1)S(1)} async-done(((bf16[16,32,256]{2,1,0:T(8,128)(2,1)}), bf16[16,32,256]{2,1,0:T(8,128)(2,1)S(1)}, u32[]{:S(2)}, u32[]{:S(2)}) %all-to-all-start.14) | async-done | bytes 262176 | tf_op jit(solution)/shard_map/all_to_all | solution.py:233
  272.9 2.9 collective-permute-done.8
  276.5 1.7 collective-permute-start.12
  279.2 1.6 collective-permute-start.10
  280.8 2.5 collective-permute-done.12
  283.3 3.0 collective-permute-done.11
  286.8 22.4 %collective-permute-start.6 = (bf16[2,32,256]{2,1,0:T(8,128)(2,1)S(1)}, bf16[2,32,256]{2,1,0:T(8,128)(2,1)S(1)}, u32[]{:S(2)}, u32[]{:S(2)}) collective-permute-start(bf16[2,32,256]{2,1,0:T(8,128)(2,1)S(1)} %broadcast_select_fusion.7), channel_id=1, source_target_pairs={{0,64},{64,0},{1,65},{65,1},{2,66},{66,2},{3,67},{67,3},{4,68},{68... | collective-permute-start | bytes 98312 | tf_op jit(solution)/shard_map/ppermute | solution.py:205
  309.5 4.2 %collective-permute-start.14 = (f32[32,512]{1,0:T(8,128)S(1)}, f32[32,512]{1,0:T(8,128)S(1)}, u32[]{:S(2)}, u32[]{:S(2)}) collective-permute-start(f32[32,512]{1,0:T(8,128)S(1)} %fusion.3), channel_id=1, source_target_pairs={{0,64},{64,0},{1,65},{65,1},{2,66},{66,2},{3,67},{67,3},{4,68},{68... | collective-permute-start | bytes 196616 | tf_op jit(solution)/shard_map/ppermute | solution.py:205
  315.2 2.5 collective-permute-start.17
  319.7 2.1 collective-permute-done.16
  (94 shorter events, 35.3 us)
Async XLA Ops:
  0.6 308.6 %copy-start = (bf16[512,512]{1,0:T(8,128)(2,1)S(1)}, bf16[512,512]{1,0:T(8,128)(2,1)}, u32[]{:S(2)}) copy-start(bf16[512,512]{1,0:T(8,128)(2,1)} %param.13) | copy-start | bytes 1572868
  1.7 4.2 %collective-permute-start.2 = (bf16[2,32,256]{2,1,0:T(8,128)(2,1)S(1)}, bf16[2,32,256]{2,1,0:T(8,128)(2,1)S(1)}, u32[]{:S(2)}, u32[]{:S(2)}) collective-permute-start(bf16[2,32,256]{2,1,0:T(8,128)(2,1)S(1)} %select_bitcast_fusion.7), channel_id=1, source_target_pairs={{0,64},{64,0},{1,65},{65,1},{2,66},{66,2},{3,67},{67,3},{4,68},{68... | collective-permute-start | bytes 98312 | tf_op jit(solution)/shard_map/ppermute | solution.py:205
  6.6 20.5 %collective-permute-start.3 = (bf16[2,256,4096]{2,1,0:T(8,128)(2,1)}, bf16[2,256,4096]{2,1,0:T(8,128)(2,1)}, u32[]{:S(2)}, u32[]{:S(2)}) collective-permute-start(bf16[2,256,4096]{2,1,0:T(8,128)(2,1)} %refs_0_.1), channel_id=1, source_target_pairs={{0,64},{64,0},{1,65},{65,1},{2,66},{66,2},{3,67},{67,3},{4,68},{68... | collective-permute-start | bytes 12582920 | tf_op jit(solution)/shard_map/ppermute | solution.py:205
  7.0 24.0 %collective-permute-start.1 = (bf16[2,512,256]{2,1,0:T(8,128)(2,1)}, bf16[2,512,256]{2,1,0:T(8,128)(2,1)S(1)}, u32[]{:S(2)}, u32[]{:S(2)}) collective-permute-start(bf16[2,512,256]{2,1,0:T(8,128)(2,1)} %param.12), channel_id=1, source_target_pairs={{0,64},{64,0},{1,65},{65,1},{2,66},{66,2},{3,67},{67,3},{4,68},{68... | collective-permute-start | bytes 1572872 | tf_op jit(solution)/shard_map/ppermute | solution.py:205
  7.1 19.9 %all-to-all-start = ((bf16[16,32,256]{2,1,0:T(8,128)(2,1)}), bf16[16,32,256]{2,1,0:T(8,128)(2,1)S(1)}, u32[]{:S(2)}, u32[]{:S(2)}) async-start(bf16[16,32,256]{2,1,0:T(8,128)(2,1)} %broadcast_in_dim.14), calls=%async_computation | async-start | bytes 524288 | tf_op jit(solution)/shard_map/all_to_all | solution.py:233
  16.3 19.9 %collective-permute-start.4 = (bf16[2,2,4,128,128]{4,3,2,1,0:T(8,128)(2,1)}, bf16[2,2,4,128,128]{4,3,2,1,0:T(8,128)(2,1)S(1)}, u32[]{:S(2)}, u32[]{:S(2)}) collective-permute-start(bf16[2,2,4,128,128]{4,3,2,1,0:T(8,128)(2,1)} %param.10), channel_id=1, source_target_pairs={{0,64},{64,0},{1,65},{65,1},{2,66},{66,2},{3,67},{67,3},{4,68},{68... | collective-permute-start | bytes 1572872 | tf_op jit(solution)/shard_map/ppermute | solution.py:205
  17.0 19.1 %collective-permute-start = (s32[2,2,4]{2,1,0:T(2,128)}, s32[2,2,4]{2,1,0:T(2,128)S(1)}, u32[]{:S(2)}, u32[]{:S(2)}) collective-permute-start(s32[2,2,4]{2,1,0:T(2,128)} %param.11), channel_id=1, source_target_pairs={{0,64},{64,0},{1,65},{65,1},{2,66},{66,2},{3,67},{67,3},{4,68},{68... | collective-permute-start | bytes 200 | tf_op jit(solution)/shard_map/ppermute | solution.py:205
  17.2 18.9 %copy-start.14 = (s32[2,2,4]{2,1,0:T(2,128)S(1)}, s32[2,2,4]{2,1,0:T(2,128)}, u32[]{:S(2)}) copy-start(s32[2,2,4]{2,1,0:T(2,128)} %param.11) | copy-start | bytes 196
  17.2 19.0 %copy-start.12 = (bf16[2,2,4,128,128]{4,3,2,1,0:T(8,128)(2,1)S(1)}, bf16[2,2,4,128,128]{4,3,2,1,0:T(8,128)(2,1)}, u32[]{:S(2)}) copy-start(bf16[2,2,4,128,128]{4,3,2,1,0:T(8,128)(2,1)} %param.10) | copy-start | bytes 1572868
  31.0 5.3 %copy-start.11 = (bf16[2,512,256]{2,1,0:T(8,128)(2,1)}, bf16[2,512,256]{2,1,0:T(8,128)(2,1)S(1)}, u32[]{:S(2)}) copy-start(bf16[2,512,256]{2,1,0:T(8,128)(2,1)S(1)} %collective-permute-done.1) | copy-start | bytes 1572868
  31.0 15.3 %all-to-all-start.1 = ((bf16[16,32,256]{2,1,0:T(8,128)(2,1)}), bf16[16,32,256]{2,1,0:T(8,128)(2,1)S(1)}, u32[]{:S(2)}, u32[]{:S(2)}) async-start(bf16[16,32,256]{2,1,0:T(8,128)(2,1)} %get-tuple-element.31), calls=%async_computation.1 | async-start | bytes 524288 | tf_op jit(solution)/shard_map/all_to_all | solution.py:233
  47.7 15.0 %all-to-all-start.2 = ((bf16[16,32,256]{2,1,0:T(8,128)(2,1)}), bf16[16,32,256]{2,1,0:T(8,128)(2,1)}, u32[]{:S(2)}, u32[]{:S(2)}) async-start(bf16[16,32,256]{2,1,0:T(8,128)(2,1)} %couple.7), calls=%async_computation.2 | async-start | bytes 524288 | tf_op jit(solution)/shard_map/all_to_all | solution.py:233
  65.4 0.7 copy-start.9
  66.1 13.9 %all-to-all-start.3 = ((bf16[16,32,256]{2,1,0:T(8,128)(2,1)}), bf16[16,32,256]{2,1,0:T(8,128)(2,1)S(1)}, u32[]{:S(2)}, u32[]{:S(2)}) async-start(bf16[16,32,256]{2,1,0:T(8,128)(2,1)} %copy-done.9), calls=%async_computation.3 | async-start | bytes 524288 | tf_op jit(solution)/shard_map/all_to_all | solution.py:233
  81.5 14.3 %all-to-all-start.4 = ((bf16[16,32,256]{2,1,0:T(8,128)(2,1)}), bf16[16,32,256]{2,1,0:T(8,128)(2,1)}, u32[]{:S(2)}, u32[]{:S(2)}) async-start(bf16[16,32,256]{2,1,0:T(8,128)(2,1)} %couple.8), calls=%async_computation.4 | async-start | bytes 524288 | tf_op jit(solution)/shard_map/all_to_all | solution.py:233
  113.5 14.1 %all-to-all-start.6 = ((bf16[16,32,256]{2,1,0:T(8,128)(2,1)}), bf16[16,32,256]{2,1,0:T(8,128)(2,1)}, u32[]{:S(2)}, u32[]{:S(2)}) async-start(bf16[16,32,256]{2,1,0:T(8,128)(2,1)} %couple.9), calls=%async_computation.6 | async-start | bytes 524288 | tf_op jit(solution)/shard_map/all_to_all | solution.py:233
  127.7 18.9 %copy-start.8 = (bf16[2,4,128,128]{3,2,1,0:T(8,128)(2,1)S(1)}, bf16[2,4,128,128]{3,2,1,0:T(8,128)(2,1)}, u32[]{:S(2)}) copy-start(bf16[2,4,128,128]{3,2,1,0:T(8,128)(2,1)} %get-tuple-element.66.c_ref) | copy-start | bytes 786436
  129.7 2.9 collective-permute-start.5
  148.0 14.2 %all-to-all-start.8 = ((bf16[16,32,256]{2,1,0:T(8,128)(2,1)}), bf16[16,32,256]{2,1,0:T(8,128)(2,1)}, u32[]{:S(2)}, u32[]{:S(2)}) async-start(bf16[16,32,256]{2,1,0:T(8,128)(2,1)} %couple.10), calls=%async_computation.8 | async-start | bytes 524288 | tf_op jit(solution)/shard_map/all_to_all | solution.py:233
  152.2 2.2 copy-start.1
  157.2 1.4 copy-start.2
  158.6 1.4 copy-start.4
  160.0 1.4 copy-start.6
  162.2 1.6 copy-start.7
  163.8 35.5 %copy-start.5 = (bf16[256,4096]{1,0:T(8,128)(2,1)S(1)}, bf16[256,4096]{1,0:T(8,128)(2,1)}, u32[]{:S(2)}) copy-start(bf16[256,4096]{1,0:T(8,128)(2,1)} %copy-done.4) | copy-start | bytes 6291460
  199.3 32.8 %copy-start.3 = (bf16[256,4096]{1,0:T(8,128)(2,1)S(1)}, bf16[256,4096]{1,0:T(8,128)(2,1)}, u32[]{:S(2)}) copy-start(bf16[256,4096]{1,0:T(8,128)(2,1)} %copy-done.2) | copy-start | bytes 6291460
  233.9 15.6 %all-to-all-start.13 = ((bf16[16,32,256]{2,1,0:T(8,128)(2,1)}), bf16[16,32,256]{2,1,0:T(8,128)(2,1)S(1)}, u32[]{:S(2)}, u32[]{:S(2)}) async-start(bf16[16,32,256]{2,1,0:T(8,128)(2,1)} %get-tuple-element.51), calls=%async_computation.13 | async-start | bytes 524288 | tf_op jit(solution)/shard_map/all_to_all | solution.py:233
  251.0 18.6 %copy-start.10 = (bf16[2,512,256]{2,1,0:T(8,128)(2,1)S(1)}, bf16[2,512,256]{2,1,0:T(8,128)(2,1)}, u32[]{:S(2)}) copy-start(bf16[2,512,256]{2,1,0:T(8,128)(2,1)} %get-tuple-element.64) | copy-start | bytes 1572868
  251.0 17.5 %all-to-all-start.14 = ((bf16[16,32,256]{2,1,0:T(8,128)(2,1)}), bf16[16,32,256]{2,1,0:T(8,128)(2,1)S(1)}, u32[]{:S(2)}, u32[]{:S(2)}) async-start(bf16[16,32,256]{2,1,0:T(8,128)(2,1)} %couple.13), calls=%async_computation.14 | async-start | bytes 524288 | tf_op jit(solution)/shard_map/all_to_all | solution.py:233
  268.5 40.7 %copy-start.13 = (s32[64,512]{1,0:T(8,128)S(1)}, s32[64,512]{1,0:T(8,128)}, u32[]{:S(2)}) copy-start(s32[64,512]{1,0:T(8,128)} %param.8) | copy-start | bytes 393220
  269.8 3.2 collective-permute-start.9
  271.2 4.7 %collective-permute-start.8 = (f32[32,512]{1,0:T(8,128)S(1)}, f32[32,512]{1,0:T(8,128)S(1)}, u32[]{:S(2)}, u32[]{:S(2)}) collective-permute-start(f32[32,512]{1,0:T(8,128)S(1)} %convolution_add_fusion), channel_id=1, source_target_pairs={{0,8},{4,12},{8,0},{12,4},{1,9},{5,13},{9,1},{13,5},{2,10},{6,14},... | collective-permute-start | bytes 196616 | tf_op jit(solution)/shard_map/ppermute | solution.py:198
  271.6 4.9 %collective-permute-start.7 = (f32[32,512]{1,0:T(8,128)S(1)}, f32[32,512]{1,0:T(8,128)S(1)}, u32[]{:S(2)}, u32[]{:S(2)}) collective-permute-start(f32[32,512]{1,0:T(8,128)S(1)} %convolution_add_fusion), channel_id=1, source_target_pairs={{0,4},{4,8},{8,12},{12,0},{1,5},{5,9},{9,13},{13,1},{2,6},{6,10},{... | collective-permute-start | bytes 196616 | tf_op jit(solution)/shard_map/ppermute | solution.py:198
  276.5 6.8 %collective-permute-start.12 = (f32[32,512]{1,0:T(8,128)S(1)}, f32[32,512]{1,0:T(8,128)S(1)}, u32[]{:S(2)}, u32[]{:S(2)}) collective-permute-start(f32[32,512]{1,0:T(8,128)S(1)} %add_add_fusion.1), channel_id=1, source_target_pairs={{0,48},{16,0},{32,16},{48,32},{1,49},{17,1},{33,17},{49,33},{2,50}... | collective-permute-start | bytes 196616 | tf_op jit(solution)/shard_map/ppermute | solution.py:198
  278.2 8.1 %collective-permute-start.11 = (f32[32,512]{1,0:T(8,128)S(1)}, f32[32,512]{1,0:T(8,128)S(1)}, u32[]{:S(2)}, u32[]{:S(2)}) collective-permute-start(f32[32,512]{1,0:T(8,128)S(1)} %add_add_fusion.1), channel_id=1, source_target_pairs={{0,32},{16,48},{32,0},{48,16},{1,33},{17,49},{33,1},{49,17},{2,34}... | collective-permute-start | bytes 196616 | tf_op jit(solution)/shard_map/ppermute | solution.py:198
  279.2 7.4 %collective-permute-start.10 = (f32[32,512]{1,0:T(8,128)S(1)}, f32[32,512]{1,0:T(8,128)S(1)}, u32[]{:S(2)}, u32[]{:S(2)}) collective-permute-start(f32[32,512]{1,0:T(8,128)S(1)} %add_add_fusion.1), channel_id=1, source_target_pairs={{0,16},{16,32},{32,48},{48,0},{1,17},{17,33},{33,49},{49,1},{2,18}... | collective-permute-start | bytes 196616 | tf_op jit(solution)/shard_map/ppermute | solution.py:198
  286.7 22.5 %collective-permute-start.13 = (f32[32,512]{1,0:T(8,128)S(1)}, f32[32,512]{1,0:T(8,128)S(1)}, u32[]{:S(2)}, u32[]{:S(2)}) collective-permute-start(f32[32,512]{1,0:T(8,128)S(1)} %add_add_fusion), channel_id=1, source_target_pairs={{0,128},{128,0},{1,129},{129,1},{2,130},{130,2},{3,131},{131,3},{4... | collective-permute-start | bytes 196616 | tf_op jit(solution)/shard_map/ppermute | solution.py:198
  286.8 26.8 %collective-permute-start.6 = (bf16[2,32,256]{2,1,0:T(8,128)(2,1)S(1)}, bf16[2,32,256]{2,1,0:T(8,128)(2,1)S(1)}, u32[]{:S(2)}, u32[]{:S(2)}) collective-permute-start(bf16[2,32,256]{2,1,0:T(8,128)(2,1)S(1)} %broadcast_select_fusion.7), channel_id=1, source_target_pairs={{0,64},{64,0},{1,65},{65,1},{2,66},{66,2},{3,67},{67,3},{4,68},{68... | collective-permute-start | bytes 98312 | tf_op jit(solution)/shard_map/ppermute | solution.py:205
  309.5 5.1 %collective-permute-start.14 = (f32[32,512]{1,0:T(8,128)S(1)}, f32[32,512]{1,0:T(8,128)S(1)}, u32[]{:S(2)}, u32[]{:S(2)}) collective-permute-start(f32[32,512]{1,0:T(8,128)S(1)} %fusion.3), channel_id=1, source_target_pairs={{0,64},{64,0},{1,65},{65,1},{2,66},{66,2},{3,67},{67,3},{4,68},{68... | collective-permute-start | bytes 196616 | tf_op jit(solution)/shard_map/ppermute | solution.py:205
  315.2 4.5 %collective-permute-start.17 = (f32[8,128]{1,0:T(8,128)S(1)}, f32[8,128]{1,0:T(8,128)S(1)}, u32[]{:S(2)}, u32[]{:S(2)}) collective-permute-start(f32[8,128]{1,0:T(8,128)S(1)} %pad_maximum_fusion.3), channel_id=1, source_target_pairs={{0,3},{1,0},{2,1},{3,2},{4,7},{5,4},{6,5},{7,6},{8,11},{9,8},{10,9... | collective-permute-start | bytes 12296 | tf_op jit(solution)/shard_map/ppermute | solution.py:198
  317.8 4.0 %collective-permute-start.16 = (f32[8,128]{1,0:T(8,128)S(1)}, f32[8,128]{1,0:T(8,128)S(1)}, u32[]{:S(2)}, u32[]{:S(2)}) collective-permute-start(f32[8,128]{1,0:T(8,128)S(1)} %pad_maximum_fusion.3), channel_id=1, source_target_pairs={{0,2},{1,3},{2,0},{3,1},{4,6},{5,7},{6,4},{7,5},{8,10},{9,11},{10,... | collective-permute-start | bytes 12296 | tf_op jit(solution)/shard_map/ppermute | solution.py:198
  318.3 3.7 %collective-permute-start.15 = (f32[8,128]{1,0:T(8,128)S(1)}, f32[8,128]{1,0:T(8,128)S(1)}, u32[]{:S(2)}, u32[]{:S(2)}) collective-permute-start(f32[8,128]{1,0:T(8,128)S(1)} %pad_maximum_fusion.3), channel_id=1, source_target_pairs={{0,1},{1,2},{2,3},{3,0},{4,5},{5,6},{6,7},{7,4},{8,9},{9,10},{10,1... | collective-permute-start | bytes 12296 | tf_op jit(solution)/shard_map/ppermute | solution.py:198

commit v10 on v6

--- a/solution.py
+++ b/solution.py
@@ -242,8 +242,6 @@
         for step in range(1 if turn == 0 else 0, steps):
             if step > 0:
                 pieces = everywhere(outs[1])
-            if turn == 0 and step == 1:
-                pieces, *factors = lax.optimization_barrier((pieces, *factors))
             resid = couple_early(
                 place, own_cols, pieces, own_source[step], couplings, other_couplings, step
             )

time: 315 us -> 318 us (level)
  blocking collectives: 145 us -> 127 us
  starting transfers between devices: 75.7 us -> 87.4 us
  waiting for transfers between devices: 52.8 us -> 59.2 us
    all_to_all x10 -> x9, blocking collectives: 145 us -> 127 us  [everywhere(): return lax.all_to_all(value, NODES, 0, 0)]
    all_to_all x5 -> x6, starting transfers between devices: 28.3 us -> 38.2 us  [everywhere(): return lax.all_to_all(value, NODES, 0, 0)]
    all_to_all x5 -> x6, waiting for transfers between devices: 42.2 us -> 48.6 us  [everywhere(): return lax.all_to_all(value, NODES, 0, 0)]
  transfers between devices with their start and end apart: 23 -> 24, of which waited for: 13 -> 15; matrix products, arithmetic and copies ran while one was open for 1% -> 1% of each run, Pallas kernels for 2% -> 2%
where the time goes in v10:
time: 318 us; the launch traced here: 316 us
  blocking collectives  127 us (40%)
  starting transfers between devices  87.4 us (27%)
  waiting for transfers between devices  59.2 us (19%)
  Pallas kernels  23.9 us (8%)
  local copies, waits for them, and re-layouts  13.6 us (4%)
    all_to_all x9, blocking collectives, everywhere(): return lax.all_to_all(value, NODES, 0, 0)  127 us
    all_to_all x6, waiting for transfers between devices, everywhere(): return lax.all_to_all(value, NODES, 0, 0)  48.6 us
    all_to_all x6, starting transfers between devices, everywhere(): return lax.all_to_all(value, NODES, 0, 0)  38.2 us
    ppermute x7, starting transfers between devices, swap(): return lax.ppermute(value, 'core', [(0, 1), (1, 0)])  33.6 us
    ppermute x10, starting transfers between devices, line(): lax.ppermute(value, axis, [(i, (i + k) % size) for i in range(size)])  13.4 us
    unnamed x35, local copies, waits for them, and re-layouts  11.5 us
    pallas_call x7, Pallas kernels, apply_factor(): pl.pallas_call(apply_kernel, out_shape=shapes, in_specs=[VMEM, VMEM], out...  9.65 us
    pallas_call x7, Pallas kernels, couple_early(): pl.pallas_call(functools.partial(early_couple_kernel, step=step, per_core...  7.6 us
  transfers between devices with their start and end apart: 24, of which 15 were waited for; matrix products, arithmetic and copies ran while one was open for 1% of the time, Pallas kernels for 2%

profile of v10, /device:TPU:1, one launch (start us, length us, event | category | flops | bytes accessed | tf_op | source)
XLA Modules:
  0.0 316.4 jit_solution(742761385675387424)
XLA Ops:
  1.7 3.3 %collective-permute-start.2 = (bf16[2,32,256]{2,1,0:T(8,128)(2,1)S(1)}, bf16[2,32,256]{2,1,0:T(8,128)(2,1)S(1)}, u32[]{:S(2)}, u32[]{:S(2)}) collective-permute-start(bf16[2,32,256]{2,1,0:T(8,128)(2,1)S(1)} %select_bitcast_fusion), channel_id=1, source_target_pairs={{0,64},{64,0},{1,65},{65,1},{2,66},{66,2},{3,67},{67,3},{4,68},{68... | collective-permute-start | bytes 98312 | tf_op jit(solution)/shard_map/ppermute | solution.py:205
  7.1 9.2 %all-to-all-start = ((bf16[16,32,256]{2,1,0:T(8,128)(2,1)}), bf16[16,32,256]{2,1,0:T(8,128)(2,1)S(1)}, u32[]{:S(2)}, u32[]{:S(2)}) async-start(bf16[16,32,256]{2,1,0:T(8,128)(2,1)} %broadcast_in_dim.14), calls=%async_computation | async-start | bytes 524288 | tf_op jit(solution)/shard_map/all_to_all | solution.py:233
  17.1 9.9 %all-to-all-done.r_ref = bf16[16,32,256]{2,1,0:T(8,128)(2,1)S(1)} async-done(((bf16[16,32,256]{2,1,0:T(8,128)(2,1)}), bf16[16,32,256]{2,1,0:T(8,128)(2,1)S(1)}, u32[]{:S(2)}, u32[]{:S(2)}) %all-to-all-start) | async-done | bytes 262176 | tf_op jit(solution)/shard_map/all_to_all | solution.py:233
  27.1 3.8 %apply_early.1 = (bf16[32,256]{1,0:T(8,128)(2,1)S(1)}, bf16[16,32,256]{2,1,0:T(8,128)(2,1)}) custom-call(s32[3]{0:T(128)S(1)} %pad_add_fusion.1.place, bf16[16,32,256]{2,1,0:T(8,128)(2,1)S(1)} %all-to-all-done.r_ref, bf16[2,256,4096]{2,1,0:T(8,128)(2,1)} %refs_0_.1, bf16[2,256,4096]{2,1,0:T(8,128)(2,1)} %collective-permute-done.3.other_ref.refs_1_), custom_call_target="tpu_custom_call" | custom-call | tf_op jit(solution)/shard_map/apply_early/pallas_call | solution.py:169
  30.9 5.1 %all-to-all-start.1 = ((bf16[16,32,256]{2,1,0:T(8,128)(2,1)}), bf16[16,32,256]{2,1,0:T(8,128)(2,1)S(1)}, u32[]{:S(2)}, u32[]{:S(2)}) async-start(bf16[16,32,256]{2,1,0:T(8,128)(2,1)} %get-tuple-element.25), calls=%async_computation.1 | async-start | bytes 524288 | tf_op jit(solution)/shard_map/all_to_all | solution.py:233
  36.0 1.9 collective-permute-start
  38.9 7.3 %all-to-all-done.1.x_ref = bf16[16,32,256]{2,1,0:T(8,128)(2,1)S(1)} async-done(((bf16[16,32,256]{2,1,0:T(8,128)(2,1)}), bf16[16,32,256]{2,1,0:T(8,128)(2,1)S(1)}, u32[]{:S(2)}, u32[]{:S(2)}) %all-to-all-start.1) | async-done | bytes 262176 | tf_op jit(solution)/shard_map/all_to_all | solution.py:233
  46.2 1.6 couple_early.7
  47.8 4.9 %all-to-all-start.2 = ((bf16[16,32,256]{2,1,0:T(8,128)(2,1)}), bf16[16,32,256]{2,1,0:T(8,128)(2,1)S(1)}, u32[]{:S(2)}, u32[]{:S(2)}) async-start(bf16[16,32,256]{2,1,0:T(8,128)(2,1)} %couple_early.7), calls=%async_computation.2 | async-start | bytes 524288 | tf_op jit(solution)/shard_map/all_to_all | solution.py:233
  52.7 2.2 copy-done.2
  54.9 2.8 factors.1
  57.7 1.3 copy-done.3
  59.1 1.4 copy-done.6
  60.4 1.4 copy-done.8
  61.8 1.4 copy-done.11
  63.2 1.6 copy-done.9
  64.8 1.8 apply.7
  66.6 9.1 %all-to-all-start.3 = ((bf16[16,32,256]{2,1,0:T(8,128)(2,1)}), bf16[16,32,256]{2,1,0:T(8,128)(2,1)S(1)}, u32[]{:S(2)}, u32[]{:S(2)}) async-start(bf16[16,32,256]{2,1,0:T(8,128)(2,1)} %get-tuple-element.28), calls=%async_computation.3 | async-start | bytes 524288 | tf_op jit(solution)/shard_map/all_to_all | solution.py:233
  75.7 10.0 %all-to-all-done.3.x_ref = bf16[16,32,256]{2,1,0:T(8,128)(2,1)S(1)} async-done(((bf16[16,32,256]{2,1,0:T(8,128)(2,1)}), bf16[16,32,256]{2,1,0:T(8,128)(2,1)S(1)}, u32[]{:S(2)}, u32[]{:S(2)}) %all-to-all-start.3) | async-done | bytes 262176 | tf_op jit(solution)/shard_map/all_to_all | solution.py:233
  86.5 13.7 %all_to_all.75.r_ref = bf16[16,32,256]{2,1,0:T(8,128)(2,1)S(1)} all-to-all(bf16[16,32,256]{2,1,0:T(8,128)(2,1)S(1)} %couple_early.8), channel_id=1, replica_groups=mesh['zl'=2,'core'=2,'zh'=4,'y'=4,'x'=4] {'zh','y'}, dimensions={0} | all-to-all | bytes 524288 | tf_op jit(solution)/shard_map/all_to_all | solution.py:233
  100.2 1.7 apply.8
  101.9 13.7 %all_to_all.76.x_ref = bf16[16,32,256]{2,1,0:T(8,128)(2,1)S(1)} all-to-all(bf16[16,32,256]{2,1,0:T(8,128)(2,1)S(1)} %get-tuple-element.30), channel_id=1, replica_groups=mesh['zl'=2,'core'=2,'zh'=4,'y'=4,'x'=4] {'zh','y'}, dimensions={0} | all-to-all | bytes 524288 | tf_op jit(solution)/shard_map/all_to_all | solution.py:233
  116.4 13.6 %all_to_all.77.r_ref = bf16[16,32,256]{2,1,0:T(8,128)(2,1)S(1)} all-to-all(bf16[16,32,256]{2,1,0:T(8,128)(2,1)S(1)} %couple_early.9), channel_id=1, replica_groups=mesh['zl'=2,'core'=2,'zh'=4,'y'=4,'x'=4] {'zh','y'}, dimensions={0} | all-to-all | bytes 524288 | tf_op jit(solution)/shard_map/all_to_all | solution.py:233
  131.2 2.3 collective-permute-start.5
  134.3 13.7 %all_to_all.78.x_ref = bf16[16,32,256]{2,1,0:T(8,128)(2,1)S(1)} all-to-all(bf16[16,32,256]{2,1,0:T(8,128)(2,1)S(1)} %broadcast_in_dim.15), channel_id=1, replica_groups=mesh['zl'=2,'core'=2,'zh'=4,'y'=4,'x'=4] {'zh','y'}, dimensions={0} | all-to-all | bytes 524288 | tf_op jit(solution)/shard_map/all_to_all | solution.py:233
  148.9 14.2 %all_to_all.79.r_ref = bf16[16,32,256]{2,1,0:T(8,128)(2,1)S(1)} all-to-all(bf16[16,32,256]{2,1,0:T(8,128)(2,1)S(1)} %couple_early.10), channel_id=1, replica_groups=mesh['zl'=2,'core'=2,'zh'=4,'y'=4,'x'=4] {'zh','y'}, dimensions={0} | all-to-all | bytes 524288 | tf_op jit(solution)/shard_map/all_to_all | solution.py:233
  164.2 14.0 %all_to_all.80.x_ref = bf16[16,32,256]{2,1,0:T(8,128)(2,1)S(1)} all-to-all(bf16[16,32,256]{2,1,0:T(8,128)(2,1)S(1)} %get-tuple-element.34), channel_id=1, replica_groups=mesh['zl'=2,'core'=2,'zh'=4,'y'=4,'x'=4] {'zh','y'}, dimensions={0} | all-to-all | bytes 524288 | tf_op jit(solution)/shard_map/all_to_all | solution.py:233
  179.0 14.0 %all_to_all.81.r_ref = bf16[16,32,256]{2,1,0:T(8,128)(2,1)S(1)} all-to-all(bf16[16,32,256]{2,1,0:T(8,128)(2,1)S(1)} %couple_early.11), channel_id=1, replica_groups=mesh['zl'=2,'core'=2,'zh'=4,'y'=4,'x'=4] {'zh','y'}, dimensions={0} | all-to-all | bytes 524288 | tf_op jit(solution)/shard_map/all_to_all | solution.py:233
  194.2 15.6 %all_to_all.82.x_ref = bf16[16,32,256]{2,1,0:T(8,128)(2,1)S(1)} all-to-all(bf16[16,32,256]{2,1,0:T(8,128)(2,1)S(1)} %get-tuple-element.36), channel_id=1, replica_groups=mesh['zl'=2,'core'=2,'zh'=4,'y'=4,'x'=4] {'zh','y'}, dimensions={0} | all-to-all | bytes 524288 | tf_op jit(solution)/shard_map/all_to_all | solution.py:233
  210.7 14.8 %all_to_all.83.r_ref = bf16[16,32,256]{2,1,0:T(8,128)(2,1)S(1)} all-to-all(bf16[16,32,256]{2,1,0:T(8,128)(2,1)S(1)} %couple_early.12), channel_id=1, replica_groups=mesh['zl'=2,'core'=2,'zh'=4,'y'=4,'x'=4] {'zh','y'}, dimensions={0} | all-to-all | bytes 524288 | tf_op jit(solution)/shard_map/all_to_all | solution.py:233
  225.5 1.8 apply.12
  227.3 5.2 %all-to-all-start.13 = ((bf16[16,32,256]{2,1,0:T(8,128)(2,1)}), bf16[16,32,256]{2,1,0:T(8,128)(2,1)S(1)}, u32[]{:S(2)}, u32[]{:S(2)}) async-start(bf16[16,32,256]{2,1,0:T(8,128)(2,1)} %get-tuple-element.38), calls=%async_computation.13 | async-start | bytes 524288 | tf_op jit(solution)/shard_map/all_to_all | solution.py:233
  233.6 10.6 %all-to-all-done.13.x_ref = bf16[16,32,256]{2,1,0:T(8,128)(2,1)S(1)} async-done(((bf16[16,32,256]{2,1,0:T(8,128)(2,1)}), bf16[16,32,256]{2,1,0:T(8,128)(2,1)S(1)}, u32[]{:S(2)}, u32[]{:S(2)}) %all-to-all-start.13) | async-done | bytes 262176 | tf_op jit(solution)/shard_map/all_to_all | solution.py:233
  244.2 1.6 couple_early.13
  245.8 4.8 %all-to-all-start.14 = ((bf16[16,32,256]{2,1,0:T(8,128)(2,1)}), bf16[16,32,256]{2,1,0:T(8,128)(2,1)S(1)}, u32[]{:S(2)}, u32[]{:S(2)}) async-start(bf16[16,32,256]{2,1,0:T(8,128)(2,1)} %couple_early.13), calls=%async_computation.14 | async-start | bytes 524288 | tf_op jit(solution)/shard_map/all_to_all | solution.py:233
  251.2 10.8 %all-to-all-done.14.r_ref = bf16[16,32,256]{2,1,0:T(8,128)(2,1)S(1)} async-done(((bf16[16,32,256]{2,1,0:T(8,128)(2,1)}), bf16[16,32,256]{2,1,0:T(8,128)(2,1)S(1)}, u32[]{:S(2)}, u32[]{:S(2)}) %all-to-all-start.14) | async-done | bytes 262176 | tf_op jit(solution)/shard_map/all_to_all | solution.py:233
  262.0 1.6 copy-done.5
  264.9 2.2 collective-permute-start.8
  267.0 1.2 collective-permute-start.9
  268.2 1.6 collective-permute-done.7
  270.6 4.0 %collective-permute-start.11 = (f32[32,512]{1,0:T(8,128)S(1)}, f32[32,512]{1,0:T(8,128)S(1)}, u32[]{:S(2)}, u32[]{:S(2)}) collective-permute-start(f32[32,512]{1,0:T(8,128)S(1)} %add_add_fusion.1), channel_id=1, source_target_pairs={{0,32},{16,48},{32,0},{48,16},{1,33},{17,49},{33,1},{49,17},{2,34}... | collective-permute-start | bytes 196616 | tf_op jit(solution)/shard_map/ppermute | solution.py:198
  274.6 1.6 collective-permute-start.12
  277.4 2.3 collective-permute-done.11
  279.8 23.4 %collective-permute-start.6 = (bf16[2,32,256]{2,1,0:T(8,128)(2,1)S(1)}, bf16[2,32,256]{2,1,0:T(8,128)(2,1)S(1)}, u32[]{:S(2)}, u32[]{:S(2)}) collective-permute-start(bf16[2,32,256]{2,1,0:T(8,128)(2,1)S(1)} %broadcast_select_fusion.7), channel_id=1, source_target_pairs={{0,64},{64,0},{1,65},{65,1},{2,66},{66,2},{3,67},{67,3},{4,68},{68... | collective-permute-start | bytes 98312 | tf_op jit(solution)/shard_map/ppermute | solution.py:205
  303.4 3.7 %collective-permute-start.14 = (f32[32,512]{1,0:T(8,128)S(1)}, f32[32,512]{1,0:T(8,128)S(1)}, u32[]{:S(2)}, u32[]{:S(2)}) collective-permute-start(f32[32,512]{1,0:T(8,128)S(1)} %fusion.3), channel_id=1, source_target_pairs={{0,64},{64,0},{1,65},{65,1},{2,66},{66,2},{3,67},{67,3},{4,68},{68... | collective-permute-start | bytes 196616 | tf_op jit(solution)/shard_map/ppermute | solution.py:205
  308.8 1.3 collective-permute-start.15
  310.0 2.4 collective-permute-start.16
  314.0 1.2 collective-permute-done.17
  (91 shorter events, 22.9 us)
Async XLA Ops:
  0.6 302.5 %copy-start = (bf16[512,512]{1,0:T(8,128)(2,1)S(1)}, bf16[512,512]{1,0:T(8,128)(2,1)}, u32[]{:S(2)}) copy-start(bf16[512,512]{1,0:T(8,128)(2,1)} %param.13) | copy-start | bytes 1572868
  1.7 4.2 %collective-permute-start.2 = (bf16[2,32,256]{2,1,0:T(8,128)(2,1)S(1)}, bf16[2,32,256]{2,1,0:T(8,128)(2,1)S(1)}, u32[]{:S(2)}, u32[]{:S(2)}) collective-permute-start(bf16[2,32,256]{2,1,0:T(8,128)(2,1)S(1)} %select_bitcast_fusion), channel_id=1, source_target_pairs={{0,64},{64,0},{1,65},{65,1},{2,66},{66,2},{3,67},{67,3},{4,68},{68... | collective-permute-start | bytes 98312 | tf_op jit(solution)/shard_map/ppermute | solution.py:205
  6.6 20.5 %collective-permute-start.3 = (bf16[2,256,4096]{2,1,0:T(8,128)(2,1)}, bf16[2,256,4096]{2,1,0:T(8,128)(2,1)}, u32[]{:S(2)}, u32[]{:S(2)}) collective-permute-start(bf16[2,256,4096]{2,1,0:T(8,128)(2,1)} %refs_0_.1), channel_id=1, source_target_pairs={{0,64},{64,0},{1,65},{65,1},{2,66},{66,2},{3,67},{67,3},{4,68},{68... | collective-permute-start | bytes 12582920 | tf_op jit(solution)/shard_map/ppermute | solution.py:205
  6.9 23.9 %collective-permute-start.1 = (bf16[2,512,256]{2,1,0:T(8,128)(2,1)}, bf16[2,512,256]{2,1,0:T(8,128)(2,1)S(1)}, u32[]{:S(2)}, u32[]{:S(2)}) collective-permute-start(bf16[2,512,256]{2,1,0:T(8,128)(2,1)} %param.12), channel_id=1, source_target_pairs={{0,64},{64,0},{1,65},{65,1},{2,66},{66,2},{3,67},{67,3},{4,68},{68... | collective-permute-start | bytes 1572872 | tf_op jit(solution)/shard_map/ppermute | solution.py:205
  7.1 19.9 %all-to-all-start = ((bf16[16,32,256]{2,1,0:T(8,128)(2,1)}), bf16[16,32,256]{2,1,0:T(8,128)(2,1)S(1)}, u32[]{:S(2)}, u32[]{:S(2)}) async-start(bf16[16,32,256]{2,1,0:T(8,128)(2,1)} %broadcast_in_dim.14), calls=%async_computation | async-start | bytes 524288 | tf_op jit(solution)/shard_map/all_to_all | solution.py:233
  16.3 22.6 %collective-permute-start.4 = (bf16[2,2,4,128,128]{4,3,2,1,0:T(8,128)(2,1)}, bf16[2,2,4,128,128]{4,3,2,1,0:T(8,128)(2,1)S(1)}, u32[]{:S(2)}, u32[]{:S(2)}) collective-permute-start(bf16[2,2,4,128,128]{4,3,2,1,0:T(8,128)(2,1)} %own_ref.15), channel_id=1, source_target_pairs={{0,64},{64,0},{1,65},{65,1},{2,66},{66,2},{3,67},{67,3},{4,68},{68... | collective-permute-start | bytes 1572872 | tf_op jit(solution)/shard_map/ppermute | solution.py:205
  17.1 18.9 %copy-start.16 = (s32[2,2,4]{2,1,0:T(2,128)S(1)}, s32[2,2,4]{2,1,0:T(2,128)}, u32[]{:S(2)}) copy-start(s32[2,2,4]{2,1,0:T(2,128)} %param.11) | copy-start | bytes 196
  17.1 29.1 %copy-start.1 = (bf16[2,2,4,128,128]{4,3,2,1,0:T(8,128)(2,1)S(1)}, bf16[2,2,4,128,128]{4,3,2,1,0:T(8,128)(2,1)}, u32[]{:S(2)}) copy-start(bf16[2,2,4,128,128]{4,3,2,1,0:T(8,128)(2,1)} %own_ref.15) | copy-start | bytes 1572868
  30.9 26.8 %copy-start.14 = (bf16[2,512,256]{2,1,0:T(8,128)(2,1)}, bf16[2,512,256]{2,1,0:T(8,128)(2,1)S(1)}, u32[]{:S(2)}) copy-start(bf16[2,512,256]{2,1,0:T(8,128)(2,1)S(1)} %collective-permute-done.1) | copy-start | bytes 1572868
  30.9 15.3 %all-to-all-start.1 = ((bf16[16,32,256]{2,1,0:T(8,128)(2,1)}), bf16[16,32,256]{2,1,0:T(8,128)(2,1)S(1)}, u32[]{:S(2)}, u32[]{:S(2)}) async-start(bf16[16,32,256]{2,1,0:T(8,128)(2,1)} %get-tuple-element.25), calls=%async_computation.1 | async-start | bytes 524288 | tf_op jit(solution)/shard_map/all_to_all | solution.py:233
  36.0 2.8 collective-permute-start
  47.8 15.4 %all-to-all-start.2 = ((bf16[16,32,256]{2,1,0:T(8,128)(2,1)}), bf16[16,32,256]{2,1,0:T(8,128)(2,1)S(1)}, u32[]{:S(2)}, u32[]{:S(2)}) async-start(bf16[16,32,256]{2,1,0:T(8,128)(2,1)} %couple_early.7), calls=%async_computation.2 | async-start | bytes 524288 | tf_op jit(solution)/shard_map/all_to_all | solution.py:233
  52.7 2.2 copy-start.2
  57.7 1.3 copy-start.3
  59.1 1.4 copy-start.6
  60.4 1.4 copy-start.8
  61.8 1.4 copy-start.11
  63.2 1.6 copy-start.9
  66.6 19.0 %all-to-all-start.3 = ((bf16[16,32,256]{2,1,0:T(8,128)(2,1)}), bf16[16,32,256]{2,1,0:T(8,128)(2,1)S(1)}, u32[]{:S(2)}, u32[]{:S(2)}) async-start(bf16[16,32,256]{2,1,0:T(8,128)(2,1)} %get-tuple-element.28), calls=%async_computation.3 | async-start | bytes 524288 | tf_op jit(solution)/shard_map/all_to_all | solution.py:233
  85.6 14.5 %copy-start.7 = (bf16[256,4096]{1,0:T(8,128)(2,1)S(1)}, bf16[256,4096]{1,0:T(8,128)(2,1)}, u32[]{:S(2)}) copy-start(bf16[256,4096]{1,0:T(8,128)(2,1)} %copy-done.6) | copy-start | bytes 6291460
  100.2 29.9 %copy-start.4 = (bf16[256,4096]{1,0:T(8,128)(2,1)S(1)}, bf16[256,4096]{1,0:T(8,128)(2,1)}, u32[]{:S(2)}) copy-start(bf16[256,4096]{1,0:T(8,128)(2,1)} %copy-done.3) | copy-start | bytes 6291460
  130.1 33.0 %copy-start.12 = (bf16[256,4096]{1,0:T(8,128)(2,1)S(1)}, bf16[256,4096]{1,0:T(8,128)(2,1)}, u32[]{:S(2)}) copy-start(bf16[256,4096]{1,0:T(8,128)(2,1)} %copy-done.11) | copy-start | bytes 6291460
  131.2 3.1 collective-permute-start.5
  163.1 30.0 %copy-start.10 = (bf16[256,4096]{1,0:T(8,128)(2,1)S(1)}, bf16[256,4096]{1,0:T(8,128)(2,1)}, u32[]{:S(2)}) copy-start(bf16[256,4096]{1,0:T(8,128)(2,1)} %copy-done.8) | copy-start | bytes 6291460
  210.7 21.8 %copy-start.13 = (bf16[2,512,256]{2,1,0:T(8,128)(2,1)S(1)}, bf16[2,512,256]{2,1,0:T(8,128)(2,1)}, u32[]{:S(2)}) copy-start(bf16[2,512,256]{2,1,0:T(8,128)(2,1)} %param.12) | copy-start | bytes 1572868
  227.3 16.9 %all-to-all-start.13 = ((bf16[16,32,256]{2,1,0:T(8,128)(2,1)}), bf16[16,32,256]{2,1,0:T(8,128)(2,1)S(1)}, u32[]{:S(2)}, u32[]{:S(2)}) async-start(bf16[16,32,256]{2,1,0:T(8,128)(2,1)} %get-tuple-element.38), calls=%async_computation.13 | async-start | bytes 524288 | tf_op jit(solution)/shard_map/all_to_all | solution.py:233
  245.8 16.2 %all-to-all-start.14 = ((bf16[16,32,256]{2,1,0:T(8,128)(2,1)}), bf16[16,32,256]{2,1,0:T(8,128)(2,1)S(1)}, u32[]{:S(2)}, u32[]{:S(2)}) async-start(bf16[16,32,256]{2,1,0:T(8,128)(2,1)} %couple_early.13), calls=%async_computation.14 | async-start | bytes 524288 | tf_op jit(solution)/shard_map/all_to_all | solution.py:233
  250.8 52.4 %copy-start.15 = (s32[64,512]{1,0:T(8,128)S(1)}, s32[64,512]{1,0:T(8,128)}, u32[]{:S(2)}) copy-start(s32[64,512]{1,0:T(8,128)} %param.8) | copy-start | bytes 393220
  262.0 1.6 copy-start.5
  264.8 5.1 %collective-permute-start.7 = (f32[32,512]{1,0:T(8,128)S(1)}, f32[32,512]{1,0:T(8,128)S(1)}, u32[]{:S(2)}, u32[]{:S(2)}) collective-permute-start(f32[32,512]{1,0:T(8,128)S(1)} %convolution_add_fusion), channel_id=1, source_target_pairs={{0,4},{4,8},{8,12},{12,0},{1,5},{5,9},{9,13},{13,1},{2,6},{6,10},{... | collective-permute-start | bytes 196616 | tf_op jit(solution)/shard_map/ppermute | solution.py:198
  264.9 5.0 %collective-permute-start.8 = (f32[32,512]{1,0:T(8,128)S(1)}, f32[32,512]{1,0:T(8,128)S(1)}, u32[]{:S(2)}, u32[]{:S(2)}) collective-permute-start(f32[32,512]{1,0:T(8,128)S(1)} %convolution_add_fusion), channel_id=1, source_target_pairs={{0,8},{4,12},{8,0},{12,4},{1,9},{5,13},{9,1},{13,5},{2,10},{6,14},... | collective-permute-start | bytes 196616 | tf_op jit(solution)/shard_map/ppermute | solution.py:198
  267.0 3.4 %collective-permute-start.9 = (f32[32,512]{1,0:T(8,128)S(1)}, f32[32,512]{1,0:T(8,128)S(1)}, u32[]{:S(2)}, u32[]{:S(2)}) collective-permute-start(f32[32,512]{1,0:T(8,128)S(1)} %convolution_add_fusion), channel_id=1, source_target_pairs={{0,12},{4,0},{8,4},{12,8},{1,13},{5,1},{9,5},{13,9},{2,14},{6,2},{... | collective-permute-start | bytes 196616 | tf_op jit(solution)/shard_map/ppermute | solution.py:198
  270.5 6.9 %collective-permute-start.10 = (f32[32,512]{1,0:T(8,128)S(1)}, f32[32,512]{1,0:T(8,128)S(1)}, u32[]{:S(2)}, u32[]{:S(2)}) collective-permute-start(f32[32,512]{1,0:T(8,128)S(1)} %add_add_fusion.1), channel_id=1, source_target_pairs={{0,16},{16,32},{32,48},{48,0},{1,17},{17,33},{33,49},{49,1},{2,18}... | collective-permute-start | bytes 196616 | tf_op jit(solution)/shard_map/ppermute | solution.py:198
  270.6 9.1 %collective-permute-start.11 = (f32[32,512]{1,0:T(8,128)S(1)}, f32[32,512]{1,0:T(8,128)S(1)}, u32[]{:S(2)}, u32[]{:S(2)}) collective-permute-start(f32[32,512]{1,0:T(8,128)S(1)} %add_add_fusion.1), channel_id=1, source_target_pairs={{0,32},{16,48},{32,0},{48,16},{1,33},{17,49},{33,1},{49,17},{2,34}... | collective-permute-start | bytes 196616 | tf_op jit(solution)/shard_map/ppermute | solution.py:198
  274.6 5.0 %collective-permute-start.12 = (f32[32,512]{1,0:T(8,128)S(1)}, f32[32,512]{1,0:T(8,128)S(1)}, u32[]{:S(2)}, u32[]{:S(2)}) collective-permute-start(f32[32,512]{1,0:T(8,128)S(1)} %add_add_fusion.1), channel_id=1, source_target_pairs={{0,48},{16,0},{32,16},{48,32},{1,49},{17,1},{33,17},{49,33},{2,50}... | collective-permute-start | bytes 196616 | tf_op jit(solution)/shard_map/ppermute | solution.py:198
  279.7 23.5 %collective-permute-start.13 = (f32[32,512]{1,0:T(8,128)S(1)}, f32[32,512]{1,0:T(8,128)S(1)}, u32[]{:S(2)}, u32[]{:S(2)}) collective-permute-start(f32[32,512]{1,0:T(8,128)S(1)} %add_add_fusion), channel_id=1, source_target_pairs={{0,128},{128,0},{1,129},{129,1},{2,130},{130,2},{3,131},{131,3},{4... | collective-permute-start | bytes 196616 | tf_op jit(solution)/shard_map/ppermute | solution.py:198
  279.8 27.4 %collective-permute-start.6 = (bf16[2,32,256]{2,1,0:T(8,128)(2,1)S(1)}, bf16[2,32,256]{2,1,0:T(8,128)(2,1)S(1)}, u32[]{:S(2)}, u32[]{:S(2)}) collective-permute-start(bf16[2,32,256]{2,1,0:T(8,128)(2,1)S(1)} %broadcast_select_fusion.7), channel_id=1, source_target_pairs={{0,64},{64,0},{1,65},{65,1},{2,66},{66,2},{3,67},{67,3},{4,68},{68... | collective-permute-start | bytes 98312 | tf_op jit(solution)/shard_map/ppermute | solution.py:205
  303.4 4.6 %collective-permute-start.14 = (f32[32,512]{1,0:T(8,128)S(1)}, f32[32,512]{1,0:T(8,128)S(1)}, u32[]{:S(2)}, u32[]{:S(2)}) collective-permute-start(f32[32,512]{1,0:T(8,128)S(1)} %fusion.3), channel_id=1, source_target_pairs={{0,64},{64,0},{1,65},{65,1},{2,66},{66,2},{3,67},{67,3},{4,68},{68... | collective-permute-start | bytes 196616 | tf_op jit(solution)/shard_map/ppermute | solution.py:205
  308.8 4.9 %collective-permute-start.15 = (f32[8,128]{1,0:T(8,128)S(1)}, f32[8,128]{1,0:T(8,128)S(1)}, u32[]{:S(2)}, u32[]{:S(2)}) collective-permute-start(f32[8,128]{1,0:T(8,128)S(1)} %pad_maximum_fusion.3), channel_id=1, source_target_pairs={{0,1},{1,2},{2,3},{3,0},{4,5},{5,6},{6,7},{7,4},{8,9},{9,10},{10,1... | collective-permute-start | bytes 12296 | tf_op jit(solution)/shard_map/ppermute | solution.py:198
  310.0 4.0 %collective-permute-start.16 = (f32[8,128]{1,0:T(8,128)S(1)}, f32[8,128]{1,0:T(8,128)S(1)}, u32[]{:S(2)}, u32[]{:S(2)}) collective-permute-start(f32[8,128]{1,0:T(8,128)S(1)} %pad_maximum_fusion.3), channel_id=1, source_target_pairs={{0,2},{1,3},{2,0},{3,1},{4,6},{5,7},{6,4},{7,5},{8,10},{9,11},{10,... | collective-permute-start | bytes 12296 | tf_op jit(solution)/shard_map/ppermute | solution.py:198
  312.5 2.8 collective-permute-start.17
